TPU v7x, 32 devices: a whole 2x2x4 slice. The times are simulated.
32 devices in a mesh: dp: 2 (over core), space: 16 (over z, y, x).
Axes of the slice: x: 2, y: 2, z: 4, core: 2. Of those that a mesh axis runs over, the one named last changes fastest.
Arguments:
- master: float32 [1156352], P(('dp', 'space')), may hold values from -0.375 to 0.375
- moment1: float32 [1156352], P(('dp', 'space')), may hold values from -7.6293945e-05 to 7.6293945e-05
- moment2: float32 [1156352], P(('dp', 'space')), may hold values from 2.1619713e-12 to 8.647885e-12
- inputs: bfloat16 [2, 78, 8192], P('dp', None, 'space'), may hold values from -6 to 6
- targets: bfloat16 [2, 78, 8192], P('dp', None, 'space'), may hold values from -6 to 6
- valid: int32 [2, 78, 8192], P('dp', None, 'space'), may hold values from 0 to 1
- owner: int32 [2, 8192, 1], P('dp', 'space'), may hold values from 0 to 15; in each aligned block of 512 rows (0 to 511, 512 to 1023, ..., all dimensions but the last counted through in order) at most 64 rows name the same one
- slot: int32 [2, 8192], P('dp', 'space'), may hold values from 0 to 2047
- neighbours: int32 [32768, 6], P('space'), may hold values from 0 to 32767, as said below
- partner: int32 [8192], P('space'), may hold values from 0 to 8191, as said below
Outputs:
- loss_total: float32 [1], replicated
- valid_count: float32 [1], replicated
- grad_norm: float32 [1], replicated
- new_master: float32 [1156352], P(('dp', 'space'))
- new_moment1: float32 [1156352], P(('dp', 'space'))
- new_moment2: float32 [1156352], P(('dp', 'space'))
- new_copy: bfloat16 [1156352], P(('dp', 'space'))
- final_mesh: float32 [2, 32768, 256], P('dp', 'space')
- node_grads: float32 [2, 32768, 256], P('dp', 'space')
- pred_grads: float32 [2, 78, 8192], P('dp', None, 'space')
Inputs may be any that keep to these rules, and one draw needn't show every extreme that they name: `neighbours`: each entry is a node number within 2048 of its row's own number, counted cyclically over 32768; a distance of exactly 2048 occurs in both directions. partner[g] - g lies in 358 to 360; where that passes the last point, partner[g] = g.
All inputs are finite; a program needn't handle non-finite values.
Results may differ from a plain program's by a relative error of at most 0.014.
Values may be sent and summed in bfloat16 or wider, within the bound.
No kernel may reach another device: no remote copies, remote signals or barrier semaphores. Data moves between devices by JAX's collectives and lax.ppermute only.
A program may use at most 192 MiB of HBM per device.

v0:
```python
import functools

import jax
import jax.numpy as jnp
from jax import lax
from jax.experimental import pallas as pl
from jax.experimental.pallas import tpu as pltpu
from jax.sharding import PartitionSpec as P

D = 256
HALF = 128
CH = 78
ROUNDS = 3
K = 6
ROWW = 360
NEAR = 358
STEP = 10
H = 2048
ALL = ("dp", "space")
LIMIT = pltpu.CompilerParams(vmem_limit_bytes=60 * 2**20)


def cost(micros):
    return pl.CostEstimate(flops=0, bytes_accessed=micros * 3_000_000, transcendentals=0)


def inner(left, right, left_dim, right_dim):
    return lax.dot_general(
        left, right, (((left_dim,), (right_dim,)), ((), ())), preferred_element_type=jnp.float32
    )


def sigmoid(value):
    return 0.5 * jnp.tanh(0.5 * value) + 0.5


def silu(value):
    return value * sigmoid(value)


def slope(value):
    sigma = sigmoid(value)
    return sigma * (1.0 + value * (1.0 - sigma))


def shifted(shard, axis, by):
    peers = lax.axis_size(axis)
    pairs = [(i, i + by) for i in range(peers) if 0 <= i + by < peers]
    return lax.ppermute(shard, axis, pairs)


def walk_of(mesh):
    count = mesh.shape["space"]
    chips = [getattr(device, "coords", None) for device in mesh.devices[0].reshape(-1)]
    if any(chip is None for chip in chips) or len(set(map(tuple, chips))) != count:
        return list(range(count))
    at = {tuple(chip): n for n, chip in enumerate(chips)}
    xs, ys, zs = (sorted({chip[n] for chip in at}) for n in range(3))
    if len(xs) * len(ys) * len(zs) != count:
        return list(range(count))
    if (len(xs), len(ys), len(zs)) == (2, 2, 4):
        corners = [(0, 0), (1, 0), (0, 1), (1, 1)]
        planes = [(0, 1, 3, 2), (2, 0, 1, 3), (3, 1, 0, 2), (2, 3, 1, 0)]
        steps = [(*corners[n], z) for z, plane in enumerate(planes) for n in plane]
        return [at[(xs[x], ys[y], zs[z])] for x, y, z in steps]
    walk, plane = [], []
    for n, y in enumerate(ys):
        plane = plane + [(x, y) for x in (xs if n % 2 == 0 else xs[::-1])]
    for n, z in enumerate(zs):
        walk = walk + [at[(x, y, z)] for x, y in (plane if n % 2 == 0 else plane[::-1])]
    return walk


def halo(walk, last, initial):
    up = list(zip(walk, walk[1:] + walk[:1]))
    down = [(j, i) for i, j in up]
    return lax.ppermute(last, "space", up), lax.ppermute(initial, "space", down)


def pieces_of(total, peers):
    share = total // peers
    starts = [share * d // D for d in range(peers)]
    counts = [-(-share * (d + 1) // D) - starts[d] for d in range(peers)]
    shared = [share * d % D != 0 for d in range(peers)]
    height = -(-max(counts) // 16) * 16
    return starts, counts, shared, height


def parts_of():
    return [CH, D, D, CH] + [5 * D] * ROUNDS + [3 + 2 * ROUNDS]


def swapped(value, axis, bit):
    return lax.ppermute(value, axis, [(i, i ^ bit) for i in range(lax.axis_size(axis))])


def bits_of(axis):
    return [1 << n for n in range(lax.axis_size(axis).bit_length() - 1)]


def others(value, axis, bits):
    masks = [sum(bit for n, bit in enumerate(bits) if m >> n & 1) for m in range(1, 1 << len(bits))]
    return [swapped(value, axis, mask) for mask in masks]


def upper_groups():
    bits = bits_of("space")[2:]
    return [tuple(bits[n : n + 2]) for n in range(0, len(bits), 2)]


def orders():
    return [(1, 2), (2, 1)]


def summed_everywhere(value, arriving):
    for bits in reversed(upper_groups()):
        value = sum(others(value, "space", bits), value)
    value = value + swapped(value, "dp", 1)
    value, arriving = lax.optimization_barrier((value, arriving))
    return sum(others(value, "space", (1, 2)), value), arriving


def gathered_blocks(piece, posted):
    held, weights, size = piece[None], {}, 1
    for bits in reversed(upper_groups()):
        held = jnp.concatenate([held] + others(held, "space", bits), 0)
        for n, bit in enumerate(bits):
            weights[bit] = size << n
        size = size << len(bits)
    half = piece.shape[0] // 2
    held = [held[:, :half], held[:, half:]]
    ranks = [dict(weights), dict(weights)]
    for turn in (1, 0):
        if turn == 0:
            held[0], held[1], posted = lax.optimization_barrier((*held, posted))
        for n, order in enumerate(orders()):
            held[n] = jnp.concatenate([held[n], swapped(held[n], "space", order[turn])], 0)
            ranks[n][order[turn]] = size
        size = size << 1
    return (held, [swapped(part, "dp", 1) for part in held], ranks), posted


def spread_rows(gathered, total, peers, place):
    (first, second), (first_far, second_far), ranks = gathered
    starts, counts, shared, height = pieces_of(total, peers)
    half, group = height // 2, first.shape[0]
    rows = -(-total // D)
    sizes = parts_of()
    def at(rank, relative):
        spot = 0
        for bit, weight in rank.items():
            spot = spot + jnp.where((relative & bit) != 0, weight, 0)
        return spot

    def body(place_ref, *refs):
        sources, outs, buffer = refs[:4], refs[4:-1], refs[-1]
        me = place_ref[0]
        mine = me // group
        for d in range(peers):
            relative = (me ^ d) & (group - 1)
            spots = [at(rank, relative) for rank in ranks]

            def lay(one, two, d=d, spots=spots):
                piece = jnp.concatenate([one[spots[0]], two[spots[1]]], 0).astype(jnp.float32)
                start, count = starts[d], counts[d]
                if shared[d]:
                    buffer[start : start + 1, :] = buffer[start : start + 1, :] + piece[:1]
                    buffer[start + 1 : start + count, :] = piece[1:count]
                else:
                    buffer[start : start + count, :] = piece[:count]

            @pl.when(mine == d // group)
            def _():
                lay(sources[0], sources[1])

            @pl.when(mine != d // group)
            def _():
                lay(sources[2], sources[3])

        start = 0
        for out, size in zip(outs, sizes):
            out[:size, :] = buffer[start : start + size, :].astype(out.dtype)
            if out.shape[0] > size:
                out[size:, :] = jnp.zeros((out.shape[0] - size, D), out.dtype)
            start = start + size

    kinds = [jnp.bfloat16] * (4 + ROUNDS) + [jnp.float32]
    talls = [HALF] + sizes[1:]
    return pl.pallas_call(
        body,
        grid_spec=pltpu.PrefetchScalarGridSpec(
            num_scalar_prefetch=1,
            grid=(1,),
            in_specs=[whole(first.shape)] * 4,
            out_specs=[whole((tall, D)) for tall in talls],
            scratch_shapes=[pltpu.VMEM((-(-rows // 8) * 8 + 8, D), jnp.float32)],
        ),
        out_shape=[jax.ShapeDtypeStruct((tall, D), kind) for tall, kind in zip(talls, kinds)],
        compiler_params=LIMIT,
        cost_estimate=cost(4),
        name="spread_rows",
    )(place.reshape(1), first, second, first_far, second_far)


def collect_rows(parts, total, peers, place):
    starts, counts, shared, height = pieces_of(total, peers)
    rows = -(-total // D)
    sizes = [min(part.shape[0], size) for part, size in zip(parts, tall_parts())]
    group = lax.axis_size("space")

    def body(place_ref, *refs):
        sources, keep, send, buffer = refs[:-3], refs[-3], refs[-2], refs[-1]
        start = 0
        for source, size in zip(sources, sizes):
            buffer[start : start + size, :] = source[:size, :]
            start = start + size
        if buffer.shape[0] > start:
            buffer[start:, :] = jnp.zeros((buffer.shape[0] - start, D), jnp.float32)
        me = place_ref[0]
        mine = me // group
        for d in range(peers):
            relative = (me ^ d) & (group - 1)

            @pl.when(mine == d // group)
            def _():
                keep[relative] = buffer[starts[d] : starts[d] + height, :]

            @pl.when(mine != d // group)
            def _():
                send[relative] = buffer[starts[d] : starts[d] + height, :].astype(jnp.bfloat16)

    shape = (group, height, D)
    return pl.pallas_call(
        body,
        grid_spec=pltpu.PrefetchScalarGridSpec(
            num_scalar_prefetch=1,
            grid=(1,),
            in_specs=[whole(part.shape) for part in parts],
            out_specs=[whole(shape), whole(shape)],
            scratch_shapes=[pltpu.VMEM((-(-rows // 8) * 8 + height + 8, D), jnp.float32)],
        ),
        out_shape=[
            jax.ShapeDtypeStruct(shape, jnp.float32),
            jax.ShapeDtypeStruct(shape, jnp.bfloat16),
        ],
        compiler_params=LIMIT,
        cost_estimate=cost(5),
        name="collect_rows",
    )(place.reshape(1), *parts)


def reduced_piece(keep, send, leaving):
    kept = keep + swapped(send, "dp", 1).astype(jnp.float32)
    half = kept.shape[1] // 2
    groups = upper_groups()
    inner_shape = (kept.shape[0] // 4, 2, 2, half, D)
    parts = [kept[:, :half].reshape(inner_shape), kept[:, half:].reshape(inner_shape)]
    for n, order in enumerate(orders()):
        for bit in order:
            spot = 2 if bit == 1 and parts[n].ndim == 5 else 1
            stay = lax.index_in_dim(parts[n], 0, spot, keepdims=False)
            leave = lax.index_in_dim(parts[n], 1, spot, keepdims=False)
            parts[n] = stay + swapped(leave.astype(jnp.bfloat16), "space", bit).astype(jnp.float32)
    part = jnp.concatenate(parts, 1)
    part, leaving = lax.optimization_barrier((part, leaving))
    for bits in groups:
        part = part.reshape((-1, 1 << len(bits)) + part.shape[1:])
        masks = [sum(bit for n, bit in enumerate(bits) if m >> n & 1) for m in range(1 << len(bits))]
        low = part.astype(jnp.bfloat16)
        part = sum(
            [
                swapped(low[:, m], "space", mask).astype(jnp.float32)
                for m, mask in enumerate(masks)
                if m
            ],
            part[:, 0],
        )
    return part[0], leaving


def tall_parts():
    return [CH, D, D, CH] + [D, 4 * D] * ROUNDS + [2, 1] + [2] * ROUNDS


def weave(ref, value):
    rows = value.shape[0]
    ref[pl.ds(0, rows, stride=2), :] = value[:, :HALF]
    ref[pl.ds(1, rows, stride=2), :] = value[:, HALF:]


def unweave(ref):
    rows = ref.shape[0] // 2
    return ref[pl.ds(0, rows, stride=2), :], ref[pl.ds(1, rows, stride=2), :]


def selector():
    row = lax.broadcasted_iota(jnp.int32, (8, HALF), 0)
    lane = lax.broadcasted_iota(jnp.int32, (8, HALF), 1)
    slot = jnp.where(lane == CH, 64.0, jnp.where(lane == CH + 1, 1.0, 0.0))
    known = jnp.where(lane == CH + 2, 1.0, 0.0)
    return jnp.where(row == 0, slot, jnp.where(row == 1, known, 0.0)).astype(jnp.bfloat16)


def ids_along(arrived):
    codes = inner(selector(), arrived, 1, 1)
    return jnp.where(codes[1:2, :] > 0, codes[0:1, :], -1.0).astype(jnp.int32)


def ids_down(arrived):
    codes = inner(arrived, selector(), 1, 1)
    return jnp.where(codes[:, 1:2] > 0, codes[:, 0:1], -1.0).astype(jnp.int32)


def whole(shape):
    return pl.BlockSpec(shape, lambda *_: (0,) * len(shape))


def node_terms(mesh, mats, bias):
    blocks = mesh.shape[0]
    tile = 1024

    def body(mesh_ref, mats_ref, bias_ref, dest_ref, self_ref):
        lowered = mesh_ref[...].astype(jnp.bfloat16)
        weave(dest_ref, inner(lowered, mats_ref[1], 1, 0) + bias_ref[0:1, :])
        self_ref[...] = inner(lowered, mats_ref[3], 1, 0) + bias_ref[1:2, :]

    rows = pl.BlockSpec((tile, D), lambda i: (i, 0))
    woven = pl.BlockSpec((2 * tile, HALF), lambda i: (i, 0))
    return pl.pallas_call(
        body,
        grid=(blocks // tile,),
        in_specs=[rows, whole(mats.shape), whole(bias.shape)],
        out_specs=[woven, rows],
        out_shape=[
            jax.ShapeDtypeStruct((2 * blocks, HALF), jnp.float32),
            jax.ShapeDtypeStruct((blocks, D), jnp.float32),
        ],
        compiler_params=LIMIT,
        cost_estimate=cost(4),
        name="node_terms",
    )(mesh, mats, bias)


def round_forward(index, mesh, pieces, mats, terms, following, decoder=(), half=None, into=()):
    blocks = mesh.shape[0]
    tile, chunk = 512, 16
    turns, high = tile // chunk, 2 * chunk
    more = following is not None
    reach = 2 * (blocks + 2 * H)
    steps = blocks // tile if half is None else blocks // tile // 2
    shift = 0 if half is None else half * steps

    def body(index_ref, mesh_ref, *refs):
        sources, refs = refs[: len(pieces)], refs[len(pieces) :]
        (mats_ref, dest_ref, self_ref), refs = refs[:3], refs[3:]
        table, rows, wide = refs[-3:]
        if more:
            next_ref, refs = refs[0], refs[1 + len(into) :]
            new_ref, back_ref, update_ref, agg_ref, slope_ref, sent_ref = refs[:6]
        else:
            ids_ref, dec_ref, out_ref, head_ref = refs[:4]
            new_ref, back_ref, update_ref, agg_ref, slope_ref = refs[4:9]
            branch_ref, fetched_ref, decoded_ref, turn_ref, total_ref = refs[9:14]
        step = pl.program_id(0)

        @pl.when(step == 0)
        def _():
            for source, (_, start) in zip(sources, pieces):

                @pl.loop(0, source.shape[0] // 256)
                def _(i, source=source, start=start):
                    at = pl.multiple_of(i * 256, 256)
                    to = pl.multiple_of(start + at, 256)
                    table[pl.ds(to, 256), :] = source[pl.ds(at, 256), :].astype(jnp.float32)

        mesh_in = mesh_ref[...]

        def fetch(turn):
            for edge in range(K):
                base = edge * blocks + (step + shift) * tile + turn * chunk
                spots = [index_ref[base + u] for u in range(chunk)]
                values = [table[pl.ds(pl.multiple_of(spot, 2), 2), :] for spot in spots]
                for u in range(chunk):
                    spot = pl.multiple_of(edge * 2 * tile + turn * high + 2 * u, 2)
                    rows[pl.ds(spot, 2), :] = values[u]

        def load(turn):
            at = pl.multiple_of(turn * high, high)
            taken = [
                rows[pl.ds(pl.multiple_of(edge * 2 * tile + turn * high, high), high), :]
                for edge in range(K)
            ]
            return at, dest_ref[pl.ds(at, high), :], taken

        def dense(at, dest, taken):
            total = None
            for edge in range(K):
                value = taken[edge] + dest
                sigma = sigmoid(value)
                out = value * sigma
                slope_ref[edge, pl.ds(at, high), :] = (sigma + out * (1.0 - sigma)).astype(
                    jnp.bfloat16
                )
                total = out if total is None else total + out
            wide[pl.ds(at, high), :] = total * (1.0 / K)

        def some(turn, carry):
            loaded = load(turn - 1)
            fetch(turn)
            dense(*loaded)
            return carry

        fetch(0)
        lax.fori_loop(1, turns, some, 0)
        dense(*load(turns - 1))
        first, second = unweave(wide)
        first, second = first.astype(jnp.bfloat16), second.astype(jnp.bfloat16)
        agg_ref[:, :HALF] = first
        agg_ref[:, HALF:] = second
        update_in = (
            inner(first, mats_ref[2, :HALF, :], 1, 0)
            + inner(second, mats_ref[2, HALF:, :], 1, 0)
            + self_ref[...]
        )
        sigma = sigmoid(update_in)
        out = update_in * sigma
        back_ref[...] = sigma + out * (1.0 - sigma)
        update = out.astype(jnp.bfloat16)
        update_ref[...] = update
        new = mesh_in + inner(update, mats_ref[4], 1, 0)
        new_ref[...] = new
        lowered = new.astype(jnp.bfloat16)
        if more:
            weave(wide, inner(lowered, next_ref[0], 1, 0))
            sent_ref[...] = wide[...].astype(jnp.bfloat16)
            return
        nodes = lax.broadcasted_iota(jnp.int32, (ids_ref.shape[0], tile), 1) + step * tile
        chooser = jnp.where(nodes == ids_ref[...], 1.0, 0.0).astype(jnp.bfloat16)
        found = inner(chooser, lowered, 1, 0)

        @pl.when(step == 0)
        def _():
            total_ref[...] = found

        @pl.when(step > 0)
        def _():
            total_ref[...] += found

        @pl.when(step == blocks // tile - 1)
        def _():
            fetched = total_ref[...].astype(jnp.bfloat16)
            fetched_ref[...] = fetched
            value = inner(fetched, dec_ref[...], 1, 0) + head_ref[2:3, :]
            sigma = sigmoid(value)
            out = value * sigma
            turn_ref[...] = sigma + out * (1.0 - sigma)
            decoded = out.astype(jnp.bfloat16)
            decoded_ref[...] = decoded
            branch_ref[...] = inner(decoded, out_ref[...], 1, 0).astype(jnp.bfloat16)

    whole_rows = pl.BlockSpec((tile, D), lambda i, *_: (i + shift, 0))
    woven = pl.BlockSpec((2 * tile, HALF), lambda i, *_: (i + shift, 0))
    ins = [whole_rows] + [pl.BlockSpec(memory_space=pltpu.VMEM)] * len(pieces)
    ins = ins + [whole(mats.shape), woven, whole_rows]
    outs = [whole_rows] * 4 + [pl.BlockSpec((K, 2 * tile, HALF), lambda i, *_: (0, i + shift, 0))]
    shapes = [
        jax.ShapeDtypeStruct((blocks, D), jnp.float32),
        jax.ShapeDtypeStruct((blocks, D), jnp.float32),
        jax.ShapeDtypeStruct((blocks, D), jnp.bfloat16),
        jax.ShapeDtypeStruct((blocks, D), jnp.bfloat16),
        jax.ShapeDtypeStruct((K, 2 * blocks, HALF), jnp.bfloat16),
    ]
    args = [index, mesh] + [rows for rows, _ in pieces] + [mats, *terms]
    if more:
        ins.append(pl.BlockSpec((1, D, D), lambda *_: (0, 0, 0)))
        outs.append(pl.BlockSpec((2 * tile, HALF), lambda i, *_: (i, 0)))
        shapes.append(jax.ShapeDtypeStruct((2 * tile * steps, HALF), jnp.bfloat16))
        args.append(following)
    aliases = {len(args) + n: n for n in range(len(into))}
    ins = ins + [pl.BlockSpec(memory_space=pl.ANY)] * len(into)
    args = args + list(into)
    scratch = []
    if decoder:
        posts = decoder[0].shape[0]
        ins = ins + [whole(arg.shape) for arg in decoder]
        args = args + list(decoder)
        for width, kind in ((HALF, jnp.bfloat16), (D, jnp.bfloat16), (D, jnp.bfloat16), (D, jnp.float32)):
            outs.append(whole((posts, width)))
            shapes.append(jax.ShapeDtypeStruct((posts, width), kind))
        scratch = [pltpu.VMEM((posts, D), jnp.float32)]
    return pl.pallas_call(
        body,
        grid_spec=pltpu.PrefetchScalarGridSpec(
            num_scalar_prefetch=1,
            grid=(steps,),
            in_specs=ins,
            out_specs=outs,
            scratch_shapes=scratch
            + [
                pltpu.VMEM((reach, HALF), jnp.float32),
                pltpu.VMEM((K * 2 * tile, HALF), jnp.float32),
                pltpu.VMEM((2 * tile, HALF), jnp.float32),
            ],
        ),
        out_shape=shapes,
        input_output_aliases=aliases,
        compiler_params=pltpu.CompilerParams(vmem_limit_bytes=54 * 2**20),
        cost_estimate=cost(24 if half is None else 14),
        name="round_forward",
    )(*args)


def edges_backward(index, back, slopes, mats, carried=(), landed=()):
    blocks = back.shape[0]
    tile, chunk = 512, 16
    steps, turns, high = blocks // tile, tile // chunk, 2 * chunk
    reach = 2 * (blocks + 2 * H)

    def body(*refs):
        if carried:
            index_ref, back_ref, slope_ref, mats_ref = refs[:4]
            past, rest = refs[4:9], refs[9:]
            (new_ref, out_ref, sent_ref), rest = rest[:3], rest[3:]
        else:
            index_ref, back_ref, slope_ref, mats_ref = refs[:4]
            (ids_ref, landed_ref, turn_ref, w_out_ref, w_dec_ref), rest = refs[4:9], refs[9:]
            (new_ref, out_ref, gdec_ref), rest = rest[:3], rest[3:]
            gathered, rest = rest[5], rest[:5] + rest[6:]
        guin_ref, low_ref, before_ref, own_ref, after_ref, wide, wider, flows, *tables = rest
        step = pl.program_id(0)

        @pl.when(step == 0)
        def _():
            @pl.loop(0, reach // 256)
            def _(i):
                for table in tables:
                    table[pl.ds(pl.multiple_of(i * 256, 256), 256), :] = jnp.zeros(
                        (256, HALF), jnp.float32
                    )

        if carried:
            new, one, two = ended(*past, wide)
            sent_ref[:, :HALF] = one
            sent_ref[:, HALF:] = two
            new_ref[...] = new
            grad_out = new.astype(jnp.bfloat16)
            out_ref[...] = grad_out
        else:

            @pl.when(step == 0)
            def _():
                grad_dec = inner(landed_ref[...], w_out_ref[...], 1, 1) * turn_ref[...]
                grad_dec = grad_dec.astype(jnp.bfloat16)
                gdec_ref[...] = grad_dec
                gathered[...] = inner(grad_dec, w_dec_ref[...], 1, 1).astype(jnp.bfloat16)

            nodes = lax.broadcasted_iota(jnp.int32, (tile, landed_ref.shape[0]), 0) + step * tile
            chooser = jnp.where(nodes == ids_ref[...], 1.0, 0.0).astype(jnp.bfloat16)
            new = inner(chooser, gathered[...], 1, 0)
            new_ref[...] = new
            grad_out = new.astype(jnp.bfloat16)
            out_ref[...] = grad_out
        grad_uin = (inner(grad_out, mats_ref[4], 1, 1) * back_ref[...]).astype(jnp.bfloat16)
        guin_ref[...] = grad_uin
        weave(wide, inner(grad_uin, mats_ref[2], 1, 1) * (1.0 / K))

        def dense(turn):
            at = pl.multiple_of(turn * high, high)
            grad_agg = wide[pl.ds(at, high), :]
            total, parts = None, []
            for edge in range(K):
                flow = grad_agg * slope_ref[edge, pl.ds(at, high), :].astype(jnp.float32)
                parts.append(flow)
                total = flow if total is None else total + flow
            return at, total, parts

        def keep(turn, at, total, parts):
            for edge in range(K):
                spot = pl.multiple_of(edge * 2 * tile + turn * high, high)
                flows[pl.ds(spot, high), :] = parts[edge]
            wider[pl.ds(at, high), :] = total

        def scatter(turn):
            for u in range(chunk):
                spots, sums = [], []
                for edge in range(K):
                    base = edge * blocks + step * tile + turn * chunk
                    spots.append(pl.multiple_of(index_ref[base + u], 2))
                for edge in range(K):
                    spot = pl.multiple_of(edge * 2 * tile + turn * high + 2 * u, 2)
                    sums.append(tables[edge][pl.ds(spots[edge], 2), :] + flows[pl.ds(spot, 2), :])
                for edge in range(K):
                    tables[edge][pl.ds(spots[edge], 2), :] = sums[edge]

        def some(turn, carry):
            found = dense(turn)
            scatter(turn - 1)
            keep(turn, *found)
            return carry

        keep(0, *dense(0))
        lax.fori_loop(1, turns, some, 0)
        scatter(turns - 1)
        first, second = unweave(wider)
        low_ref[:, :HALF] = first.astype(jnp.bfloat16)
        low_ref[:, HALF:] = second.astype(jnp.bfloat16)

        @pl.when(step == steps - 1)
        def _():
            def summed(at):
                value = tables[0][pl.ds(at, 256), :]
                for table in tables[1:]:
                    value = value + table[pl.ds(at, 256), :]
                return value

            @pl.loop(0, 2 * H // 256)
            def _(i):
                at = pl.multiple_of(i * 256, 256)
                far = pl.multiple_of(2 * H + 2 * blocks + at, 256)
                before_ref[pl.ds(at, 256), :] = summed(at).astype(jnp.bfloat16)
                after_ref[pl.ds(at, 256), :] = summed(far).astype(jnp.bfloat16)

            @pl.loop(0, 2 * blocks // 256)
            def _(i):
                at = pl.multiple_of(i * 256, 256)
                own_ref[pl.ds(at, 256), :] = summed(pl.multiple_of(2 * H + at, 256))

    rows = pl.BlockSpec((tile, D), lambda i, *_: (i, 0))
    woven = pl.BlockSpec((2 * tile, HALF), lambda i, *_: (i, 0))
    low = jax.ShapeDtypeStruct((blocks, D), jnp.bfloat16)
    low_posts = (landed[1].shape[0], D) if landed else None
    last = low if carried else jax.ShapeDtypeStruct(low_posts, jnp.bfloat16)
    return pl.pallas_call(
        body,
        grid_spec=pltpu.PrefetchScalarGridSpec(
            num_scalar_prefetch=1,
            grid=(steps,),
            in_specs=[
                rows,
                pl.BlockSpec((K, 2 * tile, HALF), lambda i, *_: (0, i, 0)),
                whole(mats.shape),
            ]
            + ([rows] + [woven] * 3 + [whole(mats.shape)] if carried else [])
            + [whole(arg.shape) for arg in landed],
            out_specs=([rows] * 3 if carried else [rows, rows, whole(low_posts)])
            + [
                rows, rows,
                whole((2 * H, HALF)), whole((2 * blocks, HALF)), whole((2 * H, HALF)),
            ],
            scratch_shapes=([] if carried else [pltpu.VMEM(low_posts, jnp.bfloat16)])
            + [
                pltpu.VMEM((2 * tile, HALF), jnp.float32),
                pltpu.VMEM((2 * tile, HALF), jnp.float32),
                pltpu.VMEM((2 * tile * K, HALF), jnp.float32),
            ]
            + [pltpu.VMEM((reach, HALF), jnp.float32)] * K,
        ),
        out_shape=[
            jax.ShapeDtypeStruct((blocks, D), jnp.float32),
            low,
            last,
            low,
            low,
            jax.ShapeDtypeStruct((2 * H, HALF), jnp.bfloat16),
            jax.ShapeDtypeStruct((2 * blocks, HALF), jnp.float32),
            jax.ShapeDtypeStruct((2 * H, HALF), jnp.bfloat16),
        ],
        compiler_params=LIMIT,
        cost_estimate=cost(28 if carried else 25),
        name="edges_backward",
    )(index, back, slopes, mats, *carried, *landed)


def ended(part_ref, own_ref, first_ref, last_ref, mats_ref, wide):
    wide[...] = (
        own_ref[...] + first_ref[...].astype(jnp.float32) + last_ref[...].astype(jnp.float32)
    )
    one, two = unweave(wide)
    one, two = one.astype(jnp.bfloat16), two.astype(jnp.bfloat16)
    new = (
        part_ref[...]
        + inner(one, mats_ref[0, :, :HALF], 1, 1)
        + inner(two, mats_ref[0, :, HALF:], 1, 1)
    )
    return new, one, two


def weight_grads(mesh, dest_low, agg, grad_uin, update, leaving, grad_mesh, mats, past=()):
    blocks = mesh.shape[0]
    tile = 512

    def body(mesh_ref, dest_ref, agg_ref, guin_ref, update_ref, out_ref, grad_ref, mats_ref, *refs):
        if past:
            (old_ref, sent_ref), refs = refs[:2], refs[2:]
        part_ref, grads_ref, bias_ref = refs[:3]

        @pl.when(pl.program_id(0) == 0)
        def _():
            for ref in refs[1:]:
                ref[...] = jnp.zeros(ref.shape, jnp.float32)

        lowered = mesh_ref[...].astype(jnp.bfloat16)
        dest, guin = dest_ref[...], guin_ref[...]
        grads_ref[:D, :] += inner(lowered, dest, 0, 0)
        grads_ref[D : 2 * D, :] += inner(agg_ref[...], guin, 0, 0)
        grads_ref[2 * D : 3 * D, :] += inner(lowered, guin, 0, 0)
        grads_ref[3 * D :, :] += inner(update_ref[...], out_ref[...], 0, 0)
        bias_ref[0:1, :] += jnp.sum(dest.astype(jnp.float32), 0, keepdims=True)
        bias_ref[1:2, :] += jnp.sum(guin.astype(jnp.float32), 0, keepdims=True)
        part_ref[...] = (
            grad_ref[...] + inner(guin, mats_ref[3], 1, 1) + inner(dest, mats_ref[1], 1, 1)
        )
        if past:
            refs[3][...] += inner(old_ref[...].astype(jnp.bfloat16), sent_ref[...], 0, 0)

    rows = pl.BlockSpec((tile, D), lambda i: (i, 0))
    shapes = [(4 * D, D), (2, D)] + ([(D, D)] if past else [])
    return pl.pallas_call(
        body,
        grid=(blocks // tile,),
        in_specs=[rows] * 7 + [whole(mats.shape)] + [rows] * len(past),
        out_specs=[rows] + [whole(shape) for shape in shapes],
        out_shape=[jax.ShapeDtypeStruct((blocks, D), jnp.float32)]
        + [jax.ShapeDtypeStruct(shape, jnp.float32) for shape in shapes],
        compiler_params=LIMIT,
        cost_estimate=cost(10),
        name="weight_grads",
    )(mesh, dest_low, agg, grad_uin, update, leaving, grad_mesh, mats, *past)


def decode_grads(decoded, landed, fetched, grad_dec):
    def body(decoded_ref, landed_ref, fetched_ref, grad_ref, gout_ref, gdec_ref, bias_ref):
        gout_ref[...] = inner(decoded_ref[...], landed_ref[...], 0, 0)
        gdec_ref[...] = inner(fetched_ref[...], grad_ref[...], 0, 0)
        bias_ref[...] = jnp.sum(grad_ref[...].astype(jnp.float32), 0, keepdims=True)

    return pl.pallas_call(
        body,
        out_shape=[jax.ShapeDtypeStruct(shape, jnp.float32) for shape in ((D, HALF), (D, D), (1, D))],
        compiler_params=LIMIT,
        cost_estimate=cost(3),
        name="decode_grads",
    )(decoded, landed, fetched, grad_dec)


def encode_rows(arrived, w_in, w_node, biases, source):
    posts = arrived.shape[0]
    tile = 512

    def body(
        arrived_ref, in_ref, node_ref, bias_ref, source_ref,
        mesh_ref, gathered_ref, sent_ref, ids_ref, down_ref, encoded, wide,
    ):
        step = pl.program_id(0)

        @pl.when(step == 0)
        def _():
            entering = inner(arrived_ref[...], in_ref[...], 1, 0) + bias_ref[0:1, :]
            encoded[...] = silu(entering).astype(jnp.bfloat16)
            ids_ref[...] = ids_along(arrived_ref[...])
            down_ref[...] = ids_down(arrived_ref[...])

        nodes = lax.broadcasted_iota(jnp.int32, (tile, posts), 0) + step * tile
        chooser = jnp.where(nodes == ids_ref[...], 1.0, 0.0).astype(jnp.bfloat16)
        gathered = inner(chooser, encoded[...], 1, 0).astype(jnp.bfloat16)
        gathered_ref[...] = gathered
        mesh = silu(inner(gathered, node_ref[...], 1, 0) + bias_ref[1:2, :])
        mesh_ref[...] = mesh
        weave(wide, inner(mesh.astype(jnp.bfloat16), source_ref[0], 1, 0))
        sent_ref[...] = wide[...].astype(jnp.bfloat16)

    rows = pl.BlockSpec((tile, D), lambda i: (i, 0))
    args = (arrived, w_in, w_node, biases, source)
    return pl.pallas_call(
        body,
        grid=(H // tile,),
        in_specs=[whole(arg.shape) for arg in args[:-1]]
        + [pl.BlockSpec((1, D, D), lambda *_: (0, 0, 0))],
        out_specs=[rows, rows, pl.BlockSpec((2 * tile, HALF), lambda i: (i, 0))]
        + [whole((1, posts)), whole((posts, 1))],
        out_shape=[
            jax.ShapeDtypeStruct((H, D), jnp.float32),
            jax.ShapeDtypeStruct((H, D), jnp.bfloat16),
            jax.ShapeDtypeStruct((2 * H, HALF), jnp.bfloat16),
            jax.ShapeDtypeStruct((1, posts), jnp.int32),
            jax.ShapeDtypeStruct((posts, 1), jnp.int32),
        ],
        scratch_shapes=[pltpu.VMEM((posts, D), jnp.bfloat16), pltpu.VMEM((2 * tile, HALF), jnp.float32)],
        compiler_params=LIMIT,
        cost_estimate=cost(5),
        name="encode_rows",
    )(*args)


def encode_backward(carried, mesh, gathered, arrived, ids, w_in, w_node, biases):
    blocks = mesh.shape[0]
    posts = arrived.shape[0]
    tile = 512
    steps = blocks // tile

    def body(
        part_ref, own_ref, first_ref, last_ref, mats_ref,
        mesh_ref, gathered_ref, arrived_ref, ids_ref, in_ref, node_ref, bias_ref,
        new_ref, out_ref, gin_ref, gnode_ref, gbias_ref, gsource_ref, total, wide,
    ):
        step = pl.program_id(0)

        @pl.when(step == 0)
        def _():
            for ref in (total, gnode_ref, gbias_ref, gsource_ref):
                ref[...] = jnp.zeros(ref.shape, jnp.float32)

        new, one, two = ended(part_ref, own_ref, first_ref, last_ref, mats_ref, wide)
        new_ref[...] = new
        out_ref[...] = new.astype(jnp.bfloat16)
        lowered = mesh_ref[...].astype(jnp.bfloat16)
        gsource_ref[:, :HALF] += inner(lowered, one, 0, 0)
        gsource_ref[:, HALF:] += inner(lowered, two, 0, 0)
        node_in = inner(gathered_ref[...], node_ref[...], 1, 0) + bias_ref[1:2, :]
        grad_node = (new * slope(node_in)).astype(jnp.bfloat16)
        gbias_ref[1:2, :] += jnp.sum(grad_node.astype(jnp.float32), 0, keepdims=True)
        gnode_ref[...] += inner(gathered_ref[...], grad_node, 0, 0)
        back = inner(grad_node, node_ref[...], 1, 1).astype(jnp.bfloat16)
        nodes = lax.broadcasted_iota(jnp.int32, (posts, tile), 1) + step * tile
        chooser = jnp.where(nodes == ids_ref[...], 1.0, 0.0).astype(jnp.bfloat16)
        total[...] += inner(chooser, back, 1, 0)

        @pl.when(step == steps - 1)
        def _():
            entering = inner(arrived_ref[...], in_ref[...], 1, 0) + bias_ref[0:1, :]
            grad_enc = (total[...] * slope(entering)).astype(jnp.bfloat16)
            gbias_ref[0:1, :] = jnp.sum(grad_enc.astype(jnp.float32), 0, keepdims=True)
            gin_ref[...] = inner(arrived_ref[...], grad_enc, 0, 0)

    rows = pl.BlockSpec((tile, D), lambda i: (i, 0))
    woven = pl.BlockSpec((2 * tile, HALF), lambda i: (i, 0))
    args = (arrived, ids, w_in, w_node, biases)
    shapes = [(HALF, D), (D, D), (2, D), (D, D)]
    return pl.pallas_call(
        body,
        grid=(steps,),
        in_specs=[rows] + [woven] * 3 + [whole(carried[4].shape), rows, rows]
        + [whole(arg.shape) for arg in args],
        out_specs=[rows, rows] + [whole(shape) for shape in shapes],
        out_shape=[
            jax.ShapeDtypeStruct((blocks, D), jnp.float32),
            jax.ShapeDtypeStruct((blocks, D), jnp.bfloat16),
        ]
        + [jax.ShapeDtypeStruct(shape, jnp.float32) for shape in shapes],
        scratch_shapes=[pltpu.VMEM((posts, D), jnp.float32), pltpu.VMEM((2 * tile, HALF), jnp.float32)],
        compiler_params=LIMIT,
        cost_estimate=cost(10),
        name="encode_backward",
    )(*carried, mesh, gathered, *args)


def shards(walk, master, moment1, moment2, inputs, targets, valid, owner, slot, neighbours, partner):
    bands = lax.axis_size("space")
    band = lax.axis_index("space")
    peers = lax.axis_size(ALL)
    place = lax.axis_index(ALL)
    shard = master.shape[0]
    total_size = shard * peers
    height = pieces_of(total_size, peers)[3]
    offset = lax.rem(lax.rem(shard, D) * place, D)
    piece = lax.dynamic_update_slice_in_dim(
        jnp.zeros((height * D,), jnp.bfloat16), master.astype(jnp.bfloat16), offset, 0
    )
    state_in = inputs[0]
    counted = valid[0].astype(jnp.float32)
    local_count = jnp.sum(valid[0])
    digits = (local_count >> jnp.array([16, 8, 0], jnp.int32)) & 255
    digits = jnp.pad(digits, (CH + 3, HALF - CH - 6)).astype(jnp.float32)[None, :]
    points = state_in.shape[1]
    blocks = neighbours.shape[0]
    assert blocks == H
    capacity = max(2, 2 * points // bands)
    target_band = owner[0, :, 0]
    hits = (target_band[:, None] == jnp.arange(bands, dtype=jnp.int32)[None, :]).astype(jnp.int32)
    ranks = jnp.sum(jnp.cumsum(hits, 0) * hits, 1) - 1
    places_out = jnp.sum(hits * jnp.asarray(walk, jnp.int32)[None, :], 1) * capacity + ranks
    poster = (
        jnp.arange(bands * capacity, dtype=jnp.int32)[:, None] == places_out[None, :]
    ).astype(jnp.bfloat16)
    spots = slot[0][None, :]
    columns = jnp.concatenate(
        [
            state_in,
            (spots // 64).astype(jnp.bfloat16),
            (spots % 64).astype(jnp.bfloat16),
            jnp.ones((1, points), jnp.bfloat16),
            jnp.zeros((HALF - CH - 3, points), jnp.bfloat16),
        ],
        0,
    )

    def exchanged(rows):
        return lax.all_to_all(
            rows.reshape(bands, capacity, HALF), "space", split_axis=0, concat_axis=0, tiled=True
        ).reshape(bands * capacity, HALF)

    held, posted = gathered_blocks(
        piece.reshape(height, D), (inner(poster, columns, 1, 1) + digits).astype(jnp.bfloat16)
    )
    arrived = exchanged(posted)
    w_in, w_node, w_dec, w_out, *w_round, biases = spread_rows(
        held, total_size, peers, place
    )
    arrived, biases = lax.optimization_barrier((arrived, biases))
    counts = arrived.reshape(bands, capacity, HALF)[:, 0, CH + 3 : CH + 6].astype(jnp.float32)
    counts = jnp.sum(counts, 0, keepdims=True)
    w_out = jnp.pad(w_out.reshape(D, CH), ((0, 0), (0, HALF - CH)))
    w_round = [mats.reshape(5, D, D) for mats in w_round]
    b_head = biases[:3]
    b_round = biases[3:].reshape(ROUNDS, 2, D)
    mesh, gathered, sent, ids_row, ids = encode_rows(
        arrived, w_in, w_node, biases, w_round[0]
    )
    sent, partner, neighbours, counted, counts = lax.optimization_barrier(
        (sent, partner, neighbours, counted, counts)
    )
    counts = counts + swapped(counts, "dp", 1)
    index = 2 * ((neighbours - band * blocks + H) % (blocks * bands)).T.reshape(-1)
    moved = [(n, place) for n, place in enumerate(walk) if n != place]
    stays = jnp.asarray([n == place for n, place in enumerate(walk)])[band]
    index = lax.ppermute(index, "space", list(enumerate(walk)))

    def at_home(rows):
        return lax.ppermute(rows, "space", [(j, i) for i, j in moved])

    def settled(own, came):
        return jnp.where(stays, own, came.astype(jnp.float32))

    partner_by = partner - band * points - jnp.arange(points, dtype=jnp.int32)
    coded = jnp.where(partner_by >= NEAR, partner_by - NEAR + 1, 0).astype(jnp.bfloat16)
    low_valid = jnp.concatenate([counted.astype(jnp.bfloat16), coded[None, :]], 0)
    valid_around = jnp.concatenate(
        [
            shifted(low_valid[:, points - ROWW :], "space", 1),
            low_valid,
            shifted(low_valid[:, :ROWW], "space", -1),
        ],
        1,
    )
    kept = []
    sent = [sent]
    for layer in range(ROUNDS):
        pieces, start = [], 0
        arrivals = [halo(walk, sent[0], sent[0])]
        if len(sent) > 1:
            sent[1], arrivals[0] = lax.optimization_barrier((sent[1], arrivals[0]))
            arrivals.append(halo(walk, sent[1], sent[1]))
        terms = node_terms(mesh, w_round[layer], b_round[layer])
        if layer == 0:
            (before, after), valid_around, counts = lax.optimization_barrier(
                (arrivals[0], valid_around, counts)
            )
            arrivals = [(before, after)]
        for side in ([rows for rows, _ in arrivals], sent, [rows for _, rows in arrivals]):
            for rows in side:
                pieces.append((rows, start))
                start = start + rows.shape[0]
        mats = w_round[layer]
        if layer + 1 < ROUNDS:
            following = w_round[layer + 1]
            *outs, first = round_forward(index, mesh, pieces, mats, terms, following, half=0)
            *outs, second = round_forward(
                index, mesh, pieces, mats, terms, following, half=1, into=outs
            )
            sent = [first, second]
        else:
            decoder = (ids, w_dec, w_out, biases)
            outs = round_forward(index, mesh, pieces, mats, terms, None, decoder)
            outs, rest = outs[:5], outs[5:]
        kept.append((mesh, *outs[1:]))
        mesh = outs[0]
    count = counts[0, 0] * 65536.0 + counts[0, 1] * 256.0 + counts[0, 2]
    wide_valid = valid_around[:CH].astype(jnp.float32)
    coded = valid_around[CH : CH + 1, : points + ROWW].astype(jnp.float32)
    weights = [
        (
            by,
            jnp.where(coded == by - NEAR + 1, 1.0, 0.0)
            * wide_valid[:, : points + ROWW]
            * wide_valid[:, by : by + points + ROWW],
        )
        for by in range(NEAR, ROWW + 1)
    ]
    branch_rows, fetched, decoded, dec_turn = rest
    returned = exchanged(branch_rows)
    branch = inner(returned, poster, 0, 0)[:CH]
    err = state_in.astype(jnp.float32) + branch - targets[0].astype(jnp.float32)
    def widened(values):
        low = values.astype(jnp.bfloat16)
        before = shifted(low[:, points - ROWW :], "space", 1).astype(jnp.float32)
        after = shifted(low[:, :ROWW], "space", -1).astype(jnp.float32)
        return jnp.concatenate([before, values, after], 1)

    wide_err = widened(err)
    paired = jnp.zeros((CH, points + ROWW), jnp.float32)
    pair_total = jnp.zeros((CH, points), jnp.float32)
    for by, both in weights:
        gap = both * (wide_err[:, : points + ROWW] - wide_err[:, by : by + points + ROWW])
        paired = paired + gap
        pair_total = pair_total + gap[:, ROWW:] * (
            wide_err[:, ROWW : ROWW + points] - wide_err[:, ROWW + by : ROWW + by + points]
        )
    local_total = jnp.sum(counted * err * err) + 0.5 * jnp.sum(pair_total)
    grad_pred = 2.0 * counted * err + paired[:, ROWW:]
    for by, both in weights:
        gap = both * (wide_err[:, : points + ROWW] - wide_err[:, by : by + points + ROWW])
        grad_pred = grad_pred - gap[:, ROWW - by : ROWW - by + points]
    grad_pred = grad_pred / count
    grad_rows = jnp.pad(grad_pred.astype(jnp.bfloat16), ((0, HALF - CH), (0, 0)))
    landed = exchanged(inner(poster, grad_rows, 1, 1).astype(jnp.bfloat16))
    landed, final_mesh = lax.optimization_barrier((landed, mesh.astype(jnp.bfloat16)))
    final_mesh = at_home(final_mesh)
    mats_grads = [None] * (2 * ROUNDS)
    bias_grads = [None] * ROUNDS
    carried = ()
    for layer in reversed(range(ROUNDS)):
        old, back, update, agg, slopes = kept[layer]
        first_step = not carried
        grad_mesh, leaving, extra, grad_uin, dest_low, to_before, own, to_after = edges_backward(
            index, back, slopes, w_round[layer], carried,
            (ids_row, landed, dec_turn, w_out, w_dec) if first_step else (),
        )
        if first_step:
            to_before, to_after, final_mesh = lax.optimization_barrier(
                (to_before, to_after, final_mesh)
            )
        from_before, from_after = halo(walk, to_after, to_before)
        if first_step:
            grad_wout, grad_wdec, grad_bdec = decode_grads(decoded, landed, fetched, extra)
            from_before, final_mesh = lax.optimization_barrier(
                (from_before, settled(mesh, final_mesh))
            )
        past = () if first_step else (kept[layer + 1][0], extra)
        part, mats_grads[2 * layer + 1], bias_grads[layer], *source = weight_grads(
            old, dest_low, agg, grad_uin, update, leaving, grad_mesh, w_round[layer], past
        )
        if past:
            mats_grads[2 * layer + 2] = source[0]
        carried = (part, own, from_before, from_after, w_round[layer])
    grad_mesh, leaving, grad_win, grad_wnode, grad_bpair, mats_grads[0] = encode_backward(
        carried, kept[0][0], gathered, arrived, ids, w_in, w_node, biases
    )
    parts = [grad_win, grad_wnode, grad_wdec, grad_wout[:, :CH].reshape(CH, D)]
    parts = parts + mats_grads
    parts = parts + [grad_bpair, grad_bdec] + bias_grads
    keep, send = collect_rows(parts, total_size, peers, place)
    mine, leaving = reduced_piece(keep, send, leaving)
    late = at_home(leaving)
    mine = lax.dynamic_slice_in_dim(mine.reshape(-1), offset, shard)
    lane = lax.broadcasted_iota(jnp.int32, (8, HALF), 1)
    sums, late = summed_everywhere(
        jnp.where(lane == 0, local_total, jnp.sum(mine * mine)), late
    )
    total, norm = sums[0, 0], jnp.sqrt(sums[0, 1])
    node_grads = settled(grad_mesh, late)
    clipped = mine * jnp.minimum(1.0, 0.05 / norm)
    first = 0.9 * moment1 + 0.1 * clipped
    second = 0.999 * moment2 + 0.001 * clipped * clipped
    first_hat = first / (1.0 - 0.9**STEP)
    second_hat = second / (1.0 - 0.999**STEP)
    updated = master - 0.1 * (first_hat / (jnp.sqrt(second_hat) + 1e-08) + 0.1 * master)
    return (
        total.reshape(1),
        count.reshape(1),
        norm.reshape(1),
        updated,
        first,
        second,
        updated.astype(jnp.bfloat16),
        final_mesh.reshape(1, blocks, D),
        node_grads.reshape(1, blocks, D),
        grad_pred.reshape(1, grad_pred.shape[0], points),
    )


def solution(mesh):
    return jax.shard_map(
        functools.partial(shards, walk_of(mesh)),
        mesh=mesh,
        in_specs=(
            P(("dp", "space")),
            P(("dp", "space")),
            P(("dp", "space")),
            P("dp", None, "space"),
            P("dp", None, "space"),
            P("dp", None, "space"),
            P("dp", "space", None),
            P("dp", "space"),
            P("space", None),
            P("space"),
        ),
        out_specs=(
            P(),
            P(),
            P(),
            P(("dp", "space")),
            P(("dp", "space")),
            P(("dp", "space")),
            P(("dp", "space")),
            P("dp", "space", None),
            P("dp", "space", None),
            P("dp", None, "space"),
        ),
        check_vma=False,
    )
```

profile of v0, /device:TPU:0, one launch (start us, length us, event | category | flops | bytes accessed | tf_op | source)
XLA Modules:
  0.0 458.5 jit_solution(3175855006213309100)
XLA Ops:
  2.5 5.1 %collective-permute-start.2 = (bf16[1,144,256]{2,1,0:T(8,128)(2,1)S(1)}, bf16[1,144,256]{2,1,0:T(8,128)(2,1)S(1)}, u32[]{:S(2)}, u32[]{:S(2)}) collective-permute-start(bf16[1,144,256]{2,1,0:T(8,128)(2,1)S(1)} %broadcast_in_dim_reshape.3), channel_id=1, source_target_pairs={{0,12},{1,13},{2,14},{3,15},{4,8},{5,9},{6,10},{7,11},{8,4},{9,5},... | collective-permute-start | bytes 221192 | tf_op jit(solution)/shard_map/ppermute | solution.py:94
  26.1 4.8 %collective-permute-done.6 = bf16[8,72,256]{2,1,0:T(8,128)(2,1)S(1)} collective-permute-done((bf16[8,72,256]{2,1,0:T(8,128)(2,1)S(1)}, bf16[8,72,256]{2,1,0:T(8,128)(2,1)S(1)}, u32[]{:S(2)}, u32[]{:S(2)}) %collective-permute-start.6) | collective-permute-done | bytes 294944 | tf_op jit(solution)/shard_map/ppermute | solution.py:94
  32.4 5.2 %all-to-all-start = ((bf16[16,64,128]{2,1,0:T(8,128)(2,1)}), bf16[16,64,128]{2,1,0:T(8,128)(2,1)S(1)}, u32[]{:S(2)}, u32[]{:S(2)}) async-start(bf16[16,64,128]{2,1,0:T(8,128)(2,1)} %bitcast.4), calls=%async_computation | async-start | bytes 524288 | tf_op jit(solution)/shard_map/all_to_all | solution.py:898
  38.6 4.0 spread_rows.1
  42.6 5.4 %all-to-all-done = bf16[16,64,128]{2,1,0:T(8,128)(2,1)S(1)} async-done(((bf16[16,64,128]{2,1,0:T(8,128)(2,1)}), bf16[16,64,128]{2,1,0:T(8,128)(2,1)S(1)}, u32[]{:S(2)}, u32[]{:S(2)}) %all-to-all-start) | async-done | bytes 262176 | tf_op jit(solution)/shard_map/all_to_all | solution.py:898
  48.7 6.0 %encode_rows.1 = (f32[2048,256]{1,0:T(8,128)}, bf16[2048,256]{1,0:T(8,128)(2,1)}, bf16[4096,128]{1,0:T(8,128)(2,1)}, s32[1,1024]{1,0:T(1,128)}, s32[1024,1]{1,0:T(8,128)}) custom-call(bf16[1024,128]{1,0:T(8,128)(2,1)} %bitcast.129, bf16[128,256]{1,0:T(8,128)(2,1)} %get-tuple-element.144.in_ref, bf16[256,256]{1,0:T(8,128)(2,1)} %get-tuple-element.145.node_ref, ...), custom_call_target="tpu_custom_call" | custom-call | bytes 15000000 | tf_op jit(solution)/shard_map/encode_rows/pallas_call | solution.py:774
  60.4 4.5 collective-permute-start.12
  65.0 3.9 node_terms.3
  68.9 11.7 %collective-permute-done.13 = bf16[79,360]{1,0:T(8,128)(2,1)S(1)} collective-permute-done((bf16[79,360]{1,0:T(8,128)(2,1)S(1)}, bf16[79,360]{1,0:T(8,128)(2,1)S(1)}, u32[]{:S(2)}, u32[]{:S(2)}) %collective-permute-start.13) | collective-permute-done | bytes 56912 | tf_op jit(solution)/shard_map/ppermute | solution.py:49
  80.8 2.5 collective-permute-done.10.refs_0_
  84.2 14.6 %round_forward.5 = (f32[2048,256]{1,0:T(8,128)}, f32[2048,256]{1,0:T(8,128)}, bf16[2048,256]{1,0:T(8,128)(2,1)}, bf16[2048,256]{1,0:T(8,128)(2,1)}, bf16[6,4096,...) custom-call(s32[12288]{0:T(1024)} %copy-done.3, f32[2048,256]{1,0:T(8,128)} %get-tuple-element.151.mesh_ref, ...), custom_call_target="tpu_custom_call" | custom-call | bytes 42000000 | tf_op jit(solution)/shard_map/round_forward/pallas_call | solution.py:491
  100.9 14.7 %round_forward.6 = (f32[2048,256]{1,0:T(8,128)}, f32[2048,256]{1,0:T(8,128)}, bf16[2048,256]{1,0:T(8,128)(2,1)}, bf16[2048,256]{1,0:T(8,128)(2,1)}, bf16[6,4096,...) custom-call(s32[12288]{0:T(1024)} %copy-done.3, ...), custom_call_target="tpu_custom_call", output_to_operand_aliasing={{0}: (9, {}), {1}: (10, {}), {2}: (11, {}), {3}: (12, {}), ... | custom-call | bytes 42000000 | tf_op jit(solution)/shard_map/round_forward/pallas_call | solution.py:491
  115.6 2.8 collective-permute-start.18
  118.5 3.9 node_terms.4
  122.4 7.5 %collective-permute-done.18.refs_5_ = bf16[2048,128]{1,0:T(8,128)(2,1)S(1)} collective-permute-done((bf16[2048,128]{1,0:T(8,128)(2,1)}, bf16[2048,128]{1,0:T(8,128)(2,1)S(1)}, u32[]{:S(2)}, u32[]{:S(2)}) %collective-permute-start.18) | collective-permute-done | bytes 524320 | tf_op jit(solution)/shard_map/ppermute | solution.py:77
  132.1 14.6 %round_forward.7 = (f32[2048,256]{1,0:T(8,128)}, f32[2048,256]{1,0:T(8,128)}, bf16[2048,256]{1,0:T(8,128)(2,1)}, bf16[2048,256]{1,0:T(8,128)(2,1)}, bf16[6,4096,...) custom-call(s32[12288]{0:T(1024)} %copy-done.3, f32[2048,256]{1,0:T(8,128)} %get-tuple-element.165.mesh_ref.refs_0_, ...), custom_call_target="tpu_custom_call" | custom-call | bytes 42000000 | tf_op jit(solution)/shard_map/round_forward/pallas_call | solution.py:491
  148.7 14.8 %round_forward.8 = (f32[2048,256]{1,0:T(8,128)}, f32[2048,256]{1,0:T(8,128)}, bf16[2048,256]{1,0:T(8,128)(2,1)}, bf16[2048,256]{1,0:T(8,128)(2,1)}, bf16[6,4096,...) custom-call(s32[12288]{0:T(1024)} %copy-done.3, ...), custom_call_target="tpu_custom_call", output_to_operand_aliasing={{0}: (12, {}), {1}: (13, {}), {2}: (14, {}), {3}: (15, {}),... | custom-call | bytes 42000000 | tf_op jit(solution)/shard_map/round_forward/pallas_call | solution.py:491
  163.6 2.3 collective-permute-start.22
  166.8 3.9 node_terms.5
  170.7 4.5 collective-permute-done.22.refs_5_
  175.1 3.8 collective-permute-done.21.refs_1_
  179.8 26.4 %round_forward.9 = (f32[2048,256]{1,0:T(8,128)}, f32[2048,256]{1,0:T(8,128)}, bf16[2048,256]{1,0:T(8,128)(2,1)}, bf16[2048,256]{1,0:T(8,128)(2,1)}, bf16[6,4096,...) custom-call(s32[12288]{0:T(1024)} %copy-done.3, ...), custom_call_target="tpu_custom_call" | custom-call | bytes 72000000 | tf_op jit(solution)/shard_map/round_forward/pallas_call | solution.py:491
  206.2 3.5 all-to-all-start.1
  209.9 8.4 %all-to-all-done.1 = bf16[16,64,128]{2,1,0:T(8,128)(2,1)S(1)} async-done(((bf16[16,64,128]{2,1,0:T(8,128)(2,1)}), bf16[16,64,128]{2,1,0:T(8,128)(2,1)S(1)}, u32[]{:S(2)}, u32[]{:S(2)}) %all-to-all-start.1) | async-done | bytes 262176 | tf_op jit(solution)/shard_map/all_to_all | solution.py:898
  218.9 3.3 collective-permute-start.23
  232.0 5.8 %all-to-all-start.2 = ((bf16[16,64,128]{2,1,0:T(8,128)(2,1)}), bf16[16,64,128]{2,1,0:T(8,128)(2,1)S(1)}, u32[]{:S(2)}, u32[]{:S(2)}) async-start(bf16[16,64,128]{2,1,0:T(8,128)(2,1)} %bitcast.18), calls=%async_computation.2 | async-start | bytes 524288 | tf_op jit(solution)/shard_map/all_to_all | solution.py:898
  238.0 8.4 %all-to-all-done.2 = bf16[16,64,128]{2,1,0:T(8,128)(2,1)S(1)} async-done(((bf16[16,64,128]{2,1,0:T(8,128)(2,1)}), bf16[16,64,128]{2,1,0:T(8,128)(2,1)S(1)}, u32[]{:S(2)}, u32[]{:S(2)}) %all-to-all-start.2) | async-done | bytes 262176 | tf_op jit(solution)/shard_map/all_to_all | solution.py:898
  248.0 26.8 %edges_backward.3 = (f32[2048,256]{1,0:T(8,128)}, bf16[2048,256]{1,0:T(8,128)(2,1)}, bf16[1024,256]{1,0:T(8,128)(2,1)}, bf16[2048,256]{1,0:T(8,128)(2,1)}, bf16[...) custom-call(s32[12288]{0:T(1024)} %copy-done.3, ...), custom_call_target="tpu_custom_call" | custom-call | bytes 75000000 | tf_op jit(solution)/shard_map/edges_backward/pallas_call | solution.py:633
  276.3 2.4 collective-permute-start.27
  279.4 7.4 %weight_grads.3 = (f32[2048,256]{1,0:T(8,128)}, f32[1024,256]{1,0:T(8,128)}, f32[2,256]{1,0:T(2,128)}) custom-call(f32[2048,256]{1,0:T(8,128)} %get-tuple-element.179.mesh_ref.refs_0_, bf16[2048,256]{1,0:T(8,128)(2,1)} %get-tuple-element.203.dest_ref, bf16[2048,256]{1,0:T(8,128)(2,1)} %get-tuple-element.204.agg_ref, ...), custom_call_target="tpu_custom_call" | custom-call | bytes 30000000 | tf_op jit(solution)/shard_map/weight_grads/pallas_call | solution.py:718
  286.7 3.4 convert_select_fusion
  290.1 4.2 collective-permute-done.26.refs_6_
  295.3 26.1 %edges_backward.4 = (f32[2048,256]{1,0:T(8,128)}, bf16[2048,256]{1,0:T(8,128)(2,1)}, bf16[2048,256]{1,0:T(8,128)(2,1)}, bf16[2048,256]{1,0:T(8,128)(2,1)}, bf16[...) custom-call(s32[12288]{0:T(1024)} %copy-done.3, ...), custom_call_target="tpu_custom_call" | custom-call | bytes 84000000 | tf_op jit(solution)/shard_map/edges_backward/pallas_call | solution.py:633
  321.5 3.8 collective-permute-start.29
  325.3 8.5 %weight_grads.4 = (f32[2048,256]{1,0:T(8,128)}, f32[1024,256]{1,0:T(8,128)}, f32[2,256]{1,0:T(2,128)}, f32[256,256]{1,0:T(8,128)}) custom-call(f32[2048,256]{1,0:T(8,128)} %get-tuple-element.165.mesh_ref.refs_0_, bf16[2048,256]{1,0:T(8,128)(2,1)} %get-tuple-element.218.dest_ref, bf16[2048,256]{1,0:T(8,128)(2,1)} %get-tuple-element.219.agg_ref, ...), custom_call_target="tpu_custom_call" | custom-call | bytes 30000000 | tf_op jit(solution)/shard_map/weight_grads/pallas_call | solution.py:718
  333.8 6.2 %collective-permute-done.28.refs_6_ = bf16[4096,128]{1,0:T(8,128)(2,1)S(1)} collective-permute-done((bf16[4096,128]{1,0:T(8,128)(2,1)}, bf16[4096,128]{1,0:T(8,128)(2,1)S(1)}, u32[]{:S(2)}, u32[]{:S(2)}) %collective-permute-start.28) | collective-permute-done | bytes 1048608 | tf_op jit(solution)/shard_map/ppermute | solution.py:77
  341.3 26.2 %edges_backward.5 = (f32[2048,256]{1,0:T(8,128)}, bf16[2048,256]{1,0:T(8,128)(2,1)}, bf16[2048,256]{1,0:T(8,128)(2,1)}, bf16[2048,256]{1,0:T(8,128)(2,1)}, bf16[...) custom-call(s32[12288]{0:T(1024)} %copy-done.3, ...), custom_call_target="tpu_custom_call" | custom-call | bytes 84000000 | tf_op jit(solution)/shard_map/edges_backward/pallas_call | solution.py:633
  367.5 3.8 collective-permute-start.31
  371.3 2.6 decode_grads.1
  375.7 8.5 %weight_grads.5 = (f32[2048,256]{1,0:T(8,128)}, f32[1024,256]{1,0:T(8,128)}, f32[2,256]{1,0:T(2,128)}, f32[256,256]{1,0:T(8,128)}) custom-call(f32[2048,256]{1,0:T(8,128)} %get-tuple-element.151.mesh_ref, bf16[2048,256]{1,0:T(8,128)(2,1)} %get-tuple-element.229.dest_ref, bf16[2048,256]{1,0:T(8,128)(2,1)} %get-tuple-element.230.agg_ref, ...), custom_call_target="tpu_custom_call" | custom-call | bytes 30000000 | tf_op jit(solution)/shard_map/weight_grads/pallas_call | solution.py:718
  386.4 10.1 %encode_backward.1 = (f32[2048,256]{1,0:T(8,128)}, bf16[2048,256]{1,0:T(8,128)(2,1)}, f32[128,256]{1,0:T(8,128)}, f32[256,256]{1,0:T(8,128)}, f32[2,256]{1,0:T(2,128)}, /*index=5*/f32[256,256]{1,0:T(8,128)}) custom-call(f32[2048,256]{1,0:T(8,128)} %get-tuple-element.236.part_ref, f32[4096,128]{1,0:T(8,128)} %get-tuple-element.237.own_ref, ...), custom_call_target="tpu_custom_call" | custom-call | bytes 30000000 | tf_op jit(solution)/shard_map/encode_backward/pallas_call | solution.py:839
  396.5 5.1 %collect_rows.1 = (f32[16,144,256]{2,1,0:T(8,128)}, bf16[16,144,256]{2,1,0:T(8,128)(2,1)}) custom-call(s32[1]{0:T(128)} %bitcast.6.place_ref, f32[128,256]{1,0:T(8,128)} %get-tuple-element.241.refs_0_, f32[256,256]{1,0:T(8,128)} %get-tuple-element.242.refs_1_, f32[256,256]{1,0:T(8,128)} %get-tuple-element.246.refs_2_, f32[78,256]{1,0:T(8,128)} %reshape.155.refs_3_, ...), custom_call_target="tpu_custom_call" | custom-call | bytes 15000000 | tf_op jit(solution)/shard_map/collect_rows/pallas_call | solution.py:233
  401.6 3.1 collective-permute-done.32
  406.9 8.9 %collective-permute-done.33 = bf16[4,2,72,256]{3,2,0,1:T(8,128)(2,1)S(1)} collective-permute-done((bf16[4,2,72,256]{3,2,0,1:T(8,128)(2,1)S(1)}, bf16[4,2,72,256]{3,2,0,1:T(8,128)(2,1)S(1)}, u32[]{:S(2)}, u32[]{:S(2)}) %collective-permute-start.33) | collective-permute-done | bytes 294944 | tf_op jit(solution)/shard_map/ppermute | solution.py:94
  417.9 3.3 collective-permute-done.34
  423.4 5.2 %collective-permute-start.39 = (bf16[1,144,256]{2,1,0:T(8,128)(2,1)S(1)}, bf16[1,144,256]{2,1,0:T(8,128)(2,1)S(1)}, u32[]{:S(2)}, u32[]{:S(2)}) collective-permute-start(bf16[1,144,256]{2,1,0:T(8,128)(2,1)S(1)} %get-tuple-element.311), channel_id=1, source_target_pairs={{0,12},{1,13},{2,14},{3,15},{4,8},{5,9},{6,10},{7,11},{8,4},{9,5},... | collective-permute-start | bytes 221192 | tf_op jit(solution)/shard_map/ppermute | solution.py:94
  443.7 5.3 %collective-permute-start.47 = (f32[8,128]{1,0:T(8,128)S(1)}, f32[8,128]{1,0:T(8,128)S(1)}, u32[]{:S(2)}, u32[]{:S(2)}) collective-permute-start(f32[8,128]{1,0:T(8,128)S(1)} %add.191), channel_id=1, source_target_pairs={{0,3},{1,2},{2,1},{3,0},{4,7},{5,6},{6,5},{7,4},{8,11},{9,10},{10,... | collective-permute-start | bytes 12296 | tf_op jit(solution)/shard_map/ppermute | solution.py:94
  450.5 3.4 select_bitcast_fusion
  (228 shorter events, 80.1 us)
Async XLA Ops:
  2.5 14.5 %collective-permute-start.2 = (bf16[1,144,256]{2,1,0:T(8,128)(2,1)S(1)}, bf16[1,144,256]{2,1,0:T(8,128)(2,1)S(1)}, u32[]{:S(2)}, u32[]{:S(2)}) collective-permute-start(bf16[1,144,256]{2,1,0:T(8,128)(2,1)S(1)} %broadcast_in_dim_reshape.3), channel_id=1, source_target_pairs={{0,12},{1,13},{2,14},{3,15},{4,8},{5,9},{6,10},{7,11},{8,4},{9,5},... | collective-permute-start | bytes 221192 | tf_op jit(solution)/shard_map/ppermute | solution.py:94
  7.6 9.4 %collective-permute-start.1 = (bf16[1,144,256]{2,1,0:T(8,128)(2,1)S(1)}, bf16[1,144,256]{2,1,0:T(8,128)(2,1)S(1)}, u32[]{:S(2)}, u32[]{:S(2)}) collective-permute-start(bf16[1,144,256]{2,1,0:T(8,128)(2,1)S(1)} %broadcast_in_dim_reshape.3), channel_id=1, source_target_pairs={{0,8},{1,9},{2,10},{3,11},{4,12},{5,13},{6,14},{7,15},{8,0},{9,1},... | collective-permute-start | bytes 221192 | tf_op jit(solution)/shard_map/ppermute | solution.py:94
  7.6 9.4 %collective-permute-start = (bf16[1,144,256]{2,1,0:T(8,128)(2,1)S(1)}, bf16[1,144,256]{2,1,0:T(8,128)(2,1)S(1)}, u32[]{:S(2)}, u32[]{:S(2)}) collective-permute-start(bf16[1,144,256]{2,1,0:T(8,128)(2,1)S(1)} %broadcast_in_dim_reshape.3), channel_id=1, source_target_pairs={{0,4},{1,5},{2,6},{3,7},{4,0},{5,1},{6,2},{7,3},{8,12},{9,13},{10,... | collective-permute-start | bytes 221192 | tf_op jit(solution)/shard_map/ppermute | solution.py:94
  17.0 5.2 %collective-permute-start.4 = (bf16[4,72,256]{2,1,0:T(8,128)(2,1)S(1)}, bf16[4,72,256]{2,1,0:T(8,128)(2,1)S(1)}, u32[]{:S(2)}, u32[]{:S(2)}) collective-permute-start(bf16[4,72,256]{2,1,0:T(8,128)(2,1)S(1)} %get-tuple-element.313), channel_id=1, source_target_pairs={{0,1},{1,0},{2,3},{3,2},{4,5},{5,4},{6,7},{7,6},{8,9},{9,8},{10,11... | collective-permute-start | bytes 442376 | tf_op jit(solution)/shard_map/ppermute | solution.py:94
  18.7 5.1 %collective-permute-start.3 = (bf16[4,72,256]{2,1,0:T(8,128)(2,1)S(1)}, bf16[4,72,256]{2,1,0:T(8,128)(2,1)S(1)}, u32[]{:S(2)}, u32[]{:S(2)}) collective-permute-start(bf16[4,72,256]{2,1,0:T(8,128)(2,1)S(1)} %get-tuple-element.314), channel_id=1, source_target_pairs={{0,2},{1,3},{2,0},{3,1},{4,6},{5,7},{6,4},{7,5},{8,10},{9,11},{10,... | collective-permute-start | bytes 442376 | tf_op jit(solution)/shard_map/ppermute | solution.py:94
  23.9 7.0 %collective-permute-start.6 = (bf16[8,72,256]{2,1,0:T(8,128)(2,1)S(1)}, bf16[8,72,256]{2,1,0:T(8,128)(2,1)S(1)}, u32[]{:S(2)}, u32[]{:S(2)}) collective-permute-start(bf16[8,72,256]{2,1,0:T(8,128)(2,1)S(1)} %pad_maximum_fusion.3), channel_id=1, source_target_pairs={{0,2},{1,3},{2,0},{3,1},{4,6},{5,7},{6,4},{7,5},{8,10},{9,11},{10,... | collective-permute-start | bytes 884744 | tf_op jit(solution)/shard_map/ppermute | solution.py:94
  25.5 6.7 %collective-permute-start.5 = (bf16[8,72,256]{2,1,0:T(8,128)(2,1)S(1)}, bf16[8,72,256]{2,1,0:T(8,128)(2,1)S(1)}, u32[]{:S(2)}, u32[]{:S(2)}) collective-permute-start(bf16[8,72,256]{2,1,0:T(8,128)(2,1)S(1)} %pad_maximum_fusion.2), channel_id=1, source_target_pairs={{0,1},{1,0},{2,3},{3,2},{4,5},{5,4},{6,7},{7,6},{8,9},{9,8},{10,11... | collective-permute-start | bytes 884744 | tf_op jit(solution)/shard_map/ppermute | solution.py:94
  30.9 6.7 %collective-permute-start.8 = (bf16[16,72,256]{2,1,0:T(8,128)(2,1)S(1)}, bf16[16,72,256]{2,1,0:T(8,128)(2,1)S(1)}, u32[]{:S(2)}, u32[]{:S(2)}) collective-permute-start(bf16[16,72,256]{2,1,0:T(8,128)(2,1)S(1)} %constant_dynamic-update-slice_fusion.6.refs_1_), channel_id=1, source_target_pairs={{0,16},{16,0},{1,17},{17,1},{2,18},{18,2},{3,19},{19,3},{4,20},{20... | collective-permute-start | bytes 1769480 | tf_op jit(solution)/shard_map/ppermute | solution.py:94
  32.3 5.3 %collective-permute-start.7 = (bf16[16,72,256]{2,1,0:T(8,128)(2,1)S(1)}, bf16[16,72,256]{2,1,0:T(8,128)(2,1)S(1)}, u32[]{:S(2)}, u32[]{:S(2)}) collective-permute-start(bf16[16,72,256]{2,1,0:T(8,128)(2,1)S(1)} %constant_dynamic-update-slice_fusion.4.refs_0_), channel_id=1, source_target_pairs={{0,16},{16,0},{1,17},{17,1},{2,18},{18,2},{3,19},{19,3},{4,20},{20... | collective-permute-start | bytes 1769480 | tf_op jit(solution)/shard_map/ppermute | solution.py:94
  32.4 15.6 %all-to-all-start = ((bf16[16,64,128]{2,1,0:T(8,128)(2,1)}), bf16[16,64,128]{2,1,0:T(8,128)(2,1)S(1)}, u32[]{:S(2)}, u32[]{:S(2)}) async-start(bf16[16,64,128]{2,1,0:T(8,128)(2,1)} %bitcast.4), calls=%async_computation | async-start | bytes 524288 | tf_op jit(solution)/shard_map/all_to_all | solution.py:898
  54.7 26.0 %collective-permute-start.11 = (bf16[4096,128]{1,0:T(8,128)(2,1)}, bf16[4096,128]{1,0:T(8,128)(2,1)S(1)}, u32[]{:S(2)}, u32[]{:S(2)}) collective-permute-start(bf16[4096,128]{1,0:T(8,128)(2,1)} %get-tuple-element.152.refs_1_), channel_id=1, source_target_pairs={{1,0},{3,1},{2,3},{6,2},{4,6},{5,4},{7,5},{11,7},{9,11},{8,9},{10,... | collective-permute-start | bytes 3145736 | tf_op jit(solution)/shard_map/ppermute | solution.py:77
  56.5 26.8 %collective-permute-start.10 = (bf16[4096,128]{1,0:T(8,128)(2,1)}, bf16[4096,128]{1,0:T(8,128)(2,1)S(1)}, u32[]{:S(2)}, u32[]{:S(2)}) collective-permute-start(bf16[4096,128]{1,0:T(8,128)(2,1)} %get-tuple-element.152.refs_1_), channel_id=1, source_target_pairs={{0,1},{1,3},{3,2},{2,6},{6,4},{4,5},{5,7},{7,11},{11,9},{9,8},{8,1... | collective-permute-start | bytes 3145736 | tf_op jit(solution)/shard_map/ppermute | solution.py:77
  56.8 3.7 collective-permute-start.14
  56.9 26.3 %collective-permute-start.9 = (s32[12288]{0:T(1024)S(1)}, s32[12288]{0:T(1024)S(1)}, u32[]{:S(2)}, u32[]{:S(2)}) collective-permute-start(s32[12288]{0:T(1024)S(1)} %mul.177), channel_id=1, source_target_pairs={{0,0},{1,1},{2,3},{3,2},{4,6},{5,4},{6,5},{7,7},{8,11},{9,9},{10,8... | collective-permute-start | bytes 147464 | tf_op jit(solution)/shard_map/ppermute | solution.py:926
  57.7 22.8 %collective-permute-start.13 = (bf16[79,360]{1,0:T(8,128)(2,1)S(1)}, bf16[79,360]{1,0:T(8,128)(2,1)S(1)}, u32[]{:S(2)}, u32[]{:S(2)}) collective-permute-start(bf16[79,360]{1,0:T(8,128)(2,1)S(1)} %get-tuple-element.315), channel_id=1, source_target_pairs={{1,0},{2,1},{3,2},{4,3},{5,4},{6,5},{7,6},{8,7},{9,8},{10,9},{11,1... | collective-permute-start | bytes 170648 | tf_op jit(solution)/shard_map/ppermute | solution.py:49
  60.4 20.1 %collective-permute-start.12 = (bf16[79,360]{1,0:T(8,128)(2,1)S(1)}, bf16[79,360]{1,0:T(8,128)(2,1)S(1)}, u32[]{:S(2)}, u32[]{:S(2)}) collective-permute-start(bf16[79,360]{1,0:T(8,128)(2,1)S(1)} %get-tuple-element.316), channel_id=1, source_target_pairs={{0,1},{1,2},{2,3},{3,4},{4,5},{5,6},{6,7},{7,8},{8,9},{9,10},{10,1... | collective-permute-start | bytes 170648 | tf_op jit(solution)/shard_map/ppermute | solution.py:49
  98.9 16.7 %collective-permute-start.16 = (bf16[2048,128]{1,0:T(8,128)(2,1)}, bf16[2048,128]{1,0:T(8,128)(2,1)S(1)}, u32[]{:S(2)}, u32[]{:S(2)}) collective-permute-start(bf16[2048,128]{1,0:T(8,128)(2,1)} %get-tuple-element.167.refs_2_), channel_id=1, source_target_pairs={{1,0},{3,1},{2,3},{6,2},{4,6},{5,4},{7,5},{11,7},{9,11},{8,9},{10,... | collective-permute-start | bytes 1572872 | tf_op jit(solution)/shard_map/ppermute | solution.py:77
  99.9 15.7 %collective-permute-start.15 = (bf16[2048,128]{1,0:T(8,128)(2,1)}, bf16[2048,128]{1,0:T(8,128)(2,1)S(1)}, u32[]{:S(2)}, u32[]{:S(2)}) collective-permute-start(bf16[2048,128]{1,0:T(8,128)(2,1)} %get-tuple-element.167.refs_2_), channel_id=1, source_target_pairs={{0,1},{1,3},{3,2},{2,6},{6,4},{4,5},{5,7},{7,11},{11,9},{9,8},{8,1... | collective-permute-start | bytes 1572872 | tf_op jit(solution)/shard_map/ppermute | solution.py:77
  115.6 14.3 %collective-permute-start.18 = (bf16[2048,128]{1,0:T(8,128)(2,1)}, bf16[2048,128]{1,0:T(8,128)(2,1)S(1)}, u32[]{:S(2)}, u32[]{:S(2)}) collective-permute-start(bf16[2048,128]{1,0:T(8,128)(2,1)} %get-tuple-element.169.refs_3_), channel_id=1, source_target_pairs={{1,0},{3,1},{2,3},{6,2},{4,6},{5,4},{7,5},{11,7},{9,11},{8,9},{10,... | collective-permute-start | bytes 1572872 | tf_op jit(solution)/shard_map/ppermute | solution.py:77
  118.5 12.8 %collective-permute-start.17 = (bf16[2048,128]{1,0:T(8,128)(2,1)}, bf16[2048,128]{1,0:T(8,128)(2,1)S(1)}, u32[]{:S(2)}, u32[]{:S(2)}) collective-permute-start(bf16[2048,128]{1,0:T(8,128)(2,1)} %get-tuple-element.169.refs_3_), channel_id=1, source_target_pairs={{0,1},{1,3},{3,2},{2,6},{6,4},{4,5},{5,7},{7,11},{11,9},{9,8},{8,1... | collective-permute-start | bytes 1572872 | tf_op jit(solution)/shard_map/ppermute | solution.py:77
  146.7 16.9 %collective-permute-start.20 = (bf16[2048,128]{1,0:T(8,128)(2,1)}, bf16[2048,128]{1,0:T(8,128)(2,1)S(1)}, u32[]{:S(2)}, u32[]{:S(2)}) collective-permute-start(bf16[2048,128]{1,0:T(8,128)(2,1)} %get-tuple-element.181.refs_2_), channel_id=1, source_target_pairs={{1,0},{3,1},{2,3},{6,2},{4,6},{5,4},{7,5},{11,7},{9,11},{8,9},{10,... | collective-permute-start | bytes 1572872 | tf_op jit(solution)/shard_map/ppermute | solution.py:77
  147.2 16.4 %collective-permute-start.19 = (bf16[2048,128]{1,0:T(8,128)(2,1)}, bf16[2048,128]{1,0:T(8,128)(2,1)S(1)}, u32[]{:S(2)}, u32[]{:S(2)}) collective-permute-start(bf16[2048,128]{1,0:T(8,128)(2,1)} %get-tuple-element.181.refs_2_), channel_id=1, source_target_pairs={{0,1},{1,3},{3,2},{2,6},{6,4},{4,5},{5,7},{7,11},{11,9},{9,8},{8,1... | collective-permute-start | bytes 1572872 | tf_op jit(solution)/shard_map/ppermute | solution.py:77
  163.6 11.5 %collective-permute-start.22 = (bf16[2048,128]{1,0:T(8,128)(2,1)}, bf16[2048,128]{1,0:T(8,128)(2,1)S(1)}, u32[]{:S(2)}, u32[]{:S(2)}) collective-permute-start(bf16[2048,128]{1,0:T(8,128)(2,1)} %get-tuple-element.183.refs_3_), channel_id=1, source_target_pairs={{1,0},{3,1},{2,3},{6,2},{4,6},{5,4},{7,5},{11,7},{9,11},{8,9},{10,... | collective-permute-start | bytes 1572872 | tf_op jit(solution)/shard_map/ppermute | solution.py:77
  165.9 13.1 %collective-permute-start.21 = (bf16[2048,128]{1,0:T(8,128)(2,1)}, bf16[2048,128]{1,0:T(8,128)(2,1)S(1)}, u32[]{:S(2)}, u32[]{:S(2)}) collective-permute-start(bf16[2048,128]{1,0:T(8,128)(2,1)} %get-tuple-element.183.refs_3_), channel_id=1, source_target_pairs={{0,1},{1,3},{3,2},{2,6},{6,4},{4,5},{5,7},{7,11},{11,9},{9,8},{8,1... | collective-permute-start | bytes 1572872 | tf_op jit(solution)/shard_map/ppermute | solution.py:77
  206.2 12.0 %all-to-all-start.1 = ((bf16[16,64,128]{2,1,0:T(8,128)(2,1)}), bf16[16,64,128]{2,1,0:T(8,128)(2,1)S(1)}, u32[]{:S(2)}, u32[]{:S(2)}) async-start(bf16[16,64,128]{2,1,0:T(8,128)(2,1)} %bitcast.137), calls=%async_computation.1 | async-start | bytes 524288 | tf_op jit(solution)/shard_map/all_to_all | solution.py:898
  218.9 9.5 %collective-permute-start.23 = (bf16[78,360]{1,0:T(8,128)(2,1)S(1)}, bf16[78,360]{1,0:T(8,128)(2,1)S(1)}, u32[]{:S(2)}, u32[]{:S(2)}) collective-permute-start(bf16[78,360]{1,0:T(8,128)(2,1)S(1)} %get-tuple-element.317), channel_id=1, source_target_pairs={{0,1},{1,2},{2,3},{3,4},{4,5},{5,6},{6,7},{7,8},{8,9},{9,10},{10,1... | collective-permute-start | bytes 168488 | tf_op jit(solution)/shard_map/ppermute | solution.py:49
  222.2 6.1 %collective-permute-start.24 = (bf16[78,360]{1,0:T(8,128)(2,1)S(1)}, bf16[78,360]{1,0:T(8,128)(2,1)S(1)}, u32[]{:S(2)}, u32[]{:S(2)}) collective-permute-start(bf16[78,360]{1,0:T(8,128)(2,1)S(1)} %get-tuple-element.318), channel_id=1, source_target_pairs={{1,0},{2,1},{3,2},{4,3},{5,4},{6,5},{7,6},{8,7},{9,8},{10,9},{11,1... | collective-permute-start | bytes 168488 | tf_op jit(solution)/shard_map/ppermute | solution.py:49
  232.0 14.4 %all-to-all-start.2 = ((bf16[16,64,128]{2,1,0:T(8,128)(2,1)}), bf16[16,64,128]{2,1,0:T(8,128)(2,1)S(1)}, u32[]{:S(2)}, u32[]{:S(2)}) async-start(bf16[16,64,128]{2,1,0:T(8,128)(2,1)} %bitcast.18), calls=%async_computation.2 | async-start | bytes 524288 | tf_op jit(solution)/shard_map/all_to_all | solution.py:898
  246.4 28.5 %collective-permute-start.25 = (bf16[2048,256]{1,0:T(8,128)(2,1)S(1)}, bf16[2048,256]{1,0:T(8,128)(2,1)}, u32[]{:S(2)}, u32[]{:S(2)}) collective-permute-start(bf16[2048,256]{1,0:T(8,128)(2,1)S(1)} %convert_element_type.150), channel_id=1, source_target_pairs={{3,2},{2,3},{6,4},{4,5},{5,6},{11,8},{8,10},{10,11},{14,12},{15,13... | collective-permute-start | bytes 3145736 | tf_op jit(solution)/shard_map/ppermute | solution.py:929
  274.9 19.4 %collective-permute-start.26 = (bf16[4096,128]{1,0:T(8,128)(2,1)}, bf16[4096,128]{1,0:T(8,128)(2,1)S(1)}, u32[]{:S(2)}, u32[]{:S(2)}) collective-permute-start(bf16[4096,128]{1,0:T(8,128)(2,1)} %get-tuple-element.214), channel_id=1, source_target_pairs={{0,1},{1,3},{3,2},{2,6},{6,4},{4,5},{5,7},{7,11},{11,9},{9,8},{8,1... | collective-permute-start | bytes 3145736 | tf_op jit(solution)/shard_map/ppermute | solution.py:77
  276.3 18.0 %collective-permute-start.27 = (bf16[4096,128]{1,0:T(8,128)(2,1)}, bf16[4096,128]{1,0:T(8,128)(2,1)}, u32[]{:S(2)}, u32[]{:S(2)}) collective-permute-start(bf16[4096,128]{1,0:T(8,128)(2,1)} %get-tuple-element.217), channel_id=1, source_target_pairs={{1,0},{3,1},{2,3},{6,2},{4,6},{5,4},{7,5},{11,7},{9,11},{8,9},{10,... | collective-permute-start | bytes 3145736 | tf_op jit(solution)/shard_map/ppermute | solution.py:77
  321.4 18.5 %collective-permute-start.28 = (bf16[4096,128]{1,0:T(8,128)(2,1)}, bf16[4096,128]{1,0:T(8,128)(2,1)S(1)}, u32[]{:S(2)}, u32[]{:S(2)}) collective-permute-start(bf16[4096,128]{1,0:T(8,128)(2,1)} %get-tuple-element.227), channel_id=1, source_target_pairs={{0,1},{1,3},{3,2},{2,6},{6,4},{4,5},{5,7},{7,11},{11,9},{9,8},{8,1... | collective-permute-start | bytes 3145736 | tf_op jit(solution)/shard_map/ppermute | solution.py:77
  321.5 18.4 %collective-permute-start.29 = (bf16[4096,128]{1,0:T(8,128)(2,1)}, bf16[4096,128]{1,0:T(8,128)(2,1)S(1)}, u32[]{:S(2)}, u32[]{:S(2)}) collective-permute-start(bf16[4096,128]{1,0:T(8,128)(2,1)} %get-tuple-element.228), channel_id=1, source_target_pairs={{1,0},{3,1},{2,3},{6,2},{4,6},{5,4},{7,5},{11,7},{9,11},{8,9},{10,... | collective-permute-start | bytes 3145736 | tf_op jit(solution)/shard_map/ppermute | solution.py:77
  367.5 17.6 %collective-permute-start.30 = (bf16[4096,128]{1,0:T(8,128)(2,1)}, bf16[4096,128]{1,0:T(8,128)(2,1)S(1)}, u32[]{:S(2)}, u32[]{:S(2)}) collective-permute-start(bf16[4096,128]{1,0:T(8,128)(2,1)} %get-tuple-element.238), channel_id=1, source_target_pairs={{0,1},{1,3},{3,2},{2,6},{6,4},{4,5},{5,7},{7,11},{11,9},{9,8},{8,1... | collective-permute-start | bytes 3145736 | tf_op jit(solution)/shard_map/ppermute | solution.py:77
  367.5 17.5 %collective-permute-start.31 = (bf16[4096,128]{1,0:T(8,128)(2,1)}, bf16[4096,128]{1,0:T(8,128)(2,1)S(1)}, u32[]{:S(2)}, u32[]{:S(2)}) collective-permute-start(bf16[4096,128]{1,0:T(8,128)(2,1)} %get-tuple-element.239), channel_id=1, source_target_pairs={{1,0},{3,1},{2,3},{6,2},{4,6},{5,4},{7,5},{11,7},{9,11},{8,9},{10,... | collective-permute-start | bytes 3145736 | tf_op jit(solution)/shard_map/ppermute | solution.py:77
  406.7 9.1 %collective-permute-start.33 = (bf16[4,2,72,256]{3,2,0,1:T(8,128)(2,1)S(1)}, bf16[4,2,72,256]{3,2,0,1:T(8,128)(2,1)S(1)}, u32[]{:S(2)}, u32[]{:S(2)}) collective-permute-start(bf16[4,2,72,256]{3,2,0,1:T(8,128)(2,1)S(1)} %fusion.14), channel_id=1, source_target_pairs={{0,1},{1,0},{2,3},{3,2},{4,5},{5,4},{6,7},{7,6},{8,9},{9,8},{10,11... | collective-permute-start | bytes 884744 | tf_op jit(solution)/shard_map/ppermute | solution.py:94
  406.9 9.2 %collective-permute-start.35 = (bf16[4,2,72,256]{3,2,1,0:T(8,128)(2,1)S(1)}, bf16[4,2,72,256]{3,2,1,0:T(8,128)(2,1)S(1)}, u32[]{:S(2)}, u32[]{:S(2)}) collective-permute-start(bf16[4,2,72,256]{3,2,1,0:T(8,128)(2,1)S(1)} %fusion.13), channel_id=1, source_target_pairs={{0,2},{1,3},{2,0},{3,1},{4,6},{5,7},{6,4},{7,5},{8,10},{9,11},{10,... | collective-permute-start | bytes 884744 | tf_op jit(solution)/shard_map/ppermute | solution.py:94
  416.0 5.2 %collective-permute-start.34 = (bf16[4,72,256]{2,1,0:T(8,128)(2,1)S(1)}, bf16[4,72,256]{2,1,0:T(8,128)(2,1)S(1)}, u32[]{:S(2)}, u32[]{:S(2)}) collective-permute-start(bf16[4,72,256]{2,1,0:T(8,128)(2,1)S(1)} %fusion.38), channel_id=1, source_target_pairs={{0,2},{1,3},{2,0},{3,1},{4,6},{5,7},{6,4},{7,5},{8,10},{9,11},{10,... | collective-permute-start | bytes 442376 | tf_op jit(solution)/shard_map/ppermute | solution.py:94
  416.1 5.2 %collective-permute-start.36 = (bf16[4,72,256]{2,1,0:T(8,128)(2,1)S(1)}, bf16[4,72,256]{2,1,0:T(8,128)(2,1)S(1)}, u32[]{:S(2)}, u32[]{:S(2)}) collective-permute-start(bf16[4,72,256]{2,1,0:T(8,128)(2,1)S(1)} %fusion.39), channel_id=1, source_target_pairs={{0,1},{1,0},{2,3},{3,2},{4,5},{5,4},{6,7},{7,6},{8,9},{9,8},{10,11... | collective-permute-start | bytes 442376 | tf_op jit(solution)/shard_map/ppermute | solution.py:94
  421.4 22.3 %collective-permute-start.44 = (bf16[2048,256]{1,0:T(8,128)(2,1)}, bf16[2048,256]{1,0:T(8,128)(2,1)}, u32[]{:S(2)}, u32[]{:S(2)}) collective-permute-start(bf16[2048,256]{1,0:T(8,128)(2,1)} %get-tuple-element.263), channel_id=1, source_target_pairs={{3,2},{2,3},{6,4},{4,5},{5,6},{11,8},{8,10},{10,11},{14,12},{15,13... | collective-permute-start | bytes 3145736 | tf_op jit(solution)/shard_map/ppermute | solution.py:929
  423.3 7.1 %collective-permute-start.37 = (bf16[1,144,256]{2,1,0:T(8,128)(2,1)S(1)}, bf16[1,144,256]{2,1,0:T(8,128)(2,1)S(1)}, u32[]{:S(2)}, u32[]{:S(2)}) collective-permute-start(bf16[1,144,256]{2,1,0:T(8,128)(2,1)S(1)} %get-tuple-element.310), channel_id=1, source_target_pairs={{0,4},{1,5},{2,6},{3,7},{4,0},{5,1},{6,2},{7,3},{8,12},{9,13},{10,... | collective-permute-start | bytes 221192 | tf_op jit(solution)/shard_map/ppermute | solution.py:94
  423.4 9.1 %collective-permute-start.39 = (bf16[1,144,256]{2,1,0:T(8,128)(2,1)S(1)}, bf16[1,144,256]{2,1,0:T(8,128)(2,1)S(1)}, u32[]{:S(2)}, u32[]{:S(2)}) collective-permute-start(bf16[1,144,256]{2,1,0:T(8,128)(2,1)S(1)} %get-tuple-element.311), channel_id=1, source_target_pairs={{0,12},{1,13},{2,14},{3,15},{4,8},{5,9},{6,10},{7,11},{8,4},{9,5},... | collective-permute-start | bytes 221192 | tf_op jit(solution)/shard_map/ppermute | solution.py:94
  428.6 6.1 %collective-permute-start.38 = (bf16[1,144,256]{2,1,0:T(8,128)(2,1)S(1)}, bf16[1,144,256]{2,1,0:T(8,128)(2,1)S(1)}, u32[]{:S(2)}, u32[]{:S(2)}) collective-permute-start(bf16[1,144,256]{2,1,0:T(8,128)(2,1)S(1)} %get-tuple-element.312), channel_id=1, source_target_pairs={{0,8},{1,9},{2,10},{3,11},{4,12},{5,13},{6,14},{7,15},{8,0},{9,1},... | collective-permute-start | bytes 221192 | tf_op jit(solution)/shard_map/ppermute | solution.py:94
  436.2 4.6 collective-permute-start.41
  436.7 5.4 %collective-permute-start.42 = (f32[8,128]{1,0:T(8,128)S(1)}, f32[8,128]{1,0:T(8,128)S(1)}, u32[]{:S(2)}, u32[]{:S(2)}) collective-permute-start(f32[8,128]{1,0:T(8,128)S(1)} %iota.23), channel_id=1, source_target_pairs={{0,12},{1,13},{2,14},{3,15},{4,8},{5,9},{6,10},{7,11},{8,4},{9,5},... | collective-permute-start | bytes 12296 | tf_op jit(solution)/shard_map/ppermute | solution.py:94
  443.7 10.2 %collective-permute-start.47 = (f32[8,128]{1,0:T(8,128)S(1)}, f32[8,128]{1,0:T(8,128)S(1)}, u32[]{:S(2)}, u32[]{:S(2)}) collective-permute-start(f32[8,128]{1,0:T(8,128)S(1)} %add.191), channel_id=1, source_target_pairs={{0,3},{1,2},{2,1},{3,0},{4,7},{5,6},{6,5},{7,4},{8,11},{9,10},{10,... | collective-permute-start | bytes 12296 | tf_op jit(solution)/shard_map/ppermute | solution.py:94
  449.0 4.9 %collective-permute-start.46 = (f32[8,128]{1,0:T(8,128)S(1)}, f32[8,128]{1,0:T(8,128)S(1)}, u32[]{:S(2)}, u32[]{:S(2)}) collective-permute-start(f32[8,128]{1,0:T(8,128)S(1)} %add.191), channel_id=1, source_target_pairs={{0,2},{1,3},{2,0},{3,1},{4,6},{5,7},{6,4},{7,5},{8,10},{9,11},{10,... | collective-permute-start | bytes 12296 | tf_op jit(solution)/shard_map/ppermute | solution.py:94
  449.0 4.9 %collective-permute-start.45 = (f32[8,128]{1,0:T(8,128)S(1)}, f32[8,128]{1,0:T(8,128)S(1)}, u32[]{:S(2)}, u32[]{:S(2)}) collective-permute-start(f32[8,128]{1,0:T(8,128)S(1)} %add.191), channel_id=1, source_target_pairs={{0,1},{1,0},{2,3},{3,2},{4,5},{5,4},{6,7},{7,6},{8,9},{9,8},{10,11... | collective-permute-start | bytes 12296 | tf_op jit(solution)/shard_map/ppermute | solution.py:94
  (38 other events, 366.8 us)
where the time goes:
time: 461 us; the launch traced here: 459 us
  Pallas kernels  228 us (49%)
  waiting for transfers between devices  98.4 us (21%)
  starting transfers between devices  81.4 us (18%)
  other arithmetic  22.3 us (5%)
  local copies, waits for them, and re-layouts  17.7 us (4%)
  between operations  7.8 us (2%)
    pallas_call x5, Pallas kernels, round_forward(): pl.pallas_call(body, grid_spec=pltpu.PrefetchScalarGridSpec(num_scalar_pr...  85.1 us
    pallas_call x3, Pallas kernels, edges_backward(): pl.pallas_call(body, grid_spec=pltpu.PrefetchScalarGridSpec(num_scalar_pr...  79.1 us
    ppermute x25, waiting for transfers between devices, swapped(): lax.ppermute(value, axis, [(i, i ^ bit) for i in range(lax.axis_size(axis...  31.3 us
    ppermute x25, starting transfers between devices, swapped(): lax.ppermute(value, axis, [(i, i ^ bit) for i in range(lax.axis_size(axis...  29.3 us
    pallas_call x3, Pallas kernels, weight_grads(): pl.pallas_call(body, grid=(blocks // tile,), in_specs=[rows] * 7 + [whole...  24.3 us
    all_to_all x3, waiting for transfers between devices, exchanged(): lax.all_to_all(rows.reshape(bands, capacity, HALF), 'space', split_axis=0...  22.2 us
    ppermute x8, waiting for transfers between devices, halo(): lax.ppermute(last, 'space', up)  19 us
    ppermute x8, starting transfers between devices, halo(): lax.ppermute(initial, 'space', down)  18.4 us
  transfers between devices with their start and end apart: 51, of which 27 were waited for; matrix products, arithmetic and copies ran while one was open for 5% of the time, Pallas kernels for 22%

commit v1 on v0

--- a/solution.py
+++ b/solution.py
@@ -375,9 +375,15 @@
 
         mesh_in = mesh_ref[...]
 
+        part = blocks // 2
+        if half is None:
+            origin = step // (steps // 2) * (K * part) + lax.rem(step, steps // 2) * tile
+        else:
+            origin = step * tile
+
         def fetch(turn):
             for edge in range(K):
-                base = edge * blocks + (step + shift) * tile + turn * chunk
+                base = edge * part + turn * chunk + origin
                 spots = [index_ref[base + u] for u in range(chunk)]
                 values = [table[pl.ds(pl.multiple_of(spot, 2), 2), :] for spot in spots]
                 for u in range(chunk):
@@ -580,11 +586,14 @@
                 flows[pl.ds(spot, high), :] = parts[edge]
             wider[pl.ds(at, high), :] = total
 
+        part = blocks // 2
+        origin = step // (steps // 2) * (K * part) + lax.rem(step, steps // 2) * tile
+
         def scatter(turn):
             for u in range(chunk):
                 spots, sums = [], []
                 for edge in range(K):
-                    base = edge * blocks + step * tile + turn * chunk
+                    base = edge * part + turn * chunk + origin
                     spots.append(pl.multiple_of(index_ref[base + u], 2))
                 for edge in range(K):
                     spot = pl.multiple_of(edge * 2 * tile + turn * high + 2 * u, 2)
@@ -920,7 +929,8 @@
         (sent, partner, neighbours, counted, counts)
     )
     counts = counts + swapped(counts, "dp", 1)
-    index = 2 * ((neighbours - band * blocks + H) % (blocks * bands)).T.reshape(-1)
+    index = 2 * ((neighbours - band * blocks + H) % (blocks * bands)).T
+    index = index.reshape(K, 2, blocks // 2).swapaxes(0, 1).reshape(-1)
     moved = [(n, place) for n, place in enumerate(walk) if n != place]
     stays = jnp.asarray([n == place for n, place in enumerate(walk)])[band]
     index = lax.ppermute(index, "space", list(enumerate(walk)))
@@ -963,9 +973,13 @@
         mats = w_round[layer]
         if layer + 1 < ROUNDS:
             following = w_round[layer + 1]
-            *outs, first = round_forward(index, mesh, pieces, mats, terms, following, half=0)
+            reached = [pieces, pieces] if layer == 0 else [pieces[:-1], pieces[1:]]
+            indexes = [index[: K * blocks // 2], index[K * blocks // 2 :]]
+            *outs, first = round_forward(
+                indexes[0], mesh, reached[0], mats, terms, following, half=0
+            )
             *outs, second = round_forward(
-                index, mesh, pieces, mats, terms, following, half=1, into=outs
+                indexes[1], mesh, reached[1], mats, terms, following, half=1, into=outs
             )
             sent = [first, second]
         else:
@@ -1031,10 +1045,14 @@
             )
         from_before, from_after = halo(walk, to_after, to_before)
         if first_step:
-            grad_wout, grad_wdec, grad_bdec = decode_grads(decoded, landed, fetched, extra)
-            from_before, final_mesh = lax.optimization_barrier(
-                (from_before, settled(mesh, final_mesh))
+            from_before, final_mesh, head_grads = lax.optimization_barrier(
+                (
+                    from_before,
+                    settled(mesh, final_mesh),
+                    decode_grads(decoded, landed, fetched, extra),
+                )
             )
+            grad_wout, grad_wdec, grad_bdec = head_grads
         past = () if first_step else (kept[layer + 1][0], extra)
         part, mats_grads[2 * layer + 1], bias_grads[layer], *source = weight_grads(
             old, dest_low, agg, grad_uin, update, leaving, grad_mesh, w_round[layer], past

time: 461 us -> 456 us (0.989)
  waiting for transfers between devices: 98.4 us -> 92.6 us
    ppermute x8, waiting for transfers between devices: 12 us -> 4.82 us  [halo(): lax.ppermute(initial, 'space', down)]
    unnamed x77 -> x81, local copies, waits for them, and re-layouts: 8.91 us -> 9.77 us
  transfers between devices with their start and end apart: 51 -> 51, of which waited for: 27 -> 26; matrix products, arithmetic and copies ran while one was open for 5% -> 5% of each run, Pallas kernels for 22% -> 25%
where the time goes in v1:
time: 456 us; the launch traced here: 454 us
  Pallas kernels  225 us (49%)
  waiting for transfers between devices  92.6 us (20%)
  starting transfers between devices  84.6 us (19%)
  other arithmetic  22.5 us (5%)
  local copies, waits for them, and re-layouts  18.3 us (4%)
  between operations  7.8 us (2%)
    pallas_call x5, Pallas kernels, round_forward(): pl.pallas_call(body, grid_spec=pltpu.PrefetchScalarGridSpec(num_scalar_pr...  83.2 us
    pallas_call x3, Pallas kernels, edges_backward(): pl.pallas_call(body, grid_spec=pltpu.PrefetchScalarGridSpec(num_scalar_pr...  78.6 us
    ppermute x25, waiting for transfers between devices, swapped(): lax.ppermute(value, axis, [(i, i ^ bit) for i in range(lax.axis_size(axis...  31.3 us
    ppermute x25, starting transfers between devices, swapped(): lax.ppermute(value, axis, [(i, i ^ bit) for i in range(lax.axis_size(axis...  29.3 us
    pallas_call x3, Pallas kernels, weight_grads(): pl.pallas_call(body, grid=(blocks // tile,), in_specs=[rows] * 7 + [whole...  24.3 us
    all_to_all x3, waiting for transfers between devices, exchanged(): lax.all_to_all(rows.reshape(bands, capacity, HALF), 'space', split_axis=0...  22.2 us
    ppermute x8, starting transfers between devices, halo(): lax.ppermute(initial, 'space', down)  21.8 us
    ppermute x8, waiting for transfers between devices, halo(): lax.ppermute(last, 'space', up)  21.1 us
  transfers between devices with their start and end apart: 51, of which 26 were waited for; matrix products, arithmetic and copies ran while one was open for 5% of the time, Pallas kernels for 25%

profile of v1, /device:TPU:0, one launch (start us, length us, event | category | flops | bytes accessed | tf_op | source)
XLA Modules:
  0.0 454.2 jit_solution(5151194849835870724)
XLA Ops:
  2.5 5.1 %collective-permute-start.2 = (bf16[1,144,256]{2,1,0:T(8,128)(2,1)S(1)}, bf16[1,144,256]{2,1,0:T(8,128)(2,1)S(1)}, u32[]{:S(2)}, u32[]{:S(2)}) collective-permute-start(bf16[1,144,256]{2,1,0:T(8,128)(2,1)S(1)} %broadcast_in_dim_reshape.3), channel_id=1, source_target_pairs={{0,12},{1,13},{2,14},{3,15},{4,8},{5,9},{6,10},{7,11},{8,4},{9,5},... | collective-permute-start | bytes 221192 | tf_op jit(solution)/shard_map/ppermute | solution.py:94
  26.1 4.8 %collective-permute-done.6 = bf16[8,72,256]{2,1,0:T(8,128)(2,1)S(1)} collective-permute-done((bf16[8,72,256]{2,1,0:T(8,128)(2,1)S(1)}, bf16[8,72,256]{2,1,0:T(8,128)(2,1)S(1)}, u32[]{:S(2)}, u32[]{:S(2)}) %collective-permute-start.6) | collective-permute-done | bytes 294944 | tf_op jit(solution)/shard_map/ppermute | solution.py:94
  32.4 5.2 %all-to-all-start = ((bf16[16,64,128]{2,1,0:T(8,128)(2,1)}), bf16[16,64,128]{2,1,0:T(8,128)(2,1)S(1)}, u32[]{:S(2)}, u32[]{:S(2)}) async-start(bf16[16,64,128]{2,1,0:T(8,128)(2,1)} %bitcast.4), calls=%async_computation | async-start | bytes 524288 | tf_op jit(solution)/shard_map/all_to_all | solution.py:907
  38.6 4.0 spread_rows.1
  42.6 5.4 %all-to-all-done = bf16[16,64,128]{2,1,0:T(8,128)(2,1)S(1)} async-done(((bf16[16,64,128]{2,1,0:T(8,128)(2,1)}), bf16[16,64,128]{2,1,0:T(8,128)(2,1)S(1)}, u32[]{:S(2)}, u32[]{:S(2)}) %all-to-all-start) | async-done | bytes 262176 | tf_op jit(solution)/shard_map/all_to_all | solution.py:907
  48.7 6.0 %encode_rows.1 = (f32[2048,256]{1,0:T(8,128)}, bf16[2048,256]{1,0:T(8,128)(2,1)}, bf16[4096,128]{1,0:T(8,128)(2,1)}, s32[1,1024]{1,0:T(1,128)}, s32[1024,1]{1,0:T(8,128)}) custom-call(bf16[1024,128]{1,0:T(8,128)(2,1)} %bitcast.132, bf16[128,256]{1,0:T(8,128)(2,1)} %get-tuple-element.147.in_ref, bf16[256,256]{1,0:T(8,128)(2,1)} %get-tuple-element.148.node_ref, ...), custom_call_target="tpu_custom_call" | custom-call | bytes 15000000 | tf_op jit(solution)/shard_map/encode_rows/pallas_call | solution.py:783
  60.5 3.9 node_terms.3
  64.4 4.5 collective-permute-start.12
  69.6 11.0 %collective-permute-done.13 = bf16[79,360]{1,0:T(8,128)(2,1)S(1)} collective-permute-done((bf16[79,360]{1,0:T(8,128)(2,1)S(1)}, bf16[79,360]{1,0:T(8,128)(2,1)S(1)}, u32[]{:S(2)}, u32[]{:S(2)}) %collective-permute-start.13) | collective-permute-done | bytes 56912 | tf_op jit(solution)/shard_map/ppermute | solution.py:49
  80.8 2.5 collective-permute-done.10.refs_0_
  84.3 14.3 %round_forward.5 = (f32[2048,256]{1,0:T(8,128)}, f32[2048,256]{1,0:T(8,128)}, bf16[2048,256]{1,0:T(8,128)(2,1)}, bf16[2048,256]{1,0:T(8,128)(2,1)}, bf16[6,4096,...) custom-call(s32[6144]{0:T(1024)} %get-tuple-element.325.index_ref, f32[2048,256]{1,0:T(8,128)} %get-tuple-element.154.mesh_ref, ...), custom_call_target="tpu_custom_call" | custom-call | bytes 42000000 | tf_op jit(solution)/shard_map/round_forward/pallas_call | solution.py:497
  98.5 2.5 collective-permute-start.16
  101.1 14.4 %round_forward.6 = (f32[2048,256]{1,0:T(8,128)}, f32[2048,256]{1,0:T(8,128)}, bf16[2048,256]{1,0:T(8,128)(2,1)}, bf16[2048,256]{1,0:T(8,128)(2,1)}, bf16[6,4096,...) custom-call(s32[6144]{0:T(1024)} %get-tuple-element.326.index_ref, ...), custom_call_target="tpu_custom_call", output_to_operand_aliasing={{0}: (9, {}), {1}: (10, {}), {2}: (11, {}), {3}: (12, {}), ... | custom-call | bytes 42000000 | tf_op jit(solution)/shard_map/round_forward/pallas_call | solution.py:497
  117.2 3.9 node_terms.4
  121.1 2.5 collective-permute-start.18
  123.6 5.2 %collective-permute-done.17.refs_1_.refs_0_ = bf16[2048,128]{1,0:T(8,128)(2,1)S(1)} collective-permute-done((bf16[2048,128]{1,0:T(8,128)(2,1)}, bf16[2048,128]{1,0:T(8,128)(2,1)S(1)}, u32[]{:S(2)}, u32[]{:S(2)}) %collective-permute-start.17) | collective-permute-done | bytes 524320 | tf_op jit(solution)/shard_map/ppermute | solution.py:77
  129.7 14.1 %round_forward.7 = (f32[2048,256]{1,0:T(8,128)}, f32[2048,256]{1,0:T(8,128)}, bf16[2048,256]{1,0:T(8,128)(2,1)}, bf16[2048,256]{1,0:T(8,128)(2,1)}, bf16[6,4096,...) custom-call(s32[6144]{0:T(1024)} %get-tuple-element.325.index_ref, f32[2048,256]{1,0:T(8,128)} %get-tuple-element.168.mesh_ref.refs_0_, ...), custom_call_target="tpu_custom_call" | custom-call | bytes 42000000 | tf_op jit(solution)/shard_map/round_forward/pallas_call | solution.py:497
  147.0 14.1 %round_forward.8 = (f32[2048,256]{1,0:T(8,128)}, f32[2048,256]{1,0:T(8,128)}, bf16[2048,256]{1,0:T(8,128)(2,1)}, bf16[2048,256]{1,0:T(8,128)(2,1)}, bf16[6,4096,...) custom-call(s32[6144]{0:T(1024)} %get-tuple-element.326.index_ref, ...), custom_call_target="tpu_custom_call", output_to_operand_aliasing={{0}: (11, {}), {1}: (12, {}), {2}: (13, {}), {3}: (14, {}),... | custom-call | bytes 42000000 | tf_op jit(solution)/shard_map/round_forward/pallas_call | solution.py:497
  161.2 3.2 collective-permute-start.22
  165.3 3.9 node_terms.5
  169.1 4.8 %collective-permute-done.22.refs_5_ = bf16[2048,128]{1,0:T(8,128)(2,1)S(1)} collective-permute-done((bf16[2048,128]{1,0:T(8,128)(2,1)}, bf16[2048,128]{1,0:T(8,128)(2,1)S(1)}, u32[]{:S(2)}, u32[]{:S(2)}) %collective-permute-start.22) | collective-permute-done | bytes 524320 | tf_op jit(solution)/shard_map/ppermute | solution.py:77
  173.9 3.0 collective-permute-done.21.refs_1_
  177.7 26.4 %round_forward.9 = (f32[2048,256]{1,0:T(8,128)}, f32[2048,256]{1,0:T(8,128)}, bf16[2048,256]{1,0:T(8,128)(2,1)}, bf16[2048,256]{1,0:T(8,128)(2,1)}, bf16[6,4096,...) custom-call(s32[12288]{0:T(1024)} %copy-done.11, ...), custom_call_target="tpu_custom_call" | custom-call | bytes 72000000 | tf_op jit(solution)/shard_map/round_forward/pallas_call | solution.py:497
  204.0 3.5 all-to-all-start.1
  207.7 8.4 %all-to-all-done.1 = bf16[16,64,128]{2,1,0:T(8,128)(2,1)S(1)} async-done(((bf16[16,64,128]{2,1,0:T(8,128)(2,1)}), bf16[16,64,128]{2,1,0:T(8,128)(2,1)S(1)}, u32[]{:S(2)}, u32[]{:S(2)}) %all-to-all-start.1) | async-done | bytes 262176 | tf_op jit(solution)/shard_map/all_to_all | solution.py:907
  216.7 3.3 collective-permute-start.23
  229.8 5.8 %all-to-all-start.2 = ((bf16[16,64,128]{2,1,0:T(8,128)(2,1)}), bf16[16,64,128]{2,1,0:T(8,128)(2,1)S(1)}, u32[]{:S(2)}, u32[]{:S(2)}) async-start(bf16[16,64,128]{2,1,0:T(8,128)(2,1)} %bitcast.20), calls=%async_computation.2 | async-start | bytes 524288 | tf_op jit(solution)/shard_map/all_to_all | solution.py:907
  235.8 8.4 %all-to-all-done.2 = bf16[16,64,128]{2,1,0:T(8,128)(2,1)S(1)} async-done(((bf16[16,64,128]{2,1,0:T(8,128)(2,1)}), bf16[16,64,128]{2,1,0:T(8,128)(2,1)S(1)}, u32[]{:S(2)}, u32[]{:S(2)}) %all-to-all-start.2) | async-done | bytes 262176 | tf_op jit(solution)/shard_map/all_to_all | solution.py:907
  245.8 26.8 %edges_backward.3 = (f32[2048,256]{1,0:T(8,128)}, bf16[2048,256]{1,0:T(8,128)(2,1)}, bf16[1024,256]{1,0:T(8,128)(2,1)}, bf16[2048,256]{1,0:T(8,128)(2,1)}, bf16[...) custom-call(s32[12288]{0:T(1024)} %copy-done.11, ...), custom_call_target="tpu_custom_call" | custom-call | bytes 75000000 | tf_op jit(solution)/shard_map/edges_backward/pallas_call | solution.py:642
  277.2 2.6 decode_grads.1
  279.8 7.3 %weight_grads.3 = (f32[2048,256]{1,0:T(8,128)}, f32[1024,256]{1,0:T(8,128)}, f32[2,256]{1,0:T(2,128)}) custom-call(f32[2048,256]{1,0:T(8,128)} %get-tuple-element.182.mesh_ref.refs_0_, bf16[2048,256]{1,0:T(8,128)(2,1)} %get-tuple-element.206.dest_ref, bf16[2048,256]{1,0:T(8,128)(2,1)} %get-tuple-element.207.agg_ref, ...), custom_call_target="tpu_custom_call" | custom-call | bytes 30000000 | tf_op jit(solution)/shard_map/weight_grads/pallas_call | solution.py:727
  287.1 3.4 convert_select_fusion
  292.4 25.8 %edges_backward.4 = (f32[2048,256]{1,0:T(8,128)}, bf16[2048,256]{1,0:T(8,128)(2,1)}, bf16[2048,256]{1,0:T(8,128)(2,1)}, bf16[2048,256]{1,0:T(8,128)(2,1)}, bf16[...) custom-call(s32[12288]{0:T(1024)} %copy-done.11, ...), custom_call_target="tpu_custom_call" | custom-call | bytes 84000000 | tf_op jit(solution)/shard_map/edges_backward/pallas_call | solution.py:642
  318.3 3.8 collective-permute-start.29
  322.2 8.5 %weight_grads.4 = (f32[2048,256]{1,0:T(8,128)}, f32[1024,256]{1,0:T(8,128)}, f32[2,256]{1,0:T(2,128)}, f32[256,256]{1,0:T(8,128)}) custom-call(f32[2048,256]{1,0:T(8,128)} %get-tuple-element.168.mesh_ref.refs_0_, bf16[2048,256]{1,0:T(8,128)(2,1)} %get-tuple-element.227.dest_ref, bf16[2048,256]{1,0:T(8,128)(2,1)} %get-tuple-element.228.agg_ref, ...), custom_call_target="tpu_custom_call" | custom-call | bytes 30000000 | tf_op jit(solution)/shard_map/weight_grads/pallas_call | solution.py:727
  330.7 5.5 %collective-permute-done.28.refs_6_ = bf16[4096,128]{1,0:T(8,128)(2,1)S(1)} collective-permute-done((bf16[4096,128]{1,0:T(8,128)(2,1)}, bf16[4096,128]{1,0:T(8,128)(2,1)S(1)}, u32[]{:S(2)}, u32[]{:S(2)}) %collective-permute-start.28) | collective-permute-done | bytes 1048608 | tf_op jit(solution)/shard_map/ppermute | solution.py:77
  337.6 26.0 %edges_backward.5 = (f32[2048,256]{1,0:T(8,128)}, bf16[2048,256]{1,0:T(8,128)(2,1)}, bf16[2048,256]{1,0:T(8,128)(2,1)}, bf16[2048,256]{1,0:T(8,128)(2,1)}, bf16[...) custom-call(s32[12288]{0:T(1024)} %copy-done.11, ...), custom_call_target="tpu_custom_call" | custom-call | bytes 84000000 | tf_op jit(solution)/shard_map/edges_backward/pallas_call | solution.py:642
  363.6 3.8 collective-permute-start.31
  368.3 8.5 %weight_grads.5 = (f32[2048,256]{1,0:T(8,128)}, f32[1024,256]{1,0:T(8,128)}, f32[2,256]{1,0:T(2,128)}, f32[256,256]{1,0:T(8,128)}) custom-call(f32[2048,256]{1,0:T(8,128)} %get-tuple-element.154.mesh_ref, bf16[2048,256]{1,0:T(8,128)(2,1)} %get-tuple-element.238.dest_ref, bf16[2048,256]{1,0:T(8,128)(2,1)} %get-tuple-element.239.agg_ref, ...), custom_call_target="tpu_custom_call" | custom-call | bytes 30000000 | tf_op jit(solution)/shard_map/weight_grads/pallas_call | solution.py:727
  376.7 3.9 collective-permute-done.30.first_ref
  382.0 10.1 %encode_backward.1 = (f32[2048,256]{1,0:T(8,128)}, bf16[2048,256]{1,0:T(8,128)(2,1)}, f32[128,256]{1,0:T(8,128)}, f32[256,256]{1,0:T(8,128)}, f32[2,256]{1,0:T(2,128)}, /*index=5*/f32[256,256]{1,0:T(8,128)}) custom-call(f32[2048,256]{1,0:T(8,128)} %get-tuple-element.245.part_ref, f32[4096,128]{1,0:T(8,128)} %get-tuple-element.246.own_ref, ...), custom_call_target="tpu_custom_call" | custom-call | bytes 30000000 | tf_op jit(solution)/shard_map/encode_backward/pallas_call | solution.py:848
  392.1 5.1 %collect_rows.1 = (f32[16,144,256]{2,1,0:T(8,128)}, bf16[16,144,256]{2,1,0:T(8,128)(2,1)}) custom-call(s32[1]{0:T(128)} %bitcast.6.place_ref, f32[128,256]{1,0:T(8,128)} %get-tuple-element.250.refs_0_, f32[256,256]{1,0:T(8,128)} %get-tuple-element.251.refs_1_, f32[256,256]{1,0:T(8,128)} %get-tuple-element.252.refs_2_, f32[78,256]{1,0:T(8,128)} %reshape.160.refs_3_, ...), custom_call_target="tpu_custom_call" | custom-call | bytes 15000000 | tf_op jit(solution)/shard_map/collect_rows/pallas_call | solution.py:233
  397.2 3.1 collective-permute-done.32
  402.5 8.9 %collective-permute-done.33 = bf16[4,2,72,256]{3,2,0,1:T(8,128)(2,1)S(1)} collective-permute-done((bf16[4,2,72,256]{3,2,0,1:T(8,128)(2,1)S(1)}, bf16[4,2,72,256]{3,2,0,1:T(8,128)(2,1)S(1)}, u32[]{:S(2)}, u32[]{:S(2)}) %collective-permute-start.33) | collective-permute-done | bytes 294944 | tf_op jit(solution)/shard_map/ppermute | solution.py:94
  413.4 3.3 collective-permute-done.34
  419.0 5.4 %collective-permute-start.39 = (bf16[1,144,256]{2,1,0:T(8,128)(2,1)S(1)}, bf16[1,144,256]{2,1,0:T(8,128)(2,1)S(1)}, u32[]{:S(2)}, u32[]{:S(2)}) collective-permute-start(bf16[1,144,256]{2,1,0:T(8,128)(2,1)S(1)} %get-tuple-element.317), channel_id=1, source_target_pairs={{0,12},{1,13},{2,14},{3,15},{4,8},{5,9},{6,10},{7,11},{8,4},{9,5},... | collective-permute-start | bytes 221192 | tf_op jit(solution)/shard_map/ppermute | solution.py:94
  439.5 5.2 %collective-permute-start.47 = (f32[8,128]{1,0:T(8,128)S(1)}, f32[8,128]{1,0:T(8,128)S(1)}, u32[]{:S(2)}, u32[]{:S(2)}) collective-permute-start(f32[8,128]{1,0:T(8,128)S(1)} %add.191), channel_id=1, source_target_pairs={{0,3},{1,2},{2,1},{3,0},{4,7},{5,6},{6,5},{7,4},{8,11},{9,10},{10,... | collective-permute-start | bytes 12296 | tf_op jit(solution)/shard_map/ppermute | solution.py:94
  446.1 3.5 select_bitcast_fusion
  (233 shorter events, 81.8 us)
Async XLA Ops:
  2.5 14.5 %collective-permute-start.2 = (bf16[1,144,256]{2,1,0:T(8,128)(2,1)S(1)}, bf16[1,144,256]{2,1,0:T(8,128)(2,1)S(1)}, u32[]{:S(2)}, u32[]{:S(2)}) collective-permute-start(bf16[1,144,256]{2,1,0:T(8,128)(2,1)S(1)} %broadcast_in_dim_reshape.3), channel_id=1, source_target_pairs={{0,12},{1,13},{2,14},{3,15},{4,8},{5,9},{6,10},{7,11},{8,4},{9,5},... | collective-permute-start | bytes 221192 | tf_op jit(solution)/shard_map/ppermute | solution.py:94
  7.6 9.4 %collective-permute-start.1 = (bf16[1,144,256]{2,1,0:T(8,128)(2,1)S(1)}, bf16[1,144,256]{2,1,0:T(8,128)(2,1)S(1)}, u32[]{:S(2)}, u32[]{:S(2)}) collective-permute-start(bf16[1,144,256]{2,1,0:T(8,128)(2,1)S(1)} %broadcast_in_dim_reshape.3), channel_id=1, source_target_pairs={{0,8},{1,9},{2,10},{3,11},{4,12},{5,13},{6,14},{7,15},{8,0},{9,1},... | collective-permute-start | bytes 221192 | tf_op jit(solution)/shard_map/ppermute | solution.py:94
  7.6 9.4 %collective-permute-start = (bf16[1,144,256]{2,1,0:T(8,128)(2,1)S(1)}, bf16[1,144,256]{2,1,0:T(8,128)(2,1)S(1)}, u32[]{:S(2)}, u32[]{:S(2)}) collective-permute-start(bf16[1,144,256]{2,1,0:T(8,128)(2,1)S(1)} %broadcast_in_dim_reshape.3), channel_id=1, source_target_pairs={{0,4},{1,5},{2,6},{3,7},{4,0},{5,1},{6,2},{7,3},{8,12},{9,13},{10,... | collective-permute-start | bytes 221192 | tf_op jit(solution)/shard_map/ppermute | solution.py:94
  17.0 5.2 %collective-permute-start.4 = (bf16[4,72,256]{2,1,0:T(8,128)(2,1)S(1)}, bf16[4,72,256]{2,1,0:T(8,128)(2,1)S(1)}, u32[]{:S(2)}, u32[]{:S(2)}) collective-permute-start(bf16[4,72,256]{2,1,0:T(8,128)(2,1)S(1)} %get-tuple-element.319), channel_id=1, source_target_pairs={{0,1},{1,0},{2,3},{3,2},{4,5},{5,4},{6,7},{7,6},{8,9},{9,8},{10,11... | collective-permute-start | bytes 442376 | tf_op jit(solution)/shard_map/ppermute | solution.py:94
  18.7 5.1 %collective-permute-start.3 = (bf16[4,72,256]{2,1,0:T(8,128)(2,1)S(1)}, bf16[4,72,256]{2,1,0:T(8,128)(2,1)S(1)}, u32[]{:S(2)}, u32[]{:S(2)}) collective-permute-start(bf16[4,72,256]{2,1,0:T(8,128)(2,1)S(1)} %get-tuple-element.320), channel_id=1, source_target_pairs={{0,2},{1,3},{2,0},{3,1},{4,6},{5,7},{6,4},{7,5},{8,10},{9,11},{10,... | collective-permute-start | bytes 442376 | tf_op jit(solution)/shard_map/ppermute | solution.py:94
  23.9 7.0 %collective-permute-start.6 = (bf16[8,72,256]{2,1,0:T(8,128)(2,1)S(1)}, bf16[8,72,256]{2,1,0:T(8,128)(2,1)S(1)}, u32[]{:S(2)}, u32[]{:S(2)}) collective-permute-start(bf16[8,72,256]{2,1,0:T(8,128)(2,1)S(1)} %pad_maximum_fusion.3), channel_id=1, source_target_pairs={{0,2},{1,3},{2,0},{3,1},{4,6},{5,7},{6,4},{7,5},{8,10},{9,11},{10,... | collective-permute-start | bytes 884744 | tf_op jit(solution)/shard_map/ppermute | solution.py:94
  25.5 6.7 %collective-permute-start.5 = (bf16[8,72,256]{2,1,0:T(8,128)(2,1)S(1)}, bf16[8,72,256]{2,1,0:T(8,128)(2,1)S(1)}, u32[]{:S(2)}, u32[]{:S(2)}) collective-permute-start(bf16[8,72,256]{2,1,0:T(8,128)(2,1)S(1)} %pad_maximum_fusion.2), channel_id=1, source_target_pairs={{0,1},{1,0},{2,3},{3,2},{4,5},{5,4},{6,7},{7,6},{8,9},{9,8},{10,11... | collective-permute-start | bytes 884744 | tf_op jit(solution)/shard_map/ppermute | solution.py:94
  30.9 6.7 %collective-permute-start.8 = (bf16[16,72,256]{2,1,0:T(8,128)(2,1)S(1)}, bf16[16,72,256]{2,1,0:T(8,128)(2,1)S(1)}, u32[]{:S(2)}, u32[]{:S(2)}) collective-permute-start(bf16[16,72,256]{2,1,0:T(8,128)(2,1)S(1)} %constant_dynamic-update-slice_fusion.6.refs_1_), channel_id=1, source_target_pairs={{0,16},{16,0},{1,17},{17,1},{2,18},{18,2},{3,19},{19,3},{4,20},{20... | collective-permute-start | bytes 1769480 | tf_op jit(solution)/shard_map/ppermute | solution.py:94
  32.3 5.3 %collective-permute-start.7 = (bf16[16,72,256]{2,1,0:T(8,128)(2,1)S(1)}, bf16[16,72,256]{2,1,0:T(8,128)(2,1)S(1)}, u32[]{:S(2)}, u32[]{:S(2)}) collective-permute-start(bf16[16,72,256]{2,1,0:T(8,128)(2,1)S(1)} %constant_dynamic-update-slice_fusion.4.refs_0_), channel_id=1, source_target_pairs={{0,16},{16,0},{1,17},{17,1},{2,18},{18,2},{3,19},{19,3},{4,20},{20... | collective-permute-start | bytes 1769480 | tf_op jit(solution)/shard_map/ppermute | solution.py:94
  32.4 15.6 %all-to-all-start = ((bf16[16,64,128]{2,1,0:T(8,128)(2,1)}), bf16[16,64,128]{2,1,0:T(8,128)(2,1)S(1)}, u32[]{:S(2)}, u32[]{:S(2)}) async-start(bf16[16,64,128]{2,1,0:T(8,128)(2,1)} %bitcast.4), calls=%async_computation | async-start | bytes 524288 | tf_op jit(solution)/shard_map/all_to_all | solution.py:907
  54.8 26.0 %collective-permute-start.11 = (bf16[4096,128]{1,0:T(8,128)(2,1)}, bf16[4096,128]{1,0:T(8,128)(2,1)S(1)}, u32[]{:S(2)}, u32[]{:S(2)}) collective-permute-start(bf16[4096,128]{1,0:T(8,128)(2,1)} %get-tuple-element.155.refs_1_), channel_id=1, source_target_pairs={{1,0},{3,1},{2,3},{6,2},{4,6},{5,4},{7,5},{11,7},{9,11},{8,9},{10,... | collective-permute-start | bytes 3145736 | tf_op jit(solution)/shard_map/ppermute | solution.py:77
  56.5 26.8 %collective-permute-start.10 = (bf16[4096,128]{1,0:T(8,128)(2,1)}, bf16[4096,128]{1,0:T(8,128)(2,1)S(1)}, u32[]{:S(2)}, u32[]{:S(2)}) collective-permute-start(bf16[4096,128]{1,0:T(8,128)(2,1)} %get-tuple-element.155.refs_1_), channel_id=1, source_target_pairs={{0,1},{1,3},{3,2},{2,6},{6,4},{4,5},{5,7},{7,11},{11,9},{9,8},{8,1... | collective-permute-start | bytes 3145736 | tf_op jit(solution)/shard_map/ppermute | solution.py:77
  56.9 12.0 %collective-permute-start.9 = (s32[12288]{0:T(1024)S(1)}, s32[12288]{0:T(1024)S(1)}, u32[]{:S(2)}, u32[]{:S(2)}) collective-permute-start(s32[12288]{0:T(1024)S(1)} %reshape.152), channel_id=1, source_target_pairs={{0,0},{1,1},{2,3},{3,2},{4,6},{5,4},{6,5},{7,7},{8,11},{9,9},{10,8... | collective-permute-start | bytes 147464 | tf_op jit(solution)/shard_map/ppermute | solution.py:936
  59.1 5.3 %collective-permute-start.14 = (f32[1,3]{1,0:T(1,128)S(1)}, f32[1,3]{1,0:T(1,128)S(1)}, u32[]{:S(2)}, u32[]{:S(2)}) collective-permute-start(f32[1,3]{1,0:T(1,128)S(1)} %bitcast.147), channel_id=1, source_target_pairs={{0,16},{16,0},{1,17},{17,1},{2,18},{18,2},{3,19},{19,3},{4,20},{20... | collective-permute-start | bytes 44 | tf_op jit(solution)/shard_map/ppermute | solution.py:94
  59.2 21.4 %collective-permute-start.13 = (bf16[79,360]{1,0:T(8,128)(2,1)S(1)}, bf16[79,360]{1,0:T(8,128)(2,1)S(1)}, u32[]{:S(2)}, u32[]{:S(2)}) collective-permute-start(bf16[79,360]{1,0:T(8,128)(2,1)S(1)} %get-tuple-element.321), channel_id=1, source_target_pairs={{1,0},{2,1},{3,2},{4,3},{5,4},{6,5},{7,6},{8,7},{9,8},{10,9},{11,1... | collective-permute-start | bytes 170648 | tf_op jit(solution)/shard_map/ppermute | solution.py:49
  64.4 16.2 %collective-permute-start.12 = (bf16[79,360]{1,0:T(8,128)(2,1)S(1)}, bf16[79,360]{1,0:T(8,128)(2,1)S(1)}, u32[]{:S(2)}, u32[]{:S(2)}) collective-permute-start(bf16[79,360]{1,0:T(8,128)(2,1)S(1)} %get-tuple-element.322), channel_id=1, source_target_pairs={{0,1},{1,2},{2,3},{3,4},{4,5},{5,6},{6,7},{7,8},{8,9},{9,10},{10,1... | collective-permute-start | bytes 170648 | tf_op jit(solution)/shard_map/ppermute | solution.py:49
  98.5 16.9 %collective-permute-start.16 = (bf16[2048,128]{1,0:T(8,128)(2,1)}, bf16[2048,128]{1,0:T(8,128)(2,1)S(1)}, u32[]{:S(2)}, u32[]{:S(2)}) collective-permute-start(bf16[2048,128]{1,0:T(8,128)(2,1)} %get-tuple-element.170.refs_2_.refs_1_), channel_id=1, source_target_pairs={{1,0},{3,1},{2,3},{6,2},{4,6},{5,4},{7,5},{11,7},{9,11},{8,9},{10,... | collective-permute-start | bytes 1572872 | tf_op jit(solution)/shard_map/ppermute | solution.py:77
  101.1 14.4 %collective-permute-start.15 = (bf16[2048,128]{1,0:T(8,128)(2,1)}, bf16[2048,128]{1,0:T(8,128)(2,1)S(1)}, u32[]{:S(2)}, u32[]{:S(2)}) collective-permute-start(bf16[2048,128]{1,0:T(8,128)(2,1)} %get-tuple-element.170.refs_2_.refs_1_), channel_id=1, source_target_pairs={{0,1},{1,3},{3,2},{2,6},{6,4},{4,5},{5,7},{7,11},{11,9},{9,8},{8,1... | collective-permute-start | bytes 1572872 | tf_op jit(solution)/shard_map/ppermute | solution.py:77
  115.5 13.4 %collective-permute-start.17 = (bf16[2048,128]{1,0:T(8,128)(2,1)}, bf16[2048,128]{1,0:T(8,128)(2,1)S(1)}, u32[]{:S(2)}, u32[]{:S(2)}) collective-permute-start(bf16[2048,128]{1,0:T(8,128)(2,1)} %get-tuple-element.171.refs_3_.refs_2_), channel_id=1, source_target_pairs={{0,1},{1,3},{3,2},{2,6},{6,4},{4,5},{5,7},{7,11},{11,9},{9,8},{8,1... | collective-permute-start | bytes 1572872 | tf_op jit(solution)/shard_map/ppermute | solution.py:77
  121.1 25.1 %collective-permute-start.18 = (bf16[2048,128]{1,0:T(8,128)(2,1)S(1)}, bf16[2048,128]{1,0:T(8,128)(2,1)S(1)}, u32[]{:S(2)}, u32[]{:S(2)}) collective-permute-start(bf16[2048,128]{1,0:T(8,128)(2,1)S(1)} %copy-done.6), channel_id=1, source_target_pairs={{1,0},{3,1},{2,3},{6,2},{4,6},{5,4},{7,5},{11,7},{9,11},{8,9},{10,... | collective-permute-start | bytes 1572872 | tf_op jit(solution)/shard_map/ppermute | solution.py:77
  143.7 17.4 %collective-permute-start.20 = (bf16[2048,128]{1,0:T(8,128)(2,1)}, bf16[2048,128]{1,0:T(8,128)(2,1)S(1)}, u32[]{:S(2)}, u32[]{:S(2)}) collective-permute-start(bf16[2048,128]{1,0:T(8,128)(2,1)} %get-tuple-element.184.refs_2_), channel_id=1, source_target_pairs={{1,0},{3,1},{2,3},{6,2},{4,6},{5,4},{7,5},{11,7},{9,11},{8,9},{10,... | collective-permute-start | bytes 1572872 | tf_op jit(solution)/shard_map/ppermute | solution.py:77
  145.5 15.7 %collective-permute-start.19 = (bf16[2048,128]{1,0:T(8,128)(2,1)}, bf16[2048,128]{1,0:T(8,128)(2,1)S(1)}, u32[]{:S(2)}, u32[]{:S(2)}) collective-permute-start(bf16[2048,128]{1,0:T(8,128)(2,1)} %get-tuple-element.184.refs_2_), channel_id=1, source_target_pairs={{0,1},{1,3},{3,2},{2,6},{6,4},{4,5},{5,7},{7,11},{11,9},{9,8},{8,1... | collective-permute-start | bytes 1572872 | tf_op jit(solution)/shard_map/ppermute | solution.py:77
  161.2 12.7 %collective-permute-start.22 = (bf16[2048,128]{1,0:T(8,128)(2,1)}, bf16[2048,128]{1,0:T(8,128)(2,1)S(1)}, u32[]{:S(2)}, u32[]{:S(2)}) collective-permute-start(bf16[2048,128]{1,0:T(8,128)(2,1)} %get-tuple-element.186.refs_3_), channel_id=1, source_target_pairs={{1,0},{3,1},{2,3},{6,2},{4,6},{5,4},{7,5},{11,7},{9,11},{8,9},{10,... | collective-permute-start | bytes 1572872 | tf_op jit(solution)/shard_map/ppermute | solution.py:77
  164.4 12.5 %collective-permute-start.21 = (bf16[2048,128]{1,0:T(8,128)(2,1)}, bf16[2048,128]{1,0:T(8,128)(2,1)S(1)}, u32[]{:S(2)}, u32[]{:S(2)}) collective-permute-start(bf16[2048,128]{1,0:T(8,128)(2,1)} %get-tuple-element.186.refs_3_), channel_id=1, source_target_pairs={{0,1},{1,3},{3,2},{2,6},{6,4},{4,5},{5,7},{7,11},{11,9},{9,8},{8,1... | collective-permute-start | bytes 1572872 | tf_op jit(solution)/shard_map/ppermute | solution.py:77
  204.0 12.0 %all-to-all-start.1 = ((bf16[16,64,128]{2,1,0:T(8,128)(2,1)}), bf16[16,64,128]{2,1,0:T(8,128)(2,1)S(1)}, u32[]{:S(2)}, u32[]{:S(2)}) async-start(bf16[16,64,128]{2,1,0:T(8,128)(2,1)} %bitcast.141), calls=%async_computation.1 | async-start | bytes 524288 | tf_op jit(solution)/shard_map/all_to_all | solution.py:907
  216.7 9.5 %collective-permute-start.23 = (bf16[78,360]{1,0:T(8,128)(2,1)S(1)}, bf16[78,360]{1,0:T(8,128)(2,1)S(1)}, u32[]{:S(2)}, u32[]{:S(2)}) collective-permute-start(bf16[78,360]{1,0:T(8,128)(2,1)S(1)} %get-tuple-element.323), channel_id=1, source_target_pairs={{0,1},{1,2},{2,3},{3,4},{4,5},{5,6},{6,7},{7,8},{8,9},{9,10},{10,1... | collective-permute-start | bytes 168488 | tf_op jit(solution)/shard_map/ppermute | solution.py:49
  220.0 6.1 %collective-permute-start.24 = (bf16[78,360]{1,0:T(8,128)(2,1)S(1)}, bf16[78,360]{1,0:T(8,128)(2,1)S(1)}, u32[]{:S(2)}, u32[]{:S(2)}) collective-permute-start(bf16[78,360]{1,0:T(8,128)(2,1)S(1)} %get-tuple-element.324), channel_id=1, source_target_pairs={{1,0},{2,1},{3,2},{4,3},{5,4},{6,5},{7,6},{8,7},{9,8},{10,9},{11,1... | collective-permute-start | bytes 168488 | tf_op jit(solution)/shard_map/ppermute | solution.py:49
  229.8 14.4 %all-to-all-start.2 = ((bf16[16,64,128]{2,1,0:T(8,128)(2,1)}), bf16[16,64,128]{2,1,0:T(8,128)(2,1)S(1)}, u32[]{:S(2)}, u32[]{:S(2)}) async-start(bf16[16,64,128]{2,1,0:T(8,128)(2,1)} %bitcast.20), calls=%async_computation.2 | async-start | bytes 524288 | tf_op jit(solution)/shard_map/all_to_all | solution.py:907
  244.2 28.4 %collective-permute-start.25 = (bf16[2048,256]{1,0:T(8,128)(2,1)S(1)}, bf16[2048,256]{1,0:T(8,128)(2,1)}, u32[]{:S(2)}, u32[]{:S(2)}) collective-permute-start(bf16[2048,256]{1,0:T(8,128)(2,1)S(1)} %convert_element_type.150), channel_id=1, source_target_pairs={{3,2},{2,3},{6,4},{4,5},{5,6},{11,8},{8,10},{10,11},{14,12},{15,13... | collective-permute-start | bytes 3145736 | tf_op jit(solution)/shard_map/ppermute | solution.py:939
  272.6 18.8 %collective-permute-start.26 = (bf16[4096,128]{1,0:T(8,128)(2,1)}, bf16[4096,128]{1,0:T(8,128)(2,1)S(1)}, u32[]{:S(2)}, u32[]{:S(2)}) collective-permute-start(bf16[4096,128]{1,0:T(8,128)(2,1)} %get-tuple-element.217), channel_id=1, source_target_pairs={{0,1},{1,3},{3,2},{2,6},{6,4},{4,5},{5,7},{7,11},{11,9},{9,8},{8,1... | collective-permute-start | bytes 3145736 | tf_op jit(solution)/shard_map/ppermute | solution.py:77
  274.1 17.4 %collective-permute-start.27 = (bf16[4096,128]{1,0:T(8,128)(2,1)}, bf16[4096,128]{1,0:T(8,128)(2,1)}, u32[]{:S(2)}, u32[]{:S(2)}) collective-permute-start(bf16[4096,128]{1,0:T(8,128)(2,1)} %get-tuple-element.226), channel_id=1, source_target_pairs={{1,0},{3,1},{2,3},{6,2},{4,6},{5,4},{7,5},{11,7},{9,11},{8,9},{10,... | collective-permute-start | bytes 3145736 | tf_op jit(solution)/shard_map/ppermute | solution.py:77
  318.3 17.9 %collective-permute-start.28 = (bf16[4096,128]{1,0:T(8,128)(2,1)}, bf16[4096,128]{1,0:T(8,128)(2,1)S(1)}, u32[]{:S(2)}, u32[]{:S(2)}) collective-permute-start(bf16[4096,128]{1,0:T(8,128)(2,1)} %get-tuple-element.236), channel_id=1, source_target_pairs={{0,1},{1,3},{3,2},{2,6},{6,4},{4,5},{5,7},{7,11},{11,9},{9,8},{8,1... | collective-permute-start | bytes 3145736 | tf_op jit(solution)/shard_map/ppermute | solution.py:77
  318.3 17.9 %collective-permute-start.29 = (bf16[4096,128]{1,0:T(8,128)(2,1)}, bf16[4096,128]{1,0:T(8,128)(2,1)S(1)}, u32[]{:S(2)}, u32[]{:S(2)}) collective-permute-start(bf16[4096,128]{1,0:T(8,128)(2,1)} %get-tuple-element.237), channel_id=1, source_target_pairs={{1,0},{3,1},{2,3},{6,2},{4,6},{5,4},{7,5},{11,7},{9,11},{8,9},{10,... | collective-permute-start | bytes 3145736 | tf_op jit(solution)/shard_map/ppermute | solution.py:77
  363.6 17.0 %collective-permute-start.30 = (bf16[4096,128]{1,0:T(8,128)(2,1)}, bf16[4096,128]{1,0:T(8,128)(2,1)S(1)}, u32[]{:S(2)}, u32[]{:S(2)}) collective-permute-start(bf16[4096,128]{1,0:T(8,128)(2,1)} %get-tuple-element.247), channel_id=1, source_target_pairs={{0,1},{1,3},{3,2},{2,6},{6,4},{4,5},{5,7},{7,11},{11,9},{9,8},{8,1... | collective-permute-start | bytes 3145736 | tf_op jit(solution)/shard_map/ppermute | solution.py:77
  363.6 16.9 %collective-permute-start.31 = (bf16[4096,128]{1,0:T(8,128)(2,1)}, bf16[4096,128]{1,0:T(8,128)(2,1)S(1)}, u32[]{:S(2)}, u32[]{:S(2)}) collective-permute-start(bf16[4096,128]{1,0:T(8,128)(2,1)} %get-tuple-element.248), channel_id=1, source_target_pairs={{1,0},{3,1},{2,3},{6,2},{4,6},{5,4},{7,5},{11,7},{9,11},{8,9},{10,... | collective-permute-start | bytes 3145736 | tf_op jit(solution)/shard_map/ppermute | solution.py:77
  402.3 9.1 %collective-permute-start.33 = (bf16[4,2,72,256]{3,2,0,1:T(8,128)(2,1)S(1)}, bf16[4,2,72,256]{3,2,0,1:T(8,128)(2,1)S(1)}, u32[]{:S(2)}, u32[]{:S(2)}) collective-permute-start(bf16[4,2,72,256]{3,2,0,1:T(8,128)(2,1)S(1)} %fusion.14), channel_id=1, source_target_pairs={{0,1},{1,0},{2,3},{3,2},{4,5},{5,4},{6,7},{7,6},{8,9},{9,8},{10,11... | collective-permute-start | bytes 884744 | tf_op jit(solution)/shard_map/ppermute | solution.py:94
  402.4 9.2 %collective-permute-start.35 = (bf16[4,2,72,256]{3,2,1,0:T(8,128)(2,1)S(1)}, bf16[4,2,72,256]{3,2,1,0:T(8,128)(2,1)S(1)}, u32[]{:S(2)}, u32[]{:S(2)}) collective-permute-start(bf16[4,2,72,256]{3,2,1,0:T(8,128)(2,1)S(1)} %fusion.13), channel_id=1, source_target_pairs={{0,2},{1,3},{2,0},{3,1},{4,6},{5,7},{6,4},{7,5},{8,10},{9,11},{10,... | collective-permute-start | bytes 884744 | tf_op jit(solution)/shard_map/ppermute | solution.py:94
  411.6 5.2 %collective-permute-start.34 = (bf16[4,72,256]{2,1,0:T(8,128)(2,1)S(1)}, bf16[4,72,256]{2,1,0:T(8,128)(2,1)S(1)}, u32[]{:S(2)}, u32[]{:S(2)}) collective-permute-start(bf16[4,72,256]{2,1,0:T(8,128)(2,1)S(1)} %fusion.38), channel_id=1, source_target_pairs={{0,2},{1,3},{2,0},{3,1},{4,6},{5,7},{6,4},{7,5},{8,10},{9,11},{10,... | collective-permute-start | bytes 442376 | tf_op jit(solution)/shard_map/ppermute | solution.py:94
  411.7 5.2 %collective-permute-start.36 = (bf16[4,72,256]{2,1,0:T(8,128)(2,1)S(1)}, bf16[4,72,256]{2,1,0:T(8,128)(2,1)S(1)}, u32[]{:S(2)}, u32[]{:S(2)}) collective-permute-start(bf16[4,72,256]{2,1,0:T(8,128)(2,1)S(1)} %fusion.39), channel_id=1, source_target_pairs={{0,1},{1,0},{2,3},{3,2},{4,5},{5,4},{6,7},{7,6},{8,9},{9,8},{10,11... | collective-permute-start | bytes 442376 | tf_op jit(solution)/shard_map/ppermute | solution.py:94
  417.0 22.4 %collective-permute-start.44 = (bf16[2048,256]{1,0:T(8,128)(2,1)}, bf16[2048,256]{1,0:T(8,128)(2,1)}, u32[]{:S(2)}, u32[]{:S(2)}) collective-permute-start(bf16[2048,256]{1,0:T(8,128)(2,1)} %get-tuple-element.269), channel_id=1, source_target_pairs={{3,2},{2,3},{6,4},{4,5},{5,6},{11,8},{8,10},{10,11},{14,12},{15,13... | collective-permute-start | bytes 3145736 | tf_op jit(solution)/shard_map/ppermute | solution.py:939
  418.9 7.2 %collective-permute-start.37 = (bf16[1,144,256]{2,1,0:T(8,128)(2,1)S(1)}, bf16[1,144,256]{2,1,0:T(8,128)(2,1)S(1)}, u32[]{:S(2)}, u32[]{:S(2)}) collective-permute-start(bf16[1,144,256]{2,1,0:T(8,128)(2,1)S(1)} %get-tuple-element.316), channel_id=1, source_target_pairs={{0,4},{1,5},{2,6},{3,7},{4,0},{5,1},{6,2},{7,3},{8,12},{9,13},{10,... | collective-permute-start | bytes 221192 | tf_op jit(solution)/shard_map/ppermute | solution.py:94
  419.0 9.3 %collective-permute-start.39 = (bf16[1,144,256]{2,1,0:T(8,128)(2,1)S(1)}, bf16[1,144,256]{2,1,0:T(8,128)(2,1)S(1)}, u32[]{:S(2)}, u32[]{:S(2)}) collective-permute-start(bf16[1,144,256]{2,1,0:T(8,128)(2,1)S(1)} %get-tuple-element.317), channel_id=1, source_target_pairs={{0,12},{1,13},{2,14},{3,15},{4,8},{5,9},{6,10},{7,11},{8,4},{9,5},... | collective-permute-start | bytes 221192 | tf_op jit(solution)/shard_map/ppermute | solution.py:94
  424.3 6.1 %collective-permute-start.38 = (bf16[1,144,256]{2,1,0:T(8,128)(2,1)S(1)}, bf16[1,144,256]{2,1,0:T(8,128)(2,1)S(1)}, u32[]{:S(2)}, u32[]{:S(2)}) collective-permute-start(bf16[1,144,256]{2,1,0:T(8,128)(2,1)S(1)} %get-tuple-element.318), channel_id=1, source_target_pairs={{0,8},{1,9},{2,10},{3,11},{4,12},{5,13},{6,14},{7,15},{8,0},{9,1},... | collective-permute-start | bytes 221192 | tf_op jit(solution)/shard_map/ppermute | solution.py:94
  432.0 4.6 %collective-permute-start.41 = (f32[8,128]{1,0:T(8,128)S(1)}, f32[8,128]{1,0:T(8,128)S(1)}, u32[]{:S(2)}, u32[]{:S(2)}) collective-permute-start(f32[8,128]{1,0:T(8,128)S(1)} %iota.23), channel_id=1, source_target_pairs={{0,8},{1,9},{2,10},{3,11},{4,12},{5,13},{6,14},{7,15},{8,0},{9,1},... | collective-permute-start | bytes 12296 | tf_op jit(solution)/shard_map/ppermute | solution.py:94
  432.4 5.4 %collective-permute-start.42 = (f32[8,128]{1,0:T(8,128)S(1)}, f32[8,128]{1,0:T(8,128)S(1)}, u32[]{:S(2)}, u32[]{:S(2)}) collective-permute-start(f32[8,128]{1,0:T(8,128)S(1)} %iota.23), channel_id=1, source_target_pairs={{0,12},{1,13},{2,14},{3,15},{4,8},{5,9},{6,10},{7,11},{8,4},{9,5},... | collective-permute-start | bytes 12296 | tf_op jit(solution)/shard_map/ppermute | solution.py:94
  439.5 10.1 %collective-permute-start.47 = (f32[8,128]{1,0:T(8,128)S(1)}, f32[8,128]{1,0:T(8,128)S(1)}, u32[]{:S(2)}, u32[]{:S(2)}) collective-permute-start(f32[8,128]{1,0:T(8,128)S(1)} %add.191), channel_id=1, source_target_pairs={{0,3},{1,2},{2,1},{3,0},{4,7},{5,6},{6,5},{7,4},{8,11},{9,10},{10,... | collective-permute-start | bytes 12296 | tf_op jit(solution)/shard_map/ppermute | solution.py:94
  444.6 5.0 %collective-permute-start.46 = (f32[8,128]{1,0:T(8,128)S(1)}, f32[8,128]{1,0:T(8,128)S(1)}, u32[]{:S(2)}, u32[]{:S(2)}) collective-permute-start(f32[8,128]{1,0:T(8,128)S(1)} %add.191), channel_id=1, source_target_pairs={{0,2},{1,3},{2,0},{3,1},{4,6},{5,7},{6,4},{7,5},{8,10},{9,11},{10,... | collective-permute-start | bytes 12296 | tf_op jit(solution)/shard_map/ppermute | solution.py:94
  444.6 5.0 %collective-permute-start.45 = (f32[8,128]{1,0:T(8,128)S(1)}, f32[8,128]{1,0:T(8,128)S(1)}, u32[]{:S(2)}, u32[]{:S(2)}) collective-permute-start(f32[8,128]{1,0:T(8,128)S(1)} %add.191), channel_id=1, source_target_pairs={{0,1},{1,0},{2,3},{3,2},{4,5},{5,4},{6,7},{7,6},{8,9},{9,8},{10,11... | collective-permute-start | bytes 12296 | tf_op jit(solution)/shard_map/ppermute | solution.py:94
  (40 other events, 426.0 us)

commit v2 on v1

--- a/solution.py
+++ b/solution.py
@@ -335,7 +335,7 @@
             jax.ShapeDtypeStruct((2 * blocks, HALF), jnp.float32),
             jax.ShapeDtypeStruct((blocks, D), jnp.float32),
         ],
-        compiler_params=LIMIT,
+        compiler_params=pltpu.CompilerParams(vmem_limit_bytes=63 * 2**20),
         cost_estimate=cost(4),
         name="node_terms",
     )(mesh, mats, bias)
@@ -731,7 +731,7 @@
         out_specs=[rows] + [whole(shape) for shape in shapes],
         out_shape=[jax.ShapeDtypeStruct((blocks, D), jnp.float32)]
         + [jax.ShapeDtypeStruct(shape, jnp.float32) for shape in shapes],
-        compiler_params=LIMIT,
+        compiler_params=pltpu.CompilerParams(vmem_limit_bytes=63 * 2**20),
         cost_estimate=cost(10),
         name="weight_grads",
     )(mesh, dest_low, agg, grad_uin, update, leaving, grad_mesh, mats, *past)
@@ -746,7 +746,7 @@
     return pl.pallas_call(
         body,
         out_shape=[jax.ShapeDtypeStruct(shape, jnp.float32) for shape in ((D, HALF), (D, D), (1, D))],
-        compiler_params=LIMIT,
+        compiler_params=pltpu.CompilerParams(vmem_limit_bytes=63 * 2**20),
         cost_estimate=cost(3),
         name="decode_grads",
     )(decoded, landed, fetched, grad_dec)

time: 456 us -> 450 us (0.987)
  local copies, waits for them, and re-layouts: 18.3 us -> 11.9 us
    unnamed x81 -> x55, local copies, waits for them, and re-layouts: 9.77 us -> 3.47 us
  transfers between devices with their start and end apart: 51 -> 51, of which waited for: 26 -> 26; matrix products, arithmetic and copies ran while one was open for 5% -> 6% of each run, Pallas kernels for 25% -> 25%
where the time goes in v2:
time: 450 us; the launch traced here: 447 us
  Pallas kernels  226 us (50%)
  waiting for transfers between devices  92.3 us (21%)
  starting transfers between devices  83.9 us (19%)
  other arithmetic  22.9 us (5%)
  local copies, waits for them, and re-layouts  11.9 us (3%)
  between operations  7.76 us (2%)
    pallas_call x5, Pallas kernels, round_forward(): pl.pallas_call(body, grid_spec=pltpu.PrefetchScalarGridSpec(num_scalar_pr...  83.3 us
    pallas_call x3, Pallas kernels, edges_backward(): pl.pallas_call(body, grid_spec=pltpu.PrefetchScalarGridSpec(num_scalar_pr...  78.6 us
    ppermute x25, waiting for transfers between devices, swapped(): lax.ppermute(value, axis, [(i, i ^ bit) for i in range(lax.axis_size(axis...  31.3 us
    ppermute x25, starting transfers between devices, swapped(): lax.ppermute(value, axis, [(i, i ^ bit) for i in range(lax.axis_size(axis...  29.3 us
    pallas_call x3, Pallas kernels, weight_grads(): pl.pallas_call(body, grid=(blocks // tile,), in_specs=[rows] * 7 + [whole...  24.4 us
    all_to_all x3, waiting for transfers between devices, exchanged(): lax.all_to_all(rows.reshape(bands, capacity, HALF), 'space', split_axis=0...  22.1 us
    ppermute x8, waiting for transfers between devices, halo(): lax.ppermute(last, 'space', up)  20.8 us
    ppermute x8, starting transfers between devices, halo(): lax.ppermute(initial, 'space', down)  20.6 us
  transfers between devices with their start and end apart: 51, of which 26 were waited for; matrix products, arithmetic and copies ran while one was open for 6% of the time, Pallas kernels for 25%

profile of v2, /device:TPU:0, one launch (start us, length us, event | category | flops | bytes accessed | tf_op | source)
XLA Modules:
  0.0 447.4 jit_solution(13785745725888850698)
XLA Ops:
  2.5 5.1 %collective-permute-start.2 = (bf16[1,144,256]{2,1,0:T(8,128)(2,1)S(1)}, bf16[1,144,256]{2,1,0:T(8,128)(2,1)S(1)}, u32[]{:S(2)}, u32[]{:S(2)}) collective-permute-start(bf16[1,144,256]{2,1,0:T(8,128)(2,1)S(1)} %broadcast_in_dim_reshape.3), channel_id=1, source_target_pairs={{0,12},{1,13},{2,14},{3,15},{4,8},{5,9},{6,10},{7,11},{8,4},{9,5},... | collective-permute-start | bytes 221192 | tf_op jit(solution)/shard_map/ppermute | solution.py:94
  26.1 4.8 %collective-permute-done.6 = bf16[8,72,256]{2,1,0:T(8,128)(2,1)S(1)} collective-permute-done((bf16[8,72,256]{2,1,0:T(8,128)(2,1)S(1)}, bf16[8,72,256]{2,1,0:T(8,128)(2,1)S(1)}, u32[]{:S(2)}, u32[]{:S(2)}) %collective-permute-start.6) | collective-permute-done | bytes 294944 | tf_op jit(solution)/shard_map/ppermute | solution.py:94
  32.4 5.2 %all-to-all-start = ((bf16[16,64,128]{2,1,0:T(8,128)(2,1)}), bf16[16,64,128]{2,1,0:T(8,128)(2,1)S(1)}, u32[]{:S(2)}, u32[]{:S(2)}) async-start(bf16[16,64,128]{2,1,0:T(8,128)(2,1)} %bitcast.4), calls=%async_computation | async-start | bytes 524288 | tf_op jit(solution)/shard_map/all_to_all | solution.py:907
  38.7 4.0 spread_rows.1
  42.6 5.3 %all-to-all-done = bf16[16,64,128]{2,1,0:T(8,128)(2,1)S(1)} async-done(((bf16[16,64,128]{2,1,0:T(8,128)(2,1)}), bf16[16,64,128]{2,1,0:T(8,128)(2,1)S(1)}, u32[]{:S(2)}, u32[]{:S(2)}) %all-to-all-start) | async-done | bytes 262176 | tf_op jit(solution)/shard_map/all_to_all | solution.py:907
  48.7 6.0 %encode_rows.1 = (f32[2048,256]{1,0:T(8,128)}, bf16[2048,256]{1,0:T(8,128)(2,1)}, bf16[4096,128]{1,0:T(8,128)(2,1)}, s32[1,1024]{1,0:T(1,128)}, s32[1024,1]{1,0:T(8,128)}) custom-call(bf16[1024,128]{1,0:T(8,128)(2,1)} %bitcast.132, bf16[128,256]{1,0:T(8,128)(2,1)} %get-tuple-element.147.in_ref, bf16[256,256]{1,0:T(8,128)(2,1)} %get-tuple-element.148.node_ref, ...), custom_call_target="tpu_custom_call" | custom-call | bytes 15000000 | tf_op jit(solution)/shard_map/encode_rows/pallas_call | solution.py:783
  60.4 3.9 node_terms.3
  64.3 4.5 %collective-permute-start.12 = (bf16[79,360]{1,0:T(8,128)(2,1)S(1)}, bf16[79,360]{1,0:T(8,128)(2,1)S(1)}, u32[]{:S(2)}, u32[]{:S(2)}) collective-permute-start(bf16[79,360]{1,0:T(8,128)(2,1)S(1)} %get-tuple-element.322), channel_id=1, source_target_pairs={{0,1},{1,2},{2,3},{3,4},{4,5},{5,6},{6,7},{7,8},{8,9},{9,10},{10,1... | collective-permute-start | bytes 170648 | tf_op jit(solution)/shard_map/ppermute | solution.py:49
  69.5 11.0 %collective-permute-done.13 = bf16[79,360]{1,0:T(8,128)(2,1)S(1)} collective-permute-done((bf16[79,360]{1,0:T(8,128)(2,1)S(1)}, bf16[79,360]{1,0:T(8,128)(2,1)S(1)}, u32[]{:S(2)}, u32[]{:S(2)}) %collective-permute-start.13) | collective-permute-done | bytes 56912 | tf_op jit(solution)/shard_map/ppermute | solution.py:49
  80.7 2.6 collective-permute-done.10.refs_0_
  83.3 14.3 %round_forward.5 = (f32[2048,256]{1,0:T(8,128)}, f32[2048,256]{1,0:T(8,128)}, bf16[2048,256]{1,0:T(8,128)(2,1)}, bf16[2048,256]{1,0:T(8,128)(2,1)}, bf16[6,4096,...) custom-call(s32[6144]{0:T(1024)} %get-tuple-element.325.index_ref, f32[2048,256]{1,0:T(8,128)} %get-tuple-element.154.mesh_ref, ...), custom_call_target="tpu_custom_call" | custom-call | bytes 42000000 | tf_op jit(solution)/shard_map/round_forward/pallas_call | solution.py:497
  99.8 14.3 %round_forward.6 = (f32[2048,256]{1,0:T(8,128)}, f32[2048,256]{1,0:T(8,128)}, bf16[2048,256]{1,0:T(8,128)(2,1)}, bf16[2048,256]{1,0:T(8,128)(2,1)}, bf16[6,4096,...) custom-call(s32[6144]{0:T(1024)} %get-tuple-element.326.index_ref, ...), custom_call_target="tpu_custom_call", output_to_operand_aliasing={{0}: (9, {}), {1}: (10, {}), {2}: (11, {}), {3}: (12, {}), ... | custom-call | bytes 42000000 | tf_op jit(solution)/shard_map/round_forward/pallas_call | solution.py:497
  115.9 3.9 node_terms.4
  122.0 5.8 %collective-permute-done.17.refs_1_.refs_0_ = bf16[2048,128]{1,0:T(8,128)(2,1)} collective-permute-done((bf16[2048,128]{1,0:T(8,128)(2,1)}, bf16[2048,128]{1,0:T(8,128)(2,1)}, u32[]{:S(2)}, u32[]{:S(2)}) %collective-permute-start.17) | collective-permute-done | bytes 524320 | tf_op jit(solution)/shard_map/ppermute | solution.py:77
  127.8 14.0 %round_forward.7 = (f32[2048,256]{1,0:T(8,128)}, f32[2048,256]{1,0:T(8,128)}, bf16[2048,256]{1,0:T(8,128)(2,1)}, bf16[2048,256]{1,0:T(8,128)(2,1)}, bf16[6,4096,...) custom-call(s32[6144]{0:T(1024)} %get-tuple-element.325.index_ref, f32[2048,256]{1,0:T(8,128)} %get-tuple-element.168.mesh_ref.refs_0_, ...), custom_call_target="tpu_custom_call" | custom-call | bytes 42000000 | tf_op jit(solution)/shard_map/round_forward/pallas_call | solution.py:497
  145.0 14.2 %round_forward.8 = (f32[2048,256]{1,0:T(8,128)}, f32[2048,256]{1,0:T(8,128)}, bf16[2048,256]{1,0:T(8,128)(2,1)}, bf16[2048,256]{1,0:T(8,128)(2,1)}, bf16[6,4096,...) custom-call(s32[6144]{0:T(1024)} %get-tuple-element.326.index_ref, ...), custom_call_target="tpu_custom_call", output_to_operand_aliasing={{0}: (11, {}), {1}: (12, {}), {2}: (13, {}), {3}: (14, {}),... | custom-call | bytes 42000000 | tf_op jit(solution)/shard_map/round_forward/pallas_call | solution.py:497
  159.2 3.3 collective-permute-start.22
  163.4 3.9 node_terms.5
  167.3 4.8 %collective-permute-done.22.refs_5_ = bf16[2048,128]{1,0:T(8,128)(2,1)} collective-permute-done((bf16[2048,128]{1,0:T(8,128)(2,1)}, bf16[2048,128]{1,0:T(8,128)(2,1)}, u32[]{:S(2)}, u32[]{:S(2)}) %collective-permute-start.22) | collective-permute-done | bytes 524320 | tf_op jit(solution)/shard_map/ppermute | solution.py:77
  172.0 2.9 collective-permute-done.21.refs_1_
  174.9 26.4 %round_forward.9 = (f32[2048,256]{1,0:T(8,128)}, f32[2048,256]{1,0:T(8,128)}, bf16[2048,256]{1,0:T(8,128)(2,1)}, bf16[2048,256]{1,0:T(8,128)(2,1)}, bf16[6,4096,...) custom-call(s32[12288]{0:T(1024)} %copy-done.7, ...), custom_call_target="tpu_custom_call" | custom-call | bytes 72000000 | tf_op jit(solution)/shard_map/round_forward/pallas_call | solution.py:497
  201.3 3.5 all-to-all-start.1
  204.9 8.4 %all-to-all-done.1 = bf16[16,64,128]{2,1,0:T(8,128)(2,1)S(1)} async-done(((bf16[16,64,128]{2,1,0:T(8,128)(2,1)}), bf16[16,64,128]{2,1,0:T(8,128)(2,1)S(1)}, u32[]{:S(2)}, u32[]{:S(2)}) %all-to-all-start.1) | async-done | bytes 262176 | tf_op jit(solution)/shard_map/all_to_all | solution.py:907
  213.9 3.3 collective-permute-start.23
  221.1 2.3 collective-permute-done.24
  227.0 5.8 %all-to-all-start.2 = ((bf16[16,64,128]{2,1,0:T(8,128)(2,1)}), bf16[16,64,128]{2,1,0:T(8,128)(2,1)S(1)}, u32[]{:S(2)}, u32[]{:S(2)}) async-start(bf16[16,64,128]{2,1,0:T(8,128)(2,1)} %bitcast.20), calls=%async_computation.2 | async-start | bytes 524288 | tf_op jit(solution)/shard_map/all_to_all | solution.py:907
  233.0 8.4 %all-to-all-done.2 = bf16[16,64,128]{2,1,0:T(8,128)(2,1)S(1)} async-done(((bf16[16,64,128]{2,1,0:T(8,128)(2,1)}), bf16[16,64,128]{2,1,0:T(8,128)(2,1)S(1)}, u32[]{:S(2)}, u32[]{:S(2)}) %all-to-all-start.2) | async-done | bytes 262176 | tf_op jit(solution)/shard_map/all_to_all | solution.py:907
  243.1 26.8 %edges_backward.3 = (f32[2048,256]{1,0:T(8,128)}, bf16[2048,256]{1,0:T(8,128)(2,1)}, bf16[1024,256]{1,0:T(8,128)(2,1)}, bf16[2048,256]{1,0:T(8,128)(2,1)}, bf16[...) custom-call(s32[12288]{0:T(1024)} %copy-done.7, ...), custom_call_target="tpu_custom_call" | custom-call | bytes 75000000 | tf_op jit(solution)/shard_map/edges_backward/pallas_call | solution.py:642
  271.4 2.4 collective-permute-start.27
  274.3 2.6 decode_grads.1
  277.0 7.4 %weight_grads.3 = (f32[2048,256]{1,0:T(8,128)}, f32[1024,256]{1,0:T(8,128)}, f32[2,256]{1,0:T(2,128)}) custom-call(f32[2048,256]{1,0:T(8,128)} %get-tuple-element.182.mesh_ref.refs_0_, bf16[2048,256]{1,0:T(8,128)(2,1)} %get-tuple-element.206.dest_ref, bf16[2048,256]{1,0:T(8,128)(2,1)} %get-tuple-element.207.agg_ref, ...), custom_call_target="tpu_custom_call" | custom-call | bytes 30000000 | tf_op jit(solution)/shard_map/weight_grads/pallas_call | solution.py:727
  284.4 4.0 convert_select_fusion
  288.6 25.8 %edges_backward.4 = (f32[2048,256]{1,0:T(8,128)}, bf16[2048,256]{1,0:T(8,128)(2,1)}, bf16[2048,256]{1,0:T(8,128)(2,1)}, bf16[2048,256]{1,0:T(8,128)(2,1)}, bf16[...) custom-call(s32[12288]{0:T(1024)} %copy-done.7, ...), custom_call_target="tpu_custom_call" | custom-call | bytes 84000000 | tf_op jit(solution)/shard_map/edges_backward/pallas_call | solution.py:642
  315.1 3.3 collective-permute-start.29
  318.3 8.6 %weight_grads.4 = (f32[2048,256]{1,0:T(8,128)}, f32[1024,256]{1,0:T(8,128)}, f32[2,256]{1,0:T(2,128)}, f32[256,256]{1,0:T(8,128)}) custom-call(f32[2048,256]{1,0:T(8,128)} %get-tuple-element.168.mesh_ref.refs_0_, bf16[2048,256]{1,0:T(8,128)(2,1)} %get-tuple-element.227.dest_ref, bf16[2048,256]{1,0:T(8,128)(2,1)} %get-tuple-element.228.agg_ref, ...), custom_call_target="tpu_custom_call" | custom-call | bytes 30000000 | tf_op jit(solution)/shard_map/weight_grads/pallas_call | solution.py:727
  326.9 5.4 %collective-permute-done.28.refs_6_ = bf16[4096,128]{1,0:T(8,128)(2,1)} collective-permute-done((bf16[4096,128]{1,0:T(8,128)(2,1)}, bf16[4096,128]{1,0:T(8,128)(2,1)}, u32[]{:S(2)}, u32[]{:S(2)}) %collective-permute-start.28) | collective-permute-done | bytes 1048608 | tf_op jit(solution)/shard_map/ppermute | solution.py:77
  332.3 26.0 %edges_backward.5 = (f32[2048,256]{1,0:T(8,128)}, bf16[2048,256]{1,0:T(8,128)(2,1)}, bf16[2048,256]{1,0:T(8,128)(2,1)}, bf16[2048,256]{1,0:T(8,128)(2,1)}, bf16[...) custom-call(s32[12288]{0:T(1024)} %copy-done.7, ...), custom_call_target="tpu_custom_call" | custom-call | bytes 84000000 | tf_op jit(solution)/shard_map/edges_backward/pallas_call | solution.py:642
  358.4 3.8 collective-permute-start.31
  363.0 8.5 %weight_grads.5 = (f32[2048,256]{1,0:T(8,128)}, f32[1024,256]{1,0:T(8,128)}, f32[2,256]{1,0:T(2,128)}, f32[256,256]{1,0:T(8,128)}) custom-call(f32[2048,256]{1,0:T(8,128)} %get-tuple-element.154.mesh_ref, bf16[2048,256]{1,0:T(8,128)(2,1)} %get-tuple-element.238.dest_ref, bf16[2048,256]{1,0:T(8,128)(2,1)} %get-tuple-element.239.agg_ref, ...), custom_call_target="tpu_custom_call" | custom-call | bytes 30000000 | tf_op jit(solution)/shard_map/weight_grads/pallas_call | solution.py:727
  371.4 3.8 collective-permute-done.30.first_ref
  375.3 10.1 %encode_backward.1 = (f32[2048,256]{1,0:T(8,128)}, bf16[2048,256]{1,0:T(8,128)(2,1)}, f32[128,256]{1,0:T(8,128)}, f32[256,256]{1,0:T(8,128)}, f32[2,256]{1,0:T(2,128)}, /*index=5*/f32[256,256]{1,0:T(8,128)}) custom-call(f32[2048,256]{1,0:T(8,128)} %get-tuple-element.245.part_ref, f32[4096,128]{1,0:T(8,128)} %get-tuple-element.246.own_ref, ...), custom_call_target="tpu_custom_call" | custom-call | bytes 30000000 | tf_op jit(solution)/shard_map/encode_backward/pallas_call | solution.py:848
  385.4 5.1 %collect_rows.1 = (f32[16,144,256]{2,1,0:T(8,128)}, bf16[16,144,256]{2,1,0:T(8,128)(2,1)}) custom-call(s32[1]{0:T(128)} %bitcast.6.place_ref, f32[128,256]{1,0:T(8,128)} %get-tuple-element.250.refs_0_, f32[256,256]{1,0:T(8,128)} %get-tuple-element.251.refs_1_, f32[256,256]{1,0:T(8,128)} %get-tuple-element.252.refs_2_, f32[78,256]{1,0:T(8,128)} %reshape.160.refs_3_, ...), custom_call_target="tpu_custom_call" | custom-call | bytes 15000000 | tf_op jit(solution)/shard_map/collect_rows/pallas_call | solution.py:233
  390.5 3.1 collective-permute-done.32
  395.8 8.9 %collective-permute-done.33 = bf16[4,2,72,256]{3,2,0,1:T(8,128)(2,1)S(1)} collective-permute-done((bf16[4,2,72,256]{3,2,0,1:T(8,128)(2,1)S(1)}, bf16[4,2,72,256]{3,2,0,1:T(8,128)(2,1)S(1)}, u32[]{:S(2)}, u32[]{:S(2)}) %collective-permute-start.33) | collective-permute-done | bytes 294944 | tf_op jit(solution)/shard_map/ppermute | solution.py:94
  406.7 3.3 collective-permute-done.34
  412.6 5.5 %collective-permute-start.39 = (bf16[1,144,256]{2,1,0:T(8,128)(2,1)S(1)}, bf16[1,144,256]{2,1,0:T(8,128)(2,1)S(1)}, u32[]{:S(2)}, u32[]{:S(2)}) collective-permute-start(bf16[1,144,256]{2,1,0:T(8,128)(2,1)S(1)} %get-tuple-element.317), channel_id=1, source_target_pairs={{0,12},{1,13},{2,14},{3,15},{4,8},{5,9},{6,10},{7,11},{8,4},{9,5},... | collective-permute-start | bytes 221192 | tf_op jit(solution)/shard_map/ppermute | solution.py:94
  433.3 4.7 %collective-permute-start.47 = (f32[8,128]{1,0:T(8,128)S(1)}, f32[8,128]{1,0:T(8,128)S(1)}, u32[]{:S(2)}, u32[]{:S(2)}) collective-permute-start(f32[8,128]{1,0:T(8,128)S(1)} %add.191), channel_id=1, source_target_pairs={{0,3},{1,2},{2,1},{3,0},{4,7},{5,6},{6,5},{7,4},{8,11},{9,10},{10,... | collective-permute-start | bytes 12296 | tf_op jit(solution)/shard_map/ppermute | solution.py:94
  439.4 3.4 select_bitcast_fusion
  (207 shorter events, 75.3 us)
Async XLA Ops:
  2.5 14.5 %collective-permute-start.2 = (bf16[1,144,256]{2,1,0:T(8,128)(2,1)S(1)}, bf16[1,144,256]{2,1,0:T(8,128)(2,1)S(1)}, u32[]{:S(2)}, u32[]{:S(2)}) collective-permute-start(bf16[1,144,256]{2,1,0:T(8,128)(2,1)S(1)} %broadcast_in_dim_reshape.3), channel_id=1, source_target_pairs={{0,12},{1,13},{2,14},{3,15},{4,8},{5,9},{6,10},{7,11},{8,4},{9,5},... | collective-permute-start | bytes 221192 | tf_op jit(solution)/shard_map/ppermute | solution.py:94
  7.6 9.4 %collective-permute-start.1 = (bf16[1,144,256]{2,1,0:T(8,128)(2,1)S(1)}, bf16[1,144,256]{2,1,0:T(8,128)(2,1)S(1)}, u32[]{:S(2)}, u32[]{:S(2)}) collective-permute-start(bf16[1,144,256]{2,1,0:T(8,128)(2,1)S(1)} %broadcast_in_dim_reshape.3), channel_id=1, source_target_pairs={{0,8},{1,9},{2,10},{3,11},{4,12},{5,13},{6,14},{7,15},{8,0},{9,1},... | collective-permute-start | bytes 221192 | tf_op jit(solution)/shard_map/ppermute | solution.py:94
  7.6 9.4 %collective-permute-start = (bf16[1,144,256]{2,1,0:T(8,128)(2,1)S(1)}, bf16[1,144,256]{2,1,0:T(8,128)(2,1)S(1)}, u32[]{:S(2)}, u32[]{:S(2)}) collective-permute-start(bf16[1,144,256]{2,1,0:T(8,128)(2,1)S(1)} %broadcast_in_dim_reshape.3), channel_id=1, source_target_pairs={{0,4},{1,5},{2,6},{3,7},{4,0},{5,1},{6,2},{7,3},{8,12},{9,13},{10,... | collective-permute-start | bytes 221192 | tf_op jit(solution)/shard_map/ppermute | solution.py:94
  17.0 5.2 %collective-permute-start.4 = (bf16[4,72,256]{2,1,0:T(8,128)(2,1)S(1)}, bf16[4,72,256]{2,1,0:T(8,128)(2,1)S(1)}, u32[]{:S(2)}, u32[]{:S(2)}) collective-permute-start(bf16[4,72,256]{2,1,0:T(8,128)(2,1)S(1)} %get-tuple-element.319), channel_id=1, source_target_pairs={{0,1},{1,0},{2,3},{3,2},{4,5},{5,4},{6,7},{7,6},{8,9},{9,8},{10,11... | collective-permute-start | bytes 442376 | tf_op jit(solution)/shard_map/ppermute | solution.py:94
  18.7 5.1 %collective-permute-start.3 = (bf16[4,72,256]{2,1,0:T(8,128)(2,1)S(1)}, bf16[4,72,256]{2,1,0:T(8,128)(2,1)S(1)}, u32[]{:S(2)}, u32[]{:S(2)}) collective-permute-start(bf16[4,72,256]{2,1,0:T(8,128)(2,1)S(1)} %get-tuple-element.320), channel_id=1, source_target_pairs={{0,2},{1,3},{2,0},{3,1},{4,6},{5,7},{6,4},{7,5},{8,10},{9,11},{10,... | collective-permute-start | bytes 442376 | tf_op jit(solution)/shard_map/ppermute | solution.py:94
  23.9 7.0 %collective-permute-start.6 = (bf16[8,72,256]{2,1,0:T(8,128)(2,1)S(1)}, bf16[8,72,256]{2,1,0:T(8,128)(2,1)S(1)}, u32[]{:S(2)}, u32[]{:S(2)}) collective-permute-start(bf16[8,72,256]{2,1,0:T(8,128)(2,1)S(1)} %pad_maximum_fusion.3), channel_id=1, source_target_pairs={{0,2},{1,3},{2,0},{3,1},{4,6},{5,7},{6,4},{7,5},{8,10},{9,11},{10,... | collective-permute-start | bytes 884744 | tf_op jit(solution)/shard_map/ppermute | solution.py:94
  25.5 6.7 %collective-permute-start.5 = (bf16[8,72,256]{2,1,0:T(8,128)(2,1)S(1)}, bf16[8,72,256]{2,1,0:T(8,128)(2,1)S(1)}, u32[]{:S(2)}, u32[]{:S(2)}) collective-permute-start(bf16[8,72,256]{2,1,0:T(8,128)(2,1)S(1)} %pad_maximum_fusion.2), channel_id=1, source_target_pairs={{0,1},{1,0},{2,3},{3,2},{4,5},{5,4},{6,7},{7,6},{8,9},{9,8},{10,11... | collective-permute-start | bytes 884744 | tf_op jit(solution)/shard_map/ppermute | solution.py:94
  30.9 6.7 %collective-permute-start.8 = (bf16[16,72,256]{2,1,0:T(8,128)(2,1)S(1)}, bf16[16,72,256]{2,1,0:T(8,128)(2,1)S(1)}, u32[]{:S(2)}, u32[]{:S(2)}) collective-permute-start(bf16[16,72,256]{2,1,0:T(8,128)(2,1)S(1)} %constant_dynamic-update-slice_fusion.6.refs_1_), channel_id=1, source_target_pairs={{0,16},{16,0},{1,17},{17,1},{2,18},{18,2},{3,19},{19,3},{4,20},{20... | collective-permute-start | bytes 1769480 | tf_op jit(solution)/shard_map/ppermute | solution.py:94
  32.3 5.3 %collective-permute-start.7 = (bf16[16,72,256]{2,1,0:T(8,128)(2,1)S(1)}, bf16[16,72,256]{2,1,0:T(8,128)(2,1)S(1)}, u32[]{:S(2)}, u32[]{:S(2)}) collective-permute-start(bf16[16,72,256]{2,1,0:T(8,128)(2,1)S(1)} %constant_dynamic-update-slice_fusion.4.refs_0_), channel_id=1, source_target_pairs={{0,16},{16,0},{1,17},{17,1},{2,18},{18,2},{3,19},{19,3},{4,20},{20... | collective-permute-start | bytes 1769480 | tf_op jit(solution)/shard_map/ppermute | solution.py:94
  32.4 15.6 %all-to-all-start = ((bf16[16,64,128]{2,1,0:T(8,128)(2,1)}), bf16[16,64,128]{2,1,0:T(8,128)(2,1)S(1)}, u32[]{:S(2)}, u32[]{:S(2)}) async-start(bf16[16,64,128]{2,1,0:T(8,128)(2,1)} %bitcast.4), calls=%async_computation | async-start | bytes 524288 | tf_op jit(solution)/shard_map/all_to_all | solution.py:907
  54.7 26.0 %collective-permute-start.11 = (bf16[4096,128]{1,0:T(8,128)(2,1)}, bf16[4096,128]{1,0:T(8,128)(2,1)}, u32[]{:S(2)}, u32[]{:S(2)}) collective-permute-start(bf16[4096,128]{1,0:T(8,128)(2,1)} %get-tuple-element.155.refs_1_), channel_id=1, source_target_pairs={{1,0},{3,1},{2,3},{6,2},{4,6},{5,4},{7,5},{11,7},{9,11},{8,9},{10,... | collective-permute-start | bytes 3145736 | tf_op jit(solution)/shard_map/ppermute | solution.py:77
  56.4 26.9 %collective-permute-start.10 = (bf16[4096,128]{1,0:T(8,128)(2,1)}, bf16[4096,128]{1,0:T(8,128)(2,1)}, u32[]{:S(2)}, u32[]{:S(2)}) collective-permute-start(bf16[4096,128]{1,0:T(8,128)(2,1)} %get-tuple-element.155.refs_1_), channel_id=1, source_target_pairs={{0,1},{1,3},{3,2},{2,6},{6,4},{4,5},{5,7},{7,11},{11,9},{9,8},{8,1... | collective-permute-start | bytes 3145736 | tf_op jit(solution)/shard_map/ppermute | solution.py:77
  56.8 12.0 %collective-permute-start.9 = (s32[12288]{0:T(1024)S(1)}, s32[12288]{0:T(1024)S(1)}, u32[]{:S(2)}, u32[]{:S(2)}) collective-permute-start(s32[12288]{0:T(1024)S(1)} %reshape.152), channel_id=1, source_target_pairs={{0,0},{1,1},{2,3},{3,2},{4,6},{5,4},{6,5},{7,7},{8,11},{9,9},{10,8... | collective-permute-start | bytes 147464 | tf_op jit(solution)/shard_map/ppermute | solution.py:936
  59.0 5.3 %collective-permute-start.14 = (f32[1,3]{1,0:T(1,128)S(1)}, f32[1,3]{1,0:T(1,128)S(1)}, u32[]{:S(2)}, u32[]{:S(2)}) collective-permute-start(f32[1,3]{1,0:T(1,128)S(1)} %bitcast.147), channel_id=1, source_target_pairs={{0,16},{16,0},{1,17},{17,1},{2,18},{18,2},{3,19},{19,3},{4,20},{20... | collective-permute-start | bytes 44 | tf_op jit(solution)/shard_map/ppermute | solution.py:94
  59.1 21.4 %collective-permute-start.13 = (bf16[79,360]{1,0:T(8,128)(2,1)S(1)}, bf16[79,360]{1,0:T(8,128)(2,1)S(1)}, u32[]{:S(2)}, u32[]{:S(2)}) collective-permute-start(bf16[79,360]{1,0:T(8,128)(2,1)S(1)} %get-tuple-element.321), channel_id=1, source_target_pairs={{1,0},{2,1},{3,2},{4,3},{5,4},{6,5},{7,6},{8,7},{9,8},{10,9},{11,1... | collective-permute-start | bytes 170648 | tf_op jit(solution)/shard_map/ppermute | solution.py:49
  64.3 16.2 %collective-permute-start.12 = (bf16[79,360]{1,0:T(8,128)(2,1)S(1)}, bf16[79,360]{1,0:T(8,128)(2,1)S(1)}, u32[]{:S(2)}, u32[]{:S(2)}) collective-permute-start(bf16[79,360]{1,0:T(8,128)(2,1)S(1)} %get-tuple-element.322), channel_id=1, source_target_pairs={{0,1},{1,2},{2,3},{3,4},{4,5},{5,6},{6,7},{7,8},{8,9},{9,10},{10,1... | collective-permute-start | bytes 170648 | tf_op jit(solution)/shard_map/ppermute | solution.py:49
  97.7 16.5 %collective-permute-start.16 = (bf16[2048,128]{1,0:T(8,128)(2,1)}, bf16[2048,128]{1,0:T(8,128)(2,1)S(1)}, u32[]{:S(2)}, u32[]{:S(2)}) collective-permute-start(bf16[2048,128]{1,0:T(8,128)(2,1)} %get-tuple-element.170.refs_2_.refs_1_), channel_id=1, source_target_pairs={{1,0},{3,1},{2,3},{6,2},{4,6},{5,4},{7,5},{11,7},{9,11},{8,9},{10,... | collective-permute-start | bytes 1572872 | tf_op jit(solution)/shard_map/ppermute | solution.py:77
  99.8 14.4 %collective-permute-start.15 = (bf16[2048,128]{1,0:T(8,128)(2,1)}, bf16[2048,128]{1,0:T(8,128)(2,1)}, u32[]{:S(2)}, u32[]{:S(2)}) collective-permute-start(bf16[2048,128]{1,0:T(8,128)(2,1)} %get-tuple-element.170.refs_2_.refs_1_), channel_id=1, source_target_pairs={{0,1},{1,3},{3,2},{2,6},{6,4},{4,5},{5,7},{7,11},{11,9},{9,8},{8,1... | collective-permute-start | bytes 1572872 | tf_op jit(solution)/shard_map/ppermute | solution.py:77
  114.2 13.6 %collective-permute-start.17 = (bf16[2048,128]{1,0:T(8,128)(2,1)}, bf16[2048,128]{1,0:T(8,128)(2,1)}, u32[]{:S(2)}, u32[]{:S(2)}) collective-permute-start(bf16[2048,128]{1,0:T(8,128)(2,1)} %get-tuple-element.171.refs_3_.refs_2_), channel_id=1, source_target_pairs={{0,1},{1,3},{3,2},{2,6},{6,4},{4,5},{5,7},{7,11},{11,9},{9,8},{8,1... | collective-permute-start | bytes 1572872 | tf_op jit(solution)/shard_map/ppermute | solution.py:77
  119.8 24.4 %collective-permute-start.18 = (bf16[2048,128]{1,0:T(8,128)(2,1)}, bf16[2048,128]{1,0:T(8,128)(2,1)S(1)}, u32[]{:S(2)}, u32[]{:S(2)}) collective-permute-start(bf16[2048,128]{1,0:T(8,128)(2,1)} %get-tuple-element.171.refs_3_.refs_2_), channel_id=1, source_target_pairs={{1,0},{3,1},{2,3},{6,2},{4,6},{5,4},{7,5},{11,7},{9,11},{8,9},{10,... | collective-permute-start | bytes 1572872 | tf_op jit(solution)/shard_map/ppermute | solution.py:77
  141.8 17.3 %collective-permute-start.20 = (bf16[2048,128]{1,0:T(8,128)(2,1)}, bf16[2048,128]{1,0:T(8,128)(2,1)S(1)}, u32[]{:S(2)}, u32[]{:S(2)}) collective-permute-start(bf16[2048,128]{1,0:T(8,128)(2,1)} %get-tuple-element.184.refs_2_), channel_id=1, source_target_pairs={{1,0},{3,1},{2,3},{6,2},{4,6},{5,4},{7,5},{11,7},{9,11},{8,9},{10,... | collective-permute-start | bytes 1572872 | tf_op jit(solution)/shard_map/ppermute | solution.py:77
  143.6 15.6 %collective-permute-start.19 = (bf16[2048,128]{1,0:T(8,128)(2,1)}, bf16[2048,128]{1,0:T(8,128)(2,1)}, u32[]{:S(2)}, u32[]{:S(2)}) collective-permute-start(bf16[2048,128]{1,0:T(8,128)(2,1)} %get-tuple-element.184.refs_2_), channel_id=1, source_target_pairs={{0,1},{1,3},{3,2},{2,6},{6,4},{4,5},{5,7},{7,11},{11,9},{9,8},{8,1... | collective-permute-start | bytes 1572872 | tf_op jit(solution)/shard_map/ppermute | solution.py:77
  159.2 12.8 %collective-permute-start.22 = (bf16[2048,128]{1,0:T(8,128)(2,1)}, bf16[2048,128]{1,0:T(8,128)(2,1)}, u32[]{:S(2)}, u32[]{:S(2)}) collective-permute-start(bf16[2048,128]{1,0:T(8,128)(2,1)} %get-tuple-element.186.refs_3_), channel_id=1, source_target_pairs={{1,0},{3,1},{2,3},{6,2},{4,6},{5,4},{7,5},{11,7},{9,11},{8,9},{10,... | collective-permute-start | bytes 1572872 | tf_op jit(solution)/shard_map/ppermute | solution.py:77
  162.5 12.4 %collective-permute-start.21 = (bf16[2048,128]{1,0:T(8,128)(2,1)}, bf16[2048,128]{1,0:T(8,128)(2,1)}, u32[]{:S(2)}, u32[]{:S(2)}) collective-permute-start(bf16[2048,128]{1,0:T(8,128)(2,1)} %get-tuple-element.186.refs_3_), channel_id=1, source_target_pairs={{0,1},{1,3},{3,2},{2,6},{6,4},{4,5},{5,7},{7,11},{11,9},{9,8},{8,1... | collective-permute-start | bytes 1572872 | tf_op jit(solution)/shard_map/ppermute | solution.py:77
  201.3 12.0 %all-to-all-start.1 = ((bf16[16,64,128]{2,1,0:T(8,128)(2,1)}), bf16[16,64,128]{2,1,0:T(8,128)(2,1)S(1)}, u32[]{:S(2)}, u32[]{:S(2)}) async-start(bf16[16,64,128]{2,1,0:T(8,128)(2,1)} %bitcast.141), calls=%async_computation.1 | async-start | bytes 524288 | tf_op jit(solution)/shard_map/all_to_all | solution.py:907
  213.9 9.5 %collective-permute-start.23 = (bf16[78,360]{1,0:T(8,128)(2,1)S(1)}, bf16[78,360]{1,0:T(8,128)(2,1)S(1)}, u32[]{:S(2)}, u32[]{:S(2)}) collective-permute-start(bf16[78,360]{1,0:T(8,128)(2,1)S(1)} %get-tuple-element.323), channel_id=1, source_target_pairs={{0,1},{1,2},{2,3},{3,4},{4,5},{5,6},{6,7},{7,8},{8,9},{9,10},{10,1... | collective-permute-start | bytes 168488 | tf_op jit(solution)/shard_map/ppermute | solution.py:49
  217.3 6.1 %collective-permute-start.24 = (bf16[78,360]{1,0:T(8,128)(2,1)S(1)}, bf16[78,360]{1,0:T(8,128)(2,1)S(1)}, u32[]{:S(2)}, u32[]{:S(2)}) collective-permute-start(bf16[78,360]{1,0:T(8,128)(2,1)S(1)} %get-tuple-element.324), channel_id=1, source_target_pairs={{1,0},{2,1},{3,2},{4,3},{5,4},{6,5},{7,6},{8,7},{9,8},{10,9},{11,1... | collective-permute-start | bytes 168488 | tf_op jit(solution)/shard_map/ppermute | solution.py:49
  227.0 14.4 %all-to-all-start.2 = ((bf16[16,64,128]{2,1,0:T(8,128)(2,1)}), bf16[16,64,128]{2,1,0:T(8,128)(2,1)S(1)}, u32[]{:S(2)}, u32[]{:S(2)}) async-start(bf16[16,64,128]{2,1,0:T(8,128)(2,1)} %bitcast.20), calls=%async_computation.2 | async-start | bytes 524288 | tf_op jit(solution)/shard_map/all_to_all | solution.py:907
  241.4 28.5 %collective-permute-start.25 = (bf16[2048,256]{1,0:T(8,128)(2,1)S(1)}, bf16[2048,256]{1,0:T(8,128)(2,1)}, u32[]{:S(2)}, u32[]{:S(2)}) collective-permute-start(bf16[2048,256]{1,0:T(8,128)(2,1)S(1)} %convert_element_type.150), channel_id=1, source_target_pairs={{3,2},{2,3},{6,4},{4,5},{5,6},{11,8},{8,10},{10,11},{14,12},{15,13... | collective-permute-start | bytes 3145736 | tf_op jit(solution)/shard_map/ppermute | solution.py:939
  269.9 18.7 %collective-permute-start.26 = (bf16[4096,128]{1,0:T(8,128)(2,1)}, bf16[4096,128]{1,0:T(8,128)(2,1)}, u32[]{:S(2)}, u32[]{:S(2)}) collective-permute-start(bf16[4096,128]{1,0:T(8,128)(2,1)} %get-tuple-element.217), channel_id=1, source_target_pairs={{0,1},{1,3},{3,2},{2,6},{6,4},{4,5},{5,7},{7,11},{11,9},{9,8},{8,1... | collective-permute-start | bytes 3145736 | tf_op jit(solution)/shard_map/ppermute | solution.py:77
  271.4 17.2 %collective-permute-start.27 = (bf16[4096,128]{1,0:T(8,128)(2,1)}, bf16[4096,128]{1,0:T(8,128)(2,1)}, u32[]{:S(2)}, u32[]{:S(2)}) collective-permute-start(bf16[4096,128]{1,0:T(8,128)(2,1)} %get-tuple-element.226), channel_id=1, source_target_pairs={{1,0},{3,1},{2,3},{6,2},{4,6},{5,4},{7,5},{11,7},{9,11},{8,9},{10,... | collective-permute-start | bytes 3145736 | tf_op jit(solution)/shard_map/ppermute | solution.py:77
  314.4 17.9 %collective-permute-start.28 = (bf16[4096,128]{1,0:T(8,128)(2,1)}, bf16[4096,128]{1,0:T(8,128)(2,1)}, u32[]{:S(2)}, u32[]{:S(2)}) collective-permute-start(bf16[4096,128]{1,0:T(8,128)(2,1)} %get-tuple-element.236), channel_id=1, source_target_pairs={{0,1},{1,3},{3,2},{2,6},{6,4},{4,5},{5,7},{7,11},{11,9},{9,8},{8,1... | collective-permute-start | bytes 3145736 | tf_op jit(solution)/shard_map/ppermute | solution.py:77
  315.1 17.2 %collective-permute-start.29 = (bf16[4096,128]{1,0:T(8,128)(2,1)}, bf16[4096,128]{1,0:T(8,128)(2,1)}, u32[]{:S(2)}, u32[]{:S(2)}) collective-permute-start(bf16[4096,128]{1,0:T(8,128)(2,1)} %get-tuple-element.237), channel_id=1, source_target_pairs={{1,0},{3,1},{2,3},{6,2},{4,6},{5,4},{7,5},{11,7},{9,11},{8,9},{10,... | collective-permute-start | bytes 3145736 | tf_op jit(solution)/shard_map/ppermute | solution.py:77
  358.3 17.0 %collective-permute-start.30 = (bf16[4096,128]{1,0:T(8,128)(2,1)}, bf16[4096,128]{1,0:T(8,128)(2,1)}, u32[]{:S(2)}, u32[]{:S(2)}) collective-permute-start(bf16[4096,128]{1,0:T(8,128)(2,1)} %get-tuple-element.247), channel_id=1, source_target_pairs={{0,1},{1,3},{3,2},{2,6},{6,4},{4,5},{5,7},{7,11},{11,9},{9,8},{8,1... | collective-permute-start | bytes 3145736 | tf_op jit(solution)/shard_map/ppermute | solution.py:77
  358.4 16.9 %collective-permute-start.31 = (bf16[4096,128]{1,0:T(8,128)(2,1)}, bf16[4096,128]{1,0:T(8,128)(2,1)}, u32[]{:S(2)}, u32[]{:S(2)}) collective-permute-start(bf16[4096,128]{1,0:T(8,128)(2,1)} %get-tuple-element.248), channel_id=1, source_target_pairs={{1,0},{3,1},{2,3},{6,2},{4,6},{5,4},{7,5},{11,7},{9,11},{8,9},{10,... | collective-permute-start | bytes 3145736 | tf_op jit(solution)/shard_map/ppermute | solution.py:77
  395.6 9.1 %collective-permute-start.33 = (bf16[4,2,72,256]{3,2,0,1:T(8,128)(2,1)S(1)}, bf16[4,2,72,256]{3,2,0,1:T(8,128)(2,1)S(1)}, u32[]{:S(2)}, u32[]{:S(2)}) collective-permute-start(bf16[4,2,72,256]{3,2,0,1:T(8,128)(2,1)S(1)} %fusion.14), channel_id=1, source_target_pairs={{0,1},{1,0},{2,3},{3,2},{4,5},{5,4},{6,7},{7,6},{8,9},{9,8},{10,11... | collective-permute-start | bytes 884744 | tf_op jit(solution)/shard_map/ppermute | solution.py:94
  395.7 9.2 %collective-permute-start.35 = (bf16[4,2,72,256]{3,2,1,0:T(8,128)(2,1)S(1)}, bf16[4,2,72,256]{3,2,1,0:T(8,128)(2,1)S(1)}, u32[]{:S(2)}, u32[]{:S(2)}) collective-permute-start(bf16[4,2,72,256]{3,2,1,0:T(8,128)(2,1)S(1)} %fusion.13), channel_id=1, source_target_pairs={{0,2},{1,3},{2,0},{3,1},{4,6},{5,7},{6,4},{7,5},{8,10},{9,11},{10,... | collective-permute-start | bytes 884744 | tf_op jit(solution)/shard_map/ppermute | solution.py:94
  404.9 5.2 %collective-permute-start.34 = (bf16[4,72,256]{2,1,0:T(8,128)(2,1)S(1)}, bf16[4,72,256]{2,1,0:T(8,128)(2,1)S(1)}, u32[]{:S(2)}, u32[]{:S(2)}) collective-permute-start(bf16[4,72,256]{2,1,0:T(8,128)(2,1)S(1)} %fusion.38), channel_id=1, source_target_pairs={{0,2},{1,3},{2,0},{3,1},{4,6},{5,7},{6,4},{7,5},{8,10},{9,11},{10,... | collective-permute-start | bytes 442376 | tf_op jit(solution)/shard_map/ppermute | solution.py:94
  405.0 5.2 %collective-permute-start.36 = (bf16[4,72,256]{2,1,0:T(8,128)(2,1)S(1)}, bf16[4,72,256]{2,1,0:T(8,128)(2,1)S(1)}, u32[]{:S(2)}, u32[]{:S(2)}) collective-permute-start(bf16[4,72,256]{2,1,0:T(8,128)(2,1)S(1)} %fusion.39), channel_id=1, source_target_pairs={{0,1},{1,0},{2,3},{3,2},{4,5},{5,4},{6,7},{7,6},{8,9},{9,8},{10,11... | collective-permute-start | bytes 442376 | tf_op jit(solution)/shard_map/ppermute | solution.py:94
  410.3 22.9 %collective-permute-start.44 = (bf16[2048,256]{1,0:T(8,128)(2,1)}, bf16[2048,256]{1,0:T(8,128)(2,1)}, u32[]{:S(2)}, u32[]{:S(2)}) collective-permute-start(bf16[2048,256]{1,0:T(8,128)(2,1)} %get-tuple-element.269), channel_id=1, source_target_pairs={{3,2},{2,3},{6,4},{4,5},{5,6},{11,8},{8,10},{10,11},{14,12},{15,13... | collective-permute-start | bytes 3145736 | tf_op jit(solution)/shard_map/ppermute | solution.py:939
  412.2 7.7 %collective-permute-start.37 = (bf16[1,144,256]{2,1,0:T(8,128)(2,1)S(1)}, bf16[1,144,256]{2,1,0:T(8,128)(2,1)S(1)}, u32[]{:S(2)}, u32[]{:S(2)}) collective-permute-start(bf16[1,144,256]{2,1,0:T(8,128)(2,1)S(1)} %get-tuple-element.316), channel_id=1, source_target_pairs={{0,4},{1,5},{2,6},{3,7},{4,0},{5,1},{6,2},{7,3},{8,12},{9,13},{10,... | collective-permute-start | bytes 221192 | tf_op jit(solution)/shard_map/ppermute | solution.py:94
  412.6 9.4 %collective-permute-start.39 = (bf16[1,144,256]{2,1,0:T(8,128)(2,1)S(1)}, bf16[1,144,256]{2,1,0:T(8,128)(2,1)S(1)}, u32[]{:S(2)}, u32[]{:S(2)}) collective-permute-start(bf16[1,144,256]{2,1,0:T(8,128)(2,1)S(1)} %get-tuple-element.317), channel_id=1, source_target_pairs={{0,12},{1,13},{2,14},{3,15},{4,8},{5,9},{6,10},{7,11},{8,4},{9,5},... | collective-permute-start | bytes 221192 | tf_op jit(solution)/shard_map/ppermute | solution.py:94
  418.1 6.1 %collective-permute-start.38 = (bf16[1,144,256]{2,1,0:T(8,128)(2,1)S(1)}, bf16[1,144,256]{2,1,0:T(8,128)(2,1)S(1)}, u32[]{:S(2)}, u32[]{:S(2)}) collective-permute-start(bf16[1,144,256]{2,1,0:T(8,128)(2,1)S(1)} %get-tuple-element.318), channel_id=1, source_target_pairs={{0,8},{1,9},{2,10},{3,11},{4,12},{5,13},{6,14},{7,15},{8,0},{9,1},... | collective-permute-start | bytes 221192 | tf_op jit(solution)/shard_map/ppermute | solution.py:94
  425.8 4.6 %collective-permute-start.41 = (f32[8,128]{1,0:T(8,128)S(1)}, f32[8,128]{1,0:T(8,128)S(1)}, u32[]{:S(2)}, u32[]{:S(2)}) collective-permute-start(f32[8,128]{1,0:T(8,128)S(1)} %iota.23), channel_id=1, source_target_pairs={{0,8},{1,9},{2,10},{3,11},{4,12},{5,13},{6,14},{7,15},{8,0},{9,1},... | collective-permute-start | bytes 12296 | tf_op jit(solution)/shard_map/ppermute | solution.py:94
  426.2 5.4 %collective-permute-start.42 = (f32[8,128]{1,0:T(8,128)S(1)}, f32[8,128]{1,0:T(8,128)S(1)}, u32[]{:S(2)}, u32[]{:S(2)}) collective-permute-start(f32[8,128]{1,0:T(8,128)S(1)} %iota.23), channel_id=1, source_target_pairs={{0,12},{1,13},{2,14},{3,15},{4,8},{5,9},{6,10},{7,11},{8,4},{9,5},... | collective-permute-start | bytes 12296 | tf_op jit(solution)/shard_map/ppermute | solution.py:94
  433.3 9.5 %collective-permute-start.47 = (f32[8,128]{1,0:T(8,128)S(1)}, f32[8,128]{1,0:T(8,128)S(1)}, u32[]{:S(2)}, u32[]{:S(2)}) collective-permute-start(f32[8,128]{1,0:T(8,128)S(1)} %add.191), channel_id=1, source_target_pairs={{0,3},{1,2},{2,1},{3,0},{4,7},{5,6},{6,5},{7,4},{8,11},{9,10},{10,... | collective-permute-start | bytes 12296 | tf_op jit(solution)/shard_map/ppermute | solution.py:94
  437.9 4.9 %collective-permute-start.46 = (f32[8,128]{1,0:T(8,128)S(1)}, f32[8,128]{1,0:T(8,128)S(1)}, u32[]{:S(2)}, u32[]{:S(2)}) collective-permute-start(f32[8,128]{1,0:T(8,128)S(1)} %add.191), channel_id=1, source_target_pairs={{0,2},{1,3},{2,0},{3,1},{4,6},{5,7},{6,4},{7,5},{8,10},{9,11},{10,... | collective-permute-start | bytes 12296 | tf_op jit(solution)/shard_map/ppermute | solution.py:94
  437.9 4.9 %collective-permute-start.45 = (f32[8,128]{1,0:T(8,128)S(1)}, f32[8,128]{1,0:T(8,128)S(1)}, u32[]{:S(2)}, u32[]{:S(2)}) collective-permute-start(f32[8,128]{1,0:T(8,128)S(1)} %add.191), channel_id=1, source_target_pairs={{0,1},{1,0},{2,3},{3,2},{4,5},{5,4},{6,7},{7,6},{8,9},{9,8},{10,11... | collective-permute-start | bytes 12296 | tf_op jit(solution)/shard_map/ppermute | solution.py:94
  (27 other events, 377.1 us)

commit v3 on v2

--- a/solution.py
+++ b/solution.py
@@ -510,7 +510,7 @@
         ),
         out_shape=shapes,
         input_output_aliases=aliases,
-        compiler_params=pltpu.CompilerParams(vmem_limit_bytes=54 * 2**20),
+        compiler_params=pltpu.CompilerParams(vmem_limit_bytes=63 * 2**20),
         cost_estimate=cost(24 if half is None else 14),
         name="round_forward",
     )(*args)
@@ -674,7 +674,7 @@
             jax.ShapeDtypeStruct((2 * blocks, HALF), jnp.float32),
             jax.ShapeDtypeStruct((2 * H, HALF), jnp.bfloat16),
         ],
-        compiler_params=LIMIT,
+        compiler_params=pltpu.CompilerParams(vmem_limit_bytes=63 * 2**20),
         cost_estimate=cost(28 if carried else 25),
         name="edges_backward",
     )(index, back, slopes, mats, *carried, *landed)

time: 450 us -> 449 us (level)
  no operation moved by 1% of the time
where the time goes in v3:
time: 449 us; the launch traced here: 447 us
  Pallas kernels  226 us (50%)
  waiting for transfers between devices  91.4 us (20%)
  starting transfers between devices  83.9 us (19%)
  other arithmetic  23.2 us (5%)
  local copies, waits for them, and re-layouts  11.1 us (2%)
  between operations  7.73 us (2%)
    pallas_call x5, Pallas kernels, round_forward(): pl.pallas_call(body, grid_spec=pltpu.PrefetchScalarGridSpec(num_scalar_pr...  83.1 us
    pallas_call x3, Pallas kernels, edges_backward(): pl.pallas_call(body, grid_spec=pltpu.PrefetchScalarGridSpec(num_scalar_pr...  78.7 us
    ppermute x25, waiting for transfers between devices, swapped(): lax.ppermute(value, axis, [(i, i ^ bit) for i in range(lax.axis_size(axis...  31.3 us
    ppermute x25, starting transfers between devices, swapped(): lax.ppermute(value, axis, [(i, i ^ bit) for i in range(lax.axis_size(axis...  29.3 us
    pallas_call x3, Pallas kernels, weight_grads(): pl.pallas_call(body, grid=(blocks // tile,), in_specs=[rows] * 7 + [whole...  24.4 us
    all_to_all x3, waiting for transfers between devices, exchanged(): lax.all_to_all(rows.reshape(bands, capacity, HALF), 'space', split_axis=0...  21.1 us
    ppermute x8, waiting for transfers between devices, halo(): lax.ppermute(last, 'space', up)  20.9 us
    ppermute x8, starting transfers between devices, halo(): lax.ppermute(initial, 'space', down)  20.6 us
  transfers between devices with their start and end apart: 51, of which 26 were waited for; matrix products, arithmetic and copies ran while one was open for 6% of the time, Pallas kernels for 25%

profile of v3, /device:TPU:0, one launch (start us, length us, event | category | flops | bytes accessed | tf_op | source)
XLA Modules:
  0.0 446.7 jit_solution(3468132396904173222)
XLA Ops:
  2.5 5.1 %collective-permute-start.2 = (bf16[1,144,256]{2,1,0:T(8,128)(2,1)S(1)}, bf16[1,144,256]{2,1,0:T(8,128)(2,1)S(1)}, u32[]{:S(2)}, u32[]{:S(2)}) collective-permute-start(bf16[1,144,256]{2,1,0:T(8,128)(2,1)S(1)} %broadcast_in_dim_reshape.3), channel_id=1, source_target_pairs={{0,12},{1,13},{2,14},{3,15},{4,8},{5,9},{6,10},{7,11},{8,4},{9,5},... | collective-permute-start | bytes 221192 | tf_op jit(solution)/shard_map/ppermute | solution.py:94
  26.1 4.8 %collective-permute-done.6 = bf16[8,72,256]{2,1,0:T(8,128)(2,1)S(1)} collective-permute-done((bf16[8,72,256]{2,1,0:T(8,128)(2,1)S(1)}, bf16[8,72,256]{2,1,0:T(8,128)(2,1)S(1)}, u32[]{:S(2)}, u32[]{:S(2)}) %collective-permute-start.6) | collective-permute-done | bytes 294944 | tf_op jit(solution)/shard_map/ppermute | solution.py:94
  32.4 5.2 %all-to-all-start = ((bf16[16,64,128]{2,1,0:T(8,128)(2,1)}), bf16[16,64,128]{2,1,0:T(8,128)(2,1)S(1)}, u32[]{:S(2)}, u32[]{:S(2)}) async-start(bf16[16,64,128]{2,1,0:T(8,128)(2,1)} %bitcast.4), calls=%async_computation | async-start | bytes 524288 | tf_op jit(solution)/shard_map/all_to_all | solution.py:907
  38.7 4.0 spread_rows.1
  42.7 5.3 %all-to-all-done = bf16[16,64,128]{2,1,0:T(8,128)(2,1)S(1)} async-done(((bf16[16,64,128]{2,1,0:T(8,128)(2,1)}), bf16[16,64,128]{2,1,0:T(8,128)(2,1)S(1)}, u32[]{:S(2)}, u32[]{:S(2)}) %all-to-all-start) | async-done | bytes 262176 | tf_op jit(solution)/shard_map/all_to_all | solution.py:907
  48.7 6.0 %encode_rows.1 = (f32[2048,256]{1,0:T(8,128)}, bf16[2048,256]{1,0:T(8,128)(2,1)}, bf16[4096,128]{1,0:T(8,128)(2,1)}, s32[1,1024]{1,0:T(1,128)}, s32[1024,1]{1,0:T(8,128)}) custom-call(bf16[1024,128]{1,0:T(8,128)(2,1)} %bitcast.132, bf16[128,256]{1,0:T(8,128)(2,1)} %get-tuple-element.147.in_ref, bf16[256,256]{1,0:T(8,128)(2,1)} %get-tuple-element.148.node_ref, ...), custom_call_target="tpu_custom_call" | custom-call | bytes 15000000 | tf_op jit(solution)/shard_map/encode_rows/pallas_call | solution.py:783
  60.4 3.9 node_terms.3
  64.3 4.5 %collective-permute-start.12 = (bf16[79,360]{1,0:T(8,128)(2,1)S(1)}, bf16[79,360]{1,0:T(8,128)(2,1)S(1)}, u32[]{:S(2)}, u32[]{:S(2)}) collective-permute-start(bf16[79,360]{1,0:T(8,128)(2,1)S(1)} %get-tuple-element.322), channel_id=1, source_target_pairs={{0,1},{1,2},{2,3},{3,4},{4,5},{5,6},{6,7},{7,8},{8,9},{9,10},{10,1... | collective-permute-start | bytes 170648 | tf_op jit(solution)/shard_map/ppermute | solution.py:49
  69.5 11.0 %collective-permute-done.13 = bf16[79,360]{1,0:T(8,128)(2,1)S(1)} collective-permute-done((bf16[79,360]{1,0:T(8,128)(2,1)S(1)}, bf16[79,360]{1,0:T(8,128)(2,1)S(1)}, u32[]{:S(2)}, u32[]{:S(2)}) %collective-permute-start.13) | collective-permute-done | bytes 56912 | tf_op jit(solution)/shard_map/ppermute | solution.py:49
  80.7 2.6 collective-permute-done.10.refs_0_
  83.4 14.3 %round_forward.5 = (f32[2048,256]{1,0:T(8,128)}, f32[2048,256]{1,0:T(8,128)}, bf16[2048,256]{1,0:T(8,128)(2,1)}, bf16[2048,256]{1,0:T(8,128)(2,1)}, bf16[6,4096,...) custom-call(s32[6144]{0:T(1024)} %get-tuple-element.325.index_ref, f32[2048,256]{1,0:T(8,128)} %get-tuple-element.154.mesh_ref, ...), custom_call_target="tpu_custom_call" | custom-call | bytes 42000000 | tf_op jit(solution)/shard_map/round_forward/pallas_call | solution.py:497
  99.8 14.3 %round_forward.6 = (f32[2048,256]{1,0:T(8,128)}, f32[2048,256]{1,0:T(8,128)}, bf16[2048,256]{1,0:T(8,128)(2,1)}, bf16[2048,256]{1,0:T(8,128)(2,1)}, bf16[6,4096,...) custom-call(s32[6144]{0:T(1024)} %get-tuple-element.326.index_ref, ...), custom_call_target="tpu_custom_call", output_to_operand_aliasing={{0}: (9, {}), {1}: (10, {}), {2}: (11, {}), {3}: (12, {}), ... | custom-call | bytes 42000000 | tf_op jit(solution)/shard_map/round_forward/pallas_call | solution.py:497
  115.9 3.9 node_terms.4
  122.0 5.8 %collective-permute-done.17.refs_1_.refs_0_ = bf16[2048,128]{1,0:T(8,128)(2,1)} collective-permute-done((bf16[2048,128]{1,0:T(8,128)(2,1)}, bf16[2048,128]{1,0:T(8,128)(2,1)}, u32[]{:S(2)}, u32[]{:S(2)}) %collective-permute-start.17) | collective-permute-done | bytes 524320 | tf_op jit(solution)/shard_map/ppermute | solution.py:77
  127.7 14.0 %round_forward.7 = (f32[2048,256]{1,0:T(8,128)}, f32[2048,256]{1,0:T(8,128)}, bf16[2048,256]{1,0:T(8,128)(2,1)}, bf16[2048,256]{1,0:T(8,128)(2,1)}, bf16[6,4096,...) custom-call(s32[6144]{0:T(1024)} %get-tuple-element.325.index_ref, f32[2048,256]{1,0:T(8,128)} %get-tuple-element.168.mesh_ref.refs_0_, ...), custom_call_target="tpu_custom_call" | custom-call | bytes 42000000 | tf_op jit(solution)/shard_map/round_forward/pallas_call | solution.py:497
  144.1 14.1 %round_forward.8 = (f32[2048,256]{1,0:T(8,128)}, f32[2048,256]{1,0:T(8,128)}, bf16[2048,256]{1,0:T(8,128)(2,1)}, bf16[2048,256]{1,0:T(8,128)(2,1)}, bf16[6,4096,...) custom-call(s32[6144]{0:T(1024)} %get-tuple-element.326.index_ref, ...), custom_call_target="tpu_custom_call", output_to_operand_aliasing={{0}: (11, {}), {1}: (12, {}), {2}: (13, {}), {3}: (14, {}),... | custom-call | bytes 42000000 | tf_op jit(solution)/shard_map/round_forward/pallas_call | solution.py:497
  158.3 3.3 collective-permute-start.22
  162.4 3.9 node_terms.5
  166.3 4.8 %collective-permute-done.22.refs_5_ = bf16[2048,128]{1,0:T(8,128)(2,1)} collective-permute-done((bf16[2048,128]{1,0:T(8,128)(2,1)}, bf16[2048,128]{1,0:T(8,128)(2,1)}, u32[]{:S(2)}, u32[]{:S(2)}) %collective-permute-start.22) | collective-permute-done | bytes 524320 | tf_op jit(solution)/shard_map/ppermute | solution.py:77
  171.1 2.9 collective-permute-done.21.refs_1_
  174.0 26.3 %round_forward.9 = (f32[2048,256]{1,0:T(8,128)}, f32[2048,256]{1,0:T(8,128)}, bf16[2048,256]{1,0:T(8,128)(2,1)}, bf16[2048,256]{1,0:T(8,128)(2,1)}, bf16[6,4096,...) custom-call(s32[12288]{0:T(1024)} %copy-done.7, ...), custom_call_target="tpu_custom_call" | custom-call | bytes 72000000 | tf_op jit(solution)/shard_map/round_forward/pallas_call | solution.py:497
  200.3 3.5 all-to-all-start.1
  203.9 8.4 %all-to-all-done.1 = bf16[16,64,128]{2,1,0:T(8,128)(2,1)S(1)} async-done(((bf16[16,64,128]{2,1,0:T(8,128)(2,1)}), bf16[16,64,128]{2,1,0:T(8,128)(2,1)S(1)}, u32[]{:S(2)}, u32[]{:S(2)}) %all-to-all-start.1) | async-done | bytes 262176 | tf_op jit(solution)/shard_map/all_to_all | solution.py:907
  213.8 3.3 collective-permute-start.23
  221.0 2.3 collective-permute-done.24
  226.2 5.8 %all-to-all-start.2 = ((bf16[16,64,128]{2,1,0:T(8,128)(2,1)}), bf16[16,64,128]{2,1,0:T(8,128)(2,1)S(1)}, u32[]{:S(2)}, u32[]{:S(2)}) async-start(bf16[16,64,128]{2,1,0:T(8,128)(2,1)} %bitcast.20), calls=%async_computation.2 | async-start | bytes 524288 | tf_op jit(solution)/shard_map/all_to_all | solution.py:907
  233.2 7.4 %all-to-all-done.2 = bf16[16,64,128]{2,1,0:T(8,128)(2,1)S(1)} async-done(((bf16[16,64,128]{2,1,0:T(8,128)(2,1)}), bf16[16,64,128]{2,1,0:T(8,128)(2,1)S(1)}, u32[]{:S(2)}, u32[]{:S(2)}) %all-to-all-start.2) | async-done | bytes 262176 | tf_op jit(solution)/shard_map/all_to_all | solution.py:907
  242.2 26.8 %edges_backward.3 = (f32[2048,256]{1,0:T(8,128)}, bf16[2048,256]{1,0:T(8,128)(2,1)}, bf16[1024,256]{1,0:T(8,128)(2,1)}, bf16[2048,256]{1,0:T(8,128)(2,1)}, bf16[...) custom-call(s32[12288]{0:T(1024)} %copy-done.7, ...), custom_call_target="tpu_custom_call" | custom-call | bytes 75000000 | tf_op jit(solution)/shard_map/edges_backward/pallas_call | solution.py:642
  270.6 2.4 collective-permute-start.27
  273.6 2.7 decode_grads.1
  276.2 7.4 %weight_grads.3 = (f32[2048,256]{1,0:T(8,128)}, f32[1024,256]{1,0:T(8,128)}, f32[2,256]{1,0:T(2,128)}) custom-call(f32[2048,256]{1,0:T(8,128)} %get-tuple-element.182.mesh_ref.refs_0_, bf16[2048,256]{1,0:T(8,128)(2,1)} %get-tuple-element.206.dest_ref, bf16[2048,256]{1,0:T(8,128)(2,1)} %get-tuple-element.207.agg_ref, ...), custom_call_target="tpu_custom_call" | custom-call | bytes 30000000 | tf_op jit(solution)/shard_map/weight_grads/pallas_call | solution.py:727
  283.6 4.0 convert_select_fusion
  287.8 25.8 %edges_backward.4 = (f32[2048,256]{1,0:T(8,128)}, bf16[2048,256]{1,0:T(8,128)(2,1)}, bf16[2048,256]{1,0:T(8,128)(2,1)}, bf16[2048,256]{1,0:T(8,128)(2,1)}, bf16[...) custom-call(s32[12288]{0:T(1024)} %copy-done.7, ...), custom_call_target="tpu_custom_call" | custom-call | bytes 84000000 | tf_op jit(solution)/shard_map/edges_backward/pallas_call | solution.py:642
  314.3 3.3 collective-permute-start.29
  317.6 8.6 %weight_grads.4 = (f32[2048,256]{1,0:T(8,128)}, f32[1024,256]{1,0:T(8,128)}, f32[2,256]{1,0:T(2,128)}, f32[256,256]{1,0:T(8,128)}) custom-call(f32[2048,256]{1,0:T(8,128)} %get-tuple-element.168.mesh_ref.refs_0_, bf16[2048,256]{1,0:T(8,128)(2,1)} %get-tuple-element.227.dest_ref, bf16[2048,256]{1,0:T(8,128)(2,1)} %get-tuple-element.228.agg_ref, ...), custom_call_target="tpu_custom_call" | custom-call | bytes 30000000 | tf_op jit(solution)/shard_map/weight_grads/pallas_call | solution.py:727
  326.1 5.5 %collective-permute-done.28.refs_6_ = bf16[4096,128]{1,0:T(8,128)(2,1)} collective-permute-done((bf16[4096,128]{1,0:T(8,128)(2,1)}, bf16[4096,128]{1,0:T(8,128)(2,1)}, u32[]{:S(2)}, u32[]{:S(2)}) %collective-permute-start.28) | collective-permute-done | bytes 1048608 | tf_op jit(solution)/shard_map/ppermute | solution.py:77
  331.6 26.0 %edges_backward.5 = (f32[2048,256]{1,0:T(8,128)}, bf16[2048,256]{1,0:T(8,128)(2,1)}, bf16[2048,256]{1,0:T(8,128)(2,1)}, bf16[2048,256]{1,0:T(8,128)(2,1)}, bf16[...) custom-call(s32[12288]{0:T(1024)} %copy-done.7, ...), custom_call_target="tpu_custom_call" | custom-call | bytes 84000000 | tf_op jit(solution)/shard_map/edges_backward/pallas_call | solution.py:642
  357.7 3.8 collective-permute-start.31
  362.3 8.4 %weight_grads.5 = (f32[2048,256]{1,0:T(8,128)}, f32[1024,256]{1,0:T(8,128)}, f32[2,256]{1,0:T(2,128)}, f32[256,256]{1,0:T(8,128)}) custom-call(f32[2048,256]{1,0:T(8,128)} %get-tuple-element.154.mesh_ref, bf16[2048,256]{1,0:T(8,128)(2,1)} %get-tuple-element.238.dest_ref, bf16[2048,256]{1,0:T(8,128)(2,1)} %get-tuple-element.239.agg_ref, ...), custom_call_target="tpu_custom_call" | custom-call | bytes 30000000 | tf_op jit(solution)/shard_map/weight_grads/pallas_call | solution.py:727
  370.7 3.9 collective-permute-done.30.first_ref
  374.6 10.1 %encode_backward.1 = (f32[2048,256]{1,0:T(8,128)}, bf16[2048,256]{1,0:T(8,128)(2,1)}, f32[128,256]{1,0:T(8,128)}, f32[256,256]{1,0:T(8,128)}, f32[2,256]{1,0:T(2,128)}, /*index=5*/f32[256,256]{1,0:T(8,128)}) custom-call(f32[2048,256]{1,0:T(8,128)} %get-tuple-element.245.part_ref, f32[4096,128]{1,0:T(8,128)} %get-tuple-element.246.own_ref, ...), custom_call_target="tpu_custom_call" | custom-call | bytes 30000000 | tf_op jit(solution)/shard_map/encode_backward/pallas_call | solution.py:848
  384.7 5.1 %collect_rows.1 = (f32[16,144,256]{2,1,0:T(8,128)}, bf16[16,144,256]{2,1,0:T(8,128)(2,1)}) custom-call(s32[1]{0:T(128)} %bitcast.6.place_ref, f32[128,256]{1,0:T(8,128)} %get-tuple-element.250.refs_0_, f32[256,256]{1,0:T(8,128)} %get-tuple-element.251.refs_1_, f32[256,256]{1,0:T(8,128)} %get-tuple-element.252.refs_2_, f32[78,256]{1,0:T(8,128)} %reshape.160.refs_3_, ...), custom_call_target="tpu_custom_call" | custom-call | bytes 15000000 | tf_op jit(solution)/shard_map/collect_rows/pallas_call | solution.py:233
  389.8 3.1 collective-permute-done.32
  395.2 8.9 %collective-permute-done.33 = bf16[4,2,72,256]{3,2,0,1:T(8,128)(2,1)S(1)} collective-permute-done((bf16[4,2,72,256]{3,2,0,1:T(8,128)(2,1)S(1)}, bf16[4,2,72,256]{3,2,0,1:T(8,128)(2,1)S(1)}, u32[]{:S(2)}, u32[]{:S(2)}) %collective-permute-start.33) | collective-permute-done | bytes 294944 | tf_op jit(solution)/shard_map/ppermute | solution.py:94
  406.1 3.3 collective-permute-done.34
  411.9 5.6 %collective-permute-start.39 = (bf16[1,144,256]{2,1,0:T(8,128)(2,1)S(1)}, bf16[1,144,256]{2,1,0:T(8,128)(2,1)S(1)}, u32[]{:S(2)}, u32[]{:S(2)}) collective-permute-start(bf16[1,144,256]{2,1,0:T(8,128)(2,1)S(1)} %get-tuple-element.317), channel_id=1, source_target_pairs={{0,12},{1,13},{2,14},{3,15},{4,8},{5,9},{6,10},{7,11},{8,4},{9,5},... | collective-permute-start | bytes 221192 | tf_op jit(solution)/shard_map/ppermute | solution.py:94
  432.6 4.7 %collective-permute-start.47 = (f32[8,128]{1,0:T(8,128)S(1)}, f32[8,128]{1,0:T(8,128)S(1)}, u32[]{:S(2)}, u32[]{:S(2)}) collective-permute-start(f32[8,128]{1,0:T(8,128)S(1)} %add.191), channel_id=1, source_target_pairs={{0,3},{1,2},{2,1},{3,0},{4,7},{5,6},{6,5},{7,4},{8,11},{9,10},{10,... | collective-permute-start | bytes 12296 | tf_op jit(solution)/shard_map/ppermute | solution.py:94
  438.7 3.4 select_bitcast_fusion
  (199 shorter events, 75.5 us)
Async XLA Ops:
  2.5 14.5 %collective-permute-start.2 = (bf16[1,144,256]{2,1,0:T(8,128)(2,1)S(1)}, bf16[1,144,256]{2,1,0:T(8,128)(2,1)S(1)}, u32[]{:S(2)}, u32[]{:S(2)}) collective-permute-start(bf16[1,144,256]{2,1,0:T(8,128)(2,1)S(1)} %broadcast_in_dim_reshape.3), channel_id=1, source_target_pairs={{0,12},{1,13},{2,14},{3,15},{4,8},{5,9},{6,10},{7,11},{8,4},{9,5},... | collective-permute-start | bytes 221192 | tf_op jit(solution)/shard_map/ppermute | solution.py:94
  7.6 9.4 %collective-permute-start.1 = (bf16[1,144,256]{2,1,0:T(8,128)(2,1)S(1)}, bf16[1,144,256]{2,1,0:T(8,128)(2,1)S(1)}, u32[]{:S(2)}, u32[]{:S(2)}) collective-permute-start(bf16[1,144,256]{2,1,0:T(8,128)(2,1)S(1)} %broadcast_in_dim_reshape.3), channel_id=1, source_target_pairs={{0,8},{1,9},{2,10},{3,11},{4,12},{5,13},{6,14},{7,15},{8,0},{9,1},... | collective-permute-start | bytes 221192 | tf_op jit(solution)/shard_map/ppermute | solution.py:94
  7.6 9.4 %collective-permute-start = (bf16[1,144,256]{2,1,0:T(8,128)(2,1)S(1)}, bf16[1,144,256]{2,1,0:T(8,128)(2,1)S(1)}, u32[]{:S(2)}, u32[]{:S(2)}) collective-permute-start(bf16[1,144,256]{2,1,0:T(8,128)(2,1)S(1)} %broadcast_in_dim_reshape.3), channel_id=1, source_target_pairs={{0,4},{1,5},{2,6},{3,7},{4,0},{5,1},{6,2},{7,3},{8,12},{9,13},{10,... | collective-permute-start | bytes 221192 | tf_op jit(solution)/shard_map/ppermute | solution.py:94
  17.0 5.2 %collective-permute-start.4 = (bf16[4,72,256]{2,1,0:T(8,128)(2,1)S(1)}, bf16[4,72,256]{2,1,0:T(8,128)(2,1)S(1)}, u32[]{:S(2)}, u32[]{:S(2)}) collective-permute-start(bf16[4,72,256]{2,1,0:T(8,128)(2,1)S(1)} %get-tuple-element.319), channel_id=1, source_target_pairs={{0,1},{1,0},{2,3},{3,2},{4,5},{5,4},{6,7},{7,6},{8,9},{9,8},{10,11... | collective-permute-start | bytes 442376 | tf_op jit(solution)/shard_map/ppermute | solution.py:94
  18.7 5.1 %collective-permute-start.3 = (bf16[4,72,256]{2,1,0:T(8,128)(2,1)S(1)}, bf16[4,72,256]{2,1,0:T(8,128)(2,1)S(1)}, u32[]{:S(2)}, u32[]{:S(2)}) collective-permute-start(bf16[4,72,256]{2,1,0:T(8,128)(2,1)S(1)} %get-tuple-element.320), channel_id=1, source_target_pairs={{0,2},{1,3},{2,0},{3,1},{4,6},{5,7},{6,4},{7,5},{8,10},{9,11},{10,... | collective-permute-start | bytes 442376 | tf_op jit(solution)/shard_map/ppermute | solution.py:94
  23.9 7.0 %collective-permute-start.6 = (bf16[8,72,256]{2,1,0:T(8,128)(2,1)S(1)}, bf16[8,72,256]{2,1,0:T(8,128)(2,1)S(1)}, u32[]{:S(2)}, u32[]{:S(2)}) collective-permute-start(bf16[8,72,256]{2,1,0:T(8,128)(2,1)S(1)} %pad_maximum_fusion.3), channel_id=1, source_target_pairs={{0,2},{1,3},{2,0},{3,1},{4,6},{5,7},{6,4},{7,5},{8,10},{9,11},{10,... | collective-permute-start | bytes 884744 | tf_op jit(solution)/shard_map/ppermute | solution.py:94
  25.5 6.7 %collective-permute-start.5 = (bf16[8,72,256]{2,1,0:T(8,128)(2,1)S(1)}, bf16[8,72,256]{2,1,0:T(8,128)(2,1)S(1)}, u32[]{:S(2)}, u32[]{:S(2)}) collective-permute-start(bf16[8,72,256]{2,1,0:T(8,128)(2,1)S(1)} %pad_maximum_fusion.2), channel_id=1, source_target_pairs={{0,1},{1,0},{2,3},{3,2},{4,5},{5,4},{6,7},{7,6},{8,9},{9,8},{10,11... | collective-permute-start | bytes 884744 | tf_op jit(solution)/shard_map/ppermute | solution.py:94
  30.9 6.7 %collective-permute-start.8 = (bf16[16,72,256]{2,1,0:T(8,128)(2,1)S(1)}, bf16[16,72,256]{2,1,0:T(8,128)(2,1)S(1)}, u32[]{:S(2)}, u32[]{:S(2)}) collective-permute-start(bf16[16,72,256]{2,1,0:T(8,128)(2,1)S(1)} %constant_dynamic-update-slice_fusion.6.refs_1_), channel_id=1, source_target_pairs={{0,16},{16,0},{1,17},{17,1},{2,18},{18,2},{3,19},{19,3},{4,20},{20... | collective-permute-start | bytes 1769480 | tf_op jit(solution)/shard_map/ppermute | solution.py:94
  32.3 5.3 %collective-permute-start.7 = (bf16[16,72,256]{2,1,0:T(8,128)(2,1)S(1)}, bf16[16,72,256]{2,1,0:T(8,128)(2,1)S(1)}, u32[]{:S(2)}, u32[]{:S(2)}) collective-permute-start(bf16[16,72,256]{2,1,0:T(8,128)(2,1)S(1)} %constant_dynamic-update-slice_fusion.4.refs_0_), channel_id=1, source_target_pairs={{0,16},{16,0},{1,17},{17,1},{2,18},{18,2},{3,19},{19,3},{4,20},{20... | collective-permute-start | bytes 1769480 | tf_op jit(solution)/shard_map/ppermute | solution.py:94
  32.4 15.6 %all-to-all-start = ((bf16[16,64,128]{2,1,0:T(8,128)(2,1)}), bf16[16,64,128]{2,1,0:T(8,128)(2,1)S(1)}, u32[]{:S(2)}, u32[]{:S(2)}) async-start(bf16[16,64,128]{2,1,0:T(8,128)(2,1)} %bitcast.4), calls=%async_computation | async-start | bytes 524288 | tf_op jit(solution)/shard_map/all_to_all | solution.py:907
  54.7 26.0 %collective-permute-start.11 = (bf16[4096,128]{1,0:T(8,128)(2,1)}, bf16[4096,128]{1,0:T(8,128)(2,1)}, u32[]{:S(2)}, u32[]{:S(2)}) collective-permute-start(bf16[4096,128]{1,0:T(8,128)(2,1)} %get-tuple-element.155.refs_1_), channel_id=1, source_target_pairs={{1,0},{3,1},{2,3},{6,2},{4,6},{5,4},{7,5},{11,7},{9,11},{8,9},{10,... | collective-permute-start | bytes 3145736 | tf_op jit(solution)/shard_map/ppermute | solution.py:77
  56.4 26.9 %collective-permute-start.10 = (bf16[4096,128]{1,0:T(8,128)(2,1)}, bf16[4096,128]{1,0:T(8,128)(2,1)}, u32[]{:S(2)}, u32[]{:S(2)}) collective-permute-start(bf16[4096,128]{1,0:T(8,128)(2,1)} %get-tuple-element.155.refs_1_), channel_id=1, source_target_pairs={{0,1},{1,3},{3,2},{2,6},{6,4},{4,5},{5,7},{7,11},{11,9},{9,8},{8,1... | collective-permute-start | bytes 3145736 | tf_op jit(solution)/shard_map/ppermute | solution.py:77
  56.8 12.1 %collective-permute-start.9 = (s32[12288]{0:T(1024)S(1)}, s32[12288]{0:T(1024)S(1)}, u32[]{:S(2)}, u32[]{:S(2)}) collective-permute-start(s32[12288]{0:T(1024)S(1)} %reshape.152), channel_id=1, source_target_pairs={{0,0},{1,1},{2,3},{3,2},{4,6},{5,4},{6,5},{7,7},{8,11},{9,9},{10,8... | collective-permute-start | bytes 147464 | tf_op jit(solution)/shard_map/ppermute | solution.py:936
  59.0 5.3 %collective-permute-start.14 = (f32[1,3]{1,0:T(1,128)S(1)}, f32[1,3]{1,0:T(1,128)S(1)}, u32[]{:S(2)}, u32[]{:S(2)}) collective-permute-start(f32[1,3]{1,0:T(1,128)S(1)} %bitcast.147), channel_id=1, source_target_pairs={{0,16},{16,0},{1,17},{17,1},{2,18},{18,2},{3,19},{19,3},{4,20},{20... | collective-permute-start | bytes 44 | tf_op jit(solution)/shard_map/ppermute | solution.py:94
  59.1 21.4 %collective-permute-start.13 = (bf16[79,360]{1,0:T(8,128)(2,1)S(1)}, bf16[79,360]{1,0:T(8,128)(2,1)S(1)}, u32[]{:S(2)}, u32[]{:S(2)}) collective-permute-start(bf16[79,360]{1,0:T(8,128)(2,1)S(1)} %get-tuple-element.321), channel_id=1, source_target_pairs={{1,0},{2,1},{3,2},{4,3},{5,4},{6,5},{7,6},{8,7},{9,8},{10,9},{11,1... | collective-permute-start | bytes 170648 | tf_op jit(solution)/shard_map/ppermute | solution.py:49
  64.3 16.2 %collective-permute-start.12 = (bf16[79,360]{1,0:T(8,128)(2,1)S(1)}, bf16[79,360]{1,0:T(8,128)(2,1)S(1)}, u32[]{:S(2)}, u32[]{:S(2)}) collective-permute-start(bf16[79,360]{1,0:T(8,128)(2,1)S(1)} %get-tuple-element.322), channel_id=1, source_target_pairs={{0,1},{1,2},{2,3},{3,4},{4,5},{5,6},{6,7},{7,8},{8,9},{9,10},{10,1... | collective-permute-start | bytes 170648 | tf_op jit(solution)/shard_map/ppermute | solution.py:49
  97.7 16.4 %collective-permute-start.16 = (bf16[2048,128]{1,0:T(8,128)(2,1)}, bf16[2048,128]{1,0:T(8,128)(2,1)S(1)}, u32[]{:S(2)}, u32[]{:S(2)}) collective-permute-start(bf16[2048,128]{1,0:T(8,128)(2,1)} %get-tuple-element.170.refs_2_.refs_1_), channel_id=1, source_target_pairs={{1,0},{3,1},{2,3},{6,2},{4,6},{5,4},{7,5},{11,7},{9,11},{8,9},{10,... | collective-permute-start | bytes 1572872 | tf_op jit(solution)/shard_map/ppermute | solution.py:77
  99.8 14.3 %collective-permute-start.15 = (bf16[2048,128]{1,0:T(8,128)(2,1)}, bf16[2048,128]{1,0:T(8,128)(2,1)}, u32[]{:S(2)}, u32[]{:S(2)}) collective-permute-start(bf16[2048,128]{1,0:T(8,128)(2,1)} %get-tuple-element.170.refs_2_.refs_1_), channel_id=1, source_target_pairs={{0,1},{1,3},{3,2},{2,6},{6,4},{4,5},{5,7},{7,11},{11,9},{9,8},{8,1... | collective-permute-start | bytes 1572872 | tf_op jit(solution)/shard_map/ppermute | solution.py:77
  114.1 13.6 %collective-permute-start.17 = (bf16[2048,128]{1,0:T(8,128)(2,1)}, bf16[2048,128]{1,0:T(8,128)(2,1)}, u32[]{:S(2)}, u32[]{:S(2)}) collective-permute-start(bf16[2048,128]{1,0:T(8,128)(2,1)} %get-tuple-element.171.refs_3_.refs_2_), channel_id=1, source_target_pairs={{0,1},{1,3},{3,2},{2,6},{6,4},{4,5},{5,7},{7,11},{11,9},{9,8},{8,1... | collective-permute-start | bytes 1572872 | tf_op jit(solution)/shard_map/ppermute | solution.py:77
  119.8 24.3 %collective-permute-start.18 = (bf16[2048,128]{1,0:T(8,128)(2,1)}, bf16[2048,128]{1,0:T(8,128)(2,1)}, u32[]{:S(2)}, u32[]{:S(2)}) collective-permute-start(bf16[2048,128]{1,0:T(8,128)(2,1)} %get-tuple-element.171.refs_3_.refs_2_), channel_id=1, source_target_pairs={{1,0},{3,1},{2,3},{6,2},{4,6},{5,4},{7,5},{11,7},{9,11},{8,9},{10,... | collective-permute-start | bytes 1572872 | tf_op jit(solution)/shard_map/ppermute | solution.py:77
  141.7 16.5 %collective-permute-start.20 = (bf16[2048,128]{1,0:T(8,128)(2,1)}, bf16[2048,128]{1,0:T(8,128)(2,1)S(1)}, u32[]{:S(2)}, u32[]{:S(2)}) collective-permute-start(bf16[2048,128]{1,0:T(8,128)(2,1)} %get-tuple-element.184.refs_2_), channel_id=1, source_target_pairs={{1,0},{3,1},{2,3},{6,2},{4,6},{5,4},{7,5},{11,7},{9,11},{8,9},{10,... | collective-permute-start | bytes 1572872 | tf_op jit(solution)/shard_map/ppermute | solution.py:77
  143.5 14.7 %collective-permute-start.19 = (bf16[2048,128]{1,0:T(8,128)(2,1)}, bf16[2048,128]{1,0:T(8,128)(2,1)}, u32[]{:S(2)}, u32[]{:S(2)}) collective-permute-start(bf16[2048,128]{1,0:T(8,128)(2,1)} %get-tuple-element.184.refs_2_), channel_id=1, source_target_pairs={{0,1},{1,3},{3,2},{2,6},{6,4},{4,5},{5,7},{7,11},{11,9},{9,8},{8,1... | collective-permute-start | bytes 1572872 | tf_op jit(solution)/shard_map/ppermute | solution.py:77
  158.3 12.8 %collective-permute-start.22 = (bf16[2048,128]{1,0:T(8,128)(2,1)}, bf16[2048,128]{1,0:T(8,128)(2,1)}, u32[]{:S(2)}, u32[]{:S(2)}) collective-permute-start(bf16[2048,128]{1,0:T(8,128)(2,1)} %get-tuple-element.186.refs_3_), channel_id=1, source_target_pairs={{1,0},{3,1},{2,3},{6,2},{4,6},{5,4},{7,5},{11,7},{9,11},{8,9},{10,... | collective-permute-start | bytes 1572872 | tf_op jit(solution)/shard_map/ppermute | solution.py:77
  161.6 12.4 %collective-permute-start.21 = (bf16[2048,128]{1,0:T(8,128)(2,1)}, bf16[2048,128]{1,0:T(8,128)(2,1)}, u32[]{:S(2)}, u32[]{:S(2)}) collective-permute-start(bf16[2048,128]{1,0:T(8,128)(2,1)} %get-tuple-element.186.refs_3_), channel_id=1, source_target_pairs={{0,1},{1,3},{3,2},{2,6},{6,4},{4,5},{5,7},{7,11},{11,9},{9,8},{8,1... | collective-permute-start | bytes 1572872 | tf_op jit(solution)/shard_map/ppermute | solution.py:77
  200.3 12.0 %all-to-all-start.1 = ((bf16[16,64,128]{2,1,0:T(8,128)(2,1)}), bf16[16,64,128]{2,1,0:T(8,128)(2,1)S(1)}, u32[]{:S(2)}, u32[]{:S(2)}) async-start(bf16[16,64,128]{2,1,0:T(8,128)(2,1)} %bitcast.141), calls=%async_computation.1 | async-start | bytes 524288 | tf_op jit(solution)/shard_map/all_to_all | solution.py:907
  213.8 9.5 %collective-permute-start.23 = (bf16[78,360]{1,0:T(8,128)(2,1)S(1)}, bf16[78,360]{1,0:T(8,128)(2,1)S(1)}, u32[]{:S(2)}, u32[]{:S(2)}) collective-permute-start(bf16[78,360]{1,0:T(8,128)(2,1)S(1)} %get-tuple-element.323), channel_id=1, source_target_pairs={{0,1},{1,2},{2,3},{3,4},{4,5},{5,6},{6,7},{7,8},{8,9},{9,10},{10,1... | collective-permute-start | bytes 168488 | tf_op jit(solution)/shard_map/ppermute | solution.py:49
  217.2 6.1 %collective-permute-start.24 = (bf16[78,360]{1,0:T(8,128)(2,1)S(1)}, bf16[78,360]{1,0:T(8,128)(2,1)S(1)}, u32[]{:S(2)}, u32[]{:S(2)}) collective-permute-start(bf16[78,360]{1,0:T(8,128)(2,1)S(1)} %get-tuple-element.324), channel_id=1, source_target_pairs={{1,0},{2,1},{3,2},{4,3},{5,4},{6,5},{7,6},{8,7},{9,8},{10,9},{11,1... | collective-permute-start | bytes 168488 | tf_op jit(solution)/shard_map/ppermute | solution.py:49
  226.2 14.4 %all-to-all-start.2 = ((bf16[16,64,128]{2,1,0:T(8,128)(2,1)}), bf16[16,64,128]{2,1,0:T(8,128)(2,1)S(1)}, u32[]{:S(2)}, u32[]{:S(2)}) async-start(bf16[16,64,128]{2,1,0:T(8,128)(2,1)} %bitcast.20), calls=%async_computation.2 | async-start | bytes 524288 | tf_op jit(solution)/shard_map/all_to_all | solution.py:907
  240.6 28.5 %collective-permute-start.25 = (bf16[2048,256]{1,0:T(8,128)(2,1)}, bf16[2048,256]{1,0:T(8,128)(2,1)}, u32[]{:S(2)}, u32[]{:S(2)}) collective-permute-start(bf16[2048,256]{1,0:T(8,128)(2,1)} %convert_element_type.150), channel_id=1, source_target_pairs={{3,2},{2,3},{6,4},{4,5},{5,6},{11,8},{8,10},{10,11},{14,12},{15,13... | collective-permute-start | bytes 3145736 | tf_op jit(solution)/shard_map/ppermute | solution.py:939
  269.1 18.7 %collective-permute-start.26 = (bf16[4096,128]{1,0:T(8,128)(2,1)}, bf16[4096,128]{1,0:T(8,128)(2,1)}, u32[]{:S(2)}, u32[]{:S(2)}) collective-permute-start(bf16[4096,128]{1,0:T(8,128)(2,1)} %get-tuple-element.217), channel_id=1, source_target_pairs={{0,1},{1,3},{3,2},{2,6},{6,4},{4,5},{5,7},{7,11},{11,9},{9,8},{8,1... | collective-permute-start | bytes 3145736 | tf_op jit(solution)/shard_map/ppermute | solution.py:77
  270.6 17.3 %collective-permute-start.27 = (bf16[4096,128]{1,0:T(8,128)(2,1)}, bf16[4096,128]{1,0:T(8,128)(2,1)}, u32[]{:S(2)}, u32[]{:S(2)}) collective-permute-start(bf16[4096,128]{1,0:T(8,128)(2,1)} %get-tuple-element.226), channel_id=1, source_target_pairs={{1,0},{3,1},{2,3},{6,2},{4,6},{5,4},{7,5},{11,7},{9,11},{8,9},{10,... | collective-permute-start | bytes 3145736 | tf_op jit(solution)/shard_map/ppermute | solution.py:77
  313.7 17.9 %collective-permute-start.28 = (bf16[4096,128]{1,0:T(8,128)(2,1)}, bf16[4096,128]{1,0:T(8,128)(2,1)}, u32[]{:S(2)}, u32[]{:S(2)}) collective-permute-start(bf16[4096,128]{1,0:T(8,128)(2,1)} %get-tuple-element.236), channel_id=1, source_target_pairs={{0,1},{1,3},{3,2},{2,6},{6,4},{4,5},{5,7},{7,11},{11,9},{9,8},{8,1... | collective-permute-start | bytes 3145736 | tf_op jit(solution)/shard_map/ppermute | solution.py:77
  314.3 17.3 %collective-permute-start.29 = (bf16[4096,128]{1,0:T(8,128)(2,1)}, bf16[4096,128]{1,0:T(8,128)(2,1)}, u32[]{:S(2)}, u32[]{:S(2)}) collective-permute-start(bf16[4096,128]{1,0:T(8,128)(2,1)} %get-tuple-element.237), channel_id=1, source_target_pairs={{1,0},{3,1},{2,3},{6,2},{4,6},{5,4},{7,5},{11,7},{9,11},{8,9},{10,... | collective-permute-start | bytes 3145736 | tf_op jit(solution)/shard_map/ppermute | solution.py:77
  357.6 17.0 %collective-permute-start.30 = (bf16[4096,128]{1,0:T(8,128)(2,1)}, bf16[4096,128]{1,0:T(8,128)(2,1)}, u32[]{:S(2)}, u32[]{:S(2)}) collective-permute-start(bf16[4096,128]{1,0:T(8,128)(2,1)} %get-tuple-element.247), channel_id=1, source_target_pairs={{0,1},{1,3},{3,2},{2,6},{6,4},{4,5},{5,7},{7,11},{11,9},{9,8},{8,1... | collective-permute-start | bytes 3145736 | tf_op jit(solution)/shard_map/ppermute | solution.py:77
  357.7 16.9 %collective-permute-start.31 = (bf16[4096,128]{1,0:T(8,128)(2,1)}, bf16[4096,128]{1,0:T(8,128)(2,1)}, u32[]{:S(2)}, u32[]{:S(2)}) collective-permute-start(bf16[4096,128]{1,0:T(8,128)(2,1)} %get-tuple-element.248), channel_id=1, source_target_pairs={{1,0},{3,1},{2,3},{6,2},{4,6},{5,4},{7,5},{11,7},{9,11},{8,9},{10,... | collective-permute-start | bytes 3145736 | tf_op jit(solution)/shard_map/ppermute | solution.py:77
  395.0 9.1 %collective-permute-start.33 = (bf16[4,2,72,256]{3,2,0,1:T(8,128)(2,1)S(1)}, bf16[4,2,72,256]{3,2,0,1:T(8,128)(2,1)S(1)}, u32[]{:S(2)}, u32[]{:S(2)}) collective-permute-start(bf16[4,2,72,256]{3,2,0,1:T(8,128)(2,1)S(1)} %fusion.14), channel_id=1, source_target_pairs={{0,1},{1,0},{2,3},{3,2},{4,5},{5,4},{6,7},{7,6},{8,9},{9,8},{10,11... | collective-permute-start | bytes 884744 | tf_op jit(solution)/shard_map/ppermute | solution.py:94
  395.1 9.2 %collective-permute-start.35 = (bf16[4,2,72,256]{3,2,1,0:T(8,128)(2,1)S(1)}, bf16[4,2,72,256]{3,2,1,0:T(8,128)(2,1)S(1)}, u32[]{:S(2)}, u32[]{:S(2)}) collective-permute-start(bf16[4,2,72,256]{3,2,1,0:T(8,128)(2,1)S(1)} %fusion.13), channel_id=1, source_target_pairs={{0,2},{1,3},{2,0},{3,1},{4,6},{5,7},{6,4},{7,5},{8,10},{9,11},{10,... | collective-permute-start | bytes 884744 | tf_op jit(solution)/shard_map/ppermute | solution.py:94
  404.2 5.2 %collective-permute-start.34 = (bf16[4,72,256]{2,1,0:T(8,128)(2,1)S(1)}, bf16[4,72,256]{2,1,0:T(8,128)(2,1)S(1)}, u32[]{:S(2)}, u32[]{:S(2)}) collective-permute-start(bf16[4,72,256]{2,1,0:T(8,128)(2,1)S(1)} %fusion.38), channel_id=1, source_target_pairs={{0,2},{1,3},{2,0},{3,1},{4,6},{5,7},{6,4},{7,5},{8,10},{9,11},{10,... | collective-permute-start | bytes 442376 | tf_op jit(solution)/shard_map/ppermute | solution.py:94
  404.4 5.2 %collective-permute-start.36 = (bf16[4,72,256]{2,1,0:T(8,128)(2,1)S(1)}, bf16[4,72,256]{2,1,0:T(8,128)(2,1)S(1)}, u32[]{:S(2)}, u32[]{:S(2)}) collective-permute-start(bf16[4,72,256]{2,1,0:T(8,128)(2,1)S(1)} %fusion.39), channel_id=1, source_target_pairs={{0,1},{1,0},{2,3},{3,2},{4,5},{5,4},{6,7},{7,6},{8,9},{9,8},{10,11... | collective-permute-start | bytes 442376 | tf_op jit(solution)/shard_map/ppermute | solution.py:94
  409.7 22.9 %collective-permute-start.44 = (bf16[2048,256]{1,0:T(8,128)(2,1)}, bf16[2048,256]{1,0:T(8,128)(2,1)}, u32[]{:S(2)}, u32[]{:S(2)}) collective-permute-start(bf16[2048,256]{1,0:T(8,128)(2,1)} %get-tuple-element.269), channel_id=1, source_target_pairs={{3,2},{2,3},{6,4},{4,5},{5,6},{11,8},{8,10},{10,11},{14,12},{15,13... | collective-permute-start | bytes 3145736 | tf_op jit(solution)/shard_map/ppermute | solution.py:939
  411.6 7.6 %collective-permute-start.37 = (bf16[1,144,256]{2,1,0:T(8,128)(2,1)S(1)}, bf16[1,144,256]{2,1,0:T(8,128)(2,1)S(1)}, u32[]{:S(2)}, u32[]{:S(2)}) collective-permute-start(bf16[1,144,256]{2,1,0:T(8,128)(2,1)S(1)} %get-tuple-element.316), channel_id=1, source_target_pairs={{0,4},{1,5},{2,6},{3,7},{4,0},{5,1},{6,2},{7,3},{8,12},{9,13},{10,... | collective-permute-start | bytes 221192 | tf_op jit(solution)/shard_map/ppermute | solution.py:94
  411.9 9.5 %collective-permute-start.39 = (bf16[1,144,256]{2,1,0:T(8,128)(2,1)S(1)}, bf16[1,144,256]{2,1,0:T(8,128)(2,1)S(1)}, u32[]{:S(2)}, u32[]{:S(2)}) collective-permute-start(bf16[1,144,256]{2,1,0:T(8,128)(2,1)S(1)} %get-tuple-element.317), channel_id=1, source_target_pairs={{0,12},{1,13},{2,14},{3,15},{4,8},{5,9},{6,10},{7,11},{8,4},{9,5},... | collective-permute-start | bytes 221192 | tf_op jit(solution)/shard_map/ppermute | solution.py:94
  417.4 6.1 %collective-permute-start.38 = (bf16[1,144,256]{2,1,0:T(8,128)(2,1)S(1)}, bf16[1,144,256]{2,1,0:T(8,128)(2,1)S(1)}, u32[]{:S(2)}, u32[]{:S(2)}) collective-permute-start(bf16[1,144,256]{2,1,0:T(8,128)(2,1)S(1)} %get-tuple-element.318), channel_id=1, source_target_pairs={{0,8},{1,9},{2,10},{3,11},{4,12},{5,13},{6,14},{7,15},{8,0},{9,1},... | collective-permute-start | bytes 221192 | tf_op jit(solution)/shard_map/ppermute | solution.py:94
  425.1 4.6 %collective-permute-start.41 = (f32[8,128]{1,0:T(8,128)S(1)}, f32[8,128]{1,0:T(8,128)S(1)}, u32[]{:S(2)}, u32[]{:S(2)}) collective-permute-start(f32[8,128]{1,0:T(8,128)S(1)} %iota.23), channel_id=1, source_target_pairs={{0,8},{1,9},{2,10},{3,11},{4,12},{5,13},{6,14},{7,15},{8,0},{9,1},... | collective-permute-start | bytes 12296 | tf_op jit(solution)/shard_map/ppermute | solution.py:94
  425.5 5.4 %collective-permute-start.42 = (f32[8,128]{1,0:T(8,128)S(1)}, f32[8,128]{1,0:T(8,128)S(1)}, u32[]{:S(2)}, u32[]{:S(2)}) collective-permute-start(f32[8,128]{1,0:T(8,128)S(1)} %iota.23), channel_id=1, source_target_pairs={{0,12},{1,13},{2,14},{3,15},{4,8},{5,9},{6,10},{7,11},{8,4},{9,5},... | collective-permute-start | bytes 12296 | tf_op jit(solution)/shard_map/ppermute | solution.py:94
  432.6 9.6 %collective-permute-start.47 = (f32[8,128]{1,0:T(8,128)S(1)}, f32[8,128]{1,0:T(8,128)S(1)}, u32[]{:S(2)}, u32[]{:S(2)}) collective-permute-start(f32[8,128]{1,0:T(8,128)S(1)} %add.191), channel_id=1, source_target_pairs={{0,3},{1,2},{2,1},{3,0},{4,7},{5,6},{6,5},{7,4},{8,11},{9,10},{10,... | collective-permute-start | bytes 12296 | tf_op jit(solution)/shard_map/ppermute | solution.py:94
  437.3 4.9 %collective-permute-start.46 = (f32[8,128]{1,0:T(8,128)S(1)}, f32[8,128]{1,0:T(8,128)S(1)}, u32[]{:S(2)}, u32[]{:S(2)}) collective-permute-start(f32[8,128]{1,0:T(8,128)S(1)} %add.191), channel_id=1, source_target_pairs={{0,2},{1,3},{2,0},{3,1},{4,6},{5,7},{6,4},{7,5},{8,10},{9,11},{10,... | collective-permute-start | bytes 12296 | tf_op jit(solution)/shard_map/ppermute | solution.py:94
  437.3 4.9 %collective-permute-start.45 = (f32[8,128]{1,0:T(8,128)S(1)}, f32[8,128]{1,0:T(8,128)S(1)}, u32[]{:S(2)}, u32[]{:S(2)}) collective-permute-start(f32[8,128]{1,0:T(8,128)S(1)} %add.191), channel_id=1, source_target_pairs={{0,1},{1,0},{2,3},{3,2},{4,5},{5,4},{6,7},{7,6},{8,9},{9,8},{10,11... | collective-permute-start | bytes 12296 | tf_op jit(solution)/shard_map/ppermute | solution.py:94
  (23 other events, 276.7 us)

commit v4 on v3

--- a/solution.py
+++ b/solution.py
@@ -754,7 +754,7 @@
 
 def encode_rows(arrived, w_in, w_node, biases, source):
     posts = arrived.shape[0]
-    tile = 512
+    tile = 1024
 
     def body(
         arrived_ref, in_ref, node_ref, bias_ref, source_ref,
@@ -861,6 +861,36 @@
         cost_estimate=cost(10),
         name="encode_backward",
     )(*carried, mesh, gathered, *args)
+
+
+def settled_rows(stays, own, came):
+    tile = 512
+
+    def body(stays_ref, own_ref, came_ref, out_ref):
+        @pl.when(stays_ref[0] == 1)
+        def _():
+            out_ref[...] = own_ref[...]
+
+        @pl.when(stays_ref[0] == 0)
+        def _():
+            out_ref[...] = came_ref[...].astype(jnp.float32)
+
+    return pl.pallas_call(
+        body,
+        grid_spec=pltpu.PrefetchScalarGridSpec(
+            num_scalar_prefetch=1,
+            grid=(own.shape[0] // tile,),
+            in_specs=[
+                pl.BlockSpec((tile, D), lambda i, stay: (i * stay[0], 0)),
+                pl.BlockSpec((tile, D), lambda i, stay: (i * (1 - stay[0]), 0)),
+            ],
+            out_specs=pl.BlockSpec((tile, D), lambda i, stay: (i, 0)),
+        ),
+        out_shape=jax.ShapeDtypeStruct(own.shape, jnp.float32),
+        compiler_params=LIMIT,
+        cost_estimate=cost(2),
+        name="settled_rows",
+    )(stays.astype(jnp.int32).reshape(1), own, came)
 
 
 def shards(walk, master, moment1, moment2, inputs, targets, valid, owner, slot, neighbours, partner):
@@ -1075,7 +1105,7 @@
         jnp.where(lane == 0, local_total, jnp.sum(mine * mine)), late
     )
     total, norm = sums[0, 0], jnp.sqrt(sums[0, 1])
-    node_grads = settled(grad_mesh, late)
+    node_grads = settled_rows(stays, grad_mesh, late)
     clipped = mine * jnp.minimum(1.0, 0.05 / norm)
     first = 0.9 * moment1 + 0.1 * clipped
     second = 0.999 * moment2 + 0.001 * clipped * clipped

time: 449 us -> 450 us (level)
  transfers between devices with their start and end apart: 51 -> 51, of which waited for: 26 -> 26; matrix products, arithmetic and copies ran while one was open for 6% -> 5% of each run, Pallas kernels for 25% -> 26%
where the time goes in v4:
time: 450 us; the launch traced here: 448 us
  Pallas kernels  229 us (51%)
  waiting for transfers between devices  92.4 us (21%)
  starting transfers between devices  83.4 us (19%)
  other arithmetic  19.9 us (4%)
  local copies, waits for them, and re-layouts  11.1 us (2%)
  between operations  8.4 us (2%)
    pallas_call x5, Pallas kernels, round_forward(): pl.pallas_call(body, grid_spec=pltpu.PrefetchScalarGridSpec(num_scalar_pr...  83 us
    pallas_call x3, Pallas kernels, edges_backward(): pl.pallas_call(body, grid_spec=pltpu.PrefetchScalarGridSpec(num_scalar_pr...  78.6 us
    ppermute x25, waiting for transfers between devices, swapped(): lax.ppermute(value, axis, [(i, i ^ bit) for i in range(lax.axis_size(axis...  32.2 us
    ppermute x25, starting transfers between devices, swapped(): lax.ppermute(value, axis, [(i, i ^ bit) for i in range(lax.axis_size(axis...  29.9 us
    pallas_call x3, Pallas kernels, weight_grads(): pl.pallas_call(body, grid=(blocks // tile,), in_specs=[rows] * 7 + [whole...  24.4 us
    all_to_all x3, waiting for transfers between devices, exchanged(): lax.all_to_all(rows.reshape(bands, capacity, HALF), 'space', split_axis=0...  21.1 us
    ppermute x8, waiting for transfers between devices, halo(): lax.ppermute(last, 'space', up)  20.9 us
    ppermute x8, starting transfers between devices, halo(): lax.ppermute(initial, 'space', down)  20.6 us
  transfers between devices with their start and end apart: 51, of which 26 were waited for; matrix products, arithmetic and copies ran while one was open for 5% of the time, Pallas kernels for 26%

profile of v4, /device:TPU:0, one launch (start us, length us, event | category | flops | bytes accessed | tf_op | source)
XLA Modules:
  0.0 447.8 jit_solution(6456452914640628836)
XLA Ops:
  2.5 5.1 %collective-permute-start.2 = (bf16[1,144,256]{2,1,0:T(8,128)(2,1)S(1)}, bf16[1,144,256]{2,1,0:T(8,128)(2,1)S(1)}, u32[]{:S(2)}, u32[]{:S(2)}) collective-permute-start(bf16[1,144,256]{2,1,0:T(8,128)(2,1)S(1)} %broadcast_in_dim_reshape.3), channel_id=1, source_target_pairs={{0,12},{1,13},{2,14},{3,15},{4,8},{5,9},{6,10},{7,11},{8,4},{9,5},... | collective-permute-start | bytes 221192 | tf_op jit(solution)/shard_map/ppermute | solution.py:94
  26.1 4.8 %collective-permute-done.6 = bf16[8,72,256]{2,1,0:T(8,128)(2,1)S(1)} collective-permute-done((bf16[8,72,256]{2,1,0:T(8,128)(2,1)S(1)}, bf16[8,72,256]{2,1,0:T(8,128)(2,1)S(1)}, u32[]{:S(2)}, u32[]{:S(2)}) %collective-permute-start.6) | collective-permute-done | bytes 294944 | tf_op jit(solution)/shard_map/ppermute | solution.py:94
  32.4 5.2 %all-to-all-start = ((bf16[16,64,128]{2,1,0:T(8,128)(2,1)}), bf16[16,64,128]{2,1,0:T(8,128)(2,1)S(1)}, u32[]{:S(2)}, u32[]{:S(2)}) async-start(bf16[16,64,128]{2,1,0:T(8,128)(2,1)} %bitcast.4), calls=%async_computation | async-start | bytes 524288 | tf_op jit(solution)/shard_map/all_to_all | solution.py:937
  38.6 4.0 spread_rows.1
  42.6 5.4 %all-to-all-done = bf16[16,64,128]{2,1,0:T(8,128)(2,1)S(1)} async-done(((bf16[16,64,128]{2,1,0:T(8,128)(2,1)}), bf16[16,64,128]{2,1,0:T(8,128)(2,1)S(1)}, u32[]{:S(2)}, u32[]{:S(2)}) %all-to-all-start) | async-done | bytes 262176 | tf_op jit(solution)/shard_map/all_to_all | solution.py:937
  48.7 5.5 %encode_rows.1 = (f32[2048,256]{1,0:T(8,128)}, bf16[2048,256]{1,0:T(8,128)(2,1)}, bf16[4096,128]{1,0:T(8,128)(2,1)}, s32[1,1024]{1,0:T(1,128)}, s32[1024,1]{1,0:T(8,128)}) custom-call(bf16[1024,128]{1,0:T(8,128)(2,1)} %bitcast.131, bf16[128,256]{1,0:T(8,128)(2,1)} %get-tuple-element.147.in_ref, bf16[256,256]{1,0:T(8,128)(2,1)} %get-tuple-element.148.node_ref, ...), custom_call_target="tpu_custom_call" | custom-call | bytes 15000000 | tf_op jit(solution)/shard_map/encode_rows/pallas_call | solution.py:783
  59.9 3.9 node_terms.3
  63.8 4.5 %collective-permute-start.12 = (bf16[79,360]{1,0:T(8,128)(2,1)S(1)}, bf16[79,360]{1,0:T(8,128)(2,1)S(1)}, u32[]{:S(2)}, u32[]{:S(2)}) collective-permute-start(bf16[79,360]{1,0:T(8,128)(2,1)S(1)} %get-tuple-element.322), channel_id=1, source_target_pairs={{0,1},{1,2},{2,3},{3,4},{4,5},{5,6},{6,7},{7,8},{8,9},{9,10},{10,1... | collective-permute-start | bytes 170648 | tf_op jit(solution)/shard_map/ppermute | solution.py:49
  69.0 11.1 %collective-permute-done.13 = bf16[79,360]{1,0:T(8,128)(2,1)S(1)} collective-permute-done((bf16[79,360]{1,0:T(8,128)(2,1)S(1)}, bf16[79,360]{1,0:T(8,128)(2,1)S(1)}, u32[]{:S(2)}, u32[]{:S(2)}) %collective-permute-start.13) | collective-permute-done | bytes 56912 | tf_op jit(solution)/shard_map/ppermute | solution.py:49
  80.2 2.6 collective-permute-done.10.refs_0_
  82.8 14.3 %round_forward.5 = (f32[2048,256]{1,0:T(8,128)}, f32[2048,256]{1,0:T(8,128)}, bf16[2048,256]{1,0:T(8,128)(2,1)}, bf16[2048,256]{1,0:T(8,128)(2,1)}, bf16[6,4096,...) custom-call(s32[6144]{0:T(1024)} %get-tuple-element.325.index_ref, f32[2048,256]{1,0:T(8,128)} %get-tuple-element.154.mesh_ref, ...), custom_call_target="tpu_custom_call" | custom-call | bytes 42000000 | tf_op jit(solution)/shard_map/round_forward/pallas_call | solution.py:497
  99.2 14.3 %round_forward.6 = (f32[2048,256]{1,0:T(8,128)}, f32[2048,256]{1,0:T(8,128)}, bf16[2048,256]{1,0:T(8,128)(2,1)}, bf16[2048,256]{1,0:T(8,128)(2,1)}, bf16[6,4096,...) custom-call(s32[6144]{0:T(1024)} %get-tuple-element.326.index_ref, ...), custom_call_target="tpu_custom_call", output_to_operand_aliasing={{0}: (9, {}), {1}: (10, {}), {2}: (11, {}), {3}: (12, {}), ... | custom-call | bytes 42000000 | tf_op jit(solution)/shard_map/round_forward/pallas_call | solution.py:497
  115.3 3.9 node_terms.4
  121.4 5.8 %collective-permute-done.17.refs_1_.refs_0_ = bf16[2048,128]{1,0:T(8,128)(2,1)} collective-permute-done((bf16[2048,128]{1,0:T(8,128)(2,1)}, bf16[2048,128]{1,0:T(8,128)(2,1)}, u32[]{:S(2)}, u32[]{:S(2)}) %collective-permute-start.17) | collective-permute-done | bytes 524320 | tf_op jit(solution)/shard_map/ppermute | solution.py:77
  127.2 14.0 %round_forward.7 = (f32[2048,256]{1,0:T(8,128)}, f32[2048,256]{1,0:T(8,128)}, bf16[2048,256]{1,0:T(8,128)(2,1)}, bf16[2048,256]{1,0:T(8,128)(2,1)}, bf16[6,4096,...) custom-call(s32[6144]{0:T(1024)} %get-tuple-element.325.index_ref, f32[2048,256]{1,0:T(8,128)} %get-tuple-element.168.mesh_ref.refs_0_, ...), custom_call_target="tpu_custom_call" | custom-call | bytes 42000000 | tf_op jit(solution)/shard_map/round_forward/pallas_call | solution.py:497
  143.6 14.1 %round_forward.8 = (f32[2048,256]{1,0:T(8,128)}, f32[2048,256]{1,0:T(8,128)}, bf16[2048,256]{1,0:T(8,128)(2,1)}, bf16[2048,256]{1,0:T(8,128)(2,1)}, bf16[6,4096,...) custom-call(s32[6144]{0:T(1024)} %get-tuple-element.326.index_ref, ...), custom_call_target="tpu_custom_call", output_to_operand_aliasing={{0}: (11, {}), {1}: (12, {}), {2}: (13, {}), {3}: (14, {}),... | custom-call | bytes 42000000 | tf_op jit(solution)/shard_map/round_forward/pallas_call | solution.py:497
  157.7 3.3 collective-permute-start.22
  161.9 3.9 node_terms.5
  165.8 4.8 %collective-permute-done.22.refs_5_ = bf16[2048,128]{1,0:T(8,128)(2,1)} collective-permute-done((bf16[2048,128]{1,0:T(8,128)(2,1)}, bf16[2048,128]{1,0:T(8,128)(2,1)}, u32[]{:S(2)}, u32[]{:S(2)}) %collective-permute-start.22) | collective-permute-done | bytes 524320 | tf_op jit(solution)/shard_map/ppermute | solution.py:77
  170.6 2.9 collective-permute-done.21.refs_1_
  173.4 26.3 %round_forward.9 = (f32[2048,256]{1,0:T(8,128)}, f32[2048,256]{1,0:T(8,128)}, bf16[2048,256]{1,0:T(8,128)(2,1)}, bf16[2048,256]{1,0:T(8,128)(2,1)}, bf16[6,4096,...) custom-call(s32[12288]{0:T(1024)} %copy-done.6, ...), custom_call_target="tpu_custom_call" | custom-call | bytes 72000000 | tf_op jit(solution)/shard_map/round_forward/pallas_call | solution.py:497
  199.7 3.5 all-to-all-start.1
  203.3 8.4 %all-to-all-done.1 = bf16[16,64,128]{2,1,0:T(8,128)(2,1)S(1)} async-done(((bf16[16,64,128]{2,1,0:T(8,128)(2,1)}), bf16[16,64,128]{2,1,0:T(8,128)(2,1)S(1)}, u32[]{:S(2)}, u32[]{:S(2)}) %all-to-all-start.1) | async-done | bytes 262176 | tf_op jit(solution)/shard_map/all_to_all | solution.py:937
  213.3 3.3 collective-permute-start.23
  220.5 2.3 collective-permute-done.24
  225.7 5.8 %all-to-all-start.2 = ((bf16[16,64,128]{2,1,0:T(8,128)(2,1)}), bf16[16,64,128]{2,1,0:T(8,128)(2,1)S(1)}, u32[]{:S(2)}, u32[]{:S(2)}) async-start(bf16[16,64,128]{2,1,0:T(8,128)(2,1)} %bitcast.20), calls=%async_computation.2 | async-start | bytes 524288 | tf_op jit(solution)/shard_map/all_to_all | solution.py:937
  232.6 7.4 %all-to-all-done.2 = bf16[16,64,128]{2,1,0:T(8,128)(2,1)S(1)} async-done(((bf16[16,64,128]{2,1,0:T(8,128)(2,1)}), bf16[16,64,128]{2,1,0:T(8,128)(2,1)S(1)}, u32[]{:S(2)}, u32[]{:S(2)}) %all-to-all-start.2) | async-done | bytes 262176 | tf_op jit(solution)/shard_map/all_to_all | solution.py:937
  241.7 26.8 %edges_backward.3 = (f32[2048,256]{1,0:T(8,128)}, bf16[2048,256]{1,0:T(8,128)(2,1)}, bf16[1024,256]{1,0:T(8,128)(2,1)}, bf16[2048,256]{1,0:T(8,128)(2,1)}, bf16[...) custom-call(s32[12288]{0:T(1024)} %copy-done.6, ...), custom_call_target="tpu_custom_call" | custom-call | bytes 75000000 | tf_op jit(solution)/shard_map/edges_backward/pallas_call | solution.py:642
  270.0 2.4 collective-permute-start.27
  273.0 2.6 decode_grads.1
  275.7 7.4 %weight_grads.3 = (f32[2048,256]{1,0:T(8,128)}, f32[1024,256]{1,0:T(8,128)}, f32[2,256]{1,0:T(2,128)}) custom-call(f32[2048,256]{1,0:T(8,128)} %get-tuple-element.182.mesh_ref.refs_0_, bf16[2048,256]{1,0:T(8,128)(2,1)} %get-tuple-element.206.dest_ref, bf16[2048,256]{1,0:T(8,128)(2,1)} %get-tuple-element.207.agg_ref, ...), custom_call_target="tpu_custom_call" | custom-call | bytes 30000000 | tf_op jit(solution)/shard_map/weight_grads/pallas_call | solution.py:727
  283.1 4.0 convert_select_fusion
  287.3 25.8 %edges_backward.4 = (f32[2048,256]{1,0:T(8,128)}, bf16[2048,256]{1,0:T(8,128)(2,1)}, bf16[2048,256]{1,0:T(8,128)(2,1)}, bf16[2048,256]{1,0:T(8,128)(2,1)}, bf16[...) custom-call(s32[12288]{0:T(1024)} %copy-done.6, ...), custom_call_target="tpu_custom_call" | custom-call | bytes 84000000 | tf_op jit(solution)/shard_map/edges_backward/pallas_call | solution.py:642
  313.7 3.3 collective-permute-start.29
  317.0 8.6 %weight_grads.4 = (f32[2048,256]{1,0:T(8,128)}, f32[1024,256]{1,0:T(8,128)}, f32[2,256]{1,0:T(2,128)}, f32[256,256]{1,0:T(8,128)}) custom-call(f32[2048,256]{1,0:T(8,128)} %get-tuple-element.168.mesh_ref.refs_0_, bf16[2048,256]{1,0:T(8,128)(2,1)} %get-tuple-element.227.dest_ref, bf16[2048,256]{1,0:T(8,128)(2,1)} %get-tuple-element.228.agg_ref, ...), custom_call_target="tpu_custom_call" | custom-call | bytes 30000000 | tf_op jit(solution)/shard_map/weight_grads/pallas_call | solution.py:727
  325.6 5.5 %collective-permute-done.28.refs_6_ = bf16[4096,128]{1,0:T(8,128)(2,1)} collective-permute-done((bf16[4096,128]{1,0:T(8,128)(2,1)}, bf16[4096,128]{1,0:T(8,128)(2,1)}, u32[]{:S(2)}, u32[]{:S(2)}) %collective-permute-start.28) | collective-permute-done | bytes 1048608 | tf_op jit(solution)/shard_map/ppermute | solution.py:77
  331.1 26.0 %edges_backward.5 = (f32[2048,256]{1,0:T(8,128)}, bf16[2048,256]{1,0:T(8,128)(2,1)}, bf16[2048,256]{1,0:T(8,128)(2,1)}, bf16[2048,256]{1,0:T(8,128)(2,1)}, bf16[...) custom-call(s32[12288]{0:T(1024)} %copy-done.6, ...), custom_call_target="tpu_custom_call" | custom-call | bytes 84000000 | tf_op jit(solution)/shard_map/edges_backward/pallas_call | solution.py:642
  357.1 3.8 collective-permute-start.31
  361.8 8.4 %weight_grads.5 = (f32[2048,256]{1,0:T(8,128)}, f32[1024,256]{1,0:T(8,128)}, f32[2,256]{1,0:T(2,128)}, f32[256,256]{1,0:T(8,128)}) custom-call(f32[2048,256]{1,0:T(8,128)} %get-tuple-element.154.mesh_ref, bf16[2048,256]{1,0:T(8,128)(2,1)} %get-tuple-element.238.dest_ref, bf16[2048,256]{1,0:T(8,128)(2,1)} %get-tuple-element.239.agg_ref, ...), custom_call_target="tpu_custom_call" | custom-call | bytes 30000000 | tf_op jit(solution)/shard_map/weight_grads/pallas_call | solution.py:727
  370.2 4.0 collective-permute-done.30.first_ref
  374.2 10.1 %encode_backward.1 = (f32[2048,256]{1,0:T(8,128)}, bf16[2048,256]{1,0:T(8,128)(2,1)}, f32[128,256]{1,0:T(8,128)}, f32[256,256]{1,0:T(8,128)}, f32[2,256]{1,0:T(2,128)}, /*index=5*/f32[256,256]{1,0:T(8,128)}) custom-call(f32[2048,256]{1,0:T(8,128)} %get-tuple-element.245.part_ref, f32[4096,128]{1,0:T(8,128)} %get-tuple-element.246.own_ref, ...), custom_call_target="tpu_custom_call" | custom-call | bytes 30000000 | tf_op jit(solution)/shard_map/encode_backward/pallas_call | solution.py:848
  384.2 5.1 %collect_rows.1 = (f32[16,144,256]{2,1,0:T(8,128)}, bf16[16,144,256]{2,1,0:T(8,128)(2,1)}) custom-call(s32[1]{0:T(128)} %bitcast.6.place_ref, f32[128,256]{1,0:T(8,128)} %get-tuple-element.250.refs_0_, f32[256,256]{1,0:T(8,128)} %get-tuple-element.251.refs_1_, f32[256,256]{1,0:T(8,128)} %get-tuple-element.252.refs_2_, f32[78,256]{1,0:T(8,128)} %reshape.164.refs_3_, ...), custom_call_target="tpu_custom_call" | custom-call | bytes 15000000 | tf_op jit(solution)/shard_map/collect_rows/pallas_call | solution.py:233
  389.3 3.1 collective-permute-done.32
  394.7 8.9 %collective-permute-done.33 = bf16[4,2,72,256]{3,2,0,1:T(8,128)(2,1)S(1)} collective-permute-done((bf16[4,2,72,256]{3,2,0,1:T(8,128)(2,1)S(1)}, bf16[4,2,72,256]{3,2,0,1:T(8,128)(2,1)S(1)}, u32[]{:S(2)}, u32[]{:S(2)}) %collective-permute-start.33) | collective-permute-done | bytes 294944 | tf_op jit(solution)/shard_map/ppermute | solution.py:94
  405.6 3.3 collective-permute-done.34
  411.1 5.7 %collective-permute-start.39 = (bf16[1,144,256]{2,1,0:T(8,128)(2,1)S(1)}, bf16[1,144,256]{2,1,0:T(8,128)(2,1)S(1)}, u32[]{:S(2)}, u32[]{:S(2)}) collective-permute-start(bf16[1,144,256]{2,1,0:T(8,128)(2,1)S(1)} %get-tuple-element.317), channel_id=1, source_target_pairs={{0,12},{1,13},{2,14},{3,15},{4,8},{5,9},{6,10},{7,11},{8,4},{9,5},... | collective-permute-start | bytes 221192 | tf_op jit(solution)/shard_map/ppermute | solution.py:94
  431.9 4.4 collective-permute-start.47
  439.3 3.9 settled_rows.1
  (201 shorter events, 76.0 us)
Async XLA Ops:
  2.5 14.5 %collective-permute-start.2 = (bf16[1,144,256]{2,1,0:T(8,128)(2,1)S(1)}, bf16[1,144,256]{2,1,0:T(8,128)(2,1)S(1)}, u32[]{:S(2)}, u32[]{:S(2)}) collective-permute-start(bf16[1,144,256]{2,1,0:T(8,128)(2,1)S(1)} %broadcast_in_dim_reshape.3), channel_id=1, source_target_pairs={{0,12},{1,13},{2,14},{3,15},{4,8},{5,9},{6,10},{7,11},{8,4},{9,5},... | collective-permute-start | bytes 221192 | tf_op jit(solution)/shard_map/ppermute | solution.py:94
  7.6 9.4 %collective-permute-start.1 = (bf16[1,144,256]{2,1,0:T(8,128)(2,1)S(1)}, bf16[1,144,256]{2,1,0:T(8,128)(2,1)S(1)}, u32[]{:S(2)}, u32[]{:S(2)}) collective-permute-start(bf16[1,144,256]{2,1,0:T(8,128)(2,1)S(1)} %broadcast_in_dim_reshape.3), channel_id=1, source_target_pairs={{0,8},{1,9},{2,10},{3,11},{4,12},{5,13},{6,14},{7,15},{8,0},{9,1},... | collective-permute-start | bytes 221192 | tf_op jit(solution)/shard_map/ppermute | solution.py:94
  7.6 9.4 %collective-permute-start = (bf16[1,144,256]{2,1,0:T(8,128)(2,1)S(1)}, bf16[1,144,256]{2,1,0:T(8,128)(2,1)S(1)}, u32[]{:S(2)}, u32[]{:S(2)}) collective-permute-start(bf16[1,144,256]{2,1,0:T(8,128)(2,1)S(1)} %broadcast_in_dim_reshape.3), channel_id=1, source_target_pairs={{0,4},{1,5},{2,6},{3,7},{4,0},{5,1},{6,2},{7,3},{8,12},{9,13},{10,... | collective-permute-start | bytes 221192 | tf_op jit(solution)/shard_map/ppermute | solution.py:94
  17.0 5.2 %collective-permute-start.4 = (bf16[4,72,256]{2,1,0:T(8,128)(2,1)S(1)}, bf16[4,72,256]{2,1,0:T(8,128)(2,1)S(1)}, u32[]{:S(2)}, u32[]{:S(2)}) collective-permute-start(bf16[4,72,256]{2,1,0:T(8,128)(2,1)S(1)} %get-tuple-element.319), channel_id=1, source_target_pairs={{0,1},{1,0},{2,3},{3,2},{4,5},{5,4},{6,7},{7,6},{8,9},{9,8},{10,11... | collective-permute-start | bytes 442376 | tf_op jit(solution)/shard_map/ppermute | solution.py:94
  18.7 5.1 %collective-permute-start.3 = (bf16[4,72,256]{2,1,0:T(8,128)(2,1)S(1)}, bf16[4,72,256]{2,1,0:T(8,128)(2,1)S(1)}, u32[]{:S(2)}, u32[]{:S(2)}) collective-permute-start(bf16[4,72,256]{2,1,0:T(8,128)(2,1)S(1)} %get-tuple-element.320), channel_id=1, source_target_pairs={{0,2},{1,3},{2,0},{3,1},{4,6},{5,7},{6,4},{7,5},{8,10},{9,11},{10,... | collective-permute-start | bytes 442376 | tf_op jit(solution)/shard_map/ppermute | solution.py:94
  23.9 7.0 %collective-permute-start.6 = (bf16[8,72,256]{2,1,0:T(8,128)(2,1)S(1)}, bf16[8,72,256]{2,1,0:T(8,128)(2,1)S(1)}, u32[]{:S(2)}, u32[]{:S(2)}) collective-permute-start(bf16[8,72,256]{2,1,0:T(8,128)(2,1)S(1)} %pad_maximum_fusion.3), channel_id=1, source_target_pairs={{0,2},{1,3},{2,0},{3,1},{4,6},{5,7},{6,4},{7,5},{8,10},{9,11},{10,... | collective-permute-start | bytes 884744 | tf_op jit(solution)/shard_map/ppermute | solution.py:94
  25.5 6.7 %collective-permute-start.5 = (bf16[8,72,256]{2,1,0:T(8,128)(2,1)S(1)}, bf16[8,72,256]{2,1,0:T(8,128)(2,1)S(1)}, u32[]{:S(2)}, u32[]{:S(2)}) collective-permute-start(bf16[8,72,256]{2,1,0:T(8,128)(2,1)S(1)} %pad_maximum_fusion.2), channel_id=1, source_target_pairs={{0,1},{1,0},{2,3},{3,2},{4,5},{5,4},{6,7},{7,6},{8,9},{9,8},{10,11... | collective-permute-start | bytes 884744 | tf_op jit(solution)/shard_map/ppermute | solution.py:94
  30.9 6.7 %collective-permute-start.8 = (bf16[16,72,256]{2,1,0:T(8,128)(2,1)S(1)}, bf16[16,72,256]{2,1,0:T(8,128)(2,1)S(1)}, u32[]{:S(2)}, u32[]{:S(2)}) collective-permute-start(bf16[16,72,256]{2,1,0:T(8,128)(2,1)S(1)} %constant_dynamic-update-slice_fusion.6.refs_1_), channel_id=1, source_target_pairs={{0,16},{16,0},{1,17},{17,1},{2,18},{18,2},{3,19},{19,3},{4,20},{20... | collective-permute-start | bytes 1769480 | tf_op jit(solution)/shard_map/ppermute | solution.py:94
  32.3 5.3 %collective-permute-start.7 = (bf16[16,72,256]{2,1,0:T(8,128)(2,1)S(1)}, bf16[16,72,256]{2,1,0:T(8,128)(2,1)S(1)}, u32[]{:S(2)}, u32[]{:S(2)}) collective-permute-start(bf16[16,72,256]{2,1,0:T(8,128)(2,1)S(1)} %constant_dynamic-update-slice_fusion.4.refs_0_), channel_id=1, source_target_pairs={{0,16},{16,0},{1,17},{17,1},{2,18},{18,2},{3,19},{19,3},{4,20},{20... | collective-permute-start | bytes 1769480 | tf_op jit(solution)/shard_map/ppermute | solution.py:94
  32.4 15.6 %all-to-all-start = ((bf16[16,64,128]{2,1,0:T(8,128)(2,1)}), bf16[16,64,128]{2,1,0:T(8,128)(2,1)S(1)}, u32[]{:S(2)}, u32[]{:S(2)}) async-start(bf16[16,64,128]{2,1,0:T(8,128)(2,1)} %bitcast.4), calls=%async_computation | async-start | bytes 524288 | tf_op jit(solution)/shard_map/all_to_all | solution.py:937
  54.2 26.0 %collective-permute-start.11 = (bf16[4096,128]{1,0:T(8,128)(2,1)}, bf16[4096,128]{1,0:T(8,128)(2,1)}, u32[]{:S(2)}, u32[]{:S(2)}) collective-permute-start(bf16[4096,128]{1,0:T(8,128)(2,1)} %get-tuple-element.155.refs_1_), channel_id=1, source_target_pairs={{1,0},{3,1},{2,3},{6,2},{4,6},{5,4},{7,5},{11,7},{9,11},{8,9},{10,... | collective-permute-start | bytes 3145736 | tf_op jit(solution)/shard_map/ppermute | solution.py:77
  55.9 26.9 %collective-permute-start.10 = (bf16[4096,128]{1,0:T(8,128)(2,1)}, bf16[4096,128]{1,0:T(8,128)(2,1)}, u32[]{:S(2)}, u32[]{:S(2)}) collective-permute-start(bf16[4096,128]{1,0:T(8,128)(2,1)} %get-tuple-element.155.refs_1_), channel_id=1, source_target_pairs={{0,1},{1,3},{3,2},{2,6},{6,4},{4,5},{5,7},{7,11},{11,9},{9,8},{8,1... | collective-permute-start | bytes 3145736 | tf_op jit(solution)/shard_map/ppermute | solution.py:77
  56.3 12.0 %collective-permute-start.9 = (s32[12288]{0:T(1024)S(1)}, s32[12288]{0:T(1024)S(1)}, u32[]{:S(2)}, u32[]{:S(2)}) collective-permute-start(s32[12288]{0:T(1024)S(1)} %reshape.156), channel_id=1, source_target_pairs={{0,0},{1,1},{2,3},{3,2},{4,6},{5,4},{6,5},{7,7},{8,11},{9,9},{10,8... | collective-permute-start | bytes 147464 | tf_op jit(solution)/shard_map/ppermute | solution.py:966
  58.5 5.3 %collective-permute-start.14 = (f32[1,3]{1,0:T(1,128)S(1)}, f32[1,3]{1,0:T(1,128)S(1)}, u32[]{:S(2)}, u32[]{:S(2)}) collective-permute-start(f32[1,3]{1,0:T(1,128)S(1)} %bitcast.147), channel_id=1, source_target_pairs={{0,16},{16,0},{1,17},{17,1},{2,18},{18,2},{3,19},{19,3},{4,20},{20... | collective-permute-start | bytes 44 | tf_op jit(solution)/shard_map/ppermute | solution.py:94
  58.6 21.4 %collective-permute-start.13 = (bf16[79,360]{1,0:T(8,128)(2,1)S(1)}, bf16[79,360]{1,0:T(8,128)(2,1)S(1)}, u32[]{:S(2)}, u32[]{:S(2)}) collective-permute-start(bf16[79,360]{1,0:T(8,128)(2,1)S(1)} %get-tuple-element.321), channel_id=1, source_target_pairs={{1,0},{2,1},{3,2},{4,3},{5,4},{6,5},{7,6},{8,7},{9,8},{10,9},{11,1... | collective-permute-start | bytes 170648 | tf_op jit(solution)/shard_map/ppermute | solution.py:49
  63.8 16.2 %collective-permute-start.12 = (bf16[79,360]{1,0:T(8,128)(2,1)S(1)}, bf16[79,360]{1,0:T(8,128)(2,1)S(1)}, u32[]{:S(2)}, u32[]{:S(2)}) collective-permute-start(bf16[79,360]{1,0:T(8,128)(2,1)S(1)} %get-tuple-element.322), channel_id=1, source_target_pairs={{0,1},{1,2},{2,3},{3,4},{4,5},{5,6},{6,7},{7,8},{8,9},{9,10},{10,1... | collective-permute-start | bytes 170648 | tf_op jit(solution)/shard_map/ppermute | solution.py:49
  97.1 16.4 %collective-permute-start.16 = (bf16[2048,128]{1,0:T(8,128)(2,1)}, bf16[2048,128]{1,0:T(8,128)(2,1)S(1)}, u32[]{:S(2)}, u32[]{:S(2)}) collective-permute-start(bf16[2048,128]{1,0:T(8,128)(2,1)} %get-tuple-element.170.refs_2_.refs_1_), channel_id=1, source_target_pairs={{1,0},{3,1},{2,3},{6,2},{4,6},{5,4},{7,5},{11,7},{9,11},{8,9},{10,... | collective-permute-start | bytes 1572872 | tf_op jit(solution)/shard_map/ppermute | solution.py:77
  99.2 14.3 %collective-permute-start.15 = (bf16[2048,128]{1,0:T(8,128)(2,1)}, bf16[2048,128]{1,0:T(8,128)(2,1)}, u32[]{:S(2)}, u32[]{:S(2)}) collective-permute-start(bf16[2048,128]{1,0:T(8,128)(2,1)} %get-tuple-element.170.refs_2_.refs_1_), channel_id=1, source_target_pairs={{0,1},{1,3},{3,2},{2,6},{6,4},{4,5},{5,7},{7,11},{11,9},{9,8},{8,1... | collective-permute-start | bytes 1572872 | tf_op jit(solution)/shard_map/ppermute | solution.py:77
  113.6 13.6 %collective-permute-start.17 = (bf16[2048,128]{1,0:T(8,128)(2,1)}, bf16[2048,128]{1,0:T(8,128)(2,1)}, u32[]{:S(2)}, u32[]{:S(2)}) collective-permute-start(bf16[2048,128]{1,0:T(8,128)(2,1)} %get-tuple-element.171.refs_3_.refs_2_), channel_id=1, source_target_pairs={{0,1},{1,3},{3,2},{2,6},{6,4},{4,5},{5,7},{7,11},{11,9},{9,8},{8,1... | collective-permute-start | bytes 1572872 | tf_op jit(solution)/shard_map/ppermute | solution.py:77
  119.2 24.4 %collective-permute-start.18 = (bf16[2048,128]{1,0:T(8,128)(2,1)}, bf16[2048,128]{1,0:T(8,128)(2,1)}, u32[]{:S(2)}, u32[]{:S(2)}) collective-permute-start(bf16[2048,128]{1,0:T(8,128)(2,1)} %get-tuple-element.171.refs_3_.refs_2_), channel_id=1, source_target_pairs={{1,0},{3,1},{2,3},{6,2},{4,6},{5,4},{7,5},{11,7},{9,11},{8,9},{10,... | collective-permute-start | bytes 1572872 | tf_op jit(solution)/shard_map/ppermute | solution.py:77
  141.2 16.5 %collective-permute-start.20 = (bf16[2048,128]{1,0:T(8,128)(2,1)}, bf16[2048,128]{1,0:T(8,128)(2,1)S(1)}, u32[]{:S(2)}, u32[]{:S(2)}) collective-permute-start(bf16[2048,128]{1,0:T(8,128)(2,1)} %get-tuple-element.184.refs_2_), channel_id=1, source_target_pairs={{1,0},{3,1},{2,3},{6,2},{4,6},{5,4},{7,5},{11,7},{9,11},{8,9},{10,... | collective-permute-start | bytes 1572872 | tf_op jit(solution)/shard_map/ppermute | solution.py:77
  143.0 14.7 %collective-permute-start.19 = (bf16[2048,128]{1,0:T(8,128)(2,1)}, bf16[2048,128]{1,0:T(8,128)(2,1)}, u32[]{:S(2)}, u32[]{:S(2)}) collective-permute-start(bf16[2048,128]{1,0:T(8,128)(2,1)} %get-tuple-element.184.refs_2_), channel_id=1, source_target_pairs={{0,1},{1,3},{3,2},{2,6},{6,4},{4,5},{5,7},{7,11},{11,9},{9,8},{8,1... | collective-permute-start | bytes 1572872 | tf_op jit(solution)/shard_map/ppermute | solution.py:77
  157.7 12.8 %collective-permute-start.22 = (bf16[2048,128]{1,0:T(8,128)(2,1)}, bf16[2048,128]{1,0:T(8,128)(2,1)}, u32[]{:S(2)}, u32[]{:S(2)}) collective-permute-start(bf16[2048,128]{1,0:T(8,128)(2,1)} %get-tuple-element.186.refs_3_), channel_id=1, source_target_pairs={{1,0},{3,1},{2,3},{6,2},{4,6},{5,4},{7,5},{11,7},{9,11},{8,9},{10,... | collective-permute-start | bytes 1572872 | tf_op jit(solution)/shard_map/ppermute | solution.py:77
  161.0 12.4 %collective-permute-start.21 = (bf16[2048,128]{1,0:T(8,128)(2,1)}, bf16[2048,128]{1,0:T(8,128)(2,1)}, u32[]{:S(2)}, u32[]{:S(2)}) collective-permute-start(bf16[2048,128]{1,0:T(8,128)(2,1)} %get-tuple-element.186.refs_3_), channel_id=1, source_target_pairs={{0,1},{1,3},{3,2},{2,6},{6,4},{4,5},{5,7},{7,11},{11,9},{9,8},{8,1... | collective-permute-start | bytes 1572872 | tf_op jit(solution)/shard_map/ppermute | solution.py:77
  199.7 12.0 %all-to-all-start.1 = ((bf16[16,64,128]{2,1,0:T(8,128)(2,1)}), bf16[16,64,128]{2,1,0:T(8,128)(2,1)S(1)}, u32[]{:S(2)}, u32[]{:S(2)}) async-start(bf16[16,64,128]{2,1,0:T(8,128)(2,1)} %bitcast.141), calls=%async_computation.1 | async-start | bytes 524288 | tf_op jit(solution)/shard_map/all_to_all | solution.py:937
  213.3 9.5 %collective-permute-start.23 = (bf16[78,360]{1,0:T(8,128)(2,1)S(1)}, bf16[78,360]{1,0:T(8,128)(2,1)S(1)}, u32[]{:S(2)}, u32[]{:S(2)}) collective-permute-start(bf16[78,360]{1,0:T(8,128)(2,1)S(1)} %get-tuple-element.323), channel_id=1, source_target_pairs={{0,1},{1,2},{2,3},{3,4},{4,5},{5,6},{6,7},{7,8},{8,9},{9,10},{10,1... | collective-permute-start | bytes 168488 | tf_op jit(solution)/shard_map/ppermute | solution.py:49
  216.6 6.1 %collective-permute-start.24 = (bf16[78,360]{1,0:T(8,128)(2,1)S(1)}, bf16[78,360]{1,0:T(8,128)(2,1)S(1)}, u32[]{:S(2)}, u32[]{:S(2)}) collective-permute-start(bf16[78,360]{1,0:T(8,128)(2,1)S(1)} %get-tuple-element.324), channel_id=1, source_target_pairs={{1,0},{2,1},{3,2},{4,3},{5,4},{6,5},{7,6},{8,7},{9,8},{10,9},{11,1... | collective-permute-start | bytes 168488 | tf_op jit(solution)/shard_map/ppermute | solution.py:49
  225.7 14.4 %all-to-all-start.2 = ((bf16[16,64,128]{2,1,0:T(8,128)(2,1)}), bf16[16,64,128]{2,1,0:T(8,128)(2,1)S(1)}, u32[]{:S(2)}, u32[]{:S(2)}) async-start(bf16[16,64,128]{2,1,0:T(8,128)(2,1)} %bitcast.20), calls=%async_computation.2 | async-start | bytes 524288 | tf_op jit(solution)/shard_map/all_to_all | solution.py:937
  240.1 28.5 %collective-permute-start.25 = (bf16[2048,256]{1,0:T(8,128)(2,1)}, bf16[2048,256]{1,0:T(8,128)(2,1)}, u32[]{:S(2)}, u32[]{:S(2)}) collective-permute-start(bf16[2048,256]{1,0:T(8,128)(2,1)} %convert_element_type.148), channel_id=1, source_target_pairs={{3,2},{2,3},{6,4},{4,5},{5,6},{11,8},{8,10},{10,11},{14,12},{15,13... | collective-permute-start | bytes 3145736 | tf_op jit(solution)/shard_map/ppermute | solution.py:969
  268.5 18.7 %collective-permute-start.26 = (bf16[4096,128]{1,0:T(8,128)(2,1)}, bf16[4096,128]{1,0:T(8,128)(2,1)}, u32[]{:S(2)}, u32[]{:S(2)}) collective-permute-start(bf16[4096,128]{1,0:T(8,128)(2,1)} %get-tuple-element.217), channel_id=1, source_target_pairs={{0,1},{1,3},{3,2},{2,6},{6,4},{4,5},{5,7},{7,11},{11,9},{9,8},{8,1... | collective-permute-start | bytes 3145736 | tf_op jit(solution)/shard_map/ppermute | solution.py:77
  270.0 17.3 %collective-permute-start.27 = (bf16[4096,128]{1,0:T(8,128)(2,1)}, bf16[4096,128]{1,0:T(8,128)(2,1)}, u32[]{:S(2)}, u32[]{:S(2)}) collective-permute-start(bf16[4096,128]{1,0:T(8,128)(2,1)} %get-tuple-element.226), channel_id=1, source_target_pairs={{1,0},{3,1},{2,3},{6,2},{4,6},{5,4},{7,5},{11,7},{9,11},{8,9},{10,... | collective-permute-start | bytes 3145736 | tf_op jit(solution)/shard_map/ppermute | solution.py:77
  313.1 18.0 %collective-permute-start.28 = (bf16[4096,128]{1,0:T(8,128)(2,1)}, bf16[4096,128]{1,0:T(8,128)(2,1)}, u32[]{:S(2)}, u32[]{:S(2)}) collective-permute-start(bf16[4096,128]{1,0:T(8,128)(2,1)} %get-tuple-element.236), channel_id=1, source_target_pairs={{0,1},{1,3},{3,2},{2,6},{6,4},{4,5},{5,7},{7,11},{11,9},{9,8},{8,1... | collective-permute-start | bytes 3145736 | tf_op jit(solution)/shard_map/ppermute | solution.py:77
  313.7 17.4 %collective-permute-start.29 = (bf16[4096,128]{1,0:T(8,128)(2,1)}, bf16[4096,128]{1,0:T(8,128)(2,1)}, u32[]{:S(2)}, u32[]{:S(2)}) collective-permute-start(bf16[4096,128]{1,0:T(8,128)(2,1)} %get-tuple-element.237), channel_id=1, source_target_pairs={{1,0},{3,1},{2,3},{6,2},{4,6},{5,4},{7,5},{11,7},{9,11},{8,9},{10,... | collective-permute-start | bytes 3145736 | tf_op jit(solution)/shard_map/ppermute | solution.py:77
  357.1 17.1 %collective-permute-start.30 = (bf16[4096,128]{1,0:T(8,128)(2,1)}, bf16[4096,128]{1,0:T(8,128)(2,1)}, u32[]{:S(2)}, u32[]{:S(2)}) collective-permute-start(bf16[4096,128]{1,0:T(8,128)(2,1)} %get-tuple-element.247), channel_id=1, source_target_pairs={{0,1},{1,3},{3,2},{2,6},{6,4},{4,5},{5,7},{7,11},{11,9},{9,8},{8,1... | collective-permute-start | bytes 3145736 | tf_op jit(solution)/shard_map/ppermute | solution.py:77
  357.1 17.0 %collective-permute-start.31 = (bf16[4096,128]{1,0:T(8,128)(2,1)}, bf16[4096,128]{1,0:T(8,128)(2,1)}, u32[]{:S(2)}, u32[]{:S(2)}) collective-permute-start(bf16[4096,128]{1,0:T(8,128)(2,1)} %get-tuple-element.248), channel_id=1, source_target_pairs={{1,0},{3,1},{2,3},{6,2},{4,6},{5,4},{7,5},{11,7},{9,11},{8,9},{10,... | collective-permute-start | bytes 3145736 | tf_op jit(solution)/shard_map/ppermute | solution.py:77
  394.5 9.1 %collective-permute-start.33 = (bf16[4,2,72,256]{3,2,0,1:T(8,128)(2,1)S(1)}, bf16[4,2,72,256]{3,2,0,1:T(8,128)(2,1)S(1)}, u32[]{:S(2)}, u32[]{:S(2)}) collective-permute-start(bf16[4,2,72,256]{3,2,0,1:T(8,128)(2,1)S(1)} %fusion.14), channel_id=1, source_target_pairs={{0,1},{1,0},{2,3},{3,2},{4,5},{5,4},{6,7},{7,6},{8,9},{9,8},{10,11... | collective-permute-start | bytes 884744 | tf_op jit(solution)/shard_map/ppermute | solution.py:94
  394.6 9.2 %collective-permute-start.35 = (bf16[4,2,72,256]{3,2,1,0:T(8,128)(2,1)S(1)}, bf16[4,2,72,256]{3,2,1,0:T(8,128)(2,1)S(1)}, u32[]{:S(2)}, u32[]{:S(2)}) collective-permute-start(bf16[4,2,72,256]{3,2,1,0:T(8,128)(2,1)S(1)} %fusion.13), channel_id=1, source_target_pairs={{0,2},{1,3},{2,0},{3,1},{4,6},{5,7},{6,4},{7,5},{8,10},{9,11},{10,... | collective-permute-start | bytes 884744 | tf_op jit(solution)/shard_map/ppermute | solution.py:94
  403.7 5.2 %collective-permute-start.34 = (bf16[4,72,256]{2,1,0:T(8,128)(2,1)S(1)}, bf16[4,72,256]{2,1,0:T(8,128)(2,1)S(1)}, u32[]{:S(2)}, u32[]{:S(2)}) collective-permute-start(bf16[4,72,256]{2,1,0:T(8,128)(2,1)S(1)} %fusion.38), channel_id=1, source_target_pairs={{0,2},{1,3},{2,0},{3,1},{4,6},{5,7},{6,4},{7,5},{8,10},{9,11},{10,... | collective-permute-start | bytes 442376 | tf_op jit(solution)/shard_map/ppermute | solution.py:94
  403.9 5.2 %collective-permute-start.36 = (bf16[4,72,256]{2,1,0:T(8,128)(2,1)S(1)}, bf16[4,72,256]{2,1,0:T(8,128)(2,1)S(1)}, u32[]{:S(2)}, u32[]{:S(2)}) collective-permute-start(bf16[4,72,256]{2,1,0:T(8,128)(2,1)S(1)} %fusion.39), channel_id=1, source_target_pairs={{0,1},{1,0},{2,3},{3,2},{4,5},{5,4},{6,7},{7,6},{8,9},{9,8},{10,11... | collective-permute-start | bytes 442376 | tf_op jit(solution)/shard_map/ppermute | solution.py:94
  409.2 22.7 %collective-permute-start.44 = (bf16[2048,256]{1,0:T(8,128)(2,1)S(1)}, bf16[2048,256]{1,0:T(8,128)(2,1)S(1)}, u32[]{:S(2)}, u32[]{:S(2)}) collective-permute-start(bf16[2048,256]{1,0:T(8,128)(2,1)S(1)} %copy-done.19), channel_id=1, source_target_pairs={{3,2},{2,3},{6,4},{4,5},{5,6},{11,8},{8,10},{10,11},{14,12},{15,13... | collective-permute-start | bytes 3145736 | tf_op jit(solution)/shard_map/ppermute | solution.py:969
  410.0 8.5 %collective-permute-start.37 = (bf16[1,144,256]{2,1,0:T(8,128)(2,1)S(1)}, bf16[1,144,256]{2,1,0:T(8,128)(2,1)S(1)}, u32[]{:S(2)}, u32[]{:S(2)}) collective-permute-start(bf16[1,144,256]{2,1,0:T(8,128)(2,1)S(1)} %get-tuple-element.316), channel_id=1, source_target_pairs={{0,4},{1,5},{2,6},{3,7},{4,0},{5,1},{6,2},{7,3},{8,12},{9,13},{10,... | collective-permute-start | bytes 221192 | tf_op jit(solution)/shard_map/ppermute | solution.py:94
  411.1 9.6 %collective-permute-start.39 = (bf16[1,144,256]{2,1,0:T(8,128)(2,1)S(1)}, bf16[1,144,256]{2,1,0:T(8,128)(2,1)S(1)}, u32[]{:S(2)}, u32[]{:S(2)}) collective-permute-start(bf16[1,144,256]{2,1,0:T(8,128)(2,1)S(1)} %get-tuple-element.317), channel_id=1, source_target_pairs={{0,12},{1,13},{2,14},{3,15},{4,8},{5,9},{6,10},{7,11},{8,4},{9,5},... | collective-permute-start | bytes 221192 | tf_op jit(solution)/shard_map/ppermute | solution.py:94
  416.8 6.1 %collective-permute-start.38 = (bf16[1,144,256]{2,1,0:T(8,128)(2,1)S(1)}, bf16[1,144,256]{2,1,0:T(8,128)(2,1)S(1)}, u32[]{:S(2)}, u32[]{:S(2)}) collective-permute-start(bf16[1,144,256]{2,1,0:T(8,128)(2,1)S(1)} %get-tuple-element.318), channel_id=1, source_target_pairs={{0,8},{1,9},{2,10},{3,11},{4,12},{5,13},{6,14},{7,15},{8,0},{9,1},... | collective-permute-start | bytes 221192 | tf_op jit(solution)/shard_map/ppermute | solution.py:94
  424.4 4.6 %collective-permute-start.41 = (f32[8,128]{1,0:T(8,128)S(1)}, f32[8,128]{1,0:T(8,128)S(1)}, u32[]{:S(2)}, u32[]{:S(2)}) collective-permute-start(f32[8,128]{1,0:T(8,128)S(1)} %iota.23), channel_id=1, source_target_pairs={{0,8},{1,9},{2,10},{3,11},{4,12},{5,13},{6,14},{7,15},{8,0},{9,1},... | collective-permute-start | bytes 12296 | tf_op jit(solution)/shard_map/ppermute | solution.py:94
  424.9 5.4 %collective-permute-start.42 = (f32[8,128]{1,0:T(8,128)S(1)}, f32[8,128]{1,0:T(8,128)S(1)}, u32[]{:S(2)}, u32[]{:S(2)}) collective-permute-start(f32[8,128]{1,0:T(8,128)S(1)} %iota.23), channel_id=1, source_target_pairs={{0,12},{1,13},{2,14},{3,15},{4,8},{5,9},{6,10},{7,11},{8,4},{9,5},... | collective-permute-start | bytes 12296 | tf_op jit(solution)/shard_map/ppermute | solution.py:94
  431.9 11.3 %collective-permute-start.47 = (f32[8,128]{1,0:T(8,128)S(1)}, f32[8,128]{1,0:T(8,128)S(1)}, u32[]{:S(2)}, u32[]{:S(2)}) collective-permute-start(f32[8,128]{1,0:T(8,128)S(1)} %add.191), channel_id=1, source_target_pairs={{0,3},{1,2},{2,1},{3,0},{4,7},{5,6},{6,5},{7,4},{8,11},{9,10},{10,... | collective-permute-start | bytes 12296 | tf_op jit(solution)/shard_map/ppermute | solution.py:94
  436.3 6.9 %collective-permute-start.46 = (f32[8,128]{1,0:T(8,128)S(1)}, f32[8,128]{1,0:T(8,128)S(1)}, u32[]{:S(2)}, u32[]{:S(2)}) collective-permute-start(f32[8,128]{1,0:T(8,128)S(1)} %add.191), channel_id=1, source_target_pairs={{0,2},{1,3},{2,0},{3,1},{4,6},{5,7},{6,4},{7,5},{8,10},{9,11},{10,... | collective-permute-start | bytes 12296 | tf_op jit(solution)/shard_map/ppermute | solution.py:94
  436.3 6.9 %collective-permute-start.45 = (f32[8,128]{1,0:T(8,128)S(1)}, f32[8,128]{1,0:T(8,128)S(1)}, u32[]{:S(2)}, u32[]{:S(2)}) collective-permute-start(f32[8,128]{1,0:T(8,128)S(1)} %add.191), channel_id=1, source_target_pairs={{0,1},{1,0},{2,3},{3,2},{4,5},{5,4},{6,7},{7,6},{8,9},{9,8},{10,11... | collective-permute-start | bytes 12296 | tf_op jit(solution)/shard_map/ppermute | solution.py:94
  (24 other events, 261.1 us)

commit v5 on v3

--- a/solution.py
+++ b/solution.py
@@ -754,7 +754,7 @@
 
 def encode_rows(arrived, w_in, w_node, biases, source):
     posts = arrived.shape[0]
-    tile = 512
+    tile = 1024
 
     def body(
         arrived_ref, in_ref, node_ref, bias_ref, source_ref,
@@ -915,7 +915,10 @@
     w_in, w_node, w_dec, w_out, *w_round, biases = spread_rows(
         held, total_size, peers, place
     )
-    arrived, biases = lax.optimization_barrier((arrived, biases))
+    index = 2 * ((neighbours - band * blocks + H) % (blocks * bands)).T
+    index = index.reshape(K, 2, blocks // 2).swapaxes(0, 1).reshape(-1)
+    index = lax.ppermute(index, "space", list(enumerate(walk)))
+    arrived, biases, index = lax.optimization_barrier((arrived, biases, index))
     counts = arrived.reshape(bands, capacity, HALF)[:, 0, CH + 3 : CH + 6].astype(jnp.float32)
     counts = jnp.sum(counts, 0, keepdims=True)
     w_out = jnp.pad(w_out.reshape(D, CH), ((0, 0), (0, HALF - CH)))
@@ -925,15 +928,10 @@
     mesh, gathered, sent, ids_row, ids = encode_rows(
         arrived, w_in, w_node, biases, w_round[0]
     )
-    sent, partner, neighbours, counted, counts = lax.optimization_barrier(
-        (sent, partner, neighbours, counted, counts)
-    )
+    sent, partner, counted, counts = lax.optimization_barrier((sent, partner, counted, counts))
     counts = counts + swapped(counts, "dp", 1)
-    index = 2 * ((neighbours - band * blocks + H) % (blocks * bands)).T
-    index = index.reshape(K, 2, blocks // 2).swapaxes(0, 1).reshape(-1)
     moved = [(n, place) for n, place in enumerate(walk) if n != place]
     stays = jnp.asarray([n == place for n, place in enumerate(walk)])[band]
-    index = lax.ppermute(index, "space", list(enumerate(walk)))
 
     def at_home(rows):
         return lax.ppermute(rows, "space", [(j, i) for i, j in moved])
@@ -961,11 +959,11 @@
             sent[1], arrivals[0] = lax.optimization_barrier((sent[1], arrivals[0]))
             arrivals.append(halo(walk, sent[1], sent[1]))
         terms = node_terms(mesh, w_round[layer], b_round[layer])
-        if layer == 0:
+        if layer == 1:
             (before, after), valid_around, counts = lax.optimization_barrier(
                 (arrivals[0], valid_around, counts)
             )
-            arrivals = [(before, after)]
+            arrivals[0] = (before, after)
         for side in ([rows for rows, _ in arrivals], sent, [rows for _, rows in arrivals]):
             for rows in side:
                 pieces.append((rows, start))

time: 449 us -> 449 us (level)
    ppermute x8, waiting for transfers between devices: 4.81 us -> 20.2 us  [halo(): lax.ppermute(initial, 'space', down)]
    ppermute x4, waiting for transfers between devices: 13.3 us -> 7.5 us  [shifted(): return lax.ppermute(shard, axis, pairs)]
    all_to_all x3, waiting for transfers between devices: 21.1 us -> 16.5 us  [exchanged(): lax.all_to_all(rows.reshape(bands, capacity, HALF), 'space', split_axis=0...]
  transfers between devices with their start and end apart: 51 -> 51, of which waited for: 26 -> 27; matrix products, arithmetic and copies ran while one was open for 6% -> 6% of each run, Pallas kernels for 25% -> 25%
where the time goes in v5:
time: 449 us; the launch traced here: 446 us
  Pallas kernels  225 us (50%)
  waiting for transfers between devices  89.9 us (20%)
  starting transfers between devices  85.7 us (19%)
  other arithmetic  23.3 us (5%)
  local copies, waits for them, and re-layouts  10.9 us (2%)
  between operations  7.67 us (2%)
    pallas_call x5, Pallas kernels, round_forward(): pl.pallas_call(body, grid_spec=pltpu.PrefetchScalarGridSpec(num_scalar_pr...  83.3 us
    pallas_call x3, Pallas kernels, edges_backward(): pl.pallas_call(body, grid_spec=pltpu.PrefetchScalarGridSpec(num_scalar_pr...  78.7 us
    ppermute x25, starting transfers between devices, swapped(): lax.ppermute(value, axis, [(i, i ^ bit) for i in range(lax.axis_size(axis...  29.4 us
    ppermute x25, waiting for transfers between devices, swapped(): lax.ppermute(value, axis, [(i, i ^ bit) for i in range(lax.axis_size(axis...  28.3 us
    pallas_call x3, Pallas kernels, weight_grads(): pl.pallas_call(body, grid=(blocks // tile,), in_specs=[rows] * 7 + [whole...  24.4 us
    ppermute x8, starting transfers between devices, halo(): lax.ppermute(initial, 'space', down)  20.7 us
    ppermute x8, waiting for transfers between devices, halo(): lax.ppermute(initial, 'space', down)  20.2 us
    ppermute x8, waiting for transfers between devices, halo(): lax.ppermute(last, 'space', up)  17.4 us
  transfers between devices with their start and end apart: 51, of which 27 were waited for; matrix products, arithmetic and copies ran while one was open for 6% of the time, Pallas kernels for 25%

profile of v5, /device:TPU:0, one launch (start us, length us, event | category | flops | bytes accessed | tf_op | source)
XLA Modules:
  0.0 446.4 jit_solution(7772289800714091582)
XLA Ops:
  2.5 5.1 %collective-permute-start.2 = (bf16[1,144,256]{2,1,0:T(8,128)(2,1)S(1)}, bf16[1,144,256]{2,1,0:T(8,128)(2,1)S(1)}, u32[]{:S(2)}, u32[]{:S(2)}) collective-permute-start(bf16[1,144,256]{2,1,0:T(8,128)(2,1)S(1)} %broadcast_in_dim_reshape.3), channel_id=1, source_target_pairs={{0,12},{1,13},{2,14},{3,15},{4,8},{5,9},{6,10},{7,11},{8,4},{9,5},... | collective-permute-start | bytes 221192 | tf_op jit(solution)/shard_map/ppermute | solution.py:94
  26.1 5.9 %all-to-all-start = ((bf16[16,64,128]{2,1,0:T(8,128)(2,1)}), bf16[16,64,128]{2,1,0:T(8,128)(2,1)S(1)}, u32[]{:S(2)}, u32[]{:S(2)}) async-start(bf16[16,64,128]{2,1,0:T(8,128)(2,1)} %bitcast.4), calls=%async_computation | async-start | bytes 524288 | tf_op jit(solution)/shard_map/all_to_all | solution.py:907
  35.8 4.0 spread_rows.1
  41.2 5.5 %encode_rows.1 = (f32[2048,256]{1,0:T(8,128)}, bf16[2048,256]{1,0:T(8,128)(2,1)}, bf16[4096,128]{1,0:T(8,128)(2,1)}, s32[1,1024]{1,0:T(1,128)}, s32[1024,1]{1,0:T(8,128)}) custom-call(bf16[1024,128]{1,0:T(8,128)(2,1)} %bitcast.132, bf16[128,256]{1,0:T(8,128)(2,1)} %get-tuple-element.147.in_ref, bf16[256,256]{1,0:T(8,128)(2,1)} %get-tuple-element.148.node_ref, ...), custom_call_target="tpu_custom_call" | custom-call | bytes 15000000 | tf_op jit(solution)/shard_map/encode_rows/pallas_call | solution.py:783
  46.7 4.5 %collective-permute-start.11 = (bf16[4096,128]{1,0:T(8,128)(2,1)}, bf16[4096,128]{1,0:T(8,128)(2,1)}, u32[]{:S(2)}, u32[]{:S(2)}) collective-permute-start(bf16[4096,128]{1,0:T(8,128)(2,1)} %get-tuple-element.155.refs_1_), channel_id=1, source_target_pairs={{1,0},{3,1},{2,3},{6,2},{4,6},{5,4},{7,5},{11,7},{9,11},{8,9},{10,... | collective-permute-start | bytes 3145736 | tf_op jit(solution)/shard_map/ppermute | solution.py:77
  52.6 3.9 node_terms.3
  57.1 16.8 %collective-permute-done.11.refs_2_ = bf16[4096,128]{1,0:T(8,128)(2,1)} collective-permute-done((bf16[4096,128]{1,0:T(8,128)(2,1)}, bf16[4096,128]{1,0:T(8,128)(2,1)}, u32[]{:S(2)}, u32[]{:S(2)}) %collective-permute-start.11) | collective-permute-done | bytes 1048608 | tf_op jit(solution)/shard_map/ppermute | solution.py:77
  73.9 4.0 collective-permute-done.10.refs_0_
  77.9 14.3 %round_forward.5 = (f32[2048,256]{1,0:T(8,128)}, f32[2048,256]{1,0:T(8,128)}, bf16[2048,256]{1,0:T(8,128)(2,1)}, bf16[2048,256]{1,0:T(8,128)(2,1)}, bf16[6,4096,...) custom-call(s32[6144]{0:T(1024)} %get-tuple-element.325.index_ref, f32[2048,256]{1,0:T(8,128)} %get-tuple-element.154.mesh_ref, ...), custom_call_target="tpu_custom_call" | custom-call | bytes 42000000 | tf_op jit(solution)/shard_map/round_forward/pallas_call | solution.py:497
  94.3 14.4 %round_forward.6 = (f32[2048,256]{1,0:T(8,128)}, f32[2048,256]{1,0:T(8,128)}, bf16[2048,256]{1,0:T(8,128)(2,1)}, bf16[2048,256]{1,0:T(8,128)(2,1)}, bf16[6,4096,...) custom-call(s32[6144]{0:T(1024)} %get-tuple-element.326.index_ref, ...), custom_call_target="tpu_custom_call", output_to_operand_aliasing={{0}: (9, {}), {1}: (10, {}), {2}: (11, {}), {3}: (12, {}), ... | custom-call | bytes 42000000 | tf_op jit(solution)/shard_map/round_forward/pallas_call | solution.py:497
  110.2 4.5 %collective-permute-start.15 = (bf16[79,360]{1,0:T(8,128)(2,1)S(1)}, bf16[79,360]{1,0:T(8,128)(2,1)S(1)}, u32[]{:S(2)}, u32[]{:S(2)}) collective-permute-start(bf16[79,360]{1,0:T(8,128)(2,1)S(1)} %get-tuple-element.322), channel_id=1, source_target_pairs={{0,1},{1,2},{2,3},{3,4},{4,5},{5,6},{6,7},{7,8},{8,9},{9,10},{10,1... | collective-permute-start | bytes 170648 | tf_op jit(solution)/shard_map/ppermute | solution.py:49
  116.0 5.2 %collective-permute-done.15 = bf16[79,360]{1,0:T(8,128)(2,1)S(1)} collective-permute-done((bf16[79,360]{1,0:T(8,128)(2,1)S(1)}, bf16[79,360]{1,0:T(8,128)(2,1)S(1)}, u32[]{:S(2)}, u32[]{:S(2)}) %collective-permute-start.15) | collective-permute-done | bytes 56912 | tf_op jit(solution)/shard_map/ppermute | solution.py:49
  121.4 3.9 node_terms.4
  125.3 3.9 collective-permute-start.18
  129.2 14.0 %round_forward.7 = (f32[2048,256]{1,0:T(8,128)}, f32[2048,256]{1,0:T(8,128)}, bf16[2048,256]{1,0:T(8,128)(2,1)}, bf16[2048,256]{1,0:T(8,128)(2,1)}, bf16[6,4096,...) custom-call(s32[6144]{0:T(1024)} %get-tuple-element.325.index_ref, f32[2048,256]{1,0:T(8,128)} %get-tuple-element.164.mesh_ref.refs_0_, ...), custom_call_target="tpu_custom_call" | custom-call | bytes 42000000 | tf_op jit(solution)/shard_map/round_forward/pallas_call | solution.py:497
  145.3 14.1 %round_forward.8 = (f32[2048,256]{1,0:T(8,128)}, f32[2048,256]{1,0:T(8,128)}, bf16[2048,256]{1,0:T(8,128)(2,1)}, bf16[2048,256]{1,0:T(8,128)(2,1)}, bf16[6,4096,...) custom-call(s32[6144]{0:T(1024)} %get-tuple-element.326.index_ref, ...), custom_call_target="tpu_custom_call", output_to_operand_aliasing={{0}: (11, {}), {1}: (12, {}), {2}: (13, {}), {3}: (14, {}),... | custom-call | bytes 42000000 | tf_op jit(solution)/shard_map/round_forward/pallas_call | solution.py:497
  162.4 3.9 node_terms.5
  166.3 3.4 collective-permute-done.22.refs_5_
  169.7 4.0 collective-permute-done.21.refs_1_
  173.7 26.4 %round_forward.9 = (f32[2048,256]{1,0:T(8,128)}, f32[2048,256]{1,0:T(8,128)}, bf16[2048,256]{1,0:T(8,128)(2,1)}, bf16[2048,256]{1,0:T(8,128)(2,1)}, bf16[6,4096,...) custom-call(s32[12288]{0:T(1024)} %copy-done.7, ...), custom_call_target="tpu_custom_call" | custom-call | bytes 72000000 | tf_op jit(solution)/shard_map/round_forward/pallas_call | solution.py:497
  200.1 3.5 all-to-all-start.1
  203.8 8.4 %all-to-all-done.1 = bf16[16,64,128]{2,1,0:T(8,128)(2,1)S(1)} async-done(((bf16[16,64,128]{2,1,0:T(8,128)(2,1)}), bf16[16,64,128]{2,1,0:T(8,128)(2,1)S(1)}, u32[]{:S(2)}, u32[]{:S(2)}) %all-to-all-start.1) | async-done | bytes 262176 | tf_op jit(solution)/shard_map/all_to_all | solution.py:907
  213.6 3.3 collective-permute-start.23
  220.8 2.3 collective-permute-done.24
  226.1 5.8 %all-to-all-start.2 = ((bf16[16,64,128]{2,1,0:T(8,128)(2,1)}), bf16[16,64,128]{2,1,0:T(8,128)(2,1)S(1)}, u32[]{:S(2)}, u32[]{:S(2)}) async-start(bf16[16,64,128]{2,1,0:T(8,128)(2,1)} %bitcast.20), calls=%async_computation.2 | async-start | bytes 524288 | tf_op jit(solution)/shard_map/all_to_all | solution.py:907
  233.0 7.4 %all-to-all-done.2 = bf16[16,64,128]{2,1,0:T(8,128)(2,1)S(1)} async-done(((bf16[16,64,128]{2,1,0:T(8,128)(2,1)}), bf16[16,64,128]{2,1,0:T(8,128)(2,1)S(1)}, u32[]{:S(2)}, u32[]{:S(2)}) %all-to-all-start.2) | async-done | bytes 262176 | tf_op jit(solution)/shard_map/all_to_all | solution.py:907
  242.1 26.8 %edges_backward.3 = (f32[2048,256]{1,0:T(8,128)}, bf16[2048,256]{1,0:T(8,128)(2,1)}, bf16[1024,256]{1,0:T(8,128)(2,1)}, bf16[2048,256]{1,0:T(8,128)(2,1)}, bf16[...) custom-call(s32[12288]{0:T(1024)} %copy-done.7, ...), custom_call_target="tpu_custom_call" | custom-call | bytes 75000000 | tf_op jit(solution)/shard_map/edges_backward/pallas_call | solution.py:642
  270.4 2.4 collective-permute-start.27
  273.4 2.7 decode_grads.1
  276.0 7.4 %weight_grads.3 = (f32[2048,256]{1,0:T(8,128)}, f32[1024,256]{1,0:T(8,128)}, f32[2,256]{1,0:T(2,128)}) custom-call(f32[2048,256]{1,0:T(8,128)} %get-tuple-element.182.mesh_ref.refs_0_, bf16[2048,256]{1,0:T(8,128)(2,1)} %get-tuple-element.206.dest_ref, bf16[2048,256]{1,0:T(8,128)(2,1)} %get-tuple-element.207.agg_ref, ...), custom_call_target="tpu_custom_call" | custom-call | bytes 30000000 | tf_op jit(solution)/shard_map/weight_grads/pallas_call | solution.py:727
  283.4 4.0 convert_select_fusion
  287.5 25.8 %edges_backward.4 = (f32[2048,256]{1,0:T(8,128)}, bf16[2048,256]{1,0:T(8,128)(2,1)}, bf16[2048,256]{1,0:T(8,128)(2,1)}, bf16[2048,256]{1,0:T(8,128)(2,1)}, bf16[...) custom-call(s32[12288]{0:T(1024)} %copy-done.7, ...), custom_call_target="tpu_custom_call" | custom-call | bytes 84000000 | tf_op jit(solution)/shard_map/edges_backward/pallas_call | solution.py:642
  313.9 3.3 collective-permute-start.29
  317.2 8.6 %weight_grads.4 = (f32[2048,256]{1,0:T(8,128)}, f32[1024,256]{1,0:T(8,128)}, f32[2,256]{1,0:T(2,128)}, f32[256,256]{1,0:T(8,128)}) custom-call(f32[2048,256]{1,0:T(8,128)} %get-tuple-element.164.mesh_ref.refs_0_, bf16[2048,256]{1,0:T(8,128)(2,1)} %get-tuple-element.227.dest_ref, bf16[2048,256]{1,0:T(8,128)(2,1)} %get-tuple-element.228.agg_ref, ...), custom_call_target="tpu_custom_call" | custom-call | bytes 30000000 | tf_op jit(solution)/shard_map/weight_grads/pallas_call | solution.py:727
  325.8 5.5 %collective-permute-done.28.refs_6_ = bf16[4096,128]{1,0:T(8,128)(2,1)} collective-permute-done((bf16[4096,128]{1,0:T(8,128)(2,1)}, bf16[4096,128]{1,0:T(8,128)(2,1)}, u32[]{:S(2)}, u32[]{:S(2)}) %collective-permute-start.28) | collective-permute-done | bytes 1048608 | tf_op jit(solution)/shard_map/ppermute | solution.py:77
  331.3 26.0 %edges_backward.5 = (f32[2048,256]{1,0:T(8,128)}, bf16[2048,256]{1,0:T(8,128)(2,1)}, bf16[2048,256]{1,0:T(8,128)(2,1)}, bf16[2048,256]{1,0:T(8,128)(2,1)}, bf16[...) custom-call(s32[12288]{0:T(1024)} %copy-done.7, ...), custom_call_target="tpu_custom_call" | custom-call | bytes 84000000 | tf_op jit(solution)/shard_map/edges_backward/pallas_call | solution.py:642
  357.3 3.8 collective-permute-start.31
  361.9 8.4 %weight_grads.5 = (f32[2048,256]{1,0:T(8,128)}, f32[1024,256]{1,0:T(8,128)}, f32[2,256]{1,0:T(2,128)}, f32[256,256]{1,0:T(8,128)}) custom-call(f32[2048,256]{1,0:T(8,128)} %get-tuple-element.154.mesh_ref, bf16[2048,256]{1,0:T(8,128)(2,1)} %get-tuple-element.238.dest_ref, bf16[2048,256]{1,0:T(8,128)(2,1)} %get-tuple-element.239.agg_ref, ...), custom_call_target="tpu_custom_call" | custom-call | bytes 30000000 | tf_op jit(solution)/shard_map/weight_grads/pallas_call | solution.py:727
  370.4 3.9 collective-permute-done.30.first_ref
  374.3 10.1 %encode_backward.1 = (f32[2048,256]{1,0:T(8,128)}, bf16[2048,256]{1,0:T(8,128)(2,1)}, f32[128,256]{1,0:T(8,128)}, f32[256,256]{1,0:T(8,128)}, f32[2,256]{1,0:T(2,128)}, /*index=5*/f32[256,256]{1,0:T(8,128)}) custom-call(f32[2048,256]{1,0:T(8,128)} %get-tuple-element.245.part_ref, f32[4096,128]{1,0:T(8,128)} %get-tuple-element.246.own_ref, ...), custom_call_target="tpu_custom_call" | custom-call | bytes 30000000 | tf_op jit(solution)/shard_map/encode_backward/pallas_call | solution.py:848
  384.3 5.1 %collect_rows.1 = (f32[16,144,256]{2,1,0:T(8,128)}, bf16[16,144,256]{2,1,0:T(8,128)(2,1)}) custom-call(s32[1]{0:T(128)} %bitcast.6.place_ref, f32[128,256]{1,0:T(8,128)} %get-tuple-element.250.refs_0_, f32[256,256]{1,0:T(8,128)} %get-tuple-element.251.refs_1_, f32[256,256]{1,0:T(8,128)} %get-tuple-element.252.refs_2_, f32[78,256]{1,0:T(8,128)} %reshape.160.refs_3_, ...), custom_call_target="tpu_custom_call" | custom-call | bytes 15000000 | tf_op jit(solution)/shard_map/collect_rows/pallas_call | solution.py:233
  389.4 3.1 collective-permute-done.32
  394.8 8.9 %collective-permute-done.33 = bf16[4,2,72,256]{3,2,0,1:T(8,128)(2,1)S(1)} collective-permute-done((bf16[4,2,72,256]{3,2,0,1:T(8,128)(2,1)S(1)}, bf16[4,2,72,256]{3,2,0,1:T(8,128)(2,1)S(1)}, u32[]{:S(2)}, u32[]{:S(2)}) %collective-permute-start.33) | collective-permute-done | bytes 294944 | tf_op jit(solution)/shard_map/ppermute | solution.py:94
  405.7 3.3 collective-permute-done.34
  411.4 5.7 %collective-permute-start.39 = (bf16[1,144,256]{2,1,0:T(8,128)(2,1)S(1)}, bf16[1,144,256]{2,1,0:T(8,128)(2,1)S(1)}, u32[]{:S(2)}, u32[]{:S(2)}) collective-permute-start(bf16[1,144,256]{2,1,0:T(8,128)(2,1)S(1)} %get-tuple-element.317), channel_id=1, source_target_pairs={{0,12},{1,13},{2,14},{3,15},{4,8},{5,9},{6,10},{7,11},{8,4},{9,5},... | collective-permute-start | bytes 221192 | tf_op jit(solution)/shard_map/ppermute | solution.py:94
  425.2 2.3 collective-permute-start.42
  432.2 4.7 %collective-permute-start.47 = (f32[8,128]{1,0:T(8,128)S(1)}, f32[8,128]{1,0:T(8,128)S(1)}, u32[]{:S(2)}, u32[]{:S(2)}) collective-permute-start(f32[8,128]{1,0:T(8,128)S(1)} %add.191), channel_id=1, source_target_pairs={{0,3},{1,2},{2,1},{3,0},{4,7},{5,6},{6,5},{7,4},{8,11},{9,10},{10,... | collective-permute-start | bytes 12296 | tf_op jit(solution)/shard_map/ppermute | solution.py:94
  438.4 3.4 select_bitcast_fusion
  (201 shorter events, 70.9 us)
Async XLA Ops:
  2.5 14.5 %collective-permute-start.2 = (bf16[1,144,256]{2,1,0:T(8,128)(2,1)S(1)}, bf16[1,144,256]{2,1,0:T(8,128)(2,1)S(1)}, u32[]{:S(2)}, u32[]{:S(2)}) collective-permute-start(bf16[1,144,256]{2,1,0:T(8,128)(2,1)S(1)} %broadcast_in_dim_reshape.3), channel_id=1, source_target_pairs={{0,12},{1,13},{2,14},{3,15},{4,8},{5,9},{6,10},{7,11},{8,4},{9,5},... | collective-permute-start | bytes 221192 | tf_op jit(solution)/shard_map/ppermute | solution.py:94
  7.6 9.4 %collective-permute-start.1 = (bf16[1,144,256]{2,1,0:T(8,128)(2,1)S(1)}, bf16[1,144,256]{2,1,0:T(8,128)(2,1)S(1)}, u32[]{:S(2)}, u32[]{:S(2)}) collective-permute-start(bf16[1,144,256]{2,1,0:T(8,128)(2,1)S(1)} %broadcast_in_dim_reshape.3), channel_id=1, source_target_pairs={{0,8},{1,9},{2,10},{3,11},{4,12},{5,13},{6,14},{7,15},{8,0},{9,1},... | collective-permute-start | bytes 221192 | tf_op jit(solution)/shard_map/ppermute | solution.py:94
  7.6 9.4 %collective-permute-start = (bf16[1,144,256]{2,1,0:T(8,128)(2,1)S(1)}, bf16[1,144,256]{2,1,0:T(8,128)(2,1)S(1)}, u32[]{:S(2)}, u32[]{:S(2)}) collective-permute-start(bf16[1,144,256]{2,1,0:T(8,128)(2,1)S(1)} %broadcast_in_dim_reshape.3), channel_id=1, source_target_pairs={{0,4},{1,5},{2,6},{3,7},{4,0},{5,1},{6,2},{7,3},{8,12},{9,13},{10,... | collective-permute-start | bytes 221192 | tf_op jit(solution)/shard_map/ppermute | solution.py:94
  17.0 5.2 %collective-permute-start.4 = (bf16[4,72,256]{2,1,0:T(8,128)(2,1)S(1)}, bf16[4,72,256]{2,1,0:T(8,128)(2,1)S(1)}, u32[]{:S(2)}, u32[]{:S(2)}) collective-permute-start(bf16[4,72,256]{2,1,0:T(8,128)(2,1)S(1)} %get-tuple-element.319), channel_id=1, source_target_pairs={{0,1},{1,0},{2,3},{3,2},{4,5},{5,4},{6,7},{7,6},{8,9},{9,8},{10,11... | collective-permute-start | bytes 442376 | tf_op jit(solution)/shard_map/ppermute | solution.py:94
  18.7 5.1 %collective-permute-start.3 = (bf16[4,72,256]{2,1,0:T(8,128)(2,1)S(1)}, bf16[4,72,256]{2,1,0:T(8,128)(2,1)S(1)}, u32[]{:S(2)}, u32[]{:S(2)}) collective-permute-start(bf16[4,72,256]{2,1,0:T(8,128)(2,1)S(1)} %get-tuple-element.320), channel_id=1, source_target_pairs={{0,2},{1,3},{2,0},{3,1},{4,6},{5,7},{6,4},{7,5},{8,10},{9,11},{10,... | collective-permute-start | bytes 442376 | tf_op jit(solution)/shard_map/ppermute | solution.py:94
  23.9 8.1 %collective-permute-start.6 = (bf16[8,72,256]{2,1,0:T(8,128)(2,1)S(1)}, bf16[8,72,256]{2,1,0:T(8,128)(2,1)S(1)}, u32[]{:S(2)}, u32[]{:S(2)}) collective-permute-start(bf16[8,72,256]{2,1,0:T(8,128)(2,1)S(1)} %pad_maximum_fusion.3), channel_id=1, source_target_pairs={{0,2},{1,3},{2,0},{3,1},{4,6},{5,7},{6,4},{7,5},{8,10},{9,11},{10,... | collective-permute-start | bytes 884744 | tf_op jit(solution)/shard_map/ppermute | solution.py:94
  25.5 7.1 %collective-permute-start.5 = (bf16[8,72,256]{2,1,0:T(8,128)(2,1)S(1)}, bf16[8,72,256]{2,1,0:T(8,128)(2,1)S(1)}, u32[]{:S(2)}, u32[]{:S(2)}) collective-permute-start(bf16[8,72,256]{2,1,0:T(8,128)(2,1)S(1)} %pad_maximum_fusion.2), channel_id=1, source_target_pairs={{0,1},{1,0},{2,3},{3,2},{4,5},{5,4},{6,7},{7,6},{8,9},{9,8},{10,11... | collective-permute-start | bytes 884744 | tf_op jit(solution)/shard_map/ppermute | solution.py:94
  26.1 14.4 %all-to-all-start = ((bf16[16,64,128]{2,1,0:T(8,128)(2,1)}), bf16[16,64,128]{2,1,0:T(8,128)(2,1)S(1)}, u32[]{:S(2)}, u32[]{:S(2)}) async-start(bf16[16,64,128]{2,1,0:T(8,128)(2,1)} %bitcast.4), calls=%async_computation | async-start | bytes 524288 | tf_op jit(solution)/shard_map/all_to_all | solution.py:907
  32.6 2.4 collective-permute-start.7
  32.8 7.0 %collective-permute-start.9 = (s32[12288]{0:T(1024)S(1)}, s32[12288]{0:T(1024)S(1)}, u32[]{:S(2)}, u32[]{:S(2)}) collective-permute-start(s32[12288]{0:T(1024)S(1)} %reshape.150), channel_id=1, source_target_pairs={{0,0},{1,1},{2,3},{3,2},{4,6},{5,4},{6,5},{7,7},{8,11},{9,9},{10,8... | collective-permute-start | bytes 147464 | tf_op jit(solution)/shard_map/ppermute | solution.py:920
  46.7 27.2 %collective-permute-start.11 = (bf16[4096,128]{1,0:T(8,128)(2,1)}, bf16[4096,128]{1,0:T(8,128)(2,1)}, u32[]{:S(2)}, u32[]{:S(2)}) collective-permute-start(bf16[4096,128]{1,0:T(8,128)(2,1)} %get-tuple-element.155.refs_1_), channel_id=1, source_target_pairs={{1,0},{3,1},{2,3},{6,2},{4,6},{5,4},{7,5},{11,7},{9,11},{8,9},{10,... | collective-permute-start | bytes 3145736 | tf_op jit(solution)/shard_map/ppermute | solution.py:77
  51.2 26.6 %collective-permute-start.10 = (bf16[4096,128]{1,0:T(8,128)(2,1)}, bf16[4096,128]{1,0:T(8,128)(2,1)}, u32[]{:S(2)}, u32[]{:S(2)}) collective-permute-start(bf16[4096,128]{1,0:T(8,128)(2,1)} %get-tuple-element.155.refs_1_), channel_id=1, source_target_pairs={{0,1},{1,3},{3,2},{2,6},{6,4},{4,5},{5,7},{7,11},{11,9},{9,8},{8,1... | collective-permute-start | bytes 3145736 | tf_op jit(solution)/shard_map/ppermute | solution.py:77
  92.2 16.5 %collective-permute-start.13 = (bf16[2048,128]{1,0:T(8,128)(2,1)}, bf16[2048,128]{1,0:T(8,128)(2,1)S(1)}, u32[]{:S(2)}, u32[]{:S(2)}) collective-permute-start(bf16[2048,128]{1,0:T(8,128)(2,1)} %get-tuple-element.166.refs_2_.refs_1_), channel_id=1, source_target_pairs={{1,0},{3,1},{2,3},{6,2},{4,6},{5,4},{7,5},{11,7},{9,11},{8,9},{10,... | collective-permute-start | bytes 1572872 | tf_op jit(solution)/shard_map/ppermute | solution.py:77
  92.5 16.2 %collective-permute-start.12 = (bf16[2048,128]{1,0:T(8,128)(2,1)}, bf16[2048,128]{1,0:T(8,128)(2,1)}, u32[]{:S(2)}, u32[]{:S(2)}) collective-permute-start(bf16[2048,128]{1,0:T(8,128)(2,1)} %get-tuple-element.166.refs_2_.refs_1_), channel_id=1, source_target_pairs={{0,1},{1,3},{3,2},{2,6},{6,4},{4,5},{5,7},{7,11},{11,9},{9,8},{8,1... | collective-permute-start | bytes 1572872 | tf_op jit(solution)/shard_map/ppermute | solution.py:77
  108.7 20.5 %collective-permute-start.14 = (bf16[2048,128]{1,0:T(8,128)(2,1)}, bf16[2048,128]{1,0:T(8,128)(2,1)}, u32[]{:S(2)}, u32[]{:S(2)}) collective-permute-start(bf16[2048,128]{1,0:T(8,128)(2,1)} %get-tuple-element.167.refs_3_.refs_2_), channel_id=1, source_target_pairs={{0,1},{1,3},{3,2},{2,6},{6,4},{4,5},{5,7},{7,11},{11,9},{9,8},{8,1... | collective-permute-start | bytes 1572872 | tf_op jit(solution)/shard_map/ppermute | solution.py:77
  108.9 7.1 %collective-permute-start.16 = (bf16[79,360]{1,0:T(8,128)(2,1)S(1)}, bf16[79,360]{1,0:T(8,128)(2,1)S(1)}, u32[]{:S(2)}, u32[]{:S(2)}) collective-permute-start(bf16[79,360]{1,0:T(8,128)(2,1)S(1)} %get-tuple-element.321), channel_id=1, source_target_pairs={{1,0},{2,1},{3,2},{4,3},{5,4},{6,5},{7,6},{8,7},{9,8},{10,9},{11,1... | collective-permute-start | bytes 170648 | tf_op jit(solution)/shard_map/ppermute | solution.py:49
  110.2 11.0 %collective-permute-start.15 = (bf16[79,360]{1,0:T(8,128)(2,1)S(1)}, bf16[79,360]{1,0:T(8,128)(2,1)S(1)}, u32[]{:S(2)}, u32[]{:S(2)}) collective-permute-start(bf16[79,360]{1,0:T(8,128)(2,1)S(1)} %get-tuple-element.322), channel_id=1, source_target_pairs={{0,1},{1,2},{2,3},{3,4},{4,5},{5,6},{6,7},{7,8},{8,9},{9,10},{10,1... | collective-permute-start | bytes 170648 | tf_op jit(solution)/shard_map/ppermute | solution.py:49
  125.3 20.0 %collective-permute-start.18 = (bf16[2048,128]{1,0:T(8,128)(2,1)}, bf16[2048,128]{1,0:T(8,128)(2,1)}, u32[]{:S(2)}, u32[]{:S(2)}) collective-permute-start(bf16[2048,128]{1,0:T(8,128)(2,1)} %get-tuple-element.167.refs_3_.refs_2_), channel_id=1, source_target_pairs={{1,0},{3,1},{2,3},{6,2},{4,6},{5,4},{7,5},{11,7},{9,11},{8,9},{10,... | collective-permute-start | bytes 1572872 | tf_op jit(solution)/shard_map/ppermute | solution.py:77
  143.2 16.2 %collective-permute-start.20 = (bf16[2048,128]{1,0:T(8,128)(2,1)}, bf16[2048,128]{1,0:T(8,128)(2,1)S(1)}, u32[]{:S(2)}, u32[]{:S(2)}) collective-permute-start(bf16[2048,128]{1,0:T(8,128)(2,1)} %get-tuple-element.184.refs_2_), channel_id=1, source_target_pairs={{1,0},{3,1},{2,3},{6,2},{4,6},{5,4},{7,5},{11,7},{9,11},{8,9},{10,... | collective-permute-start | bytes 1572872 | tf_op jit(solution)/shard_map/ppermute | solution.py:77
  143.5 16.0 %collective-permute-start.19 = (bf16[2048,128]{1,0:T(8,128)(2,1)}, bf16[2048,128]{1,0:T(8,128)(2,1)}, u32[]{:S(2)}, u32[]{:S(2)}) collective-permute-start(bf16[2048,128]{1,0:T(8,128)(2,1)} %get-tuple-element.184.refs_2_), channel_id=1, source_target_pairs={{0,1},{1,3},{3,2},{2,6},{6,4},{4,5},{5,7},{7,11},{11,9},{9,8},{8,1... | collective-permute-start | bytes 1572872 | tf_op jit(solution)/shard_map/ppermute | solution.py:77
  159.4 10.3 %collective-permute-start.22 = (bf16[2048,128]{1,0:T(8,128)(2,1)}, bf16[2048,128]{1,0:T(8,128)(2,1)}, u32[]{:S(2)}, u32[]{:S(2)}) collective-permute-start(bf16[2048,128]{1,0:T(8,128)(2,1)} %get-tuple-element.186.refs_3_), channel_id=1, source_target_pairs={{1,0},{3,1},{2,3},{6,2},{4,6},{5,4},{7,5},{11,7},{9,11},{8,9},{10,... | collective-permute-start | bytes 1572872 | tf_op jit(solution)/shard_map/ppermute | solution.py:77
  161.5 12.2 %collective-permute-start.21 = (bf16[2048,128]{1,0:T(8,128)(2,1)}, bf16[2048,128]{1,0:T(8,128)(2,1)}, u32[]{:S(2)}, u32[]{:S(2)}) collective-permute-start(bf16[2048,128]{1,0:T(8,128)(2,1)} %get-tuple-element.186.refs_3_), channel_id=1, source_target_pairs={{0,1},{1,3},{3,2},{2,6},{6,4},{4,5},{5,7},{7,11},{11,9},{9,8},{8,1... | collective-permute-start | bytes 1572872 | tf_op jit(solution)/shard_map/ppermute | solution.py:77
  200.1 12.0 %all-to-all-start.1 = ((bf16[16,64,128]{2,1,0:T(8,128)(2,1)}), bf16[16,64,128]{2,1,0:T(8,128)(2,1)S(1)}, u32[]{:S(2)}, u32[]{:S(2)}) async-start(bf16[16,64,128]{2,1,0:T(8,128)(2,1)} %bitcast.141), calls=%async_computation.1 | async-start | bytes 524288 | tf_op jit(solution)/shard_map/all_to_all | solution.py:907
  213.6 9.5 %collective-permute-start.23 = (bf16[78,360]{1,0:T(8,128)(2,1)S(1)}, bf16[78,360]{1,0:T(8,128)(2,1)S(1)}, u32[]{:S(2)}, u32[]{:S(2)}) collective-permute-start(bf16[78,360]{1,0:T(8,128)(2,1)S(1)} %get-tuple-element.323), channel_id=1, source_target_pairs={{0,1},{1,2},{2,3},{3,4},{4,5},{5,6},{6,7},{7,8},{8,9},{9,10},{10,1... | collective-permute-start | bytes 168488 | tf_op jit(solution)/shard_map/ppermute | solution.py:49
  217.0 6.1 %collective-permute-start.24 = (bf16[78,360]{1,0:T(8,128)(2,1)S(1)}, bf16[78,360]{1,0:T(8,128)(2,1)S(1)}, u32[]{:S(2)}, u32[]{:S(2)}) collective-permute-start(bf16[78,360]{1,0:T(8,128)(2,1)S(1)} %get-tuple-element.324), channel_id=1, source_target_pairs={{1,0},{2,1},{3,2},{4,3},{5,4},{6,5},{7,6},{8,7},{9,8},{10,9},{11,1... | collective-permute-start | bytes 168488 | tf_op jit(solution)/shard_map/ppermute | solution.py:49
  226.1 14.4 %all-to-all-start.2 = ((bf16[16,64,128]{2,1,0:T(8,128)(2,1)}), bf16[16,64,128]{2,1,0:T(8,128)(2,1)S(1)}, u32[]{:S(2)}, u32[]{:S(2)}) async-start(bf16[16,64,128]{2,1,0:T(8,128)(2,1)} %bitcast.20), calls=%async_computation.2 | async-start | bytes 524288 | tf_op jit(solution)/shard_map/all_to_all | solution.py:907
  240.4 28.5 %collective-permute-start.25 = (bf16[2048,256]{1,0:T(8,128)(2,1)}, bf16[2048,256]{1,0:T(8,128)(2,1)}, u32[]{:S(2)}, u32[]{:S(2)}) collective-permute-start(bf16[2048,256]{1,0:T(8,128)(2,1)} %convert_element_type.150), channel_id=1, source_target_pairs={{3,2},{2,3},{6,4},{4,5},{5,6},{11,8},{8,10},{10,11},{14,12},{15,13... | collective-permute-start | bytes 3145736 | tf_op jit(solution)/shard_map/ppermute | solution.py:937
  268.9 18.6 %collective-permute-start.26 = (bf16[4096,128]{1,0:T(8,128)(2,1)}, bf16[4096,128]{1,0:T(8,128)(2,1)}, u32[]{:S(2)}, u32[]{:S(2)}) collective-permute-start(bf16[4096,128]{1,0:T(8,128)(2,1)} %get-tuple-element.217), channel_id=1, source_target_pairs={{0,1},{1,3},{3,2},{2,6},{6,4},{4,5},{5,7},{7,11},{11,9},{9,8},{8,1... | collective-permute-start | bytes 3145736 | tf_op jit(solution)/shard_map/ppermute | solution.py:77
  270.4 17.1 %collective-permute-start.27 = (bf16[4096,128]{1,0:T(8,128)(2,1)}, bf16[4096,128]{1,0:T(8,128)(2,1)}, u32[]{:S(2)}, u32[]{:S(2)}) collective-permute-start(bf16[4096,128]{1,0:T(8,128)(2,1)} %get-tuple-element.226), channel_id=1, source_target_pairs={{1,0},{3,1},{2,3},{6,2},{4,6},{5,4},{7,5},{11,7},{9,11},{8,9},{10,... | collective-permute-start | bytes 3145736 | tf_op jit(solution)/shard_map/ppermute | solution.py:77
  313.3 17.9 %collective-permute-start.28 = (bf16[4096,128]{1,0:T(8,128)(2,1)}, bf16[4096,128]{1,0:T(8,128)(2,1)}, u32[]{:S(2)}, u32[]{:S(2)}) collective-permute-start(bf16[4096,128]{1,0:T(8,128)(2,1)} %get-tuple-element.236), channel_id=1, source_target_pairs={{0,1},{1,3},{3,2},{2,6},{6,4},{4,5},{5,7},{7,11},{11,9},{9,8},{8,1... | collective-permute-start | bytes 3145736 | tf_op jit(solution)/shard_map/ppermute | solution.py:77
  313.9 17.4 %collective-permute-start.29 = (bf16[4096,128]{1,0:T(8,128)(2,1)}, bf16[4096,128]{1,0:T(8,128)(2,1)}, u32[]{:S(2)}, u32[]{:S(2)}) collective-permute-start(bf16[4096,128]{1,0:T(8,128)(2,1)} %get-tuple-element.237), channel_id=1, source_target_pairs={{1,0},{3,1},{2,3},{6,2},{4,6},{5,4},{7,5},{11,7},{9,11},{8,9},{10,... | collective-permute-start | bytes 3145736 | tf_op jit(solution)/shard_map/ppermute | solution.py:77
  357.3 17.0 %collective-permute-start.30 = (bf16[4096,128]{1,0:T(8,128)(2,1)}, bf16[4096,128]{1,0:T(8,128)(2,1)}, u32[]{:S(2)}, u32[]{:S(2)}) collective-permute-start(bf16[4096,128]{1,0:T(8,128)(2,1)} %get-tuple-element.247), channel_id=1, source_target_pairs={{0,1},{1,3},{3,2},{2,6},{6,4},{4,5},{5,7},{7,11},{11,9},{9,8},{8,1... | collective-permute-start | bytes 3145736 | tf_op jit(solution)/shard_map/ppermute | solution.py:77
  357.3 17.0 %collective-permute-start.31 = (bf16[4096,128]{1,0:T(8,128)(2,1)}, bf16[4096,128]{1,0:T(8,128)(2,1)}, u32[]{:S(2)}, u32[]{:S(2)}) collective-permute-start(bf16[4096,128]{1,0:T(8,128)(2,1)} %get-tuple-element.248), channel_id=1, source_target_pairs={{1,0},{3,1},{2,3},{6,2},{4,6},{5,4},{7,5},{11,7},{9,11},{8,9},{10,... | collective-permute-start | bytes 3145736 | tf_op jit(solution)/shard_map/ppermute | solution.py:77
  389.4 3.1 collective-permute-start.32
  394.6 9.1 %collective-permute-start.33 = (bf16[4,2,72,256]{3,2,0,1:T(8,128)(2,1)S(1)}, bf16[4,2,72,256]{3,2,0,1:T(8,128)(2,1)S(1)}, u32[]{:S(2)}, u32[]{:S(2)}) collective-permute-start(bf16[4,2,72,256]{3,2,0,1:T(8,128)(2,1)S(1)} %fusion.14), channel_id=1, source_target_pairs={{0,1},{1,0},{2,3},{3,2},{4,5},{5,4},{6,7},{7,6},{8,9},{9,8},{10,11... | collective-permute-start | bytes 884744 | tf_op jit(solution)/shard_map/ppermute | solution.py:94
  394.7 9.2 %collective-permute-start.35 = (bf16[4,2,72,256]{3,2,1,0:T(8,128)(2,1)S(1)}, bf16[4,2,72,256]{3,2,1,0:T(8,128)(2,1)S(1)}, u32[]{:S(2)}, u32[]{:S(2)}) collective-permute-start(bf16[4,2,72,256]{3,2,1,0:T(8,128)(2,1)S(1)} %fusion.13), channel_id=1, source_target_pairs={{0,2},{1,3},{2,0},{3,1},{4,6},{5,7},{6,4},{7,5},{8,10},{9,11},{10,... | collective-permute-start | bytes 884744 | tf_op jit(solution)/shard_map/ppermute | solution.py:94
  403.8 5.2 %collective-permute-start.34 = (bf16[4,72,256]{2,1,0:T(8,128)(2,1)S(1)}, bf16[4,72,256]{2,1,0:T(8,128)(2,1)S(1)}, u32[]{:S(2)}, u32[]{:S(2)}) collective-permute-start(bf16[4,72,256]{2,1,0:T(8,128)(2,1)S(1)} %fusion.38), channel_id=1, source_target_pairs={{0,2},{1,3},{2,0},{3,1},{4,6},{5,7},{6,4},{7,5},{8,10},{9,11},{10,... | collective-permute-start | bytes 442376 | tf_op jit(solution)/shard_map/ppermute | solution.py:94
  404.0 5.2 %collective-permute-start.36 = (bf16[4,72,256]{2,1,0:T(8,128)(2,1)S(1)}, bf16[4,72,256]{2,1,0:T(8,128)(2,1)S(1)}, u32[]{:S(2)}, u32[]{:S(2)}) collective-permute-start(bf16[4,72,256]{2,1,0:T(8,128)(2,1)S(1)} %fusion.39), channel_id=1, source_target_pairs={{0,1},{1,0},{2,3},{3,2},{4,5},{5,4},{6,7},{7,6},{8,9},{9,8},{10,11... | collective-permute-start | bytes 442376 | tf_op jit(solution)/shard_map/ppermute | solution.py:94
  409.3 22.9 %collective-permute-start.44 = (bf16[2048,256]{1,0:T(8,128)(2,1)}, bf16[2048,256]{1,0:T(8,128)(2,1)}, u32[]{:S(2)}, u32[]{:S(2)}) collective-permute-start(bf16[2048,256]{1,0:T(8,128)(2,1)} %get-tuple-element.269), channel_id=1, source_target_pairs={{3,2},{2,3},{6,4},{4,5},{5,6},{11,8},{8,10},{10,11},{14,12},{15,13... | collective-permute-start | bytes 3145736 | tf_op jit(solution)/shard_map/ppermute | solution.py:937
  411.2 7.6 %collective-permute-start.37 = (bf16[1,144,256]{2,1,0:T(8,128)(2,1)S(1)}, bf16[1,144,256]{2,1,0:T(8,128)(2,1)S(1)}, u32[]{:S(2)}, u32[]{:S(2)}) collective-permute-start(bf16[1,144,256]{2,1,0:T(8,128)(2,1)S(1)} %get-tuple-element.316), channel_id=1, source_target_pairs={{0,4},{1,5},{2,6},{3,7},{4,0},{5,1},{6,2},{7,3},{8,12},{9,13},{10,... | collective-permute-start | bytes 221192 | tf_op jit(solution)/shard_map/ppermute | solution.py:94
  411.4 9.6 %collective-permute-start.39 = (bf16[1,144,256]{2,1,0:T(8,128)(2,1)S(1)}, bf16[1,144,256]{2,1,0:T(8,128)(2,1)S(1)}, u32[]{:S(2)}, u32[]{:S(2)}) collective-permute-start(bf16[1,144,256]{2,1,0:T(8,128)(2,1)S(1)} %get-tuple-element.317), channel_id=1, source_target_pairs={{0,12},{1,13},{2,14},{3,15},{4,8},{5,9},{6,10},{7,11},{8,4},{9,5},... | collective-permute-start | bytes 221192 | tf_op jit(solution)/shard_map/ppermute | solution.py:94
  417.1 6.1 %collective-permute-start.38 = (bf16[1,144,256]{2,1,0:T(8,128)(2,1)S(1)}, bf16[1,144,256]{2,1,0:T(8,128)(2,1)S(1)}, u32[]{:S(2)}, u32[]{:S(2)}) collective-permute-start(bf16[1,144,256]{2,1,0:T(8,128)(2,1)S(1)} %get-tuple-element.318), channel_id=1, source_target_pairs={{0,8},{1,9},{2,10},{3,11},{4,12},{5,13},{6,14},{7,15},{8,0},{9,1},... | collective-permute-start | bytes 221192 | tf_op jit(solution)/shard_map/ppermute | solution.py:94
  424.7 4.6 %collective-permute-start.41 = (f32[8,128]{1,0:T(8,128)S(1)}, f32[8,128]{1,0:T(8,128)S(1)}, u32[]{:S(2)}, u32[]{:S(2)}) collective-permute-start(f32[8,128]{1,0:T(8,128)S(1)} %iota.23), channel_id=1, source_target_pairs={{0,8},{1,9},{2,10},{3,11},{4,12},{5,13},{6,14},{7,15},{8,0},{9,1},... | collective-permute-start | bytes 12296 | tf_op jit(solution)/shard_map/ppermute | solution.py:94
  425.2 5.4 %collective-permute-start.42 = (f32[8,128]{1,0:T(8,128)S(1)}, f32[8,128]{1,0:T(8,128)S(1)}, u32[]{:S(2)}, u32[]{:S(2)}) collective-permute-start(f32[8,128]{1,0:T(8,128)S(1)} %iota.23), channel_id=1, source_target_pairs={{0,12},{1,13},{2,14},{3,15},{4,8},{5,9},{6,10},{7,11},{8,4},{9,5},... | collective-permute-start | bytes 12296 | tf_op jit(solution)/shard_map/ppermute | solution.py:94
  427.4 3.6 collective-permute-start.40
  432.2 9.6 %collective-permute-start.47 = (f32[8,128]{1,0:T(8,128)S(1)}, f32[8,128]{1,0:T(8,128)S(1)}, u32[]{:S(2)}, u32[]{:S(2)}) collective-permute-start(f32[8,128]{1,0:T(8,128)S(1)} %add.191), channel_id=1, source_target_pairs={{0,3},{1,2},{2,1},{3,0},{4,7},{5,6},{6,5},{7,4},{8,11},{9,10},{10,... | collective-permute-start | bytes 12296 | tf_op jit(solution)/shard_map/ppermute | solution.py:94
  436.9 4.9 %collective-permute-start.46 = (f32[8,128]{1,0:T(8,128)S(1)}, f32[8,128]{1,0:T(8,128)S(1)}, u32[]{:S(2)}, u32[]{:S(2)}) collective-permute-start(f32[8,128]{1,0:T(8,128)S(1)} %add.191), channel_id=1, source_target_pairs={{0,2},{1,3},{2,0},{3,1},{4,6},{5,7},{6,4},{7,5},{8,10},{9,11},{10,... | collective-permute-start | bytes 12296 | tf_op jit(solution)/shard_map/ppermute | solution.py:94
  436.9 4.9 %collective-permute-start.45 = (f32[8,128]{1,0:T(8,128)S(1)}, f32[8,128]{1,0:T(8,128)S(1)}, u32[]{:S(2)}, u32[]{:S(2)}) collective-permute-start(f32[8,128]{1,0:T(8,128)S(1)} %add.191), channel_id=1, source_target_pairs={{0,1},{1,0},{2,3},{3,2},{4,5},{5,4},{6,7},{7,6},{8,9},{9,8},{10,11... | collective-permute-start | bytes 12296 | tf_op jit(solution)/shard_map/ppermute | solution.py:94
  (24 other events, 305.7 us)

commit v6 on v5

--- a/solution.py
+++ b/solution.py
@@ -959,7 +959,7 @@
             sent[1], arrivals[0] = lax.optimization_barrier((sent[1], arrivals[0]))
             arrivals.append(halo(walk, sent[1], sent[1]))
         terms = node_terms(mesh, w_round[layer], b_round[layer])
-        if layer == 1:
+        if layer == 0:
             (before, after), valid_around, counts = lax.optimization_barrier(
                 (arrivals[0], valid_around, counts)
             )

time: 449 us -> 445 us (level)
    ppermute x8, waiting for transfers between devices: 20.2 us -> 2.89 us  [halo(): lax.ppermute(initial, 'space', down)]
    ppermute x4, waiting for transfers between devices: 7.5 us -> 15.1 us  [shifted(): return lax.ppermute(shard, axis, pairs)]
    ppermute x8, waiting for transfers between devices: 17.4 us -> 24.3 us  [halo(): lax.ppermute(last, 'space', up)]
  transfers between devices with their start and end apart: 51 -> 51, of which waited for: 27 -> 28; matrix products, arithmetic and copies ran while one was open for 6% -> 6% of each run, Pallas kernels for 25% -> 25%
where the time goes in v6:
time: 445 us; the launch traced here: 443 us
  Pallas kernels  225 us (51%)
  starting transfers between devices  86.6 us (19%)
  waiting for transfers between devices  85.9 us (19%)
  other arithmetic  23.2 us (5%)
  local copies, waits for them, and re-layouts  10.9 us (2%)
  between operations  7.67 us (2%)
    pallas_call x5, Pallas kernels, round_forward(): pl.pallas_call(body, grid_spec=pltpu.PrefetchScalarGridSpec(num_scalar_pr...  83.1 us
    pallas_call x3, Pallas kernels, edges_backward(): pl.pallas_call(body, grid_spec=pltpu.PrefetchScalarGridSpec(num_scalar_pr...  78.7 us
    ppermute x25, starting transfers between devices, swapped(): lax.ppermute(value, axis, [(i, i ^ bit) for i in range(lax.axis_size(axis...  29.4 us
    ppermute x25, waiting for transfers between devices, swapped(): lax.ppermute(value, axis, [(i, i ^ bit) for i in range(lax.axis_size(axis...  27.2 us
    pallas_call x3, Pallas kernels, weight_grads(): pl.pallas_call(body, grid=(blocks // tile,), in_specs=[rows] * 7 + [whole...  24.4 us
    ppermute x8, waiting for transfers between devices, halo(): lax.ppermute(last, 'space', up)  24.3 us
    ppermute x8, starting transfers between devices, halo(): lax.ppermute(initial, 'space', down)  22 us
    all_to_all x3, waiting for transfers between devices, exchanged(): lax.all_to_all(rows.reshape(bands, capacity, HALF), 'space', split_axis=0...  16.5 us
  transfers between devices with their start and end apart: 51, of which 28 were waited for; matrix products, arithmetic and copies ran while one was open for 6% of the time, Pallas kernels for 25%

profile of v6, /device:TPU:0, one launch (start us, length us, event | category | flops | bytes accessed | tf_op | source)
XLA Modules:
  0.0 443.2 jit_solution(975931407757585290)
XLA Ops:
  2.5 5.1 %collective-permute-start.2 = (bf16[1,144,256]{2,1,0:T(8,128)(2,1)S(1)}, bf16[1,144,256]{2,1,0:T(8,128)(2,1)S(1)}, u32[]{:S(2)}, u32[]{:S(2)}) collective-permute-start(bf16[1,144,256]{2,1,0:T(8,128)(2,1)S(1)} %broadcast_in_dim_reshape.3), channel_id=1, source_target_pairs={{0,12},{1,13},{2,14},{3,15},{4,8},{5,9},{6,10},{7,11},{8,4},{9,5},... | collective-permute-start | bytes 221192 | tf_op jit(solution)/shard_map/ppermute | solution.py:94
  26.1 5.9 %all-to-all-start = ((bf16[16,64,128]{2,1,0:T(8,128)(2,1)}), bf16[16,64,128]{2,1,0:T(8,128)(2,1)S(1)}, u32[]{:S(2)}, u32[]{:S(2)}) async-start(bf16[16,64,128]{2,1,0:T(8,128)(2,1)} %bitcast.4), calls=%async_computation | async-start | bytes 524288 | tf_op jit(solution)/shard_map/all_to_all | solution.py:907
  35.8 4.0 spread_rows.1
  41.2 5.5 %encode_rows.1 = (f32[2048,256]{1,0:T(8,128)}, bf16[2048,256]{1,0:T(8,128)(2,1)}, bf16[4096,128]{1,0:T(8,128)(2,1)}, s32[1,1024]{1,0:T(1,128)}, s32[1024,1]{1,0:T(8,128)}) custom-call(bf16[1024,128]{1,0:T(8,128)(2,1)} %bitcast.132, bf16[128,256]{1,0:T(8,128)(2,1)} %get-tuple-element.147.in_ref, bf16[256,256]{1,0:T(8,128)(2,1)} %get-tuple-element.148.node_ref, ...), custom_call_target="tpu_custom_call" | custom-call | bytes 15000000 | tf_op jit(solution)/shard_map/encode_rows/pallas_call | solution.py:783
  46.7 4.6 %collective-permute-start.11 = (bf16[4096,128]{1,0:T(8,128)(2,1)}, bf16[4096,128]{1,0:T(8,128)(2,1)}, u32[]{:S(2)}, u32[]{:S(2)}) collective-permute-start(bf16[4096,128]{1,0:T(8,128)(2,1)} %get-tuple-element.155.refs_1_), channel_id=1, source_target_pairs={{1,0},{3,1},{2,3},{6,2},{4,6},{5,4},{7,5},{11,7},{9,11},{8,9},{10,... | collective-permute-start | bytes 3145736 | tf_op jit(solution)/shard_map/ppermute | solution.py:77
  52.7 4.5 %collective-permute-start.12 = (bf16[79,360]{1,0:T(8,128)(2,1)S(1)}, bf16[79,360]{1,0:T(8,128)(2,1)S(1)}, u32[]{:S(2)}, u32[]{:S(2)}) collective-permute-start(bf16[79,360]{1,0:T(8,128)(2,1)S(1)} %get-tuple-element.322), channel_id=1, source_target_pairs={{0,1},{1,2},{2,3},{3,4},{4,5},{5,6},{6,7},{7,8},{8,9},{9,10},{10,1... | collective-permute-start | bytes 170648 | tf_op jit(solution)/shard_map/ppermute | solution.py:49
  59.4 3.9 node_terms.3
  63.3 10.3 %collective-permute-done.13 = bf16[79,360]{1,0:T(8,128)(2,1)S(1)} collective-permute-done((bf16[79,360]{1,0:T(8,128)(2,1)S(1)}, bf16[79,360]{1,0:T(8,128)(2,1)S(1)}, u32[]{:S(2)}, u32[]{:S(2)}) %collective-permute-start.13) | collective-permute-done | bytes 56912 | tf_op jit(solution)/shard_map/ppermute | solution.py:49
  73.6 2.5 collective-permute-done.12
  76.3 2.3 collective-permute-done.10.refs_0_
  78.6 14.3 %round_forward.5 = (f32[2048,256]{1,0:T(8,128)}, f32[2048,256]{1,0:T(8,128)}, bf16[2048,256]{1,0:T(8,128)(2,1)}, bf16[2048,256]{1,0:T(8,128)(2,1)}, bf16[6,4096,...) custom-call(s32[6144]{0:T(1024)} %get-tuple-element.325.index_ref, f32[2048,256]{1,0:T(8,128)} %get-tuple-element.154.mesh_ref, ...), custom_call_target="tpu_custom_call" | custom-call | bytes 42000000 | tf_op jit(solution)/shard_map/round_forward/pallas_call | solution.py:497
  95.0 14.3 %round_forward.6 = (f32[2048,256]{1,0:T(8,128)}, f32[2048,256]{1,0:T(8,128)}, bf16[2048,256]{1,0:T(8,128)(2,1)}, bf16[2048,256]{1,0:T(8,128)(2,1)}, bf16[6,4096,...) custom-call(s32[6144]{0:T(1024)} %get-tuple-element.326.index_ref, ...), custom_call_target="tpu_custom_call", output_to_operand_aliasing={{0}: (9, {}), {1}: (10, {}), {2}: (11, {}), {3}: (12, {}), ... | custom-call | bytes 42000000 | tf_op jit(solution)/shard_map/round_forward/pallas_call | solution.py:497
  110.5 3.9 node_terms.4
  114.4 2.7 collective-permute-start.18
  117.1 5.6 %collective-permute-done.17.refs_1_.refs_0_ = bf16[2048,128]{1,0:T(8,128)(2,1)} collective-permute-done((bf16[2048,128]{1,0:T(8,128)(2,1)}, bf16[2048,128]{1,0:T(8,128)(2,1)}, u32[]{:S(2)}, u32[]{:S(2)}) %collective-permute-start.17) | collective-permute-done | bytes 524320 | tf_op jit(solution)/shard_map/ppermute | solution.py:77
  122.7 14.0 %round_forward.7 = (f32[2048,256]{1,0:T(8,128)}, f32[2048,256]{1,0:T(8,128)}, bf16[2048,256]{1,0:T(8,128)(2,1)}, bf16[2048,256]{1,0:T(8,128)(2,1)}, bf16[6,4096,...) custom-call(s32[6144]{0:T(1024)} %get-tuple-element.325.index_ref, f32[2048,256]{1,0:T(8,128)} %get-tuple-element.168.mesh_ref.refs_0_, ...), custom_call_target="tpu_custom_call" | custom-call | bytes 42000000 | tf_op jit(solution)/shard_map/round_forward/pallas_call | solution.py:497
  138.8 14.1 %round_forward.8 = (f32[2048,256]{1,0:T(8,128)}, f32[2048,256]{1,0:T(8,128)}, bf16[2048,256]{1,0:T(8,128)(2,1)}, bf16[2048,256]{1,0:T(8,128)(2,1)}, bf16[6,4096,...) custom-call(s32[6144]{0:T(1024)} %get-tuple-element.326.index_ref, ...), custom_call_target="tpu_custom_call", output_to_operand_aliasing={{0}: (11, {}), {1}: (12, {}), {2}: (13, {}), {3}: (14, {}),... | custom-call | bytes 42000000 | tf_op jit(solution)/shard_map/round_forward/pallas_call | solution.py:497
  152.9 3.0 collective-permute-start.22
  156.8 3.9 node_terms.5
  160.6 2.9 collective-permute-done.22.refs_5_
  163.5 4.0 collective-permute-done.21.refs_1_
  167.5 26.3 %round_forward.9 = (f32[2048,256]{1,0:T(8,128)}, f32[2048,256]{1,0:T(8,128)}, bf16[2048,256]{1,0:T(8,128)(2,1)}, bf16[2048,256]{1,0:T(8,128)(2,1)}, bf16[6,4096,...) custom-call(s32[12288]{0:T(1024)} %copy-done.7, ...), custom_call_target="tpu_custom_call" | custom-call | bytes 72000000 | tf_op jit(solution)/shard_map/round_forward/pallas_call | solution.py:497
  193.8 3.6 all-to-all-start.1
  197.5 8.4 %all-to-all-done.1 = bf16[16,64,128]{2,1,0:T(8,128)(2,1)S(1)} async-done(((bf16[16,64,128]{2,1,0:T(8,128)(2,1)}), bf16[16,64,128]{2,1,0:T(8,128)(2,1)S(1)}, u32[]{:S(2)}, u32[]{:S(2)}) %all-to-all-start.1) | async-done | bytes 262176 | tf_op jit(solution)/shard_map/all_to_all | solution.py:907
  207.4 3.3 collective-permute-start.23
  219.8 5.9 %all-to-all-start.2 = ((bf16[16,64,128]{2,1,0:T(8,128)(2,1)}), bf16[16,64,128]{2,1,0:T(8,128)(2,1)S(1)}, u32[]{:S(2)}, u32[]{:S(2)}) async-start(bf16[16,64,128]{2,1,0:T(8,128)(2,1)} %bitcast.20), calls=%async_computation.2 | async-start | bytes 524288 | tf_op jit(solution)/shard_map/all_to_all | solution.py:907
  226.8 7.4 %all-to-all-done.2 = bf16[16,64,128]{2,1,0:T(8,128)(2,1)S(1)} async-done(((bf16[16,64,128]{2,1,0:T(8,128)(2,1)}), bf16[16,64,128]{2,1,0:T(8,128)(2,1)S(1)}, u32[]{:S(2)}, u32[]{:S(2)}) %all-to-all-start.2) | async-done | bytes 262176 | tf_op jit(solution)/shard_map/all_to_all | solution.py:907
  235.9 26.8 %edges_backward.3 = (f32[2048,256]{1,0:T(8,128)}, bf16[2048,256]{1,0:T(8,128)(2,1)}, bf16[1024,256]{1,0:T(8,128)(2,1)}, bf16[2048,256]{1,0:T(8,128)(2,1)}, bf16[...) custom-call(s32[12288]{0:T(1024)} %copy-done.7, ...), custom_call_target="tpu_custom_call" | custom-call | bytes 75000000 | tf_op jit(solution)/shard_map/edges_backward/pallas_call | solution.py:642
  264.2 2.4 collective-permute-start.27
  267.2 2.7 decode_grads.1
  269.9 7.4 %weight_grads.3 = (f32[2048,256]{1,0:T(8,128)}, f32[1024,256]{1,0:T(8,128)}, f32[2,256]{1,0:T(2,128)}) custom-call(f32[2048,256]{1,0:T(8,128)} %get-tuple-element.182.mesh_ref.refs_0_, bf16[2048,256]{1,0:T(8,128)(2,1)} %get-tuple-element.206.dest_ref, bf16[2048,256]{1,0:T(8,128)(2,1)} %get-tuple-element.207.agg_ref, ...), custom_call_target="tpu_custom_call" | custom-call | bytes 30000000 | tf_op jit(solution)/shard_map/weight_grads/pallas_call | solution.py:727
  277.3 4.0 convert_select_fusion
  282.5 25.8 %edges_backward.4 = (f32[2048,256]{1,0:T(8,128)}, bf16[2048,256]{1,0:T(8,128)(2,1)}, bf16[2048,256]{1,0:T(8,128)(2,1)}, bf16[2048,256]{1,0:T(8,128)(2,1)}, bf16[...) custom-call(s32[12288]{0:T(1024)} %copy-done.7, ...), custom_call_target="tpu_custom_call" | custom-call | bytes 84000000 | tf_op jit(solution)/shard_map/edges_backward/pallas_call | solution.py:642
  309.0 3.3 collective-permute-start.29
  312.2 8.6 %weight_grads.4 = (f32[2048,256]{1,0:T(8,128)}, f32[1024,256]{1,0:T(8,128)}, f32[2,256]{1,0:T(2,128)}, f32[256,256]{1,0:T(8,128)}) custom-call(f32[2048,256]{1,0:T(8,128)} %get-tuple-element.168.mesh_ref.refs_0_, bf16[2048,256]{1,0:T(8,128)(2,1)} %get-tuple-element.227.dest_ref, bf16[2048,256]{1,0:T(8,128)(2,1)} %get-tuple-element.228.agg_ref, ...), custom_call_target="tpu_custom_call" | custom-call | bytes 30000000 | tf_op jit(solution)/shard_map/weight_grads/pallas_call | solution.py:727
  320.8 6.3 %collective-permute-done.28.refs_6_ = bf16[4096,128]{1,0:T(8,128)(2,1)} collective-permute-done((bf16[4096,128]{1,0:T(8,128)(2,1)}, bf16[4096,128]{1,0:T(8,128)(2,1)}, u32[]{:S(2)}, u32[]{:S(2)}) %collective-permute-start.28) | collective-permute-done | bytes 1048608 | tf_op jit(solution)/shard_map/ppermute | solution.py:77
  327.2 26.0 %edges_backward.5 = (f32[2048,256]{1,0:T(8,128)}, bf16[2048,256]{1,0:T(8,128)(2,1)}, bf16[2048,256]{1,0:T(8,128)(2,1)}, bf16[2048,256]{1,0:T(8,128)(2,1)}, bf16[...) custom-call(s32[12288]{0:T(1024)} %copy-done.7, ...), custom_call_target="tpu_custom_call" | custom-call | bytes 84000000 | tf_op jit(solution)/shard_map/edges_backward/pallas_call | solution.py:642
  353.2 3.8 collective-permute-start.31
  357.8 8.4 %weight_grads.5 = (f32[2048,256]{1,0:T(8,128)}, f32[1024,256]{1,0:T(8,128)}, f32[2,256]{1,0:T(2,128)}, f32[256,256]{1,0:T(8,128)}) custom-call(f32[2048,256]{1,0:T(8,128)} %get-tuple-element.154.mesh_ref, bf16[2048,256]{1,0:T(8,128)(2,1)} %get-tuple-element.238.dest_ref, bf16[2048,256]{1,0:T(8,128)(2,1)} %get-tuple-element.239.agg_ref, ...), custom_call_target="tpu_custom_call" | custom-call | bytes 30000000 | tf_op jit(solution)/shard_map/weight_grads/pallas_call | solution.py:727
  366.3 4.8 %collective-permute-done.30.first_ref = bf16[4096,128]{1,0:T(8,128)(2,1)} collective-permute-done((bf16[4096,128]{1,0:T(8,128)(2,1)}, bf16[4096,128]{1,0:T(8,128)(2,1)}, u32[]{:S(2)}, u32[]{:S(2)}) %collective-permute-start.30) | collective-permute-done | bytes 1048608 | tf_op jit(solution)/shard_map/ppermute | solution.py:77
  371.1 10.1 %encode_backward.1 = (f32[2048,256]{1,0:T(8,128)}, bf16[2048,256]{1,0:T(8,128)(2,1)}, f32[128,256]{1,0:T(8,128)}, f32[256,256]{1,0:T(8,128)}, f32[2,256]{1,0:T(2,128)}, /*index=5*/f32[256,256]{1,0:T(8,128)}) custom-call(f32[2048,256]{1,0:T(8,128)} %get-tuple-element.245.part_ref, f32[4096,128]{1,0:T(8,128)} %get-tuple-element.246.own_ref, ...), custom_call_target="tpu_custom_call" | custom-call | bytes 30000000 | tf_op jit(solution)/shard_map/encode_backward/pallas_call | solution.py:848
  381.1 5.1 %collect_rows.1 = (f32[16,144,256]{2,1,0:T(8,128)}, bf16[16,144,256]{2,1,0:T(8,128)(2,1)}) custom-call(s32[1]{0:T(128)} %bitcast.6.place_ref, f32[128,256]{1,0:T(8,128)} %get-tuple-element.250.refs_0_, f32[256,256]{1,0:T(8,128)} %get-tuple-element.251.refs_1_, f32[256,256]{1,0:T(8,128)} %get-tuple-element.252.refs_2_, f32[78,256]{1,0:T(8,128)} %reshape.160.refs_3_, ...), custom_call_target="tpu_custom_call" | custom-call | bytes 15000000 | tf_op jit(solution)/shard_map/collect_rows/pallas_call | solution.py:233
  386.2 3.1 collective-permute-done.32
  391.6 8.9 %collective-permute-done.33 = bf16[4,2,72,256]{3,2,0,1:T(8,128)(2,1)S(1)} collective-permute-done((bf16[4,2,72,256]{3,2,0,1:T(8,128)(2,1)S(1)}, bf16[4,2,72,256]{3,2,0,1:T(8,128)(2,1)S(1)}, u32[]{:S(2)}, u32[]{:S(2)}) %collective-permute-start.33) | collective-permute-done | bytes 294944 | tf_op jit(solution)/shard_map/ppermute | solution.py:94
  402.5 3.3 collective-permute-done.34
  408.1 5.5 %collective-permute-start.39 = (bf16[1,144,256]{2,1,0:T(8,128)(2,1)S(1)}, bf16[1,144,256]{2,1,0:T(8,128)(2,1)S(1)}, u32[]{:S(2)}, u32[]{:S(2)}) collective-permute-start(bf16[1,144,256]{2,1,0:T(8,128)(2,1)S(1)} %get-tuple-element.317), channel_id=1, source_target_pairs={{0,12},{1,13},{2,14},{3,15},{4,8},{5,9},{6,10},{7,11},{8,4},{9,5},... | collective-permute-start | bytes 221192 | tf_op jit(solution)/shard_map/ppermute | solution.py:94
  428.8 4.9 %collective-permute-start.47 = (f32[8,128]{1,0:T(8,128)S(1)}, f32[8,128]{1,0:T(8,128)S(1)}, u32[]{:S(2)}, u32[]{:S(2)}) collective-permute-start(f32[8,128]{1,0:T(8,128)S(1)} %add.191), channel_id=1, source_target_pairs={{0,3},{1,2},{2,1},{3,0},{4,7},{5,6},{6,5},{7,4},{8,11},{9,10},{10,... | collective-permute-start | bytes 12296 | tf_op jit(solution)/shard_map/ppermute | solution.py:94
  435.2 3.4 select_bitcast_fusion
  (199 shorter events, 74.7 us)
Async XLA Ops:
  2.5 14.5 %collective-permute-start.2 = (bf16[1,144,256]{2,1,0:T(8,128)(2,1)S(1)}, bf16[1,144,256]{2,1,0:T(8,128)(2,1)S(1)}, u32[]{:S(2)}, u32[]{:S(2)}) collective-permute-start(bf16[1,144,256]{2,1,0:T(8,128)(2,1)S(1)} %broadcast_in_dim_reshape.3), channel_id=1, source_target_pairs={{0,12},{1,13},{2,14},{3,15},{4,8},{5,9},{6,10},{7,11},{8,4},{9,5},... | collective-permute-start | bytes 221192 | tf_op jit(solution)/shard_map/ppermute | solution.py:94
  7.6 9.4 %collective-permute-start.1 = (bf16[1,144,256]{2,1,0:T(8,128)(2,1)S(1)}, bf16[1,144,256]{2,1,0:T(8,128)(2,1)S(1)}, u32[]{:S(2)}, u32[]{:S(2)}) collective-permute-start(bf16[1,144,256]{2,1,0:T(8,128)(2,1)S(1)} %broadcast_in_dim_reshape.3), channel_id=1, source_target_pairs={{0,8},{1,9},{2,10},{3,11},{4,12},{5,13},{6,14},{7,15},{8,0},{9,1},... | collective-permute-start | bytes 221192 | tf_op jit(solution)/shard_map/ppermute | solution.py:94
  7.6 9.4 %collective-permute-start = (bf16[1,144,256]{2,1,0:T(8,128)(2,1)S(1)}, bf16[1,144,256]{2,1,0:T(8,128)(2,1)S(1)}, u32[]{:S(2)}, u32[]{:S(2)}) collective-permute-start(bf16[1,144,256]{2,1,0:T(8,128)(2,1)S(1)} %broadcast_in_dim_reshape.3), channel_id=1, source_target_pairs={{0,4},{1,5},{2,6},{3,7},{4,0},{5,1},{6,2},{7,3},{8,12},{9,13},{10,... | collective-permute-start | bytes 221192 | tf_op jit(solution)/shard_map/ppermute | solution.py:94
  17.0 5.2 %collective-permute-start.4 = (bf16[4,72,256]{2,1,0:T(8,128)(2,1)S(1)}, bf16[4,72,256]{2,1,0:T(8,128)(2,1)S(1)}, u32[]{:S(2)}, u32[]{:S(2)}) collective-permute-start(bf16[4,72,256]{2,1,0:T(8,128)(2,1)S(1)} %get-tuple-element.319), channel_id=1, source_target_pairs={{0,1},{1,0},{2,3},{3,2},{4,5},{5,4},{6,7},{7,6},{8,9},{9,8},{10,11... | collective-permute-start | bytes 442376 | tf_op jit(solution)/shard_map/ppermute | solution.py:94
  18.7 5.1 %collective-permute-start.3 = (bf16[4,72,256]{2,1,0:T(8,128)(2,1)S(1)}, bf16[4,72,256]{2,1,0:T(8,128)(2,1)S(1)}, u32[]{:S(2)}, u32[]{:S(2)}) collective-permute-start(bf16[4,72,256]{2,1,0:T(8,128)(2,1)S(1)} %get-tuple-element.320), channel_id=1, source_target_pairs={{0,2},{1,3},{2,0},{3,1},{4,6},{5,7},{6,4},{7,5},{8,10},{9,11},{10,... | collective-permute-start | bytes 442376 | tf_op jit(solution)/shard_map/ppermute | solution.py:94
  23.9 8.1 %collective-permute-start.6 = (bf16[8,72,256]{2,1,0:T(8,128)(2,1)S(1)}, bf16[8,72,256]{2,1,0:T(8,128)(2,1)S(1)}, u32[]{:S(2)}, u32[]{:S(2)}) collective-permute-start(bf16[8,72,256]{2,1,0:T(8,128)(2,1)S(1)} %pad_maximum_fusion.3), channel_id=1, source_target_pairs={{0,2},{1,3},{2,0},{3,1},{4,6},{5,7},{6,4},{7,5},{8,10},{9,11},{10,... | collective-permute-start | bytes 884744 | tf_op jit(solution)/shard_map/ppermute | solution.py:94
  25.5 7.1 %collective-permute-start.5 = (bf16[8,72,256]{2,1,0:T(8,128)(2,1)S(1)}, bf16[8,72,256]{2,1,0:T(8,128)(2,1)S(1)}, u32[]{:S(2)}, u32[]{:S(2)}) collective-permute-start(bf16[8,72,256]{2,1,0:T(8,128)(2,1)S(1)} %pad_maximum_fusion.2), channel_id=1, source_target_pairs={{0,1},{1,0},{2,3},{3,2},{4,5},{5,4},{6,7},{7,6},{8,9},{9,8},{10,11... | collective-permute-start | bytes 884744 | tf_op jit(solution)/shard_map/ppermute | solution.py:94
  26.1 14.4 %all-to-all-start = ((bf16[16,64,128]{2,1,0:T(8,128)(2,1)}), bf16[16,64,128]{2,1,0:T(8,128)(2,1)S(1)}, u32[]{:S(2)}, u32[]{:S(2)}) async-start(bf16[16,64,128]{2,1,0:T(8,128)(2,1)} %bitcast.4), calls=%async_computation | async-start | bytes 524288 | tf_op jit(solution)/shard_map/all_to_all | solution.py:907
  32.8 7.0 %collective-permute-start.9 = (s32[12288]{0:T(1024)S(1)}, s32[12288]{0:T(1024)S(1)}, u32[]{:S(2)}, u32[]{:S(2)}) collective-permute-start(s32[12288]{0:T(1024)S(1)} %reshape.150), channel_id=1, source_target_pairs={{0,0},{1,1},{2,3},{3,2},{4,6},{5,4},{6,5},{7,7},{8,11},{9,9},{10,8... | collective-permute-start | bytes 147464 | tf_op jit(solution)/shard_map/ppermute | solution.py:920
  46.7 29.6 %collective-permute-start.11 = (bf16[4096,128]{1,0:T(8,128)(2,1)}, bf16[4096,128]{1,0:T(8,128)(2,1)}, u32[]{:S(2)}, u32[]{:S(2)}) collective-permute-start(bf16[4096,128]{1,0:T(8,128)(2,1)} %get-tuple-element.155.refs_1_), channel_id=1, source_target_pairs={{1,0},{3,1},{2,3},{6,2},{4,6},{5,4},{7,5},{11,7},{9,11},{8,9},{10,... | collective-permute-start | bytes 3145736 | tf_op jit(solution)/shard_map/ppermute | solution.py:77
  51.3 27.3 %collective-permute-start.10 = (bf16[4096,128]{1,0:T(8,128)(2,1)}, bf16[4096,128]{1,0:T(8,128)(2,1)}, u32[]{:S(2)}, u32[]{:S(2)}) collective-permute-start(bf16[4096,128]{1,0:T(8,128)(2,1)} %get-tuple-element.155.refs_1_), channel_id=1, source_target_pairs={{0,1},{1,3},{3,2},{2,6},{6,4},{4,5},{5,7},{7,11},{11,9},{9,8},{8,1... | collective-permute-start | bytes 3145736 | tf_op jit(solution)/shard_map/ppermute | solution.py:77
  51.4 22.2 %collective-permute-start.13 = (bf16[79,360]{1,0:T(8,128)(2,1)S(1)}, bf16[79,360]{1,0:T(8,128)(2,1)S(1)}, u32[]{:S(2)}, u32[]{:S(2)}) collective-permute-start(bf16[79,360]{1,0:T(8,128)(2,1)S(1)} %get-tuple-element.321), channel_id=1, source_target_pairs={{1,0},{2,1},{3,2},{4,3},{5,4},{6,5},{7,6},{8,7},{9,8},{10,9},{11,1... | collective-permute-start | bytes 170648 | tf_op jit(solution)/shard_map/ppermute | solution.py:49
  52.7 23.4 %collective-permute-start.12 = (bf16[79,360]{1,0:T(8,128)(2,1)S(1)}, bf16[79,360]{1,0:T(8,128)(2,1)S(1)}, u32[]{:S(2)}, u32[]{:S(2)}) collective-permute-start(bf16[79,360]{1,0:T(8,128)(2,1)S(1)} %get-tuple-element.322), channel_id=1, source_target_pairs={{0,1},{1,2},{2,3},{3,4},{4,5},{5,6},{6,7},{7,8},{8,9},{9,10},{10,1... | collective-permute-start | bytes 170648 | tf_op jit(solution)/shard_map/ppermute | solution.py:49
  59.3 4.0 collective-permute-start.14
  92.9 16.4 %collective-permute-start.16 = (bf16[2048,128]{1,0:T(8,128)(2,1)}, bf16[2048,128]{1,0:T(8,128)(2,1)S(1)}, u32[]{:S(2)}, u32[]{:S(2)}) collective-permute-start(bf16[2048,128]{1,0:T(8,128)(2,1)} %get-tuple-element.170.refs_2_.refs_1_), channel_id=1, source_target_pairs={{1,0},{3,1},{2,3},{6,2},{4,6},{5,4},{7,5},{11,7},{9,11},{8,9},{10,... | collective-permute-start | bytes 1572872 | tf_op jit(solution)/shard_map/ppermute | solution.py:77
  94.0 15.3 %collective-permute-start.15 = (bf16[2048,128]{1,0:T(8,128)(2,1)}, bf16[2048,128]{1,0:T(8,128)(2,1)}, u32[]{:S(2)}, u32[]{:S(2)}) collective-permute-start(bf16[2048,128]{1,0:T(8,128)(2,1)} %get-tuple-element.170.refs_2_.refs_1_), channel_id=1, source_target_pairs={{0,1},{1,3},{3,2},{2,6},{6,4},{4,5},{5,7},{7,11},{11,9},{9,8},{8,1... | collective-permute-start | bytes 1572872 | tf_op jit(solution)/shard_map/ppermute | solution.py:77
  109.4 13.3 %collective-permute-start.17 = (bf16[2048,128]{1,0:T(8,128)(2,1)}, bf16[2048,128]{1,0:T(8,128)(2,1)}, u32[]{:S(2)}, u32[]{:S(2)}) collective-permute-start(bf16[2048,128]{1,0:T(8,128)(2,1)} %get-tuple-element.171.refs_3_.refs_2_), channel_id=1, source_target_pairs={{0,1},{1,3},{3,2},{2,6},{6,4},{4,5},{5,7},{7,11},{11,9},{9,8},{8,1... | collective-permute-start | bytes 1572872 | tf_op jit(solution)/shard_map/ppermute | solution.py:77
  114.4 24.3 %collective-permute-start.18 = (bf16[2048,128]{1,0:T(8,128)(2,1)}, bf16[2048,128]{1,0:T(8,128)(2,1)}, u32[]{:S(2)}, u32[]{:S(2)}) collective-permute-start(bf16[2048,128]{1,0:T(8,128)(2,1)} %get-tuple-element.171.refs_3_.refs_2_), channel_id=1, source_target_pairs={{1,0},{3,1},{2,3},{6,2},{4,6},{5,4},{7,5},{11,7},{9,11},{8,9},{10,... | collective-permute-start | bytes 1572872 | tf_op jit(solution)/shard_map/ppermute | solution.py:77
  136.7 16.2 %collective-permute-start.20 = (bf16[2048,128]{1,0:T(8,128)(2,1)}, bf16[2048,128]{1,0:T(8,128)(2,1)S(1)}, u32[]{:S(2)}, u32[]{:S(2)}) collective-permute-start(bf16[2048,128]{1,0:T(8,128)(2,1)} %get-tuple-element.184.refs_2_), channel_id=1, source_target_pairs={{1,0},{3,1},{2,3},{6,2},{4,6},{5,4},{7,5},{11,7},{9,11},{8,9},{10,... | collective-permute-start | bytes 1572872 | tf_op jit(solution)/shard_map/ppermute | solution.py:77
  137.9 15.1 %collective-permute-start.19 = (bf16[2048,128]{1,0:T(8,128)(2,1)}, bf16[2048,128]{1,0:T(8,128)(2,1)}, u32[]{:S(2)}, u32[]{:S(2)}) collective-permute-start(bf16[2048,128]{1,0:T(8,128)(2,1)} %get-tuple-element.184.refs_2_), channel_id=1, source_target_pairs={{0,1},{1,3},{3,2},{2,6},{6,4},{4,5},{5,7},{7,11},{11,9},{9,8},{8,1... | collective-permute-start | bytes 1572872 | tf_op jit(solution)/shard_map/ppermute | solution.py:77
  152.9 10.6 %collective-permute-start.22 = (bf16[2048,128]{1,0:T(8,128)(2,1)}, bf16[2048,128]{1,0:T(8,128)(2,1)}, u32[]{:S(2)}, u32[]{:S(2)}) collective-permute-start(bf16[2048,128]{1,0:T(8,128)(2,1)} %get-tuple-element.186.refs_3_), channel_id=1, source_target_pairs={{1,0},{3,1},{2,3},{6,2},{4,6},{5,4},{7,5},{11,7},{9,11},{8,9},{10,... | collective-permute-start | bytes 1572872 | tf_op jit(solution)/shard_map/ppermute | solution.py:77
  155.9 11.6 %collective-permute-start.21 = (bf16[2048,128]{1,0:T(8,128)(2,1)}, bf16[2048,128]{1,0:T(8,128)(2,1)}, u32[]{:S(2)}, u32[]{:S(2)}) collective-permute-start(bf16[2048,128]{1,0:T(8,128)(2,1)} %get-tuple-element.186.refs_3_), channel_id=1, source_target_pairs={{0,1},{1,3},{3,2},{2,6},{6,4},{4,5},{5,7},{7,11},{11,9},{9,8},{8,1... | collective-permute-start | bytes 1572872 | tf_op jit(solution)/shard_map/ppermute | solution.py:77
  193.8 12.1 %all-to-all-start.1 = ((bf16[16,64,128]{2,1,0:T(8,128)(2,1)}), bf16[16,64,128]{2,1,0:T(8,128)(2,1)S(1)}, u32[]{:S(2)}, u32[]{:S(2)}) async-start(bf16[16,64,128]{2,1,0:T(8,128)(2,1)} %bitcast.141), calls=%async_computation.1 | async-start | bytes 524288 | tf_op jit(solution)/shard_map/all_to_all | solution.py:907
  207.4 9.5 %collective-permute-start.23 = (bf16[78,360]{1,0:T(8,128)(2,1)S(1)}, bf16[78,360]{1,0:T(8,128)(2,1)S(1)}, u32[]{:S(2)}, u32[]{:S(2)}) collective-permute-start(bf16[78,360]{1,0:T(8,128)(2,1)S(1)} %get-tuple-element.323), channel_id=1, source_target_pairs={{0,1},{1,2},{2,3},{3,4},{4,5},{5,6},{6,7},{7,8},{8,9},{9,10},{10,1... | collective-permute-start | bytes 168488 | tf_op jit(solution)/shard_map/ppermute | solution.py:49
  210.8 6.1 %collective-permute-start.24 = (bf16[78,360]{1,0:T(8,128)(2,1)S(1)}, bf16[78,360]{1,0:T(8,128)(2,1)S(1)}, u32[]{:S(2)}, u32[]{:S(2)}) collective-permute-start(bf16[78,360]{1,0:T(8,128)(2,1)S(1)} %get-tuple-element.324), channel_id=1, source_target_pairs={{1,0},{2,1},{3,2},{4,3},{5,4},{6,5},{7,6},{8,7},{9,8},{10,9},{11,1... | collective-permute-start | bytes 168488 | tf_op jit(solution)/shard_map/ppermute | solution.py:49
  219.8 14.4 %all-to-all-start.2 = ((bf16[16,64,128]{2,1,0:T(8,128)(2,1)}), bf16[16,64,128]{2,1,0:T(8,128)(2,1)S(1)}, u32[]{:S(2)}, u32[]{:S(2)}) async-start(bf16[16,64,128]{2,1,0:T(8,128)(2,1)} %bitcast.20), calls=%async_computation.2 | async-start | bytes 524288 | tf_op jit(solution)/shard_map/all_to_all | solution.py:907
  234.2 28.5 %collective-permute-start.25 = (bf16[2048,256]{1,0:T(8,128)(2,1)}, bf16[2048,256]{1,0:T(8,128)(2,1)}, u32[]{:S(2)}, u32[]{:S(2)}) collective-permute-start(bf16[2048,256]{1,0:T(8,128)(2,1)} %convert_element_type.150), channel_id=1, source_target_pairs={{3,2},{2,3},{6,4},{4,5},{5,6},{11,8},{8,10},{10,11},{14,12},{15,13... | collective-permute-start | bytes 3145736 | tf_op jit(solution)/shard_map/ppermute | solution.py:937
  262.7 19.7 %collective-permute-start.26 = (bf16[4096,128]{1,0:T(8,128)(2,1)}, bf16[4096,128]{1,0:T(8,128)(2,1)}, u32[]{:S(2)}, u32[]{:S(2)}) collective-permute-start(bf16[4096,128]{1,0:T(8,128)(2,1)} %get-tuple-element.217), channel_id=1, source_target_pairs={{0,1},{1,3},{3,2},{2,6},{6,4},{4,5},{5,7},{7,11},{11,9},{9,8},{8,1... | collective-permute-start | bytes 3145736 | tf_op jit(solution)/shard_map/ppermute | solution.py:77
  264.2 18.3 %collective-permute-start.27 = (bf16[4096,128]{1,0:T(8,128)(2,1)}, bf16[4096,128]{1,0:T(8,128)(2,1)}, u32[]{:S(2)}, u32[]{:S(2)}) collective-permute-start(bf16[4096,128]{1,0:T(8,128)(2,1)} %get-tuple-element.226), channel_id=1, source_target_pairs={{1,0},{3,1},{2,3},{6,2},{4,6},{5,4},{7,5},{11,7},{9,11},{8,9},{10,... | collective-permute-start | bytes 3145736 | tf_op jit(solution)/shard_map/ppermute | solution.py:77
  308.3 18.8 %collective-permute-start.28 = (bf16[4096,128]{1,0:T(8,128)(2,1)}, bf16[4096,128]{1,0:T(8,128)(2,1)}, u32[]{:S(2)}, u32[]{:S(2)}) collective-permute-start(bf16[4096,128]{1,0:T(8,128)(2,1)} %get-tuple-element.236), channel_id=1, source_target_pairs={{0,1},{1,3},{3,2},{2,6},{6,4},{4,5},{5,7},{7,11},{11,9},{9,8},{8,1... | collective-permute-start | bytes 3145736 | tf_op jit(solution)/shard_map/ppermute | solution.py:77
  309.0 18.2 %collective-permute-start.29 = (bf16[4096,128]{1,0:T(8,128)(2,1)}, bf16[4096,128]{1,0:T(8,128)(2,1)}, u32[]{:S(2)}, u32[]{:S(2)}) collective-permute-start(bf16[4096,128]{1,0:T(8,128)(2,1)} %get-tuple-element.237), channel_id=1, source_target_pairs={{1,0},{3,1},{2,3},{6,2},{4,6},{5,4},{7,5},{11,7},{9,11},{8,9},{10,... | collective-permute-start | bytes 3145736 | tf_op jit(solution)/shard_map/ppermute | solution.py:77
  353.2 17.9 %collective-permute-start.30 = (bf16[4096,128]{1,0:T(8,128)(2,1)}, bf16[4096,128]{1,0:T(8,128)(2,1)}, u32[]{:S(2)}, u32[]{:S(2)}) collective-permute-start(bf16[4096,128]{1,0:T(8,128)(2,1)} %get-tuple-element.247), channel_id=1, source_target_pairs={{0,1},{1,3},{3,2},{2,6},{6,4},{4,5},{5,7},{7,11},{11,9},{9,8},{8,1... | collective-permute-start | bytes 3145736 | tf_op jit(solution)/shard_map/ppermute | solution.py:77
  353.2 17.8 %collective-permute-start.31 = (bf16[4096,128]{1,0:T(8,128)(2,1)}, bf16[4096,128]{1,0:T(8,128)(2,1)}, u32[]{:S(2)}, u32[]{:S(2)}) collective-permute-start(bf16[4096,128]{1,0:T(8,128)(2,1)} %get-tuple-element.248), channel_id=1, source_target_pairs={{1,0},{3,1},{2,3},{6,2},{4,6},{5,4},{7,5},{11,7},{9,11},{8,9},{10,... | collective-permute-start | bytes 3145736 | tf_op jit(solution)/shard_map/ppermute | solution.py:77
  386.2 3.1 collective-permute-start.32
  391.4 9.1 %collective-permute-start.33 = (bf16[4,2,72,256]{3,2,0,1:T(8,128)(2,1)S(1)}, bf16[4,2,72,256]{3,2,0,1:T(8,128)(2,1)S(1)}, u32[]{:S(2)}, u32[]{:S(2)}) collective-permute-start(bf16[4,2,72,256]{3,2,0,1:T(8,128)(2,1)S(1)} %fusion.14), channel_id=1, source_target_pairs={{0,1},{1,0},{2,3},{3,2},{4,5},{5,4},{6,7},{7,6},{8,9},{9,8},{10,11... | collective-permute-start | bytes 884744 | tf_op jit(solution)/shard_map/ppermute | solution.py:94
  391.5 9.2 %collective-permute-start.35 = (bf16[4,2,72,256]{3,2,1,0:T(8,128)(2,1)S(1)}, bf16[4,2,72,256]{3,2,1,0:T(8,128)(2,1)S(1)}, u32[]{:S(2)}, u32[]{:S(2)}) collective-permute-start(bf16[4,2,72,256]{3,2,1,0:T(8,128)(2,1)S(1)} %fusion.13), channel_id=1, source_target_pairs={{0,2},{1,3},{2,0},{3,1},{4,6},{5,7},{6,4},{7,5},{8,10},{9,11},{10,... | collective-permute-start | bytes 884744 | tf_op jit(solution)/shard_map/ppermute | solution.py:94
  400.6 5.2 %collective-permute-start.34 = (bf16[4,72,256]{2,1,0:T(8,128)(2,1)S(1)}, bf16[4,72,256]{2,1,0:T(8,128)(2,1)S(1)}, u32[]{:S(2)}, u32[]{:S(2)}) collective-permute-start(bf16[4,72,256]{2,1,0:T(8,128)(2,1)S(1)} %fusion.38), channel_id=1, source_target_pairs={{0,2},{1,3},{2,0},{3,1},{4,6},{5,7},{6,4},{7,5},{8,10},{9,11},{10,... | collective-permute-start | bytes 442376 | tf_op jit(solution)/shard_map/ppermute | solution.py:94
  400.8 5.2 %collective-permute-start.36 = (bf16[4,72,256]{2,1,0:T(8,128)(2,1)S(1)}, bf16[4,72,256]{2,1,0:T(8,128)(2,1)S(1)}, u32[]{:S(2)}, u32[]{:S(2)}) collective-permute-start(bf16[4,72,256]{2,1,0:T(8,128)(2,1)S(1)} %fusion.39), channel_id=1, source_target_pairs={{0,1},{1,0},{2,3},{3,2},{4,5},{5,4},{6,7},{7,6},{8,9},{9,8},{10,11... | collective-permute-start | bytes 442376 | tf_op jit(solution)/shard_map/ppermute | solution.py:94
  406.1 22.6 %collective-permute-start.44 = (bf16[2048,256]{1,0:T(8,128)(2,1)}, bf16[2048,256]{1,0:T(8,128)(2,1)}, u32[]{:S(2)}, u32[]{:S(2)}) collective-permute-start(bf16[2048,256]{1,0:T(8,128)(2,1)} %get-tuple-element.269), channel_id=1, source_target_pairs={{3,2},{2,3},{6,4},{4,5},{5,6},{11,8},{8,10},{10,11},{14,12},{15,13... | collective-permute-start | bytes 3145736 | tf_op jit(solution)/shard_map/ppermute | solution.py:937
  408.0 7.4 %collective-permute-start.37 = (bf16[1,144,256]{2,1,0:T(8,128)(2,1)S(1)}, bf16[1,144,256]{2,1,0:T(8,128)(2,1)S(1)}, u32[]{:S(2)}, u32[]{:S(2)}) collective-permute-start(bf16[1,144,256]{2,1,0:T(8,128)(2,1)S(1)} %get-tuple-element.316), channel_id=1, source_target_pairs={{0,4},{1,5},{2,6},{3,7},{4,0},{5,1},{6,2},{7,3},{8,12},{9,13},{10,... | collective-permute-start | bytes 221192 | tf_op jit(solution)/shard_map/ppermute | solution.py:94
  408.1 9.5 %collective-permute-start.39 = (bf16[1,144,256]{2,1,0:T(8,128)(2,1)S(1)}, bf16[1,144,256]{2,1,0:T(8,128)(2,1)S(1)}, u32[]{:S(2)}, u32[]{:S(2)}) collective-permute-start(bf16[1,144,256]{2,1,0:T(8,128)(2,1)S(1)} %get-tuple-element.317), channel_id=1, source_target_pairs={{0,12},{1,13},{2,14},{3,15},{4,8},{5,9},{6,10},{7,11},{8,4},{9,5},... | collective-permute-start | bytes 221192 | tf_op jit(solution)/shard_map/ppermute | solution.py:94
  413.7 6.1 %collective-permute-start.38 = (bf16[1,144,256]{2,1,0:T(8,128)(2,1)S(1)}, bf16[1,144,256]{2,1,0:T(8,128)(2,1)S(1)}, u32[]{:S(2)}, u32[]{:S(2)}) collective-permute-start(bf16[1,144,256]{2,1,0:T(8,128)(2,1)S(1)} %get-tuple-element.318), channel_id=1, source_target_pairs={{0,8},{1,9},{2,10},{3,11},{4,12},{5,13},{6,14},{7,15},{8,0},{9,1},... | collective-permute-start | bytes 221192 | tf_op jit(solution)/shard_map/ppermute | solution.py:94
  421.3 4.6 %collective-permute-start.41 = (f32[8,128]{1,0:T(8,128)S(1)}, f32[8,128]{1,0:T(8,128)S(1)}, u32[]{:S(2)}, u32[]{:S(2)}) collective-permute-start(f32[8,128]{1,0:T(8,128)S(1)} %iota.23), channel_id=1, source_target_pairs={{0,8},{1,9},{2,10},{3,11},{4,12},{5,13},{6,14},{7,15},{8,0},{9,1},... | collective-permute-start | bytes 12296 | tf_op jit(solution)/shard_map/ppermute | solution.py:94
  421.7 5.4 %collective-permute-start.42 = (f32[8,128]{1,0:T(8,128)S(1)}, f32[8,128]{1,0:T(8,128)S(1)}, u32[]{:S(2)}, u32[]{:S(2)}) collective-permute-start(f32[8,128]{1,0:T(8,128)S(1)} %iota.23), channel_id=1, source_target_pairs={{0,12},{1,13},{2,14},{3,15},{4,8},{5,9},{6,10},{7,11},{8,4},{9,5},... | collective-permute-start | bytes 12296 | tf_op jit(solution)/shard_map/ppermute | solution.py:94
  424.0 3.6 collective-permute-start.40
  428.8 9.8 %collective-permute-start.47 = (f32[8,128]{1,0:T(8,128)S(1)}, f32[8,128]{1,0:T(8,128)S(1)}, u32[]{:S(2)}, u32[]{:S(2)}) collective-permute-start(f32[8,128]{1,0:T(8,128)S(1)} %add.191), channel_id=1, source_target_pairs={{0,3},{1,2},{2,1},{3,0},{4,7},{5,6},{6,5},{7,4},{8,11},{9,10},{10,... | collective-permute-start | bytes 12296 | tf_op jit(solution)/shard_map/ppermute | solution.py:94
  433.7 4.9 %collective-permute-start.46 = (f32[8,128]{1,0:T(8,128)S(1)}, f32[8,128]{1,0:T(8,128)S(1)}, u32[]{:S(2)}, u32[]{:S(2)}) collective-permute-start(f32[8,128]{1,0:T(8,128)S(1)} %add.191), channel_id=1, source_target_pairs={{0,2},{1,3},{2,0},{3,1},{4,6},{5,7},{6,4},{7,5},{8,10},{9,11},{10,... | collective-permute-start | bytes 12296 | tf_op jit(solution)/shard_map/ppermute | solution.py:94
  433.7 4.9 %collective-permute-start.45 = (f32[8,128]{1,0:T(8,128)S(1)}, f32[8,128]{1,0:T(8,128)S(1)}, u32[]{:S(2)}, u32[]{:S(2)}) collective-permute-start(f32[8,128]{1,0:T(8,128)S(1)} %add.191), channel_id=1, source_target_pairs={{0,1},{1,0},{2,3},{3,2},{4,5},{5,4},{6,7},{7,6},{8,9},{9,8},{10,11... | collective-permute-start | bytes 12296 | tf_op jit(solution)/shard_map/ppermute | solution.py:94
  (23 other events, 267.3 us)
